TPU v7x, 32 devices: a whole 2x2x4 slice. The times are simulated.
32 devices in a mesh: ctx: 8 (over z, core), fsdp: 4 (over y, x).
Axes of the slice: x: 2, y: 2, z: 4, core: 2. Of those that a mesh axis runs over, the one named last changes fastest.
Arguments:
- inputs: bfloat16 [4, 2048, 2048], P(None, ('ctx', 'fsdp')), may hold values from -6 to 6
- cotangent: bfloat16 [4, 2048, 2048], P(None, ('ctx', 'fsdp')), may hold values from -6 to 6
- lengths: int32 [4], replicated, may hold values from 512 to 2048, as said below
- attn_gain: bfloat16 [2048], P('fsdp'), may hold values from 0.099609375 to 1.8984375
- w_qa: bfloat16 [2048, 1024], P('fsdp'), may hold values from -0.125 to 0.125
- q_gain: bfloat16 [1024], P('fsdp'), may hold values from 0.099609375 to 1.8984375
- w_qb: bfloat16 [1024, 4096], P('fsdp'), may hold values from -0.1875 to 0.1875
- w_k: bfloat16 [2048, 256], P('fsdp'), may hold values from -0.125 to 0.125
- w_v: bfloat16 [2048, 256], P('fsdp'), may hold values from -0.125 to 0.125
- w_o: bfloat16 [4096, 2048], P('fsdp'), may hold values from -1.5 to 1.5
- ffn_gain: bfloat16 [2048], P('fsdp'), may hold values from 0.099609375 to 1.8984375
- w_gate: bfloat16 [2048, 5632], P('fsdp'), may hold values from -0.125 to 0.125
- w_up: bfloat16 [2048, 5632], P('fsdp'), may hold values from -0.125 to 0.125
- w_down: bfloat16 [5632, 2048], P('fsdp'), may hold values from -0.078125 to 0.078125
Outputs:
- output: bfloat16 [4, 2048, 2048], P(None, ('ctx', 'fsdp'))
- input_grad: bfloat16 [4, 2048, 2048], P(None, ('ctx', 'fsdp'))
- grad_attn_gain: float32 [2048], P('fsdp')
- grad_w_qa: float32 [2048, 1024], P('fsdp')
- grad_q_gain: float32 [1024], P('fsdp')
- grad_w_qb: float32 [1024, 4096], P('fsdp')
- grad_w_k: float32 [2048, 256], P('fsdp')
- grad_w_v: float32 [2048, 256], P('fsdp')
- grad_w_o: float32 [4096, 2048], P('fsdp')
- grad_ffn_gain: float32 [2048], P('fsdp')
- grad_w_gate: float32 [2048, 5632], P('fsdp')
- grad_w_up: float32 [2048, 5632], P('fsdp')
- grad_w_down: float32 [5632, 2048], P('fsdp')
Inputs may be any that keep to these rules, and one draw needn't show every extreme that they name: The valid tokens of sequence s are its first lengths[s] slots; some sequence has all 2048 slots valid and another has a quarter of 2048.
All inputs are finite; a program needn't handle non-finite values.
Results may differ from a plain program's by a relative error of at most 0.023.
Values may be sent and summed in bfloat16 or wider, within the bound.
No kernel may reach another device: no remote copies, remote signals or barrier semaphores. Data moves between devices by JAX's collectives and lax.ppermute only.
A program may use at most 448 MiB of HBM per device.

v0:
```python
import math

import jax
import jax.numpy as jnp
from jax import lax
from jax.sharding import PartitionSpec as P

H = 16
HD = 256


EPS = 1e-05
THETA = 10000.0
NEG = -1e30
KEY_BLOCK = 1024


def rms_scale(values):
    return lax.rsqrt(jnp.mean(values * values, axis=-1, keepdims=True) + EPS)


def rotate_half(values):
    half = values.shape[-1] // 2
    return jnp.concatenate([-values[..., half:], values[..., :half]], axis=-1)


def rotary(values, cosine, sine):
    return values * cosine + rotate_half(values) * sine


def rotary_back(grads, cosine, sine):
    return grads * cosine - rotate_half(grads * sine)


def rope_tables(positions, width):
    half = width // 2
    freqs = THETA ** (-(jnp.arange(half, dtype=jnp.float32) * 2.0 / width))
    angle = positions.astype(jnp.float32)[:, None] * freqs[None, :]
    cosine = jnp.concatenate([jnp.cos(angle), jnp.cos(angle)], axis=-1)
    sine = jnp.concatenate([jnp.sin(angle), jnp.sin(angle)], axis=-1)
    return (cosine, sine)


def dot_rows(left, right):
    return lax.dot_general(
        left, right, (((0,), (0,)), ((), ())), preferred_element_type=jnp.float32
    )


def dot_back(left, right):
    return lax.dot_general(
        left, right, (((1,), (1,)), ((), ())), preferred_element_type=jnp.float32
    )


def norm_back(grad_out, values, scale, gain):
    weighted = grad_out * gain
    gain_grad = jnp.sum(grad_out * values * scale, axis=0)
    cubed = scale * scale * scale
    input_part = scale * weighted - values * cubed * jnp.mean(
        weighted * values, axis=-1, keepdims=True
    )
    return (input_part, gain_grad)


def key_split(count):
    block = math.gcd(count, KEY_BLOCK)
    return (block, count // block)


def on_device(
    inputs,
    cotangent,
    lengths,
    attn_gain,
    w_qa,
    q_gain,
    w_qb,
    w_k,
    w_v,
    w_o,
    ffn_gain,
    w_gate,
    w_up,
    w_down,
):
    seqs, span, width = inputs.shape
    heads = H
    head_dim = HD
    place = lax.axis_index(("ctx", "fsdp"))
    positions = place * span + jnp.arange(span, dtype=jnp.int32)
    last_pos = place * span + span - 1
    longest = jnp.max(lengths)
    valid = (positions[None, :] < lengths[:, None]).astype(jnp.float32)
    query_pos = jnp.tile(positions, heads)
    limits = lengths[:, None, None]
    gain_a, whole_qa, gain_q, whole_qb, whole_k, whole_v, whole_o = (
        lax.all_gather(attn_gain, "fsdp", axis=0, tiled=True),
        lax.all_gather(w_qa, "fsdp", axis=0, tiled=True),
        lax.all_gather(q_gain, "fsdp", axis=0, tiled=True),
        lax.all_gather(w_qb, "fsdp", axis=0, tiled=True),
        lax.all_gather(w_k, "fsdp", axis=0, tiled=True),
        lax.all_gather(w_v, "fsdp", axis=0, tiled=True),
        lax.all_gather(w_o, "fsdp", axis=0, tiled=True),
    )
    gain_f, whole_gate, whole_up, whole_down = (
        lax.all_gather(ffn_gain, "fsdp", axis=0, tiled=True),
        lax.all_gather(w_gate, "fsdp", axis=0, tiled=True),
        lax.all_gather(w_up, "fsdp", axis=0, tiled=True),
        lax.all_gather(w_down, "fsdp", axis=0, tiled=True),
    )
    rows = inputs.reshape(seqs * span, width).astype(jnp.float32)
    scale_a = rms_scale(rows)
    normed = (rows * scale_a * gain_a.astype(jnp.float32)).astype(jnp.bfloat16)
    query_low = jnp.dot(normed, whole_qa, preferred_element_type=jnp.float32)
    scale_q = rms_scale(query_low)
    query_norm = (query_low * scale_q * gain_q.astype(jnp.float32)).astype(jnp.bfloat16)
    queries = jnp.dot(query_norm, whole_qb, preferred_element_type=jnp.float32).reshape(
        seqs, span, heads, head_dim
    )
    cosine, sine = rope_tables(positions, head_dim)
    factor = head_dim ** (-0.5)
    scaled = (rotary(queries, cosine[:, None, :], sine[:, None, :]) * factor).astype(jnp.bfloat16)
    scaled = scaled.transpose(0, 2, 1, 3).reshape(seqs, heads * span, head_dim)
    key_proj = jnp.dot(normed, whole_k, preferred_element_type=jnp.float32).reshape(
        seqs, span, head_dim
    )
    keys = rotary(key_proj, cosine, sine).astype(jnp.bfloat16)
    values = (
        jnp.dot(normed, whole_v, preferred_element_type=jnp.float32)
        .astype(jnp.bfloat16)
        .reshape(seqs, span, head_dim)
    )

    def allowed_mask(start, block):
        key_pos = start + jnp.arange(block, dtype=jnp.int32)
        return (key_pos[None, None, :] <= query_pos[None, :, None]) & (
            key_pos[None, None, :] < limits
        )

    def split_piece(piece):
        piece_keys, piece_values = piece
        block, steps = key_split(piece_keys.shape[1])
        key_blocks = piece_keys.reshape(seqs, steps, block, head_dim).transpose(1, 0, 2, 3)
        value_blocks = piece_values.reshape(seqs, steps, block, head_dim).transpose(1, 0, 2, 3)
        offsets = jnp.arange(steps, dtype=jnp.int32) * block
        return (block, steps, key_blocks, value_blocks, offsets)

    start_state = (
        jnp.full((seqs, heads * span), NEG, jnp.float32),
        jnp.zeros((seqs, heads * span), jnp.float32),
        jnp.zeros((seqs, heads * span, head_dim), jnp.float32),
    )
    carry = start_state
    block, steps, key_blocks, value_blocks, offsets = split_piece(
        (
            lax.all_gather(keys, ("ctx", "fsdp"), axis=1, tiled=True),
            lax.all_gather(values, ("ctx", "fsdp"), axis=1, tiled=True),
        )
    )

    def forward_step_fn(state, items):
        key_block, value_block, offset = items
        first = offset

        def forward_work(current):
            best, total, accum = current
            scores = jnp.einsum(
                "sqd,skd->sqk", scaled, key_block, preferred_element_type=jnp.float32
            )
            allowed = allowed_mask(first, block)
            masked = jnp.where(allowed, scores, NEG)
            new_best = jnp.maximum(best, jnp.max(masked, axis=-1))
            weights = jnp.where(allowed, jnp.exp(masked - new_best[..., None]), 0.0)
            shrink = jnp.exp(best - new_best)
            total = total * shrink + jnp.sum(weights, axis=-1)
            accum = accum * shrink[..., None] + jnp.einsum(
                "sqk,skd->sqd",
                weights.astype(jnp.bfloat16),
                value_block,
                preferred_element_type=jnp.float32,
            )
            return (new_best, total, accum)

        def forward_skip(current):
            return current

        needed = (first <= last_pos) & (first < longest)
        return (lax.cond(needed, forward_work, forward_skip, state), None)

    carry, unused = lax.scan(forward_step_fn, carry, (key_blocks, value_blocks, offsets))
    best, total, accum = carry
    attended = accum / total[..., None]
    log_total = best + jnp.log(total)
    attn_out = (
        attended.reshape(seqs, heads, span, head_dim)
        .transpose(0, 2, 1, 3)
        .reshape(seqs * span, heads * head_dim)
        .astype(jnp.bfloat16)
    )
    hidden = rows + jnp.dot(attn_out, whole_o, preferred_element_type=jnp.float32)
    scale_f = rms_scale(hidden)
    ffn_in = (hidden * scale_f * gain_f.astype(jnp.float32)).astype(jnp.bfloat16)
    gate = jnp.dot(ffn_in, whole_gate, preferred_element_type=jnp.float32)
    upper = jnp.dot(ffn_in, whole_up, preferred_element_type=jnp.float32)
    sigma = jax.nn.sigmoid(gate)
    swish = gate * sigma
    inner = (swish * upper).astype(jnp.bfloat16)
    output = (
        (hidden + jnp.dot(inner, whole_down, preferred_element_type=jnp.float32))
        .astype(jnp.bfloat16)
        .reshape(seqs, span, width)
    )
    gain_f, whole_gate, whole_up, whole_down = (
        lax.all_gather(ffn_gain, "fsdp", axis=0, tiled=True),
        lax.all_gather(w_gate, "fsdp", axis=0, tiled=True),
        lax.all_gather(w_up, "fsdp", axis=0, tiled=True),
        lax.all_gather(w_down, "fsdp", axis=0, tiled=True),
    )
    signal = (cotangent.astype(jnp.float32) * valid[:, :, None]).reshape(seqs * span, width)
    signal_low = signal.astype(jnp.bfloat16)
    d_inner = dot_back(signal_low, whole_down)
    d_gate = (d_inner * upper * sigma * (1.0 + gate * (1.0 - sigma))).astype(jnp.bfloat16)
    d_upper = (d_inner * swish).astype(jnp.bfloat16)
    d_ffn = dot_back(d_gate, whole_gate) + dot_back(d_upper, whole_up)
    d_norm_f, grad_gain_f = norm_back(d_ffn, hidden, scale_f, gain_f.astype(jnp.float32))
    d_hidden = signal + d_norm_f
    gain_a, whole_qa, gain_q, whole_qb, whole_k, whole_v, whole_o = (
        lax.all_gather(attn_gain, "fsdp", axis=0, tiled=True),
        lax.all_gather(w_qa, "fsdp", axis=0, tiled=True),
        lax.all_gather(q_gain, "fsdp", axis=0, tiled=True),
        lax.all_gather(w_qb, "fsdp", axis=0, tiled=True),
        lax.all_gather(w_k, "fsdp", axis=0, tiled=True),
        lax.all_gather(w_v, "fsdp", axis=0, tiled=True),
        lax.all_gather(w_o, "fsdp", axis=0, tiled=True),
    )
    d_hidden_low = d_hidden.astype(jnp.bfloat16)
    d_attn = dot_back(d_hidden_low, whole_o)
    d_attended = (
        d_attn.reshape(seqs, span, heads, head_dim)
        .transpose(0, 2, 1, 3)
        .reshape(seqs, heads * span, head_dim)
        .astype(jnp.bfloat16)
    )
    delta = jnp.sum(d_attended.astype(jnp.float32) * attended, axis=-1)
    d_query = jnp.zeros((seqs, heads * span, head_dim), jnp.float32)
    backward_block, steps, key_blocks, value_blocks, offsets = split_piece(
        (
            lax.all_gather(keys, ("ctx", "fsdp"), axis=1, tiled=True),
            lax.all_gather(values, ("ctx", "fsdp"), axis=1, tiled=True),
        )
    )

    def backward_step_fn(d_query_now, items):
        key_block, value_block, offset = items
        first = offset

        def backward_work(d_now):
            scores = jnp.einsum(
                "sqd,skd->sqk", scaled, key_block, preferred_element_type=jnp.float32
            )
            allowed = allowed_mask(first, backward_block)
            probs = jnp.where(
                allowed, jnp.exp(jnp.where(allowed, scores, NEG) - log_total[..., None]), 0.0
            )
            d_probs = jnp.einsum(
                "sqd,skd->sqk", d_attended, value_block, preferred_element_type=jnp.float32
            )
            d_scores = (probs * (d_probs - delta[..., None])).astype(jnp.bfloat16)
            d_now = d_now + jnp.einsum(
                "sqk,skd->sqd", d_scores, key_block, preferred_element_type=jnp.float32
            )
            key_part = jnp.einsum(
                "sqk,sqd->skd", d_scores, scaled, preferred_element_type=jnp.float32
            )
            value_part = jnp.einsum(
                "sqk,sqd->skd",
                probs.astype(jnp.bfloat16),
                d_attended,
                preferred_element_type=jnp.float32,
            )
            return (d_now, (key_part, value_part))

        def backward_skip(d_now):
            empty = jnp.zeros((seqs, backward_block, head_dim), jnp.float32)
            return (d_now, (empty, empty))

        needed = (first <= last_pos) & (first < longest)
        return lax.cond(needed, backward_work, backward_skip, d_query_now)

    d_query, parts = lax.scan(backward_step_fn, d_query, (key_blocks, value_blocks, offsets))
    key_parts = parts[0].transpose(1, 0, 2, 3).reshape(seqs, steps * backward_block, head_dim)
    value_parts = parts[1].transpose(1, 0, 2, 3).reshape(seqs, steps * backward_block, head_dim)
    key_grads = key_parts
    value_grads = value_parts
    d_query, key_grads, value_grads = (d_query, key_grads, value_grads)
    own_key_grads, own_value_grads = (
        lax.psum_scatter(key_grads, ("ctx", "fsdp"), scatter_dimension=1, tiled=True),
        lax.psum_scatter(value_grads, ("ctx", "fsdp"), scatter_dimension=1, tiled=True),
    )
    d_keys = (
        rotary_back(own_key_grads, cosine, sine).astype(jnp.bfloat16).reshape(seqs * span, head_dim)
    )
    d_values = own_value_grads.astype(jnp.bfloat16).reshape(seqs * span, head_dim)
    d_scaled = d_query.reshape(seqs, heads, span, head_dim).transpose(0, 2, 1, 3)
    d_queries = (
        (rotary_back(d_scaled, cosine[:, None, :], sine[:, None, :]) * factor)
        .astype(jnp.bfloat16)
        .reshape(seqs * span, heads * head_dim)
    )
    d_query_norm = dot_back(d_queries, whole_qb)
    d_query_low, grad_gain_q = norm_back(
        d_query_norm, query_low, scale_q, gain_q.astype(jnp.float32)
    )
    d_query_low = d_query_low.astype(jnp.bfloat16)
    d_normed = (
        dot_back(d_query_low, whole_qa) + dot_back(d_keys, whole_k) + dot_back(d_values, whole_v)
    )
    d_rows, grad_gain_a = norm_back(d_normed, rows, scale_a, gain_a.astype(jnp.float32))
    input_grad = (d_hidden + d_rows).astype(jnp.bfloat16).reshape(seqs, span, width)
    (
        group_signal,
        group_gate,
        group_upper,
        group_hidden,
        group_queries,
        group_query_low,
        group_keys,
        group_values,
    ) = (
        lax.all_gather(signal_low, "fsdp", axis=0, tiled=True),
        lax.all_gather(d_gate, "fsdp", axis=0, tiled=True),
        lax.all_gather(d_upper, "fsdp", axis=0, tiled=True),
        lax.all_gather(d_hidden_low, "fsdp", axis=0, tiled=True),
        lax.all_gather(d_queries, "fsdp", axis=0, tiled=True),
        lax.all_gather(d_query_low, "fsdp", axis=0, tiled=True),
        lax.all_gather(d_keys, "fsdp", axis=0, tiled=True),
        lax.all_gather(d_values, "fsdp", axis=0, tiled=True),
    )
    own_inner, own_ffn_in, own_attn_out, own_query_norm, own_normed = (
        lax.all_to_all(inner, "fsdp", split_axis=1, concat_axis=0, tiled=True),
        lax.all_to_all(ffn_in, "fsdp", split_axis=1, concat_axis=0, tiled=True),
        lax.all_to_all(attn_out, "fsdp", split_axis=1, concat_axis=0, tiled=True),
        lax.all_to_all(query_norm, "fsdp", split_axis=1, concat_axis=0, tiled=True),
        lax.all_to_all(normed, "fsdp", split_axis=1, concat_axis=0, tiled=True),
    )
    gain_parts = (
        lax.psum_scatter(grad_gain_a, "fsdp", scatter_dimension=0, tiled=True),
        lax.psum_scatter(grad_gain_q, "fsdp", scatter_dimension=0, tiled=True),
        lax.psum_scatter(grad_gain_f, "fsdp", scatter_dimension=0, tiled=True),
    )
    pieces = (
        gain_parts[0],
        dot_rows(own_normed, group_query_low),
        gain_parts[1],
        dot_rows(own_query_norm, group_queries),
        dot_rows(own_normed, group_keys),
        dot_rows(own_normed, group_values),
        dot_rows(own_attn_out, group_hidden),
        gain_parts[2],
        dot_rows(own_ffn_in, group_gate),
        dot_rows(own_ffn_in, group_upper),
        dot_rows(own_inner, group_signal),
    )
    totals = (
        lax.psum(pieces[0].astype(jnp.bfloat16), "ctx").astype(jnp.float32),
        lax.psum(pieces[1].astype(jnp.bfloat16), "ctx").astype(jnp.float32),
        lax.psum(pieces[2].astype(jnp.bfloat16), "ctx").astype(jnp.float32),
        lax.psum(pieces[3].astype(jnp.bfloat16), "ctx").astype(jnp.float32),
        lax.psum(pieces[4].astype(jnp.bfloat16), "ctx").astype(jnp.float32),
        lax.psum(pieces[5].astype(jnp.bfloat16), "ctx").astype(jnp.float32),
        lax.psum(pieces[6].astype(jnp.bfloat16), "ctx").astype(jnp.float32),
        lax.psum(pieces[7].astype(jnp.bfloat16), "ctx").astype(jnp.float32),
        lax.psum(pieces[8].astype(jnp.bfloat16), "ctx").astype(jnp.float32),
        lax.psum(pieces[9].astype(jnp.bfloat16), "ctx").astype(jnp.float32),
        lax.psum(pieces[10].astype(jnp.bfloat16), "ctx").astype(jnp.float32),
    )
    return (
        output,
        input_grad,
        totals[0],
        totals[1],
        totals[2],
        totals[3],
        totals[4],
        totals[5],
        totals[6],
        totals[7],
        totals[8],
        totals[9],
        totals[10],
    )


def solution(mesh):
    in_specs = (
        P(None, ("ctx", "fsdp"), None),
        P(None, ("ctx", "fsdp"), None),
        P(),
        P("fsdp"),
        P("fsdp", None),
        P("fsdp"),
        P("fsdp", None),
        P("fsdp", None),
        P("fsdp", None),
        P("fsdp", None),
        P("fsdp"),
        P("fsdp", None),
        P("fsdp", None),
        P("fsdp", None),
    )
    out_specs = (
        P(None, ("ctx", "fsdp"), None),
        P(None, ("ctx", "fsdp"), None),
        P("fsdp"),
        P("fsdp", None),
        P("fsdp"),
        P("fsdp", None),
        P("fsdp", None),
        P("fsdp", None),
        P("fsdp", None),
        P("fsdp"),
        P("fsdp", None),
        P("fsdp", None),
        P("fsdp", None),
    )
    return jax.shard_map(
        on_device, mesh=mesh, in_specs=in_specs, out_specs=out_specs, check_vma=False
    )
```

profile of v0, /device:TPU:0, one launch (start us, length us, event | category | flops | bytes accessed | tf_op | source)
XLA Modules:
  0.0 2771.2 jit_solution(2648767950662481227)
XLA Ops:
  10.1 9.5 all-gather
  22.1 17.2 all-gather.20.cloned.1.call-done
  42.5 25.3 all-gather.28.cloned.1.call-done
  78.4 8.0 all-gather.1
  87.1 7.1 all-gather.2
  94.8 27.6 all-gather.24.cloned.1.call-done
  127.0 60.9 %all-gather.22.cloned.1.call-done = bf16[4,2048,256]{2,1,0:T(8,128)(2,1)} async-done(((bf16[4,64,256]{2,1,0:T(8,128)(2,1)}), bf16[4,2048,256]{2,1,0:T(8,128)(2,1)}) %all-gather.22.cloned.1.call-update) | async-done | bytes 4194320 | tf_op jit(solution)/shard_map/all_gather | solution.py:157
  192.3 59.8 %all-gather.30.cloned.1.call-done = bf16[4,2048,256]{2,1,0:T(8,128)(2,1)} async-done(((bf16[4,64,256]{2,1,0:T(8,128)(2,1)}), bf16[4,2048,256]{2,1,0:T(8,128)(2,1)}) %all-gather.30.cloned.1.call-update) | async-done | bytes 4194320 | tf_op jit(solution)/shard_map/all_gather | solution.py:158
  256.6 83.7 %all-gather.26.cloned.1.call-done = bf16[1024,4096]{1,0:T(8,128)(2,1)} async-done(((bf16[256,4096]{1,0:T(8,128)(2,1)}), bf16[1024,4096]{1,0:T(8,128)(2,1)}) %all-gather.26.cloned.1.call-update) | async-done | bytes 8388624 | tf_op jit(solution)/shard_map/all_gather | solution.py:101
  340.3 5.7 fusion.82
  352.8 31.7 %while.33 = (s32[]{:T(128)}, f32[4,1024]{1,0:T(4,128)S(1)}, f32[4,1024]{1,0:T(4,128)S(1)}, f32[4,1024,256]{2,1,0:T(8,128)}, s32[2]{0:T(128)S(1)}, /*index=5*/s32...) while((s32[]{:T(128)}, f32[4,1024]{1,0:T(4,128)S(1)}, ...), condition=%wide.region_8.9_spmd.clone, body=%wide.region_3.8_spmd.clone.sunk | while | flops 4352652288 | bytes 170178192 | solution.py:191
  355.4 26.6 conditional.6
  356.9 5.0 fusion.4
  362.0 5.4 fusion.6
  369.1 10.9 multiply_add_fusion
  392.3 107.3 %all-gather.32.cloned.1.call-done = bf16[4096,2048]{1,0:T(8,128)(2,1)} async-done(((bf16[1024,2048]{1,0:T(8,128)(2,1)}), bf16[4096,2048]{1,0:T(8,128)(2,1)}) %all-gather.32.cloned.1.call-update) | async-done | bytes 16777232 | tf_op jit(solution)/shard_map/all_gather | solution.py:104
  499.6 11.6 multiply_reduce_fusion.3
  512.8 199.2 %all-gather.34.cloned.1.call-done = bf16[2048,5632]{1,0:T(8,128)(2,1)} async-done(((bf16[512,5632]{1,0:T(8,128)(2,1)}), bf16[2048,5632]{1,0:T(8,128)(2,1)}) %all-gather.34.cloned.1.call-update) | async-done | bytes 23068688 | tf_op jit(solution)/shard_map/all_gather | solution.py:108
  712.0 14.3 fusion.83
  726.3 198.0 %all-gather.36.cloned.1.call-done = bf16[2048,5632]{1,0:T(8,128)(2,1)} async-done(((bf16[512,5632]{1,0:T(8,128)(2,1)}), bf16[2048,5632]{1,0:T(8,128)(2,1)}) %all-gather.36.cloned.1.call-update) | async-done | bytes 23068688 | tf_op jit(solution)/shard_map/all_gather | solution.py:109
  924.3 12.8 fusion.84
  937.1 199.4 %all-gather.38.cloned.1.call-done = bf16[5632,2048]{1,0:T(8,128)(2,1)} async-done(((bf16[1408,2048]{1,0:T(8,128)(2,1)}), bf16[5632,2048]{1,0:T(8,128)(2,1)}) %all-gather.38.cloned.1.call-update) | async-done | bytes 23068688 | tf_op jit(solution)/shard_map/all_gather | solution.py:110
  1136.5 26.2 multiply_convert_fusion
  1162.7 13.2 fusion.85
  1175.9 14.5 multiply_reduce_fusion.1
  1190.4 4.8 fusion.81
  1195.2 18.4 convolution_convert_fusion.4
  1222.0 79.5 %while.34 = (s32[]{:T(128)}, f32[4,1024,256]{2,1,0:T(8,128)}, f32[2,4,1024,256]{3,2,1,0:T(8,128)}, f32[2,4,1024,256]{3,2,0,1:T(8,128)}, s32[2]{0:T(128)S(1)}, /*...) while((s32[]{:T(128)}, f32[4,1024,256]{2,1,0:T(8,128)}, ...), condition=%wide.region_15.16_spmd.clone, body=%wide.region_12.15_spmd.clone.sunk | while | flops 10789852160 | bytes 210856720 | solution.py:291
  1225.0 50.4 %conditional.7 = (f32[4,1024,256]{2,1,0:T(8,128)}, f32[1,4,1024,256]{3,2,1,0:T(8,128)}, f32[1,4,1024,256]{3,2,1,0:T(8,128)}) conditional(s32[]{:T(128)} %convert_element_type.372, f32[4,1024,256]{2,1,0:T(8,128)} %get-tuple-element.847, (s32[]{:T(128)}, s32[64]{0:T(128)S(1)}, s32[4,1,1]{0,2,1:T(1,128)S(1)}, bf16[2,4,1024,256]{3,2,1,0:T(8,128)(2,1)}, ...), branch_computations={%region_13.13_spmd, %region_14.14_spmd} | conditional | flops 10789852160 | bytes 177300928 | solution.py:289
  1225.0 10.4 fusion.38
  1236.9 12.6 fusion.26
  1249.5 6.8 fusion.41
  1256.3 9.9 convolution_bitcast_fusion
  1266.2 9.2 fusion.32
  1280.0 4.7 constant_dynamic-update-slice_fusion.2
  1287.3 4.8 conditional.7
  1296.6 4.7 constant_dynamic-update-slice_fusion.2
  1301.5 4.6 multiply_bitcast_fusion
  1313.1 6.5 multiply_reduce_fusion.4
  1322.0 7.3 copy.78
  1342.9 10.5 all-to-all-done
  1353.4 4.6 all-to-all-start.4
  1366.8 29.8 %all-to-all-done.4 = bf16[256,4,1408]{2,0,1:T(8,128)(2,1)} async-done(((bf16[256,4,1408]{2,0,1:T(8,128)(2,1)}), bf16[256,4,1408]{2,0,1:T(8,128)(2,1)}, u32[]{:S(2)}, u32[]{:S(2)}) %all-to-all-start.4) | async-done | bytes 2883616 | tf_op jit(solution)/shard_map/all_to_all | solution.py:341
  1400.3 10.4 convolution_convert_fusion.2
  1410.7 25.0 all-gather.40.cloned.1.call-done
  1444.7 66.1 %all-gather.44.cloned.1.call-done = bf16[1024,2048]{1,0:T(8,128)(2,1)} async-done(((bf16[256,2048]{1,0:T(8,128)(2,1)}), bf16[1024,2048]{1,0:T(8,128)(2,1)}) %all-gather.44.cloned.1.call-update) | async-done | bytes 4194320 | tf_op jit(solution)/shard_map/all_gather | solution.py:334
  1510.9 9.4 convolution_convert_fusion.5
  1523.8 93.2 %all-gather.42.cloned.1.call-done = bf16[1024,4096]{1,0:T(8,128)(2,1)} async-done(((bf16[256,4096]{1,0:T(8,128)(2,1)}), bf16[1024,4096]{1,0:T(8,128)(2,1)}) %all-gather.42.cloned.1.call-update) | async-done | bytes 8388624 | tf_op jit(solution)/shard_map/all_gather | solution.py:335
  1617.1 7.1 convolution_convert_fusion.3
  1624.2 179.1 %reduce-scatter.3.cloned.1.call-done = f32[4,64,256]{2,1,0:T(8,128)} async-done(((f32[4,2048,256]{2,1,0:T(8,128)}), f32[4,64,256]{2,1,0:T(8,128)}) %reduce-scatter.3.cloned.1.call-update) | async-done | bytes 262160 | tf_op jit(solution)/shard_map/reduce_scatter | solution.py:298
  1805.3 185.2 %reduce-scatter.5.cloned.1.call-done = f32[4,64,256]{2,1,0:T(8,128)} async-done(((f32[4,2048,256]{2,1,0:T(8,128)}), f32[4,64,256]{2,1,0:T(8,128)}) %reduce-scatter.5.cloned.1.call-update) | async-done | bytes 262160 | tf_op jit(solution)/shard_map/reduce_scatter | solution.py:299
  1991.5 9.7 all_gather.91
  2001.1 14.2 all_gather.92
  2020.1 89.6 %all-gather.48.cloned.1.call-done = bf16[1024,5632]{1,0:T(8,128)(2,1)} async-done(((bf16[256,5632]{1,0:T(8,128)(2,1)}), bf16[1024,5632]{1,0:T(8,128)(2,1)}) %all-gather.48.cloned.1.call-update) | async-done | bytes 11534352 | tf_op jit(solution)/shard_map/all_gather | solution.py:333
  2109.8 12.3 convolution_convert_fusion
  2122.0 103.3 %all-gather.46.cloned.1.call-done = bf16[1024,5632]{1,0:T(8,128)(2,1)} async-done(((bf16[256,5632]{1,0:T(8,128)(2,1)}), bf16[1024,5632]{1,0:T(8,128)(2,1)}) %all-gather.46.cloned.1.call-update) | async-done | bytes 11534352 | tf_op jit(solution)/shard_map/all_gather | solution.py:332
  2225.3 12.3 convolution_convert_fusion.1
  2243.9 12.3 fusion.57
  2258.4 16.3 all-reduce.3
  2274.9 14.6 all-reduce.4
  2294.4 439.2 %all-reduce.8.cloned.1.call-done = (bf16[512,1024]{1,0:T(8,128)(2,1)}, bf16[256,4096]{1,0:T(8,128)(2,1)}, bf16[512,256]{1,0:T(8,128)(2,1)}, bf16[512,256]{1,0:T(...) async-done(((bf16[512,1024]{1,0:T(8,128)(2,1)}, bf16[256,4096]{1,0:T(8,128)(2,1)}, ...) | async-done | bytes 25165840 | tf_op jit(solution)/shard_map/psum | solution.py:367
  2733.6 8.7 convert_element_type.279
  2742.3 5.9 convert_element_type.281
  2748.2 6.0 convert_element_type.283
  (287 shorter events, 159.1 us)
Async XLA Ops:
  7.2 35.0 %copy-start.8 = (bf16[4,64,2048]{2,1,0:T(8,128)(2,1)S(1)}, bf16[4,64,2048]{2,1,0:T(8,128)(2,1)}, u32[]{:S(2)}) copy-start(bf16[4,64,2048]{2,1,0:T(8,128)(2,1)} %param.22) | copy-start | bytes 3145732
  7.2 32.0 %all-gather.20.cloned.1.call-start = ((), (), s32[]{:S(2)}) async-start(), calls=%async_computation.7 | async-start | bytes 1310720 | tf_op jit(solution)/shard_map/all_gather | solution.py:102
  7.9 59.8 %all-gather.28.cloned.1.call-start = ((), (), s32[]{:S(2)}) async-start(), calls=%async_computation.11 | async-start | bytes 1310720 | tf_op jit(solution)/shard_map/all_gather | solution.py:103
  8.7 113.7 %all-gather.24.cloned.1.call-start = ((), (), s32[]{:S(2)}) async-start(), calls=%async_computation.9 | async-start | bytes 5242880 | tf_op jit(solution)/shard_map/all_gather | solution.py:99
  9.4 178.5 %all-gather.22.cloned.1.call-start = ((), (), s32[]{:S(2)}) async-start(), calls=%async_computation.8 | async-start | bytes 4325376 | tf_op jit(solution)/shard_map/all_gather | solution.py:157
  19.7 50.4 %copy-start.43 = (f32[4,1,512]{2,1,0:T(1,128)}, f32[4,1,512]{2,1,0:T(1,128)S(1)}, u32[]{:S(2)}) copy-start(f32[4,1,512]{2,1,0:T(1,128)S(1)} %convert_element_type.286) | copy-start | bytes 24580
  20.5 327.7 %copy-start.34 = (f32[64,256]{1,0:T(8,128)}, f32[64,256]{1,0:T(8,128)S(1)}, u32[]{:S(2)}) copy-start(f32[64,256]{1,0:T(8,128)S(1)} %get-tuple-element.602) | copy-start | bytes 196612
  20.5 327.7 %copy-start.36 = (f32[64,256]{1,0:T(8,128)}, f32[64,256]{1,0:T(8,128)S(1)}, u32[]{:S(2)}) copy-start(f32[64,256]{1,0:T(8,128)S(1)} %get-tuple-element.601) | copy-start | bytes 196612
  42.0 210.2 %all-gather.30.cloned.1.call-start = ((), (), s32[]{:S(2)}) async-start(), calls=%async_computation.12 | async-start | bytes 4325376 | tf_op jit(solution)/shard_map/all_gather | solution.py:158
  42.1 29.3 %copy-start.49 = (f32[256]{0:T(256)}, f32[256]{0:T(256)S(1)}, u32[]{:S(2)}) copy-start(f32[256]{0:T(256)S(1)} %rsqrt.38) | copy-start | bytes 3076
  70.1 270.2 %all-gather.26.cloned.1.call-start = ((), (), s32[]{:S(2)}) async-start(), calls=%async_computation.10 | async-start | bytes 10485760 | tf_op jit(solution)/shard_map/all_gather | solution.py:101
  70.7 428.9 %all-gather.32.cloned.1.call-start = ((), (), s32[]{:S(2)}) async-start(), calls=%async_computation.13 | async-start | bytes 20971520 | tf_op jit(solution)/shard_map/all_gather | solution.py:104
  71.4 640.5 %all-gather.34.cloned.1.call-start = ((), (), s32[]{:S(2)}) async-start(), calls=%async_computation.14 | async-start | bytes 28835840 | tf_op jit(solution)/shard_map/all_gather | solution.py:108
  72.2 852.1 %all-gather.36.cloned.1.call-start = ((), (), s32[]{:S(2)}) async-start(), calls=%async_computation.15 | async-start | bytes 28835840 | tf_op jit(solution)/shard_map/all_gather | solution.py:109
  72.9 1063.6 %all-gather.38.cloned.1.call-start = ((), (), s32[]{:S(2)}) async-start(), calls=%async_computation.16 | async-start | bytes 28835840 | tf_op jit(solution)/shard_map/all_gather | solution.py:110
  73.5 1326.8 %all-gather.50.cloned.1.call-start = ((), (), s32[]{:S(2)}) async-start(), calls=%async_computation.24 | async-start | bytes 5242880 | tf_op jit(solution)/shard_map/all_gather | solution.py:331
  75.7 2.7 copy-start.58
  75.7 11.4 copy-start.57
  76.8 1359.0 %all-gather.40.cloned.1.call-start = ((), (), s32[]{:S(2)}) async-start(), calls=%async_computation.19 | async-start | bytes 2621440 | tf_op jit(solution)/shard_map/all_gather | solution.py:336
  86.4 40.6 %copy-start.51 = (f32[4,1,256]{2,1,0:T(1,128)}, f32[4,1,256]{2,1,0:T(1,128)S(1)}, u32[]{:S(2)}) copy-start(f32[4,1,256]{2,1,0:T(1,128)S(1)} %convert_element_type.287) | copy-start | bytes 12292
  126.5 65.8 %copy-start.53 = (f32[256]{0:T(256)}, f32[256]{0:T(256)S(1)}, u32[]{:S(2)}) copy-start(f32[256]{0:T(256)S(1)} %get-tuple-element.589) | copy-start | bytes 3076
  127.0 213.3 %copy-start.33 = (bf16[256,1024]{1,0:T(8,128)(2,1)}, bf16[256,1024]{1,0:T(8,128)(2,1)S(1)}, u32[]{:S(2)}) copy-start(bf16[256,1024]{1,0:T(8,128)(2,1)S(1)} %multiply_convert_fusion.5) | copy-start | bytes 1572868
  362.0 7.1 copy-start
  362.0 7.1 copy-start.10
  499.6 12.9 copy-start.45
  512.8 199.2 %copy-start.27 = (bf16[256,2048]{1,0:T(8,128)(2,1)}, bf16[256,2048]{1,0:T(8,128)(2,1)S(1)}, u32[]{:S(2)}) copy-start(bf16[256,2048]{1,0:T(8,128)(2,1)S(1)} %multiply_convert_fusion.4) | copy-start | bytes 3145732
  726.3 410.2 %copy-start.23 = (bf16[256,2048]{1,0:T(8,128)(2,1)S(1)}, bf16[256,2048]{1,0:T(8,128)(2,1)}, u32[]{:S(2)}) copy-start(bf16[256,2048]{1,0:T(8,128)(2,1)} %bitcast_convert_fusion) | copy-start | bytes 3145732
  1195.2 18.4 copy-start.24
  1218.0 3.9 copy-start.16
  1222.0 79.5 %copy-start.35 = (f32[64,256]{1,0:T(8,128)S(1)}, f32[64,256]{1,0:T(8,128)}, u32[]{:S(2)}) copy-start(f32[64,256]{1,0:T(8,128)} %copy-done.34) | copy-start | bytes 196612
  1225.0 10.5 copy-start.7
  1236.9 12.6 copy-start.1
  1236.9 12.6 copy-start.4
  1256.3 9.9 copy-start.2
  1256.3 9.9 copy-start.17
  1280.0 4.7 copy-start.6
  1296.6 4.7 copy-start.6
  1312.9 6.7 copy-start.18
  1313.1 6.5 copy-start.56
  1320.7 190.2 %all-gather.44.cloned.1.call-start = ((), (), s32[]{:S(2)}) async-start(), calls=%async_computation.21 | async-start | bytes 5242880 | tf_op jit(solution)/shard_map/all_gather | solution.py:334
  1321.4 295.6 %all-gather.42.cloned.1.call-start = ((), (), s32[]{:S(2)}) async-start(), calls=%async_computation.20 | async-start | bytes 10485760 | tf_op jit(solution)/shard_map/all_gather | solution.py:335
  1322.0 481.3 %reduce-scatter.3.cloned.1.call-start = ((), (), s32[]{:S(2)}) async-start(), calls=%async_computation.17 | async-start | bytes 8650752 | tf_op jit(solution)/shard_map/reduce_scatter | solution.py:298
  1329.4 661.1 %reduce-scatter.5.cloned.1.call-start = ((), (), s32[]{:S(2)}) async-start(), calls=%async_computation.18 | async-start | bytes 8650752 | tf_op jit(solution)/shard_map/reduce_scatter | solution.py:299
  1330.0 3.3 copy-start.50
  1330.0 779.8 %all-gather.48.cloned.1.call-start = ((), (), s32[]{:S(2)}) async-start(), calls=%async_computation.23 | async-start | bytes 14417920 | tf_op jit(solution)/shard_map/all_gather | solution.py:333
  1330.6 894.7 %all-gather.46.cloned.1.call-start = ((), (), s32[]{:S(2)}) async-start(), calls=%async_computation.22 | async-start | bytes 14417920 | tf_op jit(solution)/shard_map/all_gather | solution.py:332
  1335.0 18.4 all-to-all-start
  1342.9 17.0 copy-start.14
  1353.4 43.2 %all-to-all-start.4 = ((bf16[256,4,1408]{2,0,1:T(8,128)(2,1)}), bf16[256,4,1408]{2,0,1:T(8,128)(2,1)}, u32[]{:S(2)}, u32[]{:S(2)}) async-start(bf16[256,4,1408]{2,0,1:T(8,128)(2,1)} %bitcast.240), calls=%async_computation.6 | async-start | bytes 5767168 | tf_op jit(solution)/shard_map/all_to_all | solution.py:341
  1362.1 3.6 copy-start.28
  1396.6 43.3 %all-to-all-start.2 = ((bf16[256,4,1024]{2,0,1:T(8,128)(2,1)}), bf16[256,4,1024]{2,0,1:T(8,128)(2,1)S(1)}, u32[]{:S(2)}, u32[]{:S(2)}) async-start(bf16[256,4,1024]{2,0,1:T(8,128)(2,1)} %copy.82), calls=%async_computation.4 | async-start | bytes 4194304 | tf_op jit(solution)/shard_map/all_to_all | solution.py:343
  1441.3 79.0 %all-to-all-start.1 = ((bf16[256,4,256]{2,0,1:T(8,128)(2,1)}), bf16[256,4,256]{2,0,1:T(8,128)(2,1)S(1)}, u32[]{:S(2)}, u32[]{:S(2)}) async-start(bf16[256,4,256]{2,0,1:T(8,128)(2,1)} %bitcast.260), calls=%async_computation.3 | async-start | bytes 1048576 | tf_op jit(solution)/shard_map/all_to_all | solution.py:344
  1520.3 499.9 %all-to-all-start.3 = ((bf16[256,4,512]{2,0,1:T(8,128)(2,1)}), bf16[256,4,512]{2,0,1:T(8,128)(2,1)S(1)}, u32[]{:S(2)}, u32[]{:S(2)}) async-start(bf16[256,4,512]{2,0,1:T(8,128)(2,1)} %bitcast.219), calls=%async_computation.5 | async-start | bytes 2097152 | tf_op jit(solution)/shard_map/all_to_all | solution.py:342
  1523.8 1209.8 %all-reduce.8.cloned.1.call-start = ((), (), s32[]{:S(2)}) async-start(), calls=%async_computation.25 | async-start | bytes 50331648 | tf_op jit(solution)/shard_map/psum | solution.py:367
  2237.6 6.3 copy-start.20
  2240.1 3.8 copy-start.30
  2243.9 12.3 copy-start.40
  2733.6 8.7 copy-start.21
  2733.6 14.7 slice-start
  2742.3 5.9 slice-start.1
  2748.2 6.0 copy-start.22
  2754.3 4.5 copy-start.31
  2758.7 4.1 copy-start.42
  2758.7 4.9 copy-start.41
  (24 other events, 35.1 us)
Sparse Core Ops, SparseCore 0:
  9.9 29.3 all-gather.19
  41.1 26.6 all-gather.27
  69.6 52.7 all-gather.23
  125.7 62.1 all-gather.21
  191.3 60.8 all-gather.29
  253.9 86.3 all-gather.25
  342.1 157.4 all-gather.31
  501.5 210.4 all-gather.33
  713.8 210.4 all-gather.35
  926.0 210.4 all-gather.37
  1138.9 52.6 all-gather.49
  1320.8 114.9 all-gather.39
  1437.6 73.2 all-gather.43
  1512.6 104.4 all-gather.41
  1619.8 183.4 reduce-scatter.2
  1806.0 184.4 reduce-scatter.4
  1992.2 117.5 all-gather.47
  2111.5 113.7 all-gather.45
  2237.7 495.8 all-reduce.7
where the time goes:
time: 2780 us; the launch traced here: 2770 us
  waiting for transfers between devices  2210 us (79%)
  matrix products  274 us (10%)
  local copies, waits for them, and re-layouts  89.8 us (3%)
  blocking collectives  79.3 us (3%)
  other arithmetic  75.8 us (3%)
    psum x1, waiting for transfers between devices, on_device(): lax.psum(pieces[1].astype(jnp.bfloat16), 'ctx').astype(jnp.float32)  439 us
    all_gather x1, waiting for transfers between devices, on_device(): lax.all_gather(w_down, 'fsdp', axis=0, tiled=True)  199 us
    all_gather x1, waiting for transfers between devices, on_device(): lax.all_gather(w_gate, 'fsdp', axis=0, tiled=True)  199 us
    all_gather x1, waiting for transfers between devices, on_device(): lax.all_gather(w_up, 'fsdp', axis=0, tiled=True)  198 us
    reduce_scatter x1, waiting for transfers between devices, on_device(): lax.psum_scatter(value_grads, ('ctx', 'fsdp'), scatter_dimension=1, tiled...  185 us
    reduce_scatter x1, waiting for transfers between devices, on_device(): lax.psum_scatter(key_grads, ('ctx', 'fsdp'), scatter_dimension=1, tiled=T...  179 us
    all_gather x1, waiting for transfers between devices, on_device(): lax.all_gather(w_o, 'fsdp', axis=0, tiled=True)  107 us
    all_gather x1, waiting for transfers between devices, on_device(): lax.all_gather(d_gate, 'fsdp', axis=0, tiled=True)  103 us
  transfers between devices with their start and end apart: 24, of which 20 were waited for; matrix products, arithmetic and copies ran while one was open for 14% of the time, Pallas kernels for 0%

commit v1 on v0

v1 whole, which is shorter than its diff:
```python
import jax
import jax.numpy as jnp
from jax import lax
from jax.experimental import pallas as pl
from jax.experimental.pallas import tpu as pltpu
from jax.sharding import PartitionSpec as P

H = 16
HD = 256
HALF = HD // 2

EPS = 1e-05
THETA = 10000.0
NEG = -1e30
F32 = jnp.float32
BF16 = jnp.bfloat16


def rms_scale(values):
    return lax.rsqrt(jnp.mean(values * values, axis=-1, keepdims=True) + EPS)


def rotate_half(values):
    half = values.shape[-1] // 2
    return jnp.concatenate([-values[..., half:], values[..., :half]], axis=-1)


def rotary(values, cosine, sine):
    return values * cosine + rotate_half(values) * sine


def rotary_back(grads, cosine, sine):
    return grads * cosine - rotate_half(grads * sine)


def half_tables(positions):
    freqs = THETA ** (-(jnp.arange(HALF, dtype=F32) * 2.0 / HD))
    angle = positions.astype(F32)[:, None] * freqs[None, :]
    return jnp.cos(angle), jnp.sin(angle)


def dot(left, right):
    return jnp.dot(left, right, preferred_element_type=F32)


def dot_rows(left, right):
    return lax.dot_general(left, right, (((0,), (0,)), ((), ())), preferred_element_type=F32)


def dot_back(left, right):
    return lax.dot_general(left, right, (((1,), (1,)), ((), ())), preferred_element_type=F32)


def norm_back(grad_out, values, scale, gain):
    weighted = grad_out * gain
    gain_grad = jnp.sum(grad_out * values * scale, axis=0)
    cubed = scale * scale * scale
    input_part = scale * weighted - values * cubed * jnp.mean(
        weighted * values, axis=-1, keepdims=True
    )
    return (input_part, gain_grad)


def group_place(size, axis, block, span, index):
    shape = (size, 1) if axis == 0 else (1, size)
    inside = lax.rem(lax.broadcasted_iota(jnp.int32, shape, axis), block)
    return ((inside // span) ^ index) * span + lax.rem(inside, span)


def key_block(info_ref, step, depth):
    place, core = info_ref[0], info_ref[2]
    parity = jnp.where(step < depth, core, 1 - core)
    return 2 * (place // 2 - lax.rem(step, depth)) + parity


def allowed_keys(keys_at, place, limit, rows, block, span, index):
    own = jnp.where(keys_at == place, group_place(rows, 1, block, span, index), block)
    bound = jnp.minimum(own, limit - keys_at * block - 1)
    return group_place(block, 0, block, span, index) <= bound


def cheap():
    return pl.CostEstimate(flops=1, bytes_accessed=1, transcendentals=0)


def attend_forward(info, queries, kv_near, kv_far, cosine, sine):
    groups, seqs, span, columns = queries.shape
    heads = columns // HD
    block = groups * span
    depth = kv_near.shape[1]
    steps = 2 * depth
    rows = heads * block
    factor = HD ** (-0.5)

    def kernel(info_ref, q_ref, near_ref, far_ref, cos_ref, sin_ref, out_ref, scaled_ref, lse_ref, q_s, m_s, l_s, acc_s):
        seq, step = pl.program_id(0), pl.program_id(1)
        place, index, limit = info_ref[0], info_ref[1], info_ref[3 + seq]

        @pl.when(step == 0)
        def _():
            cosv, sinv = cos_ref[...], sin_ref[...]
            for h in range(heads):
                q = q_ref[:, 0, :, h * HD : (h + 1) * HD].reshape(block, HD)
                a, b = q[:, :HALF], q[:, HALF:]
                turned = jnp.concatenate(
                    [(a * cosv - b * sinv) * factor, (b * cosv + a * sinv) * factor], axis=1
                ).astype(BF16)
                q_s[h * block : (h + 1) * block, :] = turned
                scaled_ref[:, 0, :, h * HD : (h + 1) * HD] = turned.reshape(groups, span, HD)
            m_s[...] = jnp.full((1, rows), NEG, F32)
            l_s[...] = jnp.zeros((1, rows), F32)
            acc_s[...] = jnp.zeros((HD, rows), F32)

        keys_at = key_block(info_ref, step, depth)
        needed = (keys_at >= 0) & (keys_at <= place) & (keys_at * block < limit)

        def work(kv_ref):
            k = kv_ref[:, 0, 0, :, :HD].reshape(block, HD)
            v = kv_ref[:, 0, 0, :, HD:].reshape(block, HD)
            scores = dot_back(k, q_s[...])
            allowed = allowed_keys(keys_at, place, limit, rows, block, span, index)
            scores = jnp.where(allowed, scores, NEG)
            best = jnp.maximum(m_s[...], jnp.max(scores, axis=0, keepdims=True))
            weights = jnp.exp(scores - best)
            shrink = jnp.exp(m_s[...] - best)
            l_s[...] = l_s[...] * shrink + jnp.sum(weights, axis=0, keepdims=True)
            acc_s[...] = acc_s[...] * shrink + dot_rows(v, weights.astype(BF16))
            m_s[...] = best

        @pl.when(needed & (step < depth))
        def _():
            work(near_ref)

        @pl.when(needed & (step >= depth))
        def _():
            work(far_ref)

        @pl.when(step == steps - 1)
        def _():
            inverse = 1.0 / l_s[...]
            for h in range(heads):
                part = slice(h * block, (h + 1) * block)
                out = (acc_s[:, part] * inverse[:, part]).T.astype(BF16)
                out_ref[:, 0, :, h * HD : (h + 1) * HD] = out.reshape(groups, span, HD)
            lse_ref[0] = m_s[...] + jnp.log(l_s[...])

    tokens = pl.BlockSpec((groups, 1, span, columns), lambda s, t, i: (0, s, 0, 0))
    table = pl.BlockSpec((block, HALF), lambda s, t, i: (0, 0))
    shape = (groups, 1, 1, span, 2 * HD)
    near = pl.BlockSpec(shape, lambda s, t, i: (0, jnp.minimum(jnp.minimum(t, depth - 1), i[0] // 2), s, 0, 0))
    far = pl.BlockSpec(shape, lambda s, t, i: (0, jnp.minimum(jnp.maximum(t - depth, 0), i[0] // 2), s, 0, 0))
    return pl.pallas_call(
        kernel,
        grid_spec=pltpu.PrefetchScalarGridSpec(
            num_scalar_prefetch=1,
            grid=(seqs, steps),
            in_specs=[tokens, near, far, table, table],
            out_specs=[tokens, tokens, pl.BlockSpec((1, 1, rows), lambda s, t, i: (s, 0, 0))],
            scratch_shapes=[
                pltpu.VMEM((rows, HD), BF16),
                pltpu.VMEM((1, rows), F32),
                pltpu.VMEM((1, rows), F32),
                pltpu.VMEM((HD, rows), F32),
            ],
        ),
        out_shape=[
            jax.ShapeDtypeStruct(queries.shape, BF16),
            jax.ShapeDtypeStruct(queries.shape, BF16),
            jax.ShapeDtypeStruct((seqs, 1, rows), F32),
        ],
        compiler_params=pltpu.CompilerParams(dimension_semantics=("arbitrary", "arbitrary")),
        cost_estimate=cheap(),
        name="attend_forward",
    )(info, queries, kv_near, kv_far, cosine, sine)


def attend_backward(info, scaled, attn_out, d_attn, lse, kv_near, kv_far, cosine, sine, first, count):
    groups, _, span, columns = scaled.shape
    heads = columns // HD
    block = groups * span
    depth = kv_near.shape[1]
    steps = 2 * depth
    rows = heads * block
    factor = HD ** (-0.5)

    def kernel(info_ref, q_ref, o_ref, do_ref, lse_ref, near_ref, far_ref, cos_ref, sin_ref, dq_ref, dnear_ref, dfar_ref, q_s, do_s, delta_s, acc_s):
        seq, step = pl.program_id(0) + first, pl.program_id(1)
        place, index, limit = info_ref[0], info_ref[1], info_ref[3 + seq]

        @pl.when(step == 0)
        def _():
            for h in range(heads):
                part, lanes = slice(h * block, (h + 1) * block), slice(h * HD, (h + 1) * HD)
                q_s[part, :] = q_ref[:, 0, :, lanes].reshape(block, HD)
                grads = do_ref[:, 0, :, lanes].reshape(block, HD)
                do_s[part, :] = grads
                out = o_ref[:, 0, :, lanes].reshape(block, HD)
                both = jnp.sum(grads.astype(F32) * out.astype(F32), axis=1, keepdims=True)
                delta_s[:, part] = jnp.broadcast_to(both, (block, 128)).T[:1]
            acc_s[...] = jnp.zeros((HD, rows), F32)

        keys_at = key_block(info_ref, lax.rem(step + depth, steps), depth)
        needed = (keys_at >= 0) & (keys_at <= place) & (keys_at * block < limit)

        def work(kv_ref, dkv_ref):
            k = kv_ref[:, 0, 0, :, :HD].reshape(block, HD)
            v = kv_ref[:, 0, 0, :, HD:].reshape(block, HD)
            q, grads = q_s[...], do_s[...]
            scores = dot_back(k, q)
            allowed = allowed_keys(keys_at, place, limit, rows, block, span, index)
            probs = jnp.exp(jnp.where(allowed, scores, NEG) - lse_ref[0])
            d_probs = dot_back(v, grads)
            d_scores = (probs * (d_probs - delta_s[...])).astype(BF16)
            acc_s[...] += dot_rows(k, d_scores)
            dkv_ref[:, 0, 0, :, :HD] = dot(d_scores, q).astype(BF16).reshape(groups, span, HD)
            dkv_ref[:, 0, 0, :, HD:] = (
                dot(probs.astype(BF16), grads).astype(BF16).reshape(groups, span, HD)
            )

        for turn, kv_ref, dkv_ref in ((step < depth, far_ref, dfar_ref), (step >= depth, near_ref, dnear_ref)):

            @pl.when(needed & turn)
            def _():
                work(kv_ref, dkv_ref)

            @pl.when(jnp.logical_not(needed) & turn)
            def _():
                dkv_ref[...] = jnp.zeros(dkv_ref.shape, BF16)

        @pl.when(step == steps - 1)
        def _():
            cosv, sinv = cos_ref[...], sin_ref[...]
            for h in range(heads):
                y = acc_s[:, h * block : (h + 1) * block].T
                a, b = y[:, :HALF], y[:, HALF:]
                turned = jnp.concatenate(
                    [(a * cosv + b * sinv) * factor, (b * cosv - a * sinv) * factor], axis=1
                ).astype(BF16)
                dq_ref[:, 0, :, h * HD : (h + 1) * HD] = turned.reshape(groups, span, HD)

    tokens = pl.BlockSpec((groups, 1, span, columns), lambda s, t, i: (0, s + first, 0, 0))
    tokens_out = pl.BlockSpec((groups, 1, span, columns), lambda s, t, i: (0, s, 0, 0))
    table = pl.BlockSpec((block, HALF), lambda s, t, i: (0, 0))
    shape = (groups, 1, 1, span, 2 * HD)
    early = lambda t: jnp.minimum(t, depth - 1)
    late = lambda t: jnp.maximum(t - depth, 0)
    far = pl.BlockSpec(shape, lambda s, t, i: (0, jnp.minimum(early(t), i[0] // 2), s + first, 0, 0))
    near = pl.BlockSpec(shape, lambda s, t, i: (0, jnp.minimum(late(t), i[0] // 2), s + first, 0, 0))
    far_out = pl.BlockSpec(shape, lambda s, t, i: (0, early(t), s, 0, 0))
    near_out = pl.BlockSpec(shape, lambda s, t, i: (0, late(t), s, 0, 0))
    dkv_shape = jax.ShapeDtypeStruct((groups, depth, count, span, 2 * HD), BF16)
    return pl.pallas_call(
        kernel,
        grid_spec=pltpu.PrefetchScalarGridSpec(
            num_scalar_prefetch=1,
            grid=(count, steps),
            in_specs=[
                tokens,
                tokens,
                tokens,
                pl.BlockSpec((1, 1, rows), lambda s, t, i: (s + first, 0, 0)),
                near,
                far,
                table,
                table,
            ],
            out_specs=[tokens_out, near_out, far_out],
            scratch_shapes=[
                pltpu.VMEM((rows, HD), BF16),
                pltpu.VMEM((rows, HD), BF16),
                pltpu.VMEM((1, rows), F32),
                pltpu.VMEM((HD, rows), F32),
            ],
        ),
        out_shape=[jax.ShapeDtypeStruct((groups, count, span, columns), BF16), dkv_shape, dkv_shape],
        compiler_params=pltpu.CompilerParams(dimension_semantics=("arbitrary", "arbitrary")),
        cost_estimate=cheap(),
        name="attend_backward",
    )(info, scaled, attn_out, d_attn, lse, kv_near, kv_far, cosine, sine)


def feed_forward(x, signal, gu, down_w, last_kind):
    tokens, width = x.shape
    hidden = down_w.shape[0]
    shares, blocks, share, columns = gu.shape
    lanes = 128
    up_at = columns // 2 // lanes
    tile = 2 * lanes
    steps = -(-hidden // tile)
    tail = hidden - (steps - 1) * tile

    def kernel(x_ref, s_ref, ga_ref, gb_ref, ua_ref, ub_ref, d_ref, inner_ref, dg_ref, du_ref, y_ref, dx_ref, g_s, u_s, y_s, dx_s):
        step = pl.program_id(0)

        def work(size, start):
            for s in range(shares):
                for b in range(blocks):
                    at = slice((b * shares + s) * share, (b * shares + s + 1) * share)
                    g_s[at, :lanes] = ga_ref[s, b]
                    u_s[at, :lanes] = ua_ref[s, b]
                    if size > lanes:
                        g_s[at, lanes:] = gb_ref[s, b]
                        u_s[at, lanes:] = ub_ref[s, b]
            gate_tile, up_tile, down_tile = g_s[:, :size], u_s[:, :size], d_ref[:size, :]
            rows, grads = x_ref[...], s_ref[...]
            gate, upper = dot(rows, gate_tile), dot(rows, up_tile)
            d_inner = dot_back(grads, down_tile)
            sigma = jax.nn.sigmoid(gate)
            swish = gate * sigma
            inner = (swish * upper).astype(BF16)
            d_gate = (d_inner * upper * sigma * (1.0 + gate * (1.0 - sigma))).astype(BF16)
            d_upper = (d_inner * swish).astype(BF16)
            inner_ref[:, :size] = inner
            dg_ref[:, :size] = d_gate
            du_ref[:, :size] = d_upper
            y = dot(inner, down_tile)
            dx = dot_back(d_gate, gate_tile) + dot_back(d_upper, up_tile)
            if start:
                y_s[...] = y
                dx_s[...] = dx
            else:
                y_s[...] += y
                dx_s[...] += dx

        @pl.when(step == 0)
        def _():
            work(tile if steps > 1 else tail, True)

        if steps > 2:

            @pl.when((step > 0) & (step < steps - 1))
            def _():
                work(tile, False)

        if steps > 1:

            @pl.when(step == steps - 1)
            def _():
                work(tail, False)

        @pl.when(step == steps - 1)
        def _():
            y_ref[...] = y_s[...].astype(y_ref.dtype)
            dx_ref[...] = dx_s[...].astype(dx_ref.dtype)

    def lane_block(base, second):
        last = base + up_at - 1
        return pl.BlockSpec(
            (shares, blocks, share, lanes), lambda n: (0, 0, 0, jnp.minimum(base + 2 * n + second, last))
        )

    whole = pl.BlockSpec((tokens, width), lambda n: (0, 0))
    rows = pl.BlockSpec((tile, width), lambda n: (n, 0))
    out = pl.BlockSpec((tokens, tile), lambda n: (0, n))
    return pl.pallas_call(
        kernel,
        grid=(steps,),
        in_specs=[whole, whole, lane_block(0, 0), lane_block(0, 1), lane_block(up_at, 0), lane_block(up_at, 1), rows],
        out_specs=[out, out, out, whole, whole],
        scratch_shapes=[
            pltpu.VMEM((width, tile), BF16),
            pltpu.VMEM((width, tile), BF16),
            pltpu.VMEM((tokens, width), F32),
            pltpu.VMEM((tokens, width), F32),
        ],
        out_shape=[jax.ShapeDtypeStruct((tokens, hidden), BF16)] * 3
        + [jax.ShapeDtypeStruct((tokens, width), last_kind)] * 2,
        compiler_params=pltpu.CompilerParams(dimension_semantics=("arbitrary",)),
        cost_estimate=cheap(),
        name="feed_forward",
    )(x, signal, gu, gu, gu, gu, down_w)


def token_grad(info, lefts, rights):
    paired = isinstance(rights, tuple)
    count = len(lefts)
    tokens, height = lefts[0].shape
    width = rights[0][0].shape[1] if paired else rights[0].shape[1] // 2
    tile = 256 if height % 256 == 0 else height
    steps = height // tile
    columns = width if paired or steps > 1 or width % 512 else 512
    cuts = width // columns

    def kernel(info_ref, *refs):
        left_refs, right_refs, (own_ref, far_ref) = refs[:count], refs[count:-2], refs[-2:]
        turn, core = pl.program_id(0), info_ref[2]

        def put(chosen, out_ref):
            out_ref[...] = sum(dot_rows(l[...], r[...]) for l, r in zip(left_refs, chosen)).astype(BF16)

        def pair(chosen_core, chosen):
            @pl.when((turn == 0) & (core == 1 - chosen_core))
            def _():
                put(chosen, far_ref)

            @pl.when((turn == 1) & (core == chosen_core))
            def _():
                put(chosen, own_ref)

        if paired:
            pair(0, right_refs[:count])
            pair(1, right_refs[count:])
        else:

            @pl.when(turn == 0)
            def _():
                put(right_refs, far_ref)

            @pl.when(turn == 1)
            def _():
                put(right_refs, own_ref)

    def far_at(g, m):
        return m * (1 - g) + (steps * cuts - 1) * g

    left_spec = pl.BlockSpec((tokens, tile), lambda g, m, i: (0, m // cuts))
    if paired:
        right_specs = [pl.BlockSpec((tokens, width), lambda g, m, i: (0, 0))] * (2 * count)
        right_args = list(rights[0]) + list(rights[1])
    else:
        right_specs = [
            pl.BlockSpec((tokens, columns), lambda g, m, i: (0, (i[2] + 1 + g) % 2 * cuts + m % cuts))
        ] * count
        right_args = list(rights)
    return pl.pallas_call(
        kernel,
        grid_spec=pltpu.PrefetchScalarGridSpec(
            num_scalar_prefetch=1,
            grid=(2, steps * cuts),
            in_specs=[left_spec] * count + right_specs,
            out_specs=[
                pl.BlockSpec((tile, columns), lambda g, m, i: (m * g // cuts, m * g % cuts)),
                pl.BlockSpec((tile, columns), lambda g, m, i: (far_at(g, m) // cuts, far_at(g, m) % cuts)),
            ],
        ),
        out_shape=[jax.ShapeDtypeStruct((height, width), BF16)] * 2,
        compiler_params=pltpu.CompilerParams(dimension_semantics=("arbitrary", "arbitrary")),
        cost_estimate=cheap(),
        name="token_grad",
    )(info, *lefts, *right_args)


def project(info, inputs, own, pieces, others, cos_h, sin_h):
    seqs, span, width = inputs.shape
    tokens = seqs * span
    shard, columns = own.shape
    rank = columns - 2 * HD
    groups, part = width // shard, shard // 2
    q_part = rank // groups
    tile = min(512, columns)

    def kernel(info_ref, x_ref, own_ref, *refs):
        piece_refs, other_refs, refs = refs[: groups - 1], refs[groups - 1 : 2 * groups - 2], refs[2 * groups - 2 :]
        gain_ref, cos_ref, sin_ref, normed_ref, low_ref, norm_ref, kv_ref, gains_ref, acc_s, n_s, gain_s = refs
        index, core = info_ref[1], info_ref[2]
        for j in range(groups):
            row = gain_ref[j : j + 1, :].astype(F32)
            at = index ^ j
            gain_s[0:1, pl.ds(pl.multiple_of(at * shard, shard), shard)] = row[:, :shard]
            gain_s[1:2, pl.ds(pl.multiple_of(at * shard, shard), shard)] = row[:, shard : 2 * shard]
            gain_s[2:3, pl.ds(pl.multiple_of(at * q_part, q_part), q_part)] = row[
                :, 2 * shard : 2 * shard + q_part
            ]
        gains_ref[...] = gain_s[...]
        x = x_ref[...].reshape(tokens, width).astype(F32)
        scale = lax.rsqrt(jnp.mean(x * x, axis=1, keepdims=True) + EPS)
        normed = (x * scale * gain_s[0:1, :]).astype(BF16)
        n_s[...] = normed
        normed_ref[...] = normed
        for n in range(columns // tile):
            cut = slice(n * tile, (n + 1) * tile)
            at = pl.multiple_of(index * shard, shard)
            total = dot(n_s[:, pl.ds(at, shard)], own_ref[:, cut])
            for j in range(1, groups):
                base = (index ^ j) * shard
                at = pl.multiple_of(base + core * part, part)
                total += dot(n_s[:, pl.ds(at, part)], piece_refs[j - 1][:part, cut])
                at = pl.multiple_of(base + (1 - core) * part, part)
                total += dot(n_s[:, pl.ds(at, part)], other_refs[j - 1][:part, cut])
            acc_s[:, cut] = total
        low = acc_s[:, :rank]
        low_ref[...] = low
        scale_q = lax.rsqrt(jnp.mean(low * low, axis=1, keepdims=True) + EPS)
        norm_ref[...] = (low * scale_q * gain_s[2:3, :rank]).astype(BF16)
        cosv, sinv = cos_ref[...], sin_ref[...]
        for s in range(seqs):
            rows = slice(s * span, (s + 1) * span)
            a = acc_s[rows, rank : rank + HALF]
            b = acc_s[rows, rank + HALF : rank + HD]
            kv_ref[s, :, :HALF] = (a * cosv - b * sinv).astype(BF16)
            kv_ref[s, :, HALF:HD] = (b * cosv + a * sinv).astype(BF16)
            kv_ref[s, :, HD:] = acc_s[rows, rank + HD :].astype(BF16)

    gains = jnp.concatenate([p[part : part + 1] for p in pieces], axis=0)
    vmem = pl.BlockSpec(memory_space=pltpu.VMEM)
    return pl.pallas_call(
        kernel,
        in_specs=[pl.BlockSpec(memory_space=pltpu.SMEM)] + [vmem] * (2 * groups + 3),
        out_specs=[vmem] * 5,
        scratch_shapes=[
            pltpu.VMEM((tokens, columns), F32),
            pltpu.VMEM((tokens, width), BF16),
            pltpu.VMEM((8, width), F32),
        ],
        out_shape=[
            jax.ShapeDtypeStruct((tokens, width), BF16),
            jax.ShapeDtypeStruct((tokens, rank), F32),
            jax.ShapeDtypeStruct((tokens, rank), BF16),
            jax.ShapeDtypeStruct((seqs, span, 2 * HD), BF16),
            jax.ShapeDtypeStruct((8, width), F32),
        ],
        cost_estimate=cheap(),
        name="project",
    )(info, inputs, own, *pieces[1:], *others, gains, cos_h, sin_h)


def project_back(info, d_cat, own, pieces, others):
    tokens, columns = d_cat.shape
    shard = own.shape[0]
    groups, part = len(pieces), shard // 2
    width = groups * shard

    def kernel(info_ref, d_ref, own_ref, *refs):
        piece_refs, other_refs, out_ref = refs[: groups - 1], refs[groups - 1 : -1], refs[-1]
        index, core = info_ref[1], info_ref[2]
        d = d_ref[...]
        at = pl.multiple_of(index * shard, shard)
        out_ref[:, pl.ds(at, shard)] = dot_back(d, own_ref[...])
        for j in range(1, groups):
            base = (index ^ j) * shard
            at = pl.multiple_of(base + core * part, part)
            out_ref[:, pl.ds(at, part)] = dot_back(d, piece_refs[j - 1][:part, :])
            at = pl.multiple_of(base + (1 - core) * part, part)
            out_ref[:, pl.ds(at, part)] = dot_back(d, other_refs[j - 1][:part, :])

    vmem = pl.BlockSpec(memory_space=pltpu.VMEM)
    return pl.pallas_call(
        kernel,
        in_specs=[pl.BlockSpec(memory_space=pltpu.SMEM)] + [vmem] * (2 * groups),
        out_specs=vmem,
        out_shape=jax.ShapeDtypeStruct((tokens, width), F32),
        cost_estimate=cheap(),
        name="project_back",
    )(info, d_cat, own, *pieces[1:], *others)


def place_columns(info, mine, far, relative):
    groups = len(mine)
    rows, columns = mine[0].shape
    tile = min(rows, 64)

    def kernel(info_ref, *refs):
        first_ref, second_ref = refs[-2:]
        flag = info_ref[2] == 0
        for j in range(groups):
            a, b = refs[j][...].astype(F32), refs[groups + j][...].astype(F32)
            at = pl.ds(pl.multiple_of((info_ref[1] ^ j) * columns, 128), columns) if relative else slice(j * columns, (j + 1) * columns)
            first_ref[:, at] = jnp.where(flag, a, b)
            second_ref[:, at] = jnp.where(flag, b, a)

    block = pl.BlockSpec((tile, columns), lambda r, i: (r, 0))
    out = pl.BlockSpec((tile, groups * columns), lambda r, i: (r, 0))
    return pl.pallas_call(
        kernel,
        grid_spec=pltpu.PrefetchScalarGridSpec(
            num_scalar_prefetch=1, grid=(rows // tile,), in_specs=[block] * (2 * groups), out_specs=[out, out]
        ),
        out_shape=[jax.ShapeDtypeStruct((rows, groups * columns), F32)] * 2,
        cost_estimate=cheap(),
        name="place_columns",
    )(info, *mine, *far)


def solution(mesh):
    nf, nc = mesh.shape["fsdp"], mesh.shape["ctx"]
    nz = nc // 2

    def swap(x, j):
        return lax.ppermute(x, "fsdp", [(i, i ^ j) for i in range(nf)])

    @jax.named_scope("core_swap")
    def core_swap(x):
        return lax.ppermute(x, "ctx", [(i, i ^ 1) for i in range(nc)])

    def pick(x, index, axis=0):
        return lax.dynamic_index_in_dim(x, index, axis, keepdims=False)

    def half_of(x, index):
        size = x.shape[1] // 2
        return lax.dynamic_slice_in_dim(x, index * size, size, 1)

    def fence(*xs):
        return lax.optimization_barrier(xs)

    def add_low(a, b):
        return (a.astype(F32) + b.astype(F32)).astype(BF16)

    square = nf == 4

    def gather_first(x):
        return [swap(x, j) for j in ((1, 2) if square else range(1, nf))]

    def gather_second(got):
        if not square:
            return []
        half = got[0].shape[0] // 2
        return [swap(got[1][:half], 1), swap(got[0][half:], 2)]

    def gather_done(x, got, more):
        return [x, *got] + ([jnp.concatenate(more, axis=0)] if square else [])

    def scatter_first(parts):
        if not square:
            return [swap(parts[j].astype(BF16), j) for j in range(1, nf)]
        half = parts[3].shape[0] // 2
        return [swap(parts[3][:half].astype(BF16), 1), swap(parts[3][half:].astype(BF16), 2)]

    def scatter_second(parts, got):
        if not square:
            return got
        half = parts[1].shape[0] // 2
        one = jnp.concatenate([parts[1][:half].astype(BF16), add_low(parts[1][half:], got[1])], axis=0)
        two = jnp.concatenate([add_low(parts[2][:half], got[0]), parts[2][half:].astype(BF16)], axis=0)
        return [swap(one, 1), swap(two, 2)]

    def scatter_done(part, got):
        for item in got:
            part = part + item.astype(F32)
        return part

    def along(pairs):
        return [(2 * a + core, 2 * b + core) for a, b in pairs for core in range(2)]

    staged = nz == 4

    @jax.named_scope("line_in")
    def inward(x):
        return lax.ppermute(x, "ctx", along([(0, 1), (3, 2)])) if staged else x

    @jax.named_scope("line_across")
    def across(x):
        return lax.ppermute(x, "ctx", along([(1, 2), (2, 1)])) if staged else x

    @jax.named_scope("line_back")
    def back(x):
        return lax.ppermute(x, "ctx", along([(1, 0), (2, 3)])) if staged else x

    def joined(x, y):
        return add_low(x, y) if staged else x

    def settled(x, y):
        if staged:
            z = lax.axis_index("ctx") // 2
            return jnp.where((z == 1) | (z == 2), x, y)
        groups = [[2 * i + core for i in range(nz)] for core in range(2)]
        return lax.psum(x, "ctx", axis_index_groups=groups)

    class Line:
        def __init__(self):
            self.flight, self.done = [], {}

        def region(self, *values, new=()):
            values, arrived = fence(values, [item[3] for item in self.flight])
            flight = []
            for (key, stage, x, _), got in zip(self.flight, arrived):
                if stage == 2:
                    self.done[key] = settled(x, got)
                    continue
                x = joined(x, got)
                flight.append((key, stage + 1, x, across(x) if stage == 0 else back(x)))
            for key, x in new:
                x = x()
                flight.append((key, 0, x, inward(x)))
            self.flight = flight
            return values

    def on_device(inputs, cotangent, lengths, attn_gain, w_qa, q_gain, w_qb, w_k, w_v, w_o, ffn_gain, w_gate, w_up, w_down):
        seqs, span, width = inputs.shape
        tokens = seqs * span
        block = nf * span
        rank, head_cols = w_qa.shape[1], H * HD // nf
        hidden_cols = w_down.shape[0]
        shard = w_qa.shape[0]
        f, c = lax.axis_index("fsdp"), lax.axis_index("ctx")
        k = c % 2
        positions = (c * nf + f) * span + jnp.arange(span, dtype=jnp.int32)
        info = jnp.concatenate([jnp.stack([c, f, k]).astype(jnp.int32), lengths])
        valid = (positions[None, :] < lengths[:, None]).astype(F32)
        group_pos = c * block + jnp.concatenate(
            [(f ^ j) * span + jnp.arange(span, dtype=jnp.int32) for j in range(nf)]
        )
        cos_g, sin_g = half_tables(group_pos)
        cos_h, sin_h = cos_g[:span], sin_g[:span]
        cosine = jnp.concatenate([cos_h, cos_h], axis=-1)
        sine = jnp.concatenate([sin_h, sin_h], axis=-1)

        part = shard // 2
        gains = jnp.concatenate([attn_gain, ffn_gain, q_gain])
        cat_cols = rank + 2 * HD
        gain_rows = jnp.zeros((16, cat_cols), BF16).at[0, : gains.shape[0]].set(gains)
        cat = jnp.concatenate([w_qa, w_k, w_v], axis=1)
        mine = lax.dynamic_slice_in_dim(cat, k * part, part, 0)
        mine = jnp.concatenate([mine, gain_rows], axis=0)
        got = gather_first(mine)
        pieces = gather_done(mine, got, gather_second(got))
        others = [core_swap(p) for p in pieces[1:]]

        def turn(share, columns):
            rows_here = share.shape[0]
            share = lax.all_to_all(share, "fsdp", split_axis=1, concat_axis=0, tiled=True)
            return share.reshape(nf, rows_here, columns)

        def column_slice(turned):
            return turned.transpose(1, 0, 2, 3).reshape(-1, turned.shape[3])

        share = w_qb.shape[0] // nc
        qb = turn(lax.dynamic_slice_in_dim(w_qb, c * share, share, 0), head_cols)
        qb = lax.all_gather(qb, "ctx")
        share = shard // nc
        gu_pad = -hidden_cols % 128
        gu_share = jnp.concatenate(
            [
                jnp.pad(
                    lax.dynamic_slice_in_dim(w, c * share, share, 0).reshape(share, nf, hidden_cols),
                    ((0, 0), (0, 0), (0, gu_pad)),
                )
                for w in (w_gate, w_up)
            ],
            axis=2,
        )
        gu_cols = gu_share.shape[2]
        gu_share = gu_share.reshape(share, nf * gu_cols)
        signal = (cotangent.astype(F32) * valid[:, :, None]).reshape(tokens, width)
        signal_low = signal.astype(BF16)

        normed, query_low, query_norm, kv_own, gain_all = project(
            info, inputs, cat, pieces, others, cos_h, sin_h
        )
        gain_a, gain_f, gain_q = gain_all[0], gain_all[1], gain_all[2, :rank]
        rows = inputs.reshape(tokens, width).astype(F32)
        kv_own = kv_own.reshape(tokens, 2 * HD)

        kv_line = [
            lax.ppermute(kv_own, "ctx", [(i, i + 2 * s) for i in range(nc - 2 * s)]) for s in range(1, nz)
        ]
        norm_got = gather_first(query_norm)
        gu_share, kv_own = fence(gu_share, kv_own)
        gu = turn(gu_share, gu_cols)
        kv_line, norm_got, gu = fence(kv_line, norm_got, gu)
        gu = lax.all_gather(gu, "ctx")
        kv_mine = jnp.concatenate([kv_own] + kv_line, axis=0)
        kv_got = gather_first(kv_mine)
        norm_more = gather_second(norm_got)
        kv_got, norm_more, qb = fence(kv_got, norm_more, qb)
        qb = column_slice(qb)
        kv_more = gather_second(kv_got)
        norm_blocks = gather_done(query_norm, norm_got, norm_more)
        queries = dot(jnp.concatenate(norm_blocks, axis=0), qb).reshape(nf, seqs, span, head_cols)
        kv_more, queries, signal_low = fence(kv_more, queries, signal_low)
        kv_near = jnp.concatenate(gather_done(kv_mine, kv_got, kv_more), axis=0)
        kv_far = core_swap(kv_near)
        signal_got = [swap(signal_low, j) for j in range(1, nf)]
        kv_near = kv_near.reshape(nf, nz, seqs, span, 2 * HD)
        kv_far = kv_far.reshape(nf, nz, seqs, span, 2 * HD)
        attn_out, scaled, lse = attend_forward(info, queries, kv_near, kv_far, cos_g, sin_g)

        attn_blocks = [attn_out[j].reshape(tokens, head_cols) for j in range(nf)]
        o_parts = [None] * nf
        o_parts[nf - 1] = dot(attn_blocks[nf - 1], w_o).astype(BF16)
        if square:
            o_first = scatter_first(o_parts)
        o_parts[1:-1] = [dot(b, w_o) for b in attn_blocks[1:-1]]
        if not square:
            o_first = scatter_first(o_parts)
        o_first, o_parts[1:], signal_got = fence(o_first, o_parts[1:], signal_got)
        o_got = scatter_second(o_parts, o_first)
        o_parts[0] = dot(attn_blocks[0], w_o)
        o_got, o_parts[0], gu = fence(o_got, o_parts[0], gu)
        hidden = rows + scatter_done(o_parts[0], o_got)
        scale_f = rms_scale(hidden)
        ffn_in = (hidden * scale_f * gain_f).astype(BF16)

        weights = (gu, w_down)
        ffn_got = gather_first(ffn_in)
        done = [feed_forward(ffn_in, signal_low, *weights, F32)]
        ffn_got, first_dx = fence(ffn_got, done[0][4])
        ffn_more = gather_second(ffn_got)
        dffn_got = []
        for j, x in enumerate(ffn_got):
            done.append(feed_forward(x, signal_got[j], *weights, BF16))
            if j + 1 < len(ffn_got):
                ffn_got[j + 1], sent = fence(ffn_got[j + 1], done[-1][4])
            elif square:
                ffn_more, sent = fence(ffn_more, done[-1][4])
            else:
                sent = done[-1][4]
            dffn_got.append(swap(sent, j + 1))
        ffn_blocks = gather_done(ffn_in, ffn_got, ffn_more)
        if square:
            done.append(feed_forward(ffn_blocks[3], signal_got[2], *weights, BF16))
        inner_blocks, gate_blocks, up_blocks, y_parts, dx = (list(t) for t in zip(*done))
        late = fence(dx[nf - 1], ffn_blocks, gate_blocks, up_blocks)
        if square:
            dffn_got.append(swap(late[0], 3))

        gu_own, gu_far = token_grad(info, late[1], (late[2], late[3]))
        dffn_got, gu_own, gu_far = fence(dffn_got, gu_own, gu_far)
        gu_back = core_swap(gu_far)
        d_ffn = scatter_done(first_dx, dffn_got)
        d_norm_f, grad_gain_f = norm_back(d_ffn, hidden, scale_f, gain_f)
        d_hidden = signal + d_norm_f
        d_hidden_low = d_hidden.astype(BF16)
        line = Line()

        def rows_of(own, got, start, size):
            return lambda: add_low(own[start : start + size], got[start : start + size])

        def cuts_of(name, own, got, count):
            size = own.shape[0]
            step = -(-size // (128 * count)) * 128
            return [((name, i), rows_of(own, got, i * step, min(step, size - i * step))) for i in range(count)]

        d_hidden_low, gu_back = fence(d_hidden_low, gu_back)
        gu_cuts = cuts_of("gu", gu_own, gu_back, 5)

        line.region(new=gu_cuts[:1])
        dh_got = gather_first(d_hidden_low)
        signal_blocks = [signal_low] + signal_got
        down_lefts, down_rights, _ = fence(inner_blocks, signal_blocks, d_hidden_low)
        down_own, down_far = token_grad(info, down_lefts, down_rights)

        dh_got, down_own, down_far = line.region(dh_got, down_own, down_far, new=gu_cuts[1:2])
        dh_more = gather_second(dh_got)
        down_back = core_swap(down_far)
        d_attn = [dot_back(x, w_o).astype(BF16) for x in [d_hidden_low, *dh_got]]

        dh_more, down_back, d_attn, y_parts = line.region(dh_more, down_back, d_attn, y_parts, new=gu_cuts[2:3])
        dh_blocks = gather_done(d_hidden_low, dh_got, dh_more)
        d_attn += [dot_back(x, w_o).astype(BF16) for x in dh_blocks[len(d_attn) :]]
        d_attn = jnp.concatenate(d_attn, axis=0).reshape(nf, seqs, span, head_cols)
        y_got = [swap(y_parts[j], j) for j in range(1, nf)]
        down_cuts = cuts_of("down", down_own, down_back, 3)

        count = seqs // 2
        backward = (info, scaled, attn_out, d_attn, lse, kv_near, kv_far, cos_g, sin_g)
        dq_a, near_a, far_a = attend_backward(*backward, 0, count)
        dq_a, near_a, far_a, d_attn = line.region(dq_a, near_a, far_a, d_attn, new=gu_cuts[3:4])
        back_a = core_swap(far_a)
        backward = (info, scaled, attn_out, d_attn, lse, kv_near, kv_far, cos_g, sin_g)
        dq_b, near_b, far_b = attend_backward(*backward, count, seqs - count)
        dq_b, near_b, far_b, back_a = line.region(dq_b, near_b, far_b, back_a, new=gu_cuts[4:5])

        def kv_parts(near, far):
            total = near.astype(F32) + far.astype(F32)
            return [total[j].reshape(-1, 2 * HD) for j in range(nf)]

        back_b = core_swap(far_b)
        parts_a = kv_parts(near_a, back_a)
        first_a = scatter_first(parts_a)
        dq_blocks = [
            jnp.concatenate([dq_a[j], dq_b[j]], axis=0).reshape(tokens, head_cols) for j in range(nf)
        ]
        dq_parts = [dot_back(b, qb) for b in dq_blocks]
        first_a, back_b, dq_parts, attn_late = line.region(
            first_a, back_b, dq_parts, attn_blocks, new=down_cuts[:1]
        )

        got_a = scatter_second(parts_a, first_a)
        parts_b = kv_parts(near_b, back_b)
        first_b = scatter_first(parts_b)
        dq_first = scatter_first(dq_parts)
        o_own, o_far = token_grad(info, attn_late, dh_blocks)
        got_a, first_b, dq_first, o_own, o_far, norm_late = line.region(
            got_a, first_b, dq_first, o_own, o_far, norm_blocks, new=down_cuts[1:2]
        )

        def line_start(part, got):
            whole = scatter_done(part, got).reshape(nz, -1, 2 * HD)
            low = whole.astype(BF16)
            sent = [
                lax.ppermute(low[s], "ctx", [(i, i - 2 * s) for i in range(2 * s, nc)]) for s in range(1, nz)
            ]
            return whole[0], sent

        line_a, sent_a = line_start(parts_a[0], got_a)
        got_b = scatter_second(parts_b, first_b)
        dq_got = scatter_second(dq_parts, dq_first)
        o_back = core_swap(o_far)
        qb_own, qb_far = token_grad(info, norm_late, dq_blocks)
        sent_a, got_b, dq_got, o_back, qb_own, qb_far, normed_late, y_got = line.region(
            sent_a, got_b, dq_got, o_back, qb_own, qb_far, normed, y_got, new=down_cuts[2:3]
        )

        line_b, sent_b = line_start(parts_b[0], got_b)
        d_query_norm = scatter_done(dq_parts[0], dq_got)
        scale_q = rms_scale(query_low)
        d_query_low, grad_gain_q = norm_back(d_query_norm, query_low, scale_q, gain_q)
        d_query_low = d_query_low.astype(BF16)
        dql_got = gather_first(d_query_low)
        qb_back = core_swap(qb_far)
        output = (hidden + scatter_done(y_parts[0].astype(F32), y_got)).astype(BF16)
        output = output.reshape(seqs, span, width)
        normed_cols = lax.all_to_all(normed_late, "fsdp", split_axis=1, concat_axis=0, tiled=True)
        normed_cols = normed_cols.reshape(nf, tokens, shard)
        normed_rel = [pick(normed_cols, f ^ j) for j in range(nf)]
        o_cuts = cuts_of("o", o_own, o_back, 2)
        qb_cuts = cuts_of("qb", qb_own, qb_back, 1)
        sent_b, dql_got, qb_back, normed_rel = line.region(sent_b, dql_got, qb_back, normed_rel, new=o_cuts[:1])
        qb_cuts = cuts_of("qb", qb_own, qb_back, 1)

        dql_more = gather_second(dql_got)
        gu_done = jnp.concatenate([line.done["gu", i] for i in range(5)], axis=0)
        gu_done = gu_done.reshape(nf, shard, hidden_cols)
        if square:
            gu_mine = [pick(gu_done, f)] + [swap(pick(gu_done, f ^ j), j) for j in (1, 2)]
        else:
            gu_done = lax.all_to_all(gu_done, "fsdp", split_axis=0, concat_axis=0, tiled=True)
            gu_mine = [gu_done[j] for j in range(nf)]
        dkv_total = jnp.concatenate([scatter_done(line_a, sent_a), scatter_done(line_b, sent_b)], axis=0)
        d_keys = rotary_back(dkv_total[:, :HD].reshape(seqs, span, HD), cosine, sine)
        d_keys = d_keys.astype(BF16).reshape(tokens, HD)
        d_values = dkv_total[:, HD:].astype(BF16)
        d_cat = jnp.concatenate([d_query_low, d_keys, d_values], axis=1)
        d_normed = project_back(info, d_cat, cat, pieces, others)
        scale_a = rms_scale(rows)
        d_rows, grad_gain_a = norm_back(d_normed, rows, scale_a, gain_a)
        input_grad = (d_hidden + d_rows).astype(BF16).reshape(seqs, span, width)

        gain_parts = jnp.concatenate(
            [
                grad_gain_a.reshape(nf, shard),
                grad_gain_f.reshape(nf, shard),
                grad_gain_q.reshape(nf, rank // nf),
            ],
            axis=1,
        )
        gain_width = gain_parts.shape[1]
        lines = -(-gain_width // (2 * HD))
        gain_parts = jnp.pad(gain_parts, ((0, 0), (0, lines * 2 * HD - gain_width)))
        gain_tail = gain_parts.reshape(nf * lines, 2 * HD).astype(BF16)
        gain_tail = jnp.pad(gain_tail, ((0, 16 - nf * lines), (0, 0)))
        last = jnp.concatenate([d_cat[:, rank:], gain_tail], axis=0)
        last, dql_more = line.region(last, dql_more, new=qb_cuts)

        last_got = gather_first(last)
        dql_blocks = gather_done(d_query_low, dql_got, dql_more)
        qa_own, qa_far = token_grad(info, normed_rel, dql_blocks)
        last_got, qa_own, qa_far, gu_mine = line.region(last_got, qa_own, qa_far, gu_mine, new=o_cuts[1:])

        last_more = gather_second(last_got)
        qa_back = core_swap(qa_far)
        gu_far = [core_swap(x) for x in gu_mine]
        down_done = jnp.concatenate([line.done["down", i] for i in range(3)], axis=0)
        down_other = core_swap(down_done)
        last_more, qa_back = line.region(last_more, qa_back)

        if square:
            gu_mine.append(swap(pick(gu_done, f ^ 3), 3))
        last_blocks = gather_done(last, last_got, last_more)
        kv_part = dot_rows(
            jnp.concatenate(normed_rel, axis=0), jnp.concatenate([b[:tokens] for b in last_blocks], axis=0)
        )
        gain_sum = sum(
            lax.dynamic_slice_in_dim(b[tokens:], f * lines, lines, 0).astype(F32) for b in last_blocks
        )
        gain_sum = jnp.pad(gain_sum, ((0, 16 - lines), (0, 0)))
        kv_part = jnp.concatenate([kv_part, gain_sum], axis=0)
        kv_back = core_swap(half_of(kv_part, 1 - k).astype(BF16))
        qa_cuts = cuts_of("qa", qa_own, qa_back, 1)
        kv_back, down_done, down_other = line.region(kv_back, down_done, down_other, new=qa_cuts)

        def columns_out(own, got):
            both = jnp.where(k == 0, own, got), jnp.where(k == 0, got, own)
            return jnp.concatenate(both, axis=1).astype(F32)

        qb_done = line.done["qb", 0].reshape(nf, rank // nf, head_cols // 2)
        qb_done = lax.all_to_all(qb_done, "fsdp", split_axis=0, concat_axis=0, tiled=True)
        grad_down = columns_out(down_done, down_other)
        kv_cuts = cuts_of("kv", half_of(kv_part, k), kv_back, 1)
        qb_done, gu_mine = line.region(qb_done, gu_mine, new=kv_cuts)

        qb_other = core_swap(qb_done)
        o_done = jnp.concatenate([line.done["o", i] for i in range(2)], axis=0)
        o_other = core_swap(o_done)
        if square:
            gu_far.append(core_swap(gu_mine[3]))
        qb_other, o_other, gu_far = line.region(qb_other, o_other, gu_far)
        grad_gate, grad_up = place_columns(info, gu_mine, gu_far, square)
        grad_gate, grad_up, o_done, o_other = line.region(grad_gate, grad_up, o_done, o_other)
        qa_done = line.done["qa", 0]
        qa_other = core_swap(qa_done)
        grad_o = columns_out(o_done, o_other)
        grad_o, qa_other = line.region(grad_o, qa_other)
        grad_qa = columns_out(qa_done, qa_other)
        grad_qb = jnp.concatenate(
            [jnp.where(k == 0, qb_done, qb_other), jnp.where(k == 0, qb_other, qb_done)], axis=2
        )
        grad_qb = grad_qb.transpose(1, 0, 2).reshape(rank // nf, nf * head_cols).astype(F32)
        kv_done = line.done["kv", 0]
        kv_grad = columns_out(kv_done, core_swap(kv_done))
        gain_out = kv_grad[shard : shard + lines].reshape(lines * 2 * HD)
        return (
            output,
            input_grad,
            gain_out[:shard],
            grad_qa,
            gain_out[2 * shard : gain_width],
            grad_qb,
            kv_grad[:shard, :HD],
            kv_grad[:shard, HD:],
            grad_o,
            gain_out[shard : 2 * shard],
            grad_gate,
            grad_up,
            grad_down,
        )

    token_spec = P(None, ("ctx", "fsdp"), None)
    row, vector = P("fsdp", None), P("fsdp")
    weights = (vector, row, vector, row, row, row, row, vector, row, row, row)
    return jax.shard_map(
        on_device,
        mesh=mesh,
        in_specs=(token_spec, token_spec, P()) + weights,
        out_specs=(token_spec, token_spec) + weights,
        check_vma=False,
    )
```

time: 2780 us -> 1070 us (0.38)
  waiting for transfers between devices: 2210 us -> 311 us
  matrix products: 274 us -> 31.9 us
  starting transfers between devices: 20.2 us -> 227 us
  Pallas kernels: 0 us -> 201 us
  other arithmetic: 75.8 us -> 177 us
  blocking collectives: 79.3 us -> 0 us
    all_gather x16 -> x2, waiting for transfers between devices: 1360 us -> 0.01 us  [the longest x1 0.01 us: on_device(): qb = lax.all_gather(qb, 'ctx')]
    psum x1 -> x0, waiting for transfers between devices: 439 us -> none  [on_device(): lax.psum(pieces[1].astype(jnp.bfloat16), 'ctx').astype(jnp.float32)]
    reduce_scatter x2 -> x0, waiting for transfers between devices: 364 us -> none  [the longest x1 185 us: on_device(): lax.psum_scatter(value_grads, ('ctx', 'fsdp'), scatter_dimension=1, tiled...]
    ppermute x0 -> x122, waiting for transfers between devices: none -> 302 us  [the longest x56 178 us: swap(): return lax.ppermute(x, 'fsdp', [(i, i ^ j) for i in range(nf)])]
    ppermute x0 -> x122, starting transfers between devices: none -> 210 us  [the longest x12 92.7 us: inward(): return lax.ppermute(x, 'ctx', along([(0, 1), (3, 2)])) if staged else x]
    pallas_call x0 -> x15, Pallas kernels: none -> 201 us  [the longest x4 67.8 us: feed_forward(): pl.pallas_call(kernel, grid=(steps,), in_specs=[whole, whole, lane_block(...]
    dot_general x15 -> x5, matrix products: 129 us -> 10.8 us  [dot(): return jnp.dot(left, right, preferred_element_type=F32)]
    dot_general x8, matrix products: 84 us -> 20.4 us  [dot_back(): lax.dot_general(left, right, (((1,), (1,)), ((), ())), preferred_element_...]
  transfers between devices with their start and end apart: 24 -> 128, of which waited for: 20 -> 43; matrix products, arithmetic and copies ran while one was open for 14% -> 25% of each run, Pallas kernels for 0% -> 19%
where the time goes in v1:
time: 1070 us; the launch traced here: 1060 us
  waiting for transfers between devices  311 us (29%)
  starting transfers between devices  227 us (21%)
  Pallas kernels  201 us (19%)
  other arithmetic  177 us (17%)
  local copies, waits for them, and re-layouts  92.4 us (9%)
  matrix products  31.9 us (3%)
  between operations  17.1 us (2%)
    ppermute x56, waiting for transfers between devices, swap(): return lax.ppermute(x, 'fsdp', [(i, i ^ j) for i in range(nf)])  178 us
    ppermute x12, starting transfers between devices, inward(): return lax.ppermute(x, 'ctx', along([(0, 1), (3, 2)])) if staged else x  92.7 us
    pallas_call x4, Pallas kernels, feed_forward(): pl.pallas_call(kernel, grid=(steps,), in_specs=[whole, whole, lane_block(...  67.8 us
    convert_element_type x39, other arithmetic, add_low(): return (a.astype(F32) + b.astype(F32)).astype(BF16)  66.6 us
    ppermute x56, starting transfers between devices, swap(): return lax.ppermute(x, 'fsdp', [(i, i ^ j) for i in range(nf)])  64.2 us
    pallas_call x5, Pallas kernels, token_grad(): pl.pallas_call(kernel, grid_spec=pltpu.PrefetchScalarGridSpec(num_scalar_...  62.6 us
    ppermute x12, waiting for transfers between devices, back(): return lax.ppermute(x, 'ctx', along([(1, 0), (2, 3)])) if staged else x  53.8 us
    unnamed x271, local copies, waits for them, and re-layouts  32.6 us
  transfers between devices with their start and end apart: 128, of which 43 were waited for; matrix products, arithmetic and copies ran while one was open for 25% of the time, Pallas kernels for 19%

profile of v1, /device:TPU:0, one launch (start us, length us, event | category | flops | bytes accessed | tf_op | source)
XLA Modules:
  0.0 1057.7 jit_solution(5017914271760469147)
XLA Ops:
  9.5 5.2 all-to-all-start.1
  25.8 12.2 %collective-permute-done.1.refs_1_ = bf16[272,1536]{1,0:T(8,128)(2,1)} collective-permute-done((bf16[272,1536]{1,0:T(8,128)(2,1)}, bf16[272,1536]{1,0:T(8,128)(2,1)}, u32[]{:S(2)}, u32[]{:S(2)}) %collective-permute-start.1) | collective-permute-done | bytes 835616 | tf_op jit(solution)/shard_map/ppermute | solution.py:579
  45.1 5.7 collective-permute-done.2
  58.2 6.6 project.1
  76.7 4.5 collective-permute-start.8
  82.7 5.7 collective-permute-done.8
  88.4 4.3 collective-permute-done.9
  92.7 6.4 collective-permute-done.10.refs_1_
  110.7 23.9 %collective-permute-done.14 = bf16[128,1024]{1,0:T(8,128)(2,1)S(1)} collective-permute-done((bf16[128,1024]{1,0:T(8,128)(2,1)S(1)}, bf16[128,1024]{1,0:T(8,128)(2,1)S(1)}, u32[]{:S(2)}, u32[]{:S(2)}) %collective-permute-start.14) | collective-permute-done | bytes 262176 | tf_op jit(solution)/shard_map/ppermute | solution.py:579
  147.8 4.4 fusion.64.q_ref
  157.3 4.0 collective-permute-done.18
  161.3 17.1 %attend_forward.1 = (bf16[4,4,64,1024]{3,2,1,0:T(8,128)(2,1)}, bf16[4,4,64,1024]{3,2,1,0:T(8,128)(2,1)}, f32[4,1,1024]{2,1,0:T(1,128)}) custom-call(s32[7]{0:T(128)} %pad_add_fusion.info_ref, f32[4,4,64,1024]{3,2,1,0:T(8,128)} %fusion.64.q_ref, bf16[4,4,4,64,512]{4,3,2,1,0:T(8,128)(2,1)} %bitcast.14.near_ref, bf16[4,4,4,64,512]{4,3,2,1,0:T(8,128)(2,1)} %bitcast.15.far_ref, ...), custom_call_target="tpu_custom_call" | custom-call | flops 1 | bytes 1 | tf_op jit(solution)/shard_map/attend_forward/pallas_call | solution.py:152
  187.8 14.0 %collective-permute-done.22.s_ref.refs_6_ = bf16[256,2048]{1,0:T(8,128)(2,1)S(1)} collective-permute-done((bf16[256,2048]{1,0:T(8,128)(2,1)S(1)}, bf16[256,2048]{1,0:T(8,128)(2,1)S(1)}, u32[]{:S(2)}, u32[]{:S(2)}) %collective-permute-start.22) | collective-permute-done | bytes 1048608 | tf_op jit(solution)/shard_map/ppermute | solution.py:579
  202.3 10.8 %collective-permute-done.19 = bf16[128,2048]{1,0:T(8,128)(2,1)S(1)} collective-permute-done((bf16[128,2048]{1,0:T(8,128)(2,1)S(1)}, bf16[128,2048]{1,0:T(8,128)(2,1)S(1)}, u32[]{:S(2)}, u32[]{:S(2)}) %collective-permute-start.19) | collective-permute-done | bytes 524320 | tf_op jit(solution)/shard_map/ppermute | solution.py:579
  220.2 18.6 %collective-permute-done.24 = bf16[256,2048]{1,0:T(8,128)(2,1)S(1)} collective-permute-done((bf16[256,2048]{1,0:T(8,128)(2,1)S(1)}, bf16[256,2048]{1,0:T(8,128)(2,1)S(1)}, u32[]{:S(2)}, u32[]{:S(2)}) %collective-permute-start.24) | collective-permute-done | bytes 1048608 | tf_op jit(solution)/shard_map/ppermute | solution.py:579
  247.2 17.5 %feed_forward.4 = (bf16[256,1408]{1,0:T(8,128)(2,1)}, bf16[256,1408]{1,0:T(8,128)(2,1)}, bf16[256,1408]{1,0:T(8,128)(2,1)}, f32[256,2048]{1,0:T(8,128)}, f32[256,2048]{1,0:T(8,128)}) custom-call(bf16[256,2048]{1,0:T(8,128)(2,1)} %multiply_convert_fusion.x_ref.refs_0_, bf16[256,2048]{1,0:T(8,128)(2,1)} %copy-done.10, bf16[8,4,64,2816]{3,2,1,0:T(8,128)(2,1)} %bitcast.176, ...), custom_call_target="tpu_custom_call" | custom-call | flops 1 | bytes 1 | tf_op jit(solution)/shard_map/feed_forward/pallas_call | solution.py:355
  264.7 4.7 collective-permute-done.26.x_ref.refs_1_
  276.2 16.6 %feed_forward.5 = (bf16[256,1408]{1,0:T(8,128)(2,1)}, bf16[256,1408]{1,0:T(8,128)(2,1)}, bf16[256,1408]{1,0:T(8,128)(2,1)}, bf16[256,2048]{1,0:T(8,128)(2,1)}, bf16[256,2048]{1,0:T(8,128)(2,1)}) custom-call(bf16[256,2048]{1,0:T(8,128)(2,1)} %collective-permute-done.26.x_ref.refs_1_, bf16[256,2048]{1,0:T(8,128)(2,1)} %copy-done.25, ...), custom_call_target="tpu_custom_call" | custom-call | flops 1 | bytes 1 | tf_op jit(solution)/shard_map/feed_forward/pallas_call | solution.py:355
  293.7 17.1 %feed_forward.6 = (bf16[256,1408]{1,0:T(8,128)(2,1)}, bf16[256,1408]{1,0:T(8,128)(2,1)}, bf16[256,1408]{1,0:T(8,128)(2,1)}, bf16[256,2048]{1,0:T(8,128)(2,1)}, bf16[256,2048]{1,0:T(8,128)(2,1)}) custom-call(bf16[256,2048]{1,0:T(8,128)(2,1)} %collective-permute-done.27.x_ref.refs_2_, bf16[256,2048]{1,0:T(8,128)(2,1)} %copy-done.26, ...), custom_call_target="tpu_custom_call" | custom-call | flops 1 | bytes 1 | tf_op jit(solution)/shard_map/feed_forward/pallas_call | solution.py:355
  315.5 16.6 %feed_forward.7 = (bf16[256,1408]{1,0:T(8,128)(2,1)}, bf16[256,1408]{1,0:T(8,128)(2,1)}, bf16[256,1408]{1,0:T(8,128)(2,1)}, bf16[256,2048]{1,0:T(8,128)(2,1)}, bf16[256,2048]{1,0:T(8,128)(2,1)}) custom-call(bf16[256,2048]{1,0:T(8,128)(2,1)} %constant_dynamic-update-slice_fusion.22.x_ref.refs_3_, bf16[256,2048]{1,0:T(8,128)(2,1)} %collective-permute-done.23.s_ref.refs_7_, ...), custom_call_target="tpu_custom_call" | custom-call | flops 1 | bytes 1 | tf_op jit(solution)/shard_map/feed_forward/pallas_call | solution.py:355
  334.1 23.8 %token_grad.5 = (bf16[2048,1408]{1,0:T(8,128)(2,1)}, bf16[2048,1408]{1,0:T(8,128)(2,1)}) custom-call(s32[7]{0:T(128)} %pad_add_fusion.info_ref, bf16[256,2048]{1,0:T(8,128)(2,1)} %multiply_convert_fusion.x_ref.refs_0_, bf16[256,2048]{1,0:T(8,128)(2,1)} %collective-permute-done.26.x_ref.refs_1_, bf16[256,2048]{1,0:T(8,128)(2,1)} %collective-permute-done.27.x_ref.refs_2_, ...), custom_call_target="tpu_custom_call" | custom-call | flops 1 | bytes 1 | tf_op jit(solution)/shard_map/token_grad/pallas_call | solution.py:425
  370.6 4.5 collective-permute-start.36
  376.8 11.8 %token_grad.6 = (bf16[1408,1024]{1,0:T(8,128)(2,1)}, bf16[1408,1024]{1,0:T(8,128)(2,1)}) custom-call(s32[7]{0:T(128)} %pad_add_fusion.info_ref, bf16[256,1408]{1,0:T(8,128)(2,1)} %get-tuple-element.349.refs_0_, bf16[256,1408]{1,0:T(8,128)(2,1)} %get-tuple-element.350.refs_1_, bf16[256,1408]{1,0:T(8,128)(2,1)} %get-tuple-element.351.refs_2_, ...), custom_call_target="tpu_custom_call" | custom-call | flops 1 | bytes 1 | tf_op jit(solution)/shard_map/token_grad/pallas_call | solution.py:425
  388.6 11.8 %collective-permute-done.34.refs_5_ = bf16[256,2048]{1,0:T(8,128)(2,1)} collective-permute-done((bf16[256,2048]{1,0:T(8,128)(2,1)}, bf16[256,2048]{1,0:T(8,128)(2,1)}, u32[]{:S(2)}, u32[]{:S(2)}) %collective-permute-start.34) | collective-permute-done | bytes 1048608 | tf_op jit(solution)/shard_map/ppermute | solution.py:579
  400.9 4.6 collective-permute-done.36
  407.9 4.7 collective-permute-start.41
  429.8 14.5 %collective-permute-done.41 = bf16[512,1408]{1,0:T(8,128)(2,1)S(1)} collective-permute-done((bf16[512,1408]{1,0:T(8,128)(2,1)}, bf16[512,1408]{1,0:T(8,128)(2,1)S(1)}, u32[]{:S(2)}, u32[]{:S(2)}) %collective-permute-start.41) | collective-permute-done | bytes 1441824 | tf_op jit(solution)/shard_map/line_in/ppermute | solution.py:638
  444.3 5.4 collective-permute-start.44
  458.3 8.7 collective-permute-start.48
  475.4 13.4 %attend_backward.2 = (bf16[4,2,64,1024]{3,2,1,0:T(8,128)(2,1)}, bf16[4,4,2,64,512]{4,3,2,1,0:T(8,128)(2,1)}, bf16[4,4,2,64,512]{4,3,2,1,0:T(8,128)(2,1)}) custom-call(s32[7]{0:T(128)} %pad_add_fusion.info_ref, bf16[4,4,64,1024]{3,2,1,0:T(8,128)(2,1)} %get-tuple-element.370.q_ref, bf16[4,4,64,1024]{3,2,1,0:T(8,128)(2,1)} %get-tuple-element.290.o_ref, ...), custom_call_target="tpu_custom_call" | custom-call | flops 1 | bytes 1 | tf_op jit(solution)/shard_map/attend_backward/pallas_call | solution.py:252
  502.0 3.8 add_convert_fusion.25
  505.8 13.2 %attend_backward.3 = (bf16[4,2,64,1024]{3,2,1,0:T(8,128)(2,1)}, bf16[4,4,2,64,512]{4,3,2,1,0:T(8,128)(2,1)}, bf16[4,4,2,64,512]{4,3,2,1,0:T(8,128)(2,1)}) custom-call(s32[7]{0:T(128)} %pad_add_fusion.info_ref, bf16[4,4,64,1024]{3,2,1,0:T(8,128)(2,1)} %get-tuple-element.370.q_ref, bf16[4,4,64,1024]{3,2,1,0:T(8,128)(2,1)} %get-tuple-element.290.o_ref, ...), custom_call_target="tpu_custom_call" | custom-call | flops 1 | bytes 1 | tf_op jit(solution)/shard_map/attend_backward/pallas_call | solution.py:252
  523.2 6.9 collective-permute-done.46
  554.9 18.0 %collective-permute-start.61 = (bf16[512,1024]{1,0:T(8,128)(2,1)S(1)}, bf16[512,1024]{1,0:T(8,128)(2,1)S(1)}, u32[]{:S(2)}, u32[]{:S(2)}) collective-permute-start(bf16[512,1024]{1,0:T(8,128)(2,1)S(1)} %copy-done.31), channel_id=1, source_target_pairs={{0,8},{4,12},{24,16},{28,20},{1,9},{5,13},{25,17},{29,21},{2,10},{... | collective-permute-start | bytes 3145736 | tf_op jit(solution)/shard_map/line_in/ppermute | solution.py:638
  572.9 10.8 %collective-permute-done.52 = bf16[512,1408]{1,0:T(8,128)(2,1)S(1)} collective-permute-done((bf16[512,1408]{1,0:T(8,128)(2,1)S(1)}, bf16[512,1408]{1,0:T(8,128)(2,1)S(1)}, u32[]{:S(2)}, u32[]{:S(2)}) %collective-permute-start.52) | collective-permute-done | bytes 1441824 | tf_op jit(solution)/shard_map/line_back/ppermute | solution.py:646
  599.0 11.7 %token_grad.7 = (bf16[1024,1024]{1,0:T(8,128)(2,1)}, bf16[1024,1024]{1,0:T(8,128)(2,1)}) custom-call(s32[7]{0:T(128)} %pad_add_fusion.info_ref, bf16[256,1024]{1,0:T(8,128)(2,1)} %bitcast.219, bf16[256,1024]{1,0:T(8,128)(2,1)} %bitcast.223, bf16[256,1024]{1,0:T(8,128)(2,1)} %bitcast.221, bf16[256,1024]{1,0:T(8,128)(2,1)} %bitcast.225, ...), custom_call_target="tpu_custom_call" | custom-call | flops 1 | bytes 1 | tf_op jit(solution)/shard_map/token_grad/pallas_call | solution.py:425
  619.0 3.9 collective-permute-done.58
  626.4 7.7 collective-permute-start.74
  642.2 6.8 collective-permute-done.70
  651.2 16.5 %collective-permute-done.71 = bf16[256,2048]{1,0:T(8,128)(2,1)S(1)} collective-permute-done((bf16[256,2048]{1,0:T(8,128)(2,1)S(1)}, bf16[256,2048]{1,0:T(8,128)(2,1)S(1)}, u32[]{:S(2)}, u32[]{:S(2)}) %collective-permute-start.71) | collective-permute-done | bytes 1048608 | tf_op jit(solution)/shard_map/ppermute | solution.py:579
  678.3 5.0 collective-permute-done.63
  690.0 13.5 %pad_maximum_fusion = bf16[2048,1408]{1,0:T(8,128)(2,1)} fusion(bf16[512,1408]{1,0:T(8,128)(2,1)S(1)} %broadcast_select_fusion.4, bf16[512,1408]{1,0:T(8,128)(2,1)S(1)} %copy-done.19, bf16[512,1408]{1,0:T(8,128)(2,1)S(1)} %copy-done.18, bf16[512,1408]{1,0:T(8,128)(2,1)S(1)} %copy-done.16), kind=kLoop, calls=%fused_computation | loop fusion | flops 23068672 | bytes 11534336 | tf_op jit(solution)/shard_map/concatenate | solution.py:912
  703.5 9.3 token_grad.8
  712.8 5.4 dynamic-slice_bitcast_fusion
  718.3 5.0 collective-permute-start.83
  739.6 4.2 all-to-all-start.2
  749.6 23.6 %collective-permute-done.76 = bf16[128,512]{1,0:T(8,128)(2,1)S(1)} collective-permute-done((bf16[128,512]{1,0:T(8,128)(2,1)}, bf16[128,512]{1,0:T(8,128)(2,1)S(1)}, u32[]{:S(2)}, u32[]{:S(2)}) %collective-permute-start.76) | collective-permute-done | bytes 131104 | tf_op jit(solution)/shard_map/ppermute | solution.py:881
  778.0 4.5 add_convert_fusion.15
  802.2 6.3 project_back.1
  816.7 8.7 collective-permute-done.84
  829.4 23.1 %collective-permute-done.85 = bf16[128,1024]{1,0:T(8,128)(2,1)S(1)} collective-permute-done((bf16[128,1024]{1,0:T(8,128)(2,1)S(1)}, bf16[128,1024]{1,0:T(8,128)(2,1)S(1)}, u32[]{:S(2)}, u32[]{:S(2)}) %collective-permute-start.85) | collective-permute-done | bytes 262176 | tf_op jit(solution)/shard_map/ppermute | solution.py:579
  852.4 6.9 collective-permute-start.95
  871.8 6.0 token_grad.9
  881.6 6.5 collective-permute-start.101
  907.4 4.2 add_convert_fusion.24
  922.8 21.5 %collective-permute-start.108 = (bf16[512,512]{1,0:T(8,128)(2,1)}, bf16[512,512]{1,0:T(8,128)(2,1)}, u32[]{:S(2)}, u32[]{:S(2)}) collective-permute-start(bf16[512,512]{1,0:T(8,128)(2,1)} %add_convert_fusion.33), channel_id=1, source_target_pairs={{0,8},{4,12},{24,16},{28,20},{1,9},{5,13},{25,17},{29,21},{2,10},{... | collective-permute-start | bytes 1572872 | tf_op jit(solution)/shard_map/line_in/ppermute | solution.py:638
  944.3 11.9 %collective-permute-done.104 = bf16[1024,512]{1,0:T(8,128)(2,1)S(1)} collective-permute-done((bf16[1024,512]{1,0:T(8,128)(2,1)S(1)}, bf16[1024,512]{1,0:T(8,128)(2,1)S(1)}, u32[]{:S(2)}, u32[]{:S(2)}) %collective-permute-start.104) | collective-permute-done | bytes 1048608 | tf_op jit(solution)/shard_map/line_back/ppermute | solution.py:646
  960.1 4.3 all-to-all-start.3
  969.5 8.2 all-to-all-done.3
  977.7 9.5 collective-permute-done.107
  996.6 5.9 maximum_convert_fusion
  1006.1 13.9 %place_columns.1 = (f32[512,5632]{1,0:T(8,128)}, f32[512,5632]{1,0:T(8,128)}) custom-call(s32[7]{0:T(128)} %pad_add_fusion.info_ref, bf16[512,1408]{1,0:T(8,128)(2,1)} %get-tuple-element.498.refs_0_, bf16[512,1408]{1,0:T(8,128)(2,1)} %collective-permute-done.91.refs_1_, bf16[512,1408]{1,0:T(8,128)(2,1)} %collective-permute-done.92.refs_2_, ...), custom_call_target="tpu_custom_call" | custom-call | flops 1 | bytes 1 | tf_op jit(solution)/shard_map/place_columns/pallas_call | solution.py:563
  1027.7 4.4 maximum_convert_fusion.1
  1032.1 11.9 %collective-permute-done.120 = bf16[528,256]{1,0:T(8,128)(2,1)S(1)} collective-permute-done((bf16[528,256]{1,0:T(8,128)(2,1)S(1)}, bf16[528,256]{1,0:T(8,128)(2,1)S(1)}, u32[]{:S(2)}, u32[]{:S(2)}) %collective-permute-start.120) | collective-permute-done | bytes 270368 | tf_op jit(solution)/shard_map/line_back/ppermute | solution.py:646
  (705 shorter events, 398.5 us)
Async XLA Ops:
  14.7 121.0 %all-gather.5.cloned.1.call-start = ((), (), s32[]{:S(2)}) async-start(), calls=%async_computation.4 | async-start | bytes 2359296 | tf_op jit(solution)/shard_map/all_gather | solution.py:718
  66.1 33.1 %all-to-all-start = ((bf16[64,4,2816]{2,0,1:T(8,128)(2,1)}), bf16[64,4,2816]{2,0,1:T(8,128)(2,1)S(1)}, u32[]{:S(2)}, u32[]{:S(2)}) async-start(bf16[64,4,2816]{2,0,1:T(8,128)(2,1)} %bitcast.173), calls=%async_computation | async-start | bytes 2883584 | tf_op jit(solution)/shard_map/all_to_all | solution.py:710
  69.8 170.3 %all-gather.7.cloned.1.call-start = ((), (), s32[]{:S(2)}) async-start(), calls=%async_computation.5 | async-start | bytes 12976128 | tf_op jit(solution)/shard_map/all_gather | solution.py:750
  69.8 29.3 %collective-permute-start.10 = (bf16[256,1024]{1,0:T(8,128)(2,1)S(1)}, bf16[256,1024]{1,0:T(8,128)(2,1)S(1)}, u32[]{:S(2)}, u32[]{:S(2)}) collective-permute-start(bf16[256,1024]{1,0:T(8,128)(2,1)S(1)} %copy-done.48), channel_id=1, source_target_pairs={{0,1},{1,0},{2,3},{3,2},{4,5},{5,4},{6,7},{7,6},{8,9},{9,8},{10,11... | collective-permute-start | bytes 1572872 | tf_op jit(solution)/shard_map/ppermute | solution.py:579
  71.7 27.4 %collective-permute-start.11 = (bf16[256,1024]{1,0:T(8,128)(2,1)S(1)}, bf16[256,1024]{1,0:T(8,128)(2,1)S(1)}, u32[]{:S(2)}, u32[]{:S(2)}) collective-permute-start(bf16[256,1024]{1,0:T(8,128)(2,1)S(1)} %copy-done.48), channel_id=1, source_target_pairs={{0,2},{1,3},{2,0},{3,1},{4,6},{5,7},{6,4},{7,5},{8,10},{9,11},{10,... | collective-permute-start | bytes 1572872 | tf_op jit(solution)/shard_map/ppermute | solution.py:579
  104.6 31.1 %collective-permute-start.12 = (bf16[1024,512]{1,0:T(8,128)(2,1)}, bf16[1024,512]{1,0:T(8,128)(2,1)}, u32[]{:S(2)}, u32[]{:S(2)}) collective-permute-start(bf16[1024,512]{1,0:T(8,128)(2,1)} %get-tuple-element.607), channel_id=1, source_target_pairs={{0,1},{1,0},{2,3},{3,2},{4,5},{5,4},{6,7},{7,6},{8,9},{9,8},{10,11... | collective-permute-start | bytes 3145736 | tf_op jit(solution)/shard_map/ppermute | solution.py:579
  106.0 29.7 %collective-permute-start.13 = (bf16[1024,512]{1,0:T(8,128)(2,1)}, bf16[1024,512]{1,0:T(8,128)(2,1)}, u32[]{:S(2)}, u32[]{:S(2)}) collective-permute-start(bf16[1024,512]{1,0:T(8,128)(2,1)} %get-tuple-element.607), channel_id=1, source_target_pairs={{0,2},{1,3},{2,0},{3,1},{4,6},{5,7},{6,4},{7,5},{8,10},{9,11},{10,... | collective-permute-start | bytes 3145736 | tf_op jit(solution)/shard_map/ppermute | solution.py:579
  153.8 34.0 %collective-permute-start.21 = (bf16[256,2048]{1,0:T(8,128)(2,1)S(1)}, bf16[256,2048]{1,0:T(8,128)(2,1)S(1)}, u32[]{:S(2)}, u32[]{:S(2)}) collective-permute-start(bf16[256,2048]{1,0:T(8,128)(2,1)S(1)} %bitcast_convert_fusion.s_ref.refs_4_), channel_id=1, source_target_pairs={{0,1},{1,0},{2,3},{3,2},{4,5},{5,4},{6,7},{7,6},{8,9},{9,8},{10,11... | collective-permute-start | bytes 3145736 | tf_op jit(solution)/shard_map/ppermute | solution.py:579
  154.2 47.6 %collective-permute-start.22 = (bf16[256,2048]{1,0:T(8,128)(2,1)S(1)}, bf16[256,2048]{1,0:T(8,128)(2,1)S(1)}, u32[]{:S(2)}, u32[]{:S(2)}) collective-permute-start(bf16[256,2048]{1,0:T(8,128)(2,1)S(1)} %bitcast_convert_fusion.s_ref.refs_4_), channel_id=1, source_target_pairs={{0,2},{1,3},{2,0},{3,1},{4,6},{5,7},{6,4},{7,5},{8,10},{9,11},{10,... | collective-permute-start | bytes 3145736 | tf_op jit(solution)/shard_map/ppermute | solution.py:579
  155.6 46.7 %collective-permute-start.23 = (bf16[256,2048]{1,0:T(8,128)(2,1)S(1)}, bf16[256,2048]{1,0:T(8,128)(2,1)}, u32[]{:S(2)}, u32[]{:S(2)}) collective-permute-start(bf16[256,2048]{1,0:T(8,128)(2,1)S(1)} %bitcast_convert_fusion.s_ref.refs_4_), channel_id=1, source_target_pairs={{0,3},{1,2},{2,1},{3,0},{4,7},{5,6},{6,5},{7,4},{8,11},{9,10},{10,... | collective-permute-start | bytes 3145736 | tf_op jit(solution)/shard_map/ppermute | solution.py:579
  182.7 30.4 %collective-permute-start.19 = (bf16[128,2048]{1,0:T(8,128)(2,1)S(1)}, bf16[128,2048]{1,0:T(8,128)(2,1)S(1)}, u32[]{:S(2)}, u32[]{:S(2)}) collective-permute-start(bf16[128,2048]{1,0:T(8,128)(2,1)S(1)} %get-tuple-element.591), channel_id=1, source_target_pairs={{0,1},{1,0},{2,3},{3,2},{4,5},{5,4},{6,7},{7,6},{8,9},{9,8},{10,11... | collective-permute-start | bytes 1572872 | tf_op jit(solution)/shard_map/ppermute | solution.py:579
  183.7 29.5 %collective-permute-start.20 = (bf16[128,2048]{1,0:T(8,128)(2,1)S(1)}, bf16[128,2048]{1,0:T(8,128)(2,1)S(1)}, u32[]{:S(2)}, u32[]{:S(2)}) collective-permute-start(bf16[128,2048]{1,0:T(8,128)(2,1)S(1)} %get-tuple-element.590), channel_id=1, source_target_pairs={{0,2},{1,3},{2,0},{3,1},{4,6},{5,7},{6,4},{7,5},{8,10},{9,11},{10,... | collective-permute-start | bytes 1572872 | tf_op jit(solution)/shard_map/ppermute | solution.py:579
  271.9 39.0 %collective-permute-start.29 = (bf16[128,2048]{1,0:T(8,128)(2,1)}, bf16[128,2048]{1,0:T(8,128)(2,1)}, u32[]{:S(2)}, u32[]{:S(2)}) collective-permute-start(bf16[128,2048]{1,0:T(8,128)(2,1)} %slice.425), channel_id=1, source_target_pairs={{0,1},{1,0},{2,3},{3,2},{4,5},{5,4},{6,7},{7,6},{8,9},{9,8},{10,11... | collective-permute-start | bytes 1572872 | tf_op jit(solution)/shard_map/ppermute | solution.py:579
  274.9 36.0 %collective-permute-start.30 = (bf16[128,2048]{1,0:T(8,128)(2,1)}, bf16[128,2048]{1,0:T(8,128)(2,1)}, u32[]{:S(2)}, u32[]{:S(2)}) collective-permute-start(bf16[128,2048]{1,0:T(8,128)(2,1)} %slice.426), channel_id=1, source_target_pairs={{0,2},{1,3},{2,0},{3,1},{4,6},{5,7},{6,4},{7,5},{8,10},{9,11},{10,... | collective-permute-start | bytes 1572872 | tf_op jit(solution)/shard_map/ppermute | solution.py:579
  292.9 65.0 %collective-permute-start.28 = (bf16[256,2048]{1,0:T(8,128)(2,1)}, bf16[256,2048]{1,0:T(8,128)(2,1)}, u32[]{:S(2)}, u32[]{:S(2)}) collective-permute-start(bf16[256,2048]{1,0:T(8,128)(2,1)} %get-tuple-element.308), channel_id=1, source_target_pairs={{0,1},{1,0},{2,3},{3,2},{4,5},{5,4},{6,7},{7,6},{8,9},{9,8},{10,11... | collective-permute-start | bytes 3145736 | tf_op jit(solution)/shard_map/ppermute | solution.py:579
  310.9 47.0 %collective-permute-start.31 = (bf16[256,2048]{1,0:T(8,128)(2,1)}, bf16[256,2048]{1,0:T(8,128)(2,1)}, u32[]{:S(2)}, u32[]{:S(2)}) collective-permute-start(bf16[256,2048]{1,0:T(8,128)(2,1)} %get-tuple-element.312), channel_id=1, source_target_pairs={{0,2},{1,3},{2,0},{3,1},{4,6},{5,7},{6,4},{7,5},{8,10},{9,11},{10,... | collective-permute-start | bytes 3145736 | tf_op jit(solution)/shard_map/ppermute | solution.py:579
  370.6 34.8 %collective-permute-start.36 = (bf16[512,1408]{1,0:T(8,128)(2,1)}, bf16[512,1408]{1,0:T(8,128)(2,1)}, u32[]{:S(2)}, u32[]{:S(2)}) collective-permute-start(bf16[512,1408]{1,0:T(8,128)(2,1)} %get-tuple-element.539), channel_id=1, source_target_pairs={{0,8},{4,12},{24,16},{28,20},{1,9},{5,13},{25,17},{29,21},{2,10},{... | collective-permute-start | bytes 4325384 | tf_op jit(solution)/shard_map/line_in/ppermute | solution.py:638
  405.4 44.4 %collective-permute-start.39 = (bf16[1408,1024]{1,0:T(8,128)(2,1)}, bf16[1408,1024]{1,0:T(8,128)(2,1)}, u32[]{:S(2)}, u32[]{:S(2)}) collective-permute-start(bf16[1408,1024]{1,0:T(8,128)(2,1)} %get-tuple-element.363), channel_id=1, source_target_pairs={{0,4},{4,0},{8,12},{12,8},{16,20},{20,16},{24,28},{28,24},{1,5},{5... | collective-permute-start | bytes 8650760 | tf_op jit(solution)/shard_map/core_swap/ppermute | solution.py:583
  407.9 36.5 %collective-permute-start.41 = (bf16[512,1408]{1,0:T(8,128)(2,1)}, bf16[512,1408]{1,0:T(8,128)(2,1)S(1)}, u32[]{:S(2)}, u32[]{:S(2)}) collective-permute-start(bf16[512,1408]{1,0:T(8,128)(2,1)} %get-tuple-element.538), channel_id=1, source_target_pairs={{0,8},{4,12},{24,16},{28,20},{1,9},{5,13},{25,17},{29,21},{2,10},{... | collective-permute-start | bytes 4325384 | tf_op jit(solution)/shard_map/line_in/ppermute | solution.py:638
  414.7 35.0 %collective-permute-start.40 = (bf16[512,1408]{1,0:T(8,128)(2,1)S(1)}, bf16[512,1408]{1,0:T(8,128)(2,1)S(1)}, u32[]{:S(2)}, u32[]{:S(2)}) collective-permute-start(bf16[512,1408]{1,0:T(8,128)(2,1)S(1)} %add_convert_fusion.10), channel_id=1, source_target_pairs={{8,16},{12,20},{16,8},{20,12},{9,17},{13,21},{17,9},{21,13},{10,18... | collective-permute-start | bytes 4325384 | tf_op jit(solution)/shard_map/line_across/ppermute | solution.py:642
  420.3 29.5 %collective-permute-start.37 = (bf16[128,2048]{1,0:T(8,128)(2,1)S(1)}, bf16[128,2048]{1,0:T(8,128)(2,1)S(1)}, u32[]{:S(2)}, u32[]{:S(2)}) collective-permute-start(bf16[128,2048]{1,0:T(8,128)(2,1)S(1)} %slice.429), channel_id=1, source_target_pairs={{0,1},{1,0},{2,3},{3,2},{4,5},{5,4},{6,7},{7,6},{8,9},{9,8},{10,11... | collective-permute-start | bytes 1572872 | tf_op jit(solution)/shard_map/ppermute | solution.py:579
  422.2 27.5 %collective-permute-start.38 = (bf16[128,2048]{1,0:T(8,128)(2,1)S(1)}, bf16[128,2048]{1,0:T(8,128)(2,1)S(1)}, u32[]{:S(2)}, u32[]{:S(2)}) collective-permute-start(bf16[128,2048]{1,0:T(8,128)(2,1)S(1)} %slice.430), channel_id=1, source_target_pairs={{0,2},{1,3},{2,0},{3,1},{4,6},{5,7},{6,4},{7,5},{8,10},{9,11},{10,... | collective-permute-start | bytes 1572872 | tf_op jit(solution)/shard_map/ppermute | solution.py:579
  444.3 44.4 %collective-permute-start.44 = (bf16[512,1408]{1,0:T(8,128)(2,1)}, bf16[512,1408]{1,0:T(8,128)(2,1)}, u32[]{:S(2)}, u32[]{:S(2)}) collective-permute-start(bf16[512,1408]{1,0:T(8,128)(2,1)} %get-tuple-element.537), channel_id=1, source_target_pairs={{0,8},{4,12},{24,16},{28,20},{1,9},{5,13},{25,17},{29,21},{2,10},{... | collective-permute-start | bytes 4325384 | tf_op jit(solution)/shard_map/line_in/ppermute | solution.py:638
  451.3 37.4 %collective-permute-start.42 = (bf16[512,1408]{1,0:T(8,128)(2,1)}, bf16[512,1408]{1,0:T(8,128)(2,1)}, u32[]{:S(2)}, u32[]{:S(2)}) collective-permute-start(bf16[512,1408]{1,0:T(8,128)(2,1)} %add_convert_fusion.8), channel_id=1, source_target_pairs={{8,0},{12,4},{16,24},{20,28},{9,1},{13,5},{17,25},{21,29},{10,2},{... | collective-permute-start | bytes 4325384 | tf_op jit(solution)/shard_map/line_back/ppermute | solution.py:646
  454.1 34.6 %collective-permute-start.43 = (bf16[512,1408]{1,0:T(8,128)(2,1)}, bf16[512,1408]{1,0:T(8,128)(2,1)}, u32[]{:S(2)}, u32[]{:S(2)}) collective-permute-start(bf16[512,1408]{1,0:T(8,128)(2,1)} %add_convert_fusion.7), channel_id=1, source_target_pairs={{8,16},{12,20},{16,8},{20,12},{9,17},{13,21},{17,9},{21,13},{10,18... | collective-permute-start | bytes 4325384 | tf_op jit(solution)/shard_map/line_across/ppermute | solution.py:642
  458.3 64.9 %collective-permute-start.48 = (bf16[512,1408]{1,0:T(8,128)(2,1)}, bf16[512,1408]{1,0:T(8,128)(2,1)}, u32[]{:S(2)}, u32[]{:S(2)}) collective-permute-start(bf16[512,1408]{1,0:T(8,128)(2,1)} %get-tuple-element.536), channel_id=1, source_target_pairs={{0,8},{4,12},{24,16},{28,20},{1,9},{5,13},{25,17},{29,21},{2,10},{... | collective-permute-start | bytes 4325384 | tf_op jit(solution)/shard_map/line_in/ppermute | solution.py:638
  488.8 41.4 %collective-permute-start.45 = (bf16[4,4,2,64,512]{4,3,2,1,0:T(8,128)(2,1)}, bf16[4,4,2,64,512]{4,3,2,1,0:T(8,128)(2,1)}, u32[]{:S(2)}, u32[]{:S(2)}) collective-permute-start(bf16[4,4,2,64,512]{4,3,2,1,0:T(8,128)(2,1)} %get-tuple-element.387), channel_id=1, source_target_pairs={{0,4},{4,0},{8,12},{12,8},{16,20},{20,16},{24,28},{28,24},{1,5},{5... | collective-permute-start | bytes 6291464 | tf_op jit(solution)/shard_map/core_swap/ppermute | solution.py:583
  492.7 37.4 %collective-permute-start.46 = (bf16[512,1408]{1,0:T(8,128)(2,1)}, bf16[512,1408]{1,0:T(8,128)(2,1)}, u32[]{:S(2)}, u32[]{:S(2)}) collective-permute-start(bf16[512,1408]{1,0:T(8,128)(2,1)} %add_convert_fusion.5), channel_id=1, source_target_pairs={{8,0},{12,4},{16,24},{20,28},{9,1},{13,5},{17,25},{21,29},{10,2},{... | collective-permute-start | bytes 4325384 | tf_op jit(solution)/shard_map/line_back/ppermute | solution.py:646
  497.5 32.7 %collective-permute-start.47 = (bf16[512,1408]{1,0:T(8,128)(2,1)}, bf16[512,1408]{1,0:T(8,128)(2,1)}, u32[]{:S(2)}, u32[]{:S(2)}) collective-permute-start(bf16[512,1408]{1,0:T(8,128)(2,1)} %add_convert_fusion.4), channel_id=1, source_target_pairs={{8,16},{12,20},{16,8},{20,12},{9,17},{13,21},{17,9},{21,13},{10,18... | collective-permute-start | bytes 4325384 | tf_op jit(solution)/shard_map/line_across/ppermute | solution.py:642
  533.7 39.1 %collective-permute-start.50 = (bf16[256,512]{1,0:T(8,128)(2,1)S(1)}, bf16[256,512]{1,0:T(8,128)(2,1)S(1)}, u32[]{:S(2)}, u32[]{:S(2)}) collective-permute-start(bf16[256,512]{1,0:T(8,128)(2,1)S(1)} %bitcast.241), channel_id=1, source_target_pairs={{0,2},{1,3},{2,0},{3,1},{4,6},{5,7},{6,4},{7,5},{8,10},{9,11},{10,... | collective-permute-start | bytes 786440 | tf_op jit(solution)/shard_map/ppermute | solution.py:579
  534.7 48.9 %collective-permute-start.51 = (bf16[4,4,2,64,512]{4,3,2,1,0:T(8,128)(2,1)S(1)}, bf16[4,4,2,64,512]{4,3,2,1,0:T(8,128)(2,1)S(1)}, u32[]{:S(2)}, u32[]{:S(2)}) collective-permute-start(bf16[4,4,2,64,512]{4,3,2,1,0:T(8,128)(2,1)S(1)} %copy-done.121), channel_id=1, source_target_pairs={{0,4},{4,0},{8,12},{12,8},{16,20},{20,16},{24,28},{28,24},{1,5},{5... | collective-permute-start | bytes 6291464 | tf_op jit(solution)/shard_map/core_swap/ppermute | solution.py:583
  537.0 46.6 %collective-permute-start.52 = (bf16[512,1408]{1,0:T(8,128)(2,1)S(1)}, bf16[512,1408]{1,0:T(8,128)(2,1)S(1)}, u32[]{:S(2)}, u32[]{:S(2)}) collective-permute-start(bf16[512,1408]{1,0:T(8,128)(2,1)S(1)} %add_convert_fusion.2), channel_id=1, source_target_pairs={{8,0},{12,4},{16,24},{20,28},{9,1},{13,5},{17,25},{21,29},{10,2},{... | collective-permute-start | bytes 4325384 | tf_op jit(solution)/shard_map/line_back/ppermute | solution.py:646
  540.1 43.6 %collective-permute-start.53 = (bf16[512,1408]{1,0:T(8,128)(2,1)S(1)}, bf16[512,1408]{1,0:T(8,128)(2,1)S(1)}, u32[]{:S(2)}, u32[]{:S(2)}) collective-permute-start(bf16[512,1408]{1,0:T(8,128)(2,1)S(1)} %add_convert_fusion.1), channel_id=1, source_target_pairs={{8,16},{12,20},{16,8},{20,12},{9,17},{13,21},{17,9},{21,13},{10,18... | collective-permute-start | bytes 4325384 | tf_op jit(solution)/shard_map/line_across/ppermute | solution.py:642
  554.9 40.7 %collective-permute-start.61 = (bf16[512,1024]{1,0:T(8,128)(2,1)S(1)}, bf16[512,1024]{1,0:T(8,128)(2,1)S(1)}, u32[]{:S(2)}, u32[]{:S(2)}) collective-permute-start(bf16[512,1024]{1,0:T(8,128)(2,1)S(1)} %copy-done.31), channel_id=1, source_target_pairs={{0,8},{4,12},{24,16},{28,20},{1,9},{5,13},{25,17},{29,21},{2,10},{... | collective-permute-start | bytes 3145736 | tf_op jit(solution)/shard_map/line_in/ppermute | solution.py:638
  584.6 40.3 %collective-permute-start.54 = (bf16[512,512]{1,0:T(8,128)(2,1)}, bf16[512,512]{1,0:T(8,128)(2,1)}, u32[]{:S(2)}, u32[]{:S(2)}) collective-permute-start(bf16[512,512]{1,0:T(8,128)(2,1)} %pad_maximum_fusion.14), channel_id=1, source_target_pairs={{0,1},{1,0},{2,3},{3,2},{4,5},{5,4},{6,7},{7,6},{8,9},{9,8},{10,11... | collective-permute-start | bytes 1572872 | tf_op jit(solution)/shard_map/ppermute | solution.py:579
  586.6 39.8 %collective-permute-start.55 = (bf16[512,512]{1,0:T(8,128)(2,1)}, bf16[512,512]{1,0:T(8,128)(2,1)}, u32[]{:S(2)}, u32[]{:S(2)}) collective-permute-start(bf16[512,512]{1,0:T(8,128)(2,1)} %pad_maximum_fusion.15), channel_id=1, source_target_pairs={{0,2},{1,3},{2,0},{3,1},{4,6},{5,7},{6,4},{7,5},{8,10},{9,11},{10,... | collective-permute-start | bytes 1572872 | tf_op jit(solution)/shard_map/ppermute | solution.py:579
  589.3 44.8 %collective-permute-start.60 = (bf16[512,1408]{1,0:T(8,128)(2,1)}, bf16[512,1408]{1,0:T(8,128)(2,1)}, u32[]{:S(2)}, u32[]{:S(2)}) collective-permute-start(bf16[512,1408]{1,0:T(8,128)(2,1)} %add_convert_fusion), channel_id=1, source_target_pairs={{8,0},{12,4},{16,24},{20,28},{9,1},{13,5},{17,25},{21,29},{10,2},{... | collective-permute-start | bytes 4325384 | tf_op jit(solution)/shard_map/line_back/ppermute | solution.py:646
  624.2 43.5 %collective-permute-start.71 = (bf16[256,2048]{1,0:T(8,128)(2,1)S(1)}, bf16[256,2048]{1,0:T(8,128)(2,1)S(1)}, u32[]{:S(2)}, u32[]{:S(2)}) collective-permute-start(bf16[256,2048]{1,0:T(8,128)(2,1)S(1)} %copy-done.122), channel_id=1, source_target_pairs={{0,2},{1,3},{2,0},{3,1},{4,6},{5,7},{6,4},{7,5},{8,10},{9,11},{10,... | collective-permute-start | bytes 3145736 | tf_op jit(solution)/shard_map/ppermute | solution.py:579
  624.9 46.9 %collective-permute-start.72 = (bf16[256,2048]{1,0:T(8,128)(2,1)S(1)}, bf16[256,2048]{1,0:T(8,128)(2,1)S(1)}, u32[]{:S(2)}, u32[]{:S(2)}) collective-permute-start(bf16[256,2048]{1,0:T(8,128)(2,1)S(1)} %copy-done.124), channel_id=1, source_target_pairs={{0,3},{1,2},{2,1},{3,0},{4,7},{5,6},{6,5},{7,4},{8,11},{9,10},{10,... | collective-permute-start | bytes 3145736 | tf_op jit(solution)/shard_map/ppermute | solution.py:579
  626.4 46.7 %collective-permute-start.74 = (bf16[512,1024]{1,0:T(8,128)(2,1)S(1)}, bf16[512,1024]{1,0:T(8,128)(2,1)S(1)}, u32[]{:S(2)}, u32[]{:S(2)}) collective-permute-start(bf16[512,1024]{1,0:T(8,128)(2,1)S(1)} %copy-done.29), channel_id=1, source_target_pairs={{0,8},{4,12},{24,16},{28,20},{1,9},{5,13},{25,17},{29,21},{2,10},{... | collective-permute-start | bytes 3145736 | tf_op jit(solution)/shard_map/line_in/ppermute | solution.py:638
  638.4 84.9 %collective-permute-start.69 = (bf16[1024,1024]{1,0:T(8,128)(2,1)}, bf16[1024,1024]{1,0:T(8,128)(2,1)}, u32[]{:S(2)}, u32[]{:S(2)}) collective-permute-start(bf16[1024,1024]{1,0:T(8,128)(2,1)} %get-tuple-element.418), channel_id=1, source_target_pairs={{0,4},{4,0},{8,12},{12,8},{16,20},{20,16},{24,28},{28,24},{1,5},{5... | collective-permute-start | bytes 6291464 | tf_op jit(solution)/shard_map/core_swap/ppermute | solution.py:583
  649.0 39.3 %collective-permute-start.65 = (bf16[512,512]{1,0:T(8,128)(2,1)S(1)}, bf16[512,512]{1,0:T(8,128)(2,1)}, u32[]{:S(2)}, u32[]{:S(2)}) collective-permute-start(bf16[512,512]{1,0:T(8,128)(2,1)S(1)} %pad_maximum_fusion.17), channel_id=1, source_target_pairs={{0,1},{1,0},{2,3},{3,2},{4,5},{5,4},{6,7},{7,6},{8,9},{9,8},{10,11... | collective-permute-start | bytes 1572872 | tf_op jit(solution)/shard_map/ppermute | solution.py:579
  677.4 40.9 %collective-permute-start.66 = (bf16[512,512]{1,0:T(8,128)(2,1)}, bf16[512,512]{1,0:T(8,128)(2,1)}, u32[]{:S(2)}, u32[]{:S(2)}) collective-permute-start(bf16[512,512]{1,0:T(8,128)(2,1)} %pad_maximum_fusion.18), channel_id=1, source_target_pairs={{0,2},{1,3},{2,0},{3,1},{4,6},{5,7},{6,4},{7,5},{8,10},{9,11},{10,... | collective-permute-start | bytes 1572872 | tf_op jit(solution)/shard_map/ppermute | solution.py:579
  683.3 40.1 %collective-permute-start.67 = (bf16[256,1024]{1,0:T(8,128)(2,1)}, bf16[256,1024]{1,0:T(8,128)(2,1)}, u32[]{:S(2)}, u32[]{:S(2)}) collective-permute-start(bf16[256,1024]{1,0:T(8,128)(2,1)} %pad_maximum_fusion.19), channel_id=1, source_target_pairs={{0,1},{1,0},{2,3},{3,2},{4,5},{5,4},{6,7},{7,6},{8,9},{9,8},{10,11... | collective-permute-start | bytes 1572872 | tf_op jit(solution)/shard_map/ppermute | solution.py:579
  687.5 35.9 %collective-permute-start.68 = (bf16[256,1024]{1,0:T(8,128)(2,1)}, bf16[256,1024]{1,0:T(8,128)(2,1)}, u32[]{:S(2)}, u32[]{:S(2)}) collective-permute-start(bf16[256,1024]{1,0:T(8,128)(2,1)} %pad_maximum_fusion.20), channel_id=1, source_target_pairs={{0,2},{1,3},{2,0},{3,1},{4,6},{5,7},{6,4},{7,5},{8,10},{9,11},{10,... | collective-permute-start | bytes 1572872 | tf_op jit(solution)/shard_map/ppermute | solution.py:579
  688.3 35.0 %collective-permute-start.73 = (bf16[512,1024]{1,0:T(8,128)(2,1)}, bf16[512,1024]{1,0:T(8,128)(2,1)}, u32[]{:S(2)}, u32[]{:S(2)}) collective-permute-start(bf16[512,1024]{1,0:T(8,128)(2,1)} %add_convert_fusion.26), channel_id=1, source_target_pairs={{8,16},{12,20},{16,8},{20,12},{9,17},{13,21},{17,9},{21,13},{10,18... | collective-permute-start | bytes 3145736 | tf_op jit(solution)/shard_map/line_across/ppermute | solution.py:642
  727.9 62.6 %collective-permute-start.80 = (bf16[1024,512]{1,0:T(8,128)(2,1)}, bf16[1024,512]{1,0:T(8,128)(2,1)}, u32[]{:S(2)}, u32[]{:S(2)}) collective-permute-start(bf16[1024,512]{1,0:T(8,128)(2,1)} %get-tuple-element.442), channel_id=1, source_target_pairs={{0,4},{4,0},{8,12},{12,8},{16,20},{20,16},{24,28},{28,24},{1,5},{5... | collective-permute-start | bytes 3145736 | tf_op jit(solution)/shard_map/core_swap/ppermute | solution.py:583
  730.9 59.6 %collective-permute-start.81 = (bf16[512,1024]{1,0:T(8,128)(2,1)}, bf16[512,1024]{1,0:T(8,128)(2,1)}, u32[]{:S(2)}, u32[]{:S(2)}) collective-permute-start(bf16[512,1024]{1,0:T(8,128)(2,1)} %add_convert_fusion.23), channel_id=1, source_target_pairs={{8,0},{12,4},{16,24},{20,28},{9,1},{13,5},{17,25},{21,29},{10,2},{... | collective-permute-start | bytes 3145736 | tf_op jit(solution)/shard_map/line_back/ppermute | solution.py:646
  734.0 56.5 %collective-permute-start.82 = (bf16[512,1024]{1,0:T(8,128)(2,1)}, bf16[512,1024]{1,0:T(8,128)(2,1)}, u32[]{:S(2)}, u32[]{:S(2)}) collective-permute-start(bf16[512,1024]{1,0:T(8,128)(2,1)} %add_convert_fusion.22), channel_id=1, source_target_pairs={{8,16},{12,20},{16,8},{20,12},{9,17},{13,21},{17,9},{21,13},{10,18... | collective-permute-start | bytes 3145736 | tf_op jit(solution)/shard_map/line_across/ppermute | solution.py:642
  739.6 42.9 %all-to-all-start.2 = ((bf16[256,4,512]{2,0,1:T(8,128)(2,1)}), bf16[256,4,512]{2,0,1:T(8,128)(2,1)}, u32[]{:S(2)}, u32[]{:S(2)}) async-start(bf16[256,4,512]{2,0,1:T(8,128)(2,1)} %bitcast.212), calls=%async_computation.2 | async-start | bytes 2097152 | tf_op jit(solution)/shard_map/all_to_all | solution.py:903
  743.9 29.4 %collective-permute-start.76 = (bf16[128,512]{1,0:T(8,128)(2,1)}, bf16[128,512]{1,0:T(8,128)(2,1)S(1)}, u32[]{:S(2)}, u32[]{:S(2)}) collective-permute-start(bf16[128,512]{1,0:T(8,128)(2,1)} %get-tuple-element.597), channel_id=1, source_target_pairs={{16,0},{20,4},{24,8},{28,12},{17,1},{21,5},{25,9},{29,13},{18,2},{... | collective-permute-start | bytes 393224 | tf_op jit(solution)/shard_map/ppermute | solution.py:881
  745.3 29.1 %collective-permute-start.77 = (bf16[128,512]{1,0:T(8,128)(2,1)}, bf16[128,512]{1,0:T(8,128)(2,1)S(1)}, u32[]{:S(2)}, u32[]{:S(2)}) collective-permute-start(bf16[128,512]{1,0:T(8,128)(2,1)} %get-tuple-element.596), channel_id=1, source_target_pairs={{24,0},{28,4},{25,1},{29,5},{26,2},{30,6},{27,3},{31,7}} | collective-permute-start | bytes 393224 | tf_op jit(solution)/shard_map/ppermute | solution.py:881
  787.1 90.7 %collective-permute-start.91 = (bf16[512,1408]{1,0:T(8,128)(2,1)}, bf16[512,1408]{1,0:T(8,128)(2,1)}, u32[]{:S(2)}, u32[]{:S(2)}) collective-permute-start(bf16[512,1408]{1,0:T(8,128)(2,1)} %get-tuple-element.544), channel_id=1, source_target_pairs={{0,1},{1,0},{2,3},{3,2},{4,5},{5,4},{6,7},{7,6},{8,9},{9,8},{10,11... | collective-permute-start | bytes 4325384 | tf_op jit(solution)/shard_map/ppermute | solution.py:579
  794.6 64.7 %collective-permute-start.86 = (bf16[512,1024]{1,0:T(8,128)(2,1)}, bf16[512,1024]{1,0:T(8,128)(2,1)}, u32[]{:S(2)}, u32[]{:S(2)}) collective-permute-start(bf16[512,1024]{1,0:T(8,128)(2,1)} %add_convert_fusion.21), channel_id=1, source_target_pairs={{8,0},{12,4},{16,24},{20,28},{9,1},{13,5},{17,25},{21,29},{10,2},{... | collective-permute-start | bytes 3145736 | tf_op jit(solution)/shard_map/line_back/ppermute | solution.py:646
  800.5 58.8 %collective-permute-start.87 = (bf16[384,1024]{1,0:T(8,128)(2,1)}, bf16[384,1024]{1,0:T(8,128)(2,1)}, u32[]{:S(2)}, u32[]{:S(2)}) collective-permute-start(bf16[384,1024]{1,0:T(8,128)(2,1)} %add_convert_fusion.29), channel_id=1, source_target_pairs={{8,16},{12,20},{16,8},{20,12},{9,17},{13,21},{17,9},{21,13},{10,18... | collective-permute-start | bytes 2359304 | tf_op jit(solution)/shard_map/line_across/ppermute | solution.py:642
  814.8 64.2 %collective-permute-start.92 = (bf16[512,1408]{1,0:T(8,128)(2,1)}, bf16[512,1408]{1,0:T(8,128)(2,1)}, u32[]{:S(2)}, u32[]{:S(2)}) collective-permute-start(bf16[512,1408]{1,0:T(8,128)(2,1)} %get-tuple-element.543), channel_id=1, source_target_pairs={{0,2},{1,3},{2,0},{3,1},{4,6},{5,7},{6,4},{7,5},{8,10},{9,11},{10,... | collective-permute-start | bytes 4325384 | tf_op jit(solution)/shard_map/ppermute | solution.py:579
  825.4 27.0 %collective-permute-start.85 = (bf16[128,1024]{1,0:T(8,128)(2,1)S(1)}, bf16[128,1024]{1,0:T(8,128)(2,1)S(1)}, u32[]{:S(2)}, u32[]{:S(2)}) collective-permute-start(bf16[128,1024]{1,0:T(8,128)(2,1)S(1)} %slice.490), channel_id=1, source_target_pairs={{0,2},{1,3},{2,0},{3,1},{4,6},{5,7},{6,4},{7,5},{8,10},{9,11},{10,... | collective-permute-start | bytes 786440 | tf_op jit(solution)/shard_map/ppermute | solution.py:579
  852.4 29.2 %collective-permute-start.95 = (bf16[1024,512]{1,0:T(8,128)(2,1)}, bf16[1024,512]{1,0:T(8,128)(2,1)}, u32[]{:S(2)}, u32[]{:S(2)}) collective-permute-start(bf16[1024,512]{1,0:T(8,128)(2,1)} %add_convert_fusion.18), channel_id=1, source_target_pairs={{0,8},{4,12},{24,16},{28,20},{1,9},{5,13},{25,17},{29,21},{2,10},{... | collective-permute-start | bytes 3145736 | tf_op jit(solution)/shard_map/line_in/ppermute | solution.py:638
  895.7 60.6 %collective-permute-start.103 = (bf16[1408,1024]{1,0:T(8,128)(2,1)}, bf16[1408,1024]{1,0:T(8,128)(2,1)}, u32[]{:S(2)}, u32[]{:S(2)}) collective-permute-start(bf16[1408,1024]{1,0:T(8,128)(2,1)} %pad_maximum_fusion.1), channel_id=1, source_target_pairs={{0,4},{4,0},{8,12},{12,8},{16,20},{20,16},{24,28},{28,24},{1,5},{5... | collective-permute-start | bytes 8650760 | tf_op jit(solution)/shard_map/core_swap/ppermute | solution.py:583
  911.7 57.7 %collective-permute-start.106 = (bf16[512,1408]{1,0:T(8,128)(2,1)}, bf16[512,1408]{1,0:T(8,128)(2,1)}, u32[]{:S(2)}, u32[]{:S(2)}) collective-permute-start(bf16[512,1408]{1,0:T(8,128)(2,1)} %get-tuple-element.542), channel_id=1, source_target_pairs={{0,3},{1,2},{2,1},{3,0},{4,7},{5,6},{6,5},{7,4},{8,11},{9,10},{10,... | collective-permute-start | bytes 4325384 | tf_op jit(solution)/shard_map/ppermute | solution.py:579
  915.7 40.6 %collective-permute-start.104 = (bf16[1024,512]{1,0:T(8,128)(2,1)S(1)}, bf16[1024,512]{1,0:T(8,128)(2,1)S(1)}, u32[]{:S(2)}, u32[]{:S(2)}) collective-permute-start(bf16[1024,512]{1,0:T(8,128)(2,1)S(1)} %add_convert_fusion.14), channel_id=1, source_target_pairs={{8,0},{12,4},{16,24},{20,28},{9,1},{13,5},{17,25},{21,29},{10,2},{... | collective-permute-start | bytes 3145736 | tf_op jit(solution)/shard_map/line_back/ppermute | solution.py:646
  919.0 37.2 %collective-permute-start.105 = (bf16[512,1024]{1,0:T(8,128)(2,1)S(1)}, bf16[512,1024]{1,0:T(8,128)(2,1)S(1)}, u32[]{:S(2)}, u32[]{:S(2)}) collective-permute-start(bf16[512,1024]{1,0:T(8,128)(2,1)S(1)} %add_convert_fusion.13), channel_id=1, source_target_pairs={{8,16},{12,20},{16,8},{20,12},{9,17},{13,21},{17,9},{21,13},{10,18... | collective-permute-start | bytes 3145736 | tf_op jit(solution)/shard_map/line_across/ppermute | solution.py:642
  922.8 46.8 %collective-permute-start.108 = (bf16[512,512]{1,0:T(8,128)(2,1)}, bf16[512,512]{1,0:T(8,128)(2,1)}, u32[]{:S(2)}, u32[]{:S(2)}) collective-permute-start(bf16[512,512]{1,0:T(8,128)(2,1)} %add_convert_fusion.33), channel_id=1, source_target_pairs={{0,8},{4,12},{24,16},{28,20},{1,9},{5,13},{25,17},{29,21},{2,10},{... | collective-permute-start | bytes 1572872 | tf_op jit(solution)/shard_map/line_in/ppermute | solution.py:638
  957.6 29.5 %collective-permute-start.107 = (bf16[512,1024]{1,0:T(8,128)(2,1)}, bf16[512,1024]{1,0:T(8,128)(2,1)}, u32[]{:S(2)}, u32[]{:S(2)}) collective-permute-start(bf16[512,1024]{1,0:T(8,128)(2,1)} %add_convert_fusion.12), channel_id=1, source_target_pairs={{8,0},{12,4},{16,24},{20,28},{9,1},{13,5},{17,25},{21,29},{10,2},{... | collective-permute-start | bytes 3145736 | tf_op jit(solution)/shard_map/line_back/ppermute | solution.py:646
  (195 other events, 2158.1 us)
Sparse Core Ops, SparseCore 0:
  21.7 28.4 all-gather.4
  100.4 108.3 all-gather.6

commit v2 on v1

--- a/solution.py
+++ b/solution.py
@@ -435,9 +435,32 @@
         ),
         out_shape=[jax.ShapeDtypeStruct((height, width), BF16)] * 2,
         compiler_params=pltpu.CompilerParams(dimension_semantics=("arbitrary", "arbitrary")),
-        cost_estimate=cheap(),
+        cost_estimate=pl.CostEstimate(
+            flops=4 * count * tokens * height * width, bytes_accessed=4 * height * width, transcendentals=0
+        ),
         name="token_grad",
     )(info, *lefts, *right_args)
+
+
+def token_sum(lefts, rights):
+    count = len(lefts)
+    tokens, height = lefts[0].shape
+    width = rights[0].shape[1]
+    tile = min(height, 256)
+
+    def kernel(*refs):
+        refs[-1][...] = sum(dot_rows(l[...], r[...]) for l, r in zip(refs[:count], refs[count:-1])).astype(BF16)
+
+    return pl.pallas_call(
+        kernel,
+        grid=(height // tile,),
+        in_specs=[pl.BlockSpec((tokens, tile), lambda m: (0, m))] * count
+        + [pl.BlockSpec((tokens, width), lambda m: (0, 0))] * count,
+        out_specs=pl.BlockSpec((tile, width), lambda m: (m, 0)),
+        out_shape=jax.ShapeDtypeStruct((height, width), BF16),
+        cost_estimate=cheap(),
+        name="token_sum",
+    )(*lefts, *rights)
 
 
 def project(info, inputs, own, pieces, others, cos_h, sin_h):
@@ -628,52 +651,6 @@
             part = part + item.astype(F32)
         return part
 
-    def along(pairs):
-        return [(2 * a + core, 2 * b + core) for a, b in pairs for core in range(2)]
-
-    staged = nz == 4
-
-    @jax.named_scope("line_in")
-    def inward(x):
-        return lax.ppermute(x, "ctx", along([(0, 1), (3, 2)])) if staged else x
-
-    @jax.named_scope("line_across")
-    def across(x):
-        return lax.ppermute(x, "ctx", along([(1, 2), (2, 1)])) if staged else x
-
-    @jax.named_scope("line_back")
-    def back(x):
-        return lax.ppermute(x, "ctx", along([(1, 0), (2, 3)])) if staged else x
-
-    def joined(x, y):
-        return add_low(x, y) if staged else x
-
-    def settled(x, y):
-        if staged:
-            z = lax.axis_index("ctx") // 2
-            return jnp.where((z == 1) | (z == 2), x, y)
-        groups = [[2 * i + core for i in range(nz)] for core in range(2)]
-        return lax.psum(x, "ctx", axis_index_groups=groups)
-
-    class Line:
-        def __init__(self):
-            self.flight, self.done = [], {}
-
-        def region(self, *values, new=()):
-            values, arrived = fence(values, [item[3] for item in self.flight])
-            flight = []
-            for (key, stage, x, _), got in zip(self.flight, arrived):
-                if stage == 2:
-                    self.done[key] = settled(x, got)
-                    continue
-                x = joined(x, got)
-                flight.append((key, stage + 1, x, across(x) if stage == 0 else back(x)))
-            for key, x in new:
-                x = x()
-                flight.append((key, 0, x, inward(x)))
-            self.flight = flight
-            return values
-
     def on_device(inputs, cotangent, lengths, attn_gain, w_qa, q_gain, w_qb, w_k, w_v, w_o, ffn_gain, w_gate, w_up, w_down):
         seqs, span, width = inputs.shape
         tokens = seqs * span
@@ -810,45 +787,44 @@
         d_norm_f, grad_gain_f = norm_back(d_ffn, hidden, scale_f, gain_f)
         d_hidden = signal + d_norm_f
         d_hidden_low = d_hidden.astype(BF16)
-        line = Line()
-
-        def rows_of(own, got, start, size):
-            return lambda: add_low(own[start : start + size], got[start : start + size])
-
-        def cuts_of(name, own, got, count):
-            size = own.shape[0]
-            step = -(-size // (128 * count)) * 128
-            return [((name, i), rows_of(own, got, i * step, min(step, size - i * step))) for i in range(count)]
+        line_groups = [[2 * i + core for i in range(nz)] for core in range(2)]
 
         d_hidden_low, gu_back = fence(d_hidden_low, gu_back)
-        gu_cuts = cuts_of("gu", gu_own, gu_back, 5)
-
-        line.region(new=gu_cuts[:1])
+        gu_half = add_low(gu_own, gu_back)
+        gu_share = lax.psum_scatter(
+            gu_half, "ctx", scatter_dimension=0, axis_index_groups=line_groups, tiled=True
+        )
         dh_got = gather_first(d_hidden_low)
         signal_blocks = [signal_low] + signal_got
-        down_lefts, down_rights, _ = fence(inner_blocks, signal_blocks, d_hidden_low)
+        down_lefts, down_rights, _ = fence(inner_blocks, signal_blocks, gu_half)
         down_own, down_far = token_grad(info, down_lefts, down_rights)
 
-        dh_got, down_own, down_far = line.region(dh_got, down_own, down_far, new=gu_cuts[1:2])
+        dh_got, down_own, down_far = fence(dh_got, down_own, down_far)
         dh_more = gather_second(dh_got)
         down_back = core_swap(down_far)
         d_attn = [dot_back(x, w_o).astype(BF16) for x in [d_hidden_low, *dh_got]]
 
-        dh_more, down_back, d_attn, y_parts = line.region(dh_more, down_back, d_attn, y_parts, new=gu_cuts[2:3])
+        dh_more, down_back, d_attn, y_parts = fence(dh_more, down_back, d_attn, y_parts)
         dh_blocks = gather_done(d_hidden_low, dh_got, dh_more)
         d_attn += [dot_back(x, w_o).astype(BF16) for x in dh_blocks[len(d_attn) :]]
         d_attn = jnp.concatenate(d_attn, axis=0).reshape(nf, seqs, span, head_cols)
         y_got = [swap(y_parts[j], j) for j in range(1, nf)]
-        down_cuts = cuts_of("down", down_own, down_back, 3)
+        down_half = add_low(down_own, down_back)
+        down_share = lax.psum_scatter(
+            down_half, "ctx", scatter_dimension=0, axis_index_groups=line_groups, tiled=True
+        )
 
         count = seqs // 2
         backward = (info, scaled, attn_out, d_attn, lse, kv_near, kv_far, cos_g, sin_g)
         dq_a, near_a, far_a = attend_backward(*backward, 0, count)
-        dq_a, near_a, far_a, d_attn = line.region(dq_a, near_a, far_a, d_attn, new=gu_cuts[3:4])
+        dq_a, near_a, far_a, d_attn = fence(dq_a, near_a, far_a, d_attn)
         back_a = core_swap(far_a)
         backward = (info, scaled, attn_out, d_attn, lse, kv_near, kv_far, cos_g, sin_g)
         dq_b, near_b, far_b = attend_backward(*backward, count, seqs - count)
-        dq_b, near_b, far_b, back_a = line.region(dq_b, near_b, far_b, back_a, new=gu_cuts[4:5])
+        dq_b, near_b, far_b, back_a, gu_share = fence(
+            dq_b, near_b, far_b, back_a, gu_share
+        )
+        gu_sum = lax.all_gather(gu_share, "ctx", axis_index_groups=line_groups, tiled=True)
 
         def kv_parts(near, far):
             total = near.astype(F32) + far.astype(F32)
@@ -861,18 +837,21 @@
             jnp.concatenate([dq_a[j], dq_b[j]], axis=0).reshape(tokens, head_cols) for j in range(nf)
         ]
         dq_parts = [dot_back(b, qb) for b in dq_blocks]
-        first_a, back_b, dq_parts, attn_late = line.region(
-            first_a, back_b, dq_parts, attn_blocks, new=down_cuts[:1]
+        first_a, back_b, dq_parts, attn_late, norm_late = fence(
+            first_a, back_b, dq_parts, attn_blocks, norm_blocks
         )
 
         got_a = scatter_second(parts_a, first_a)
         parts_b = kv_parts(near_b, back_b)
         first_b = scatter_first(parts_b)
         dq_first = scatter_first(dq_parts)
-        o_own, o_far = token_grad(info, attn_late, dh_blocks)
-        got_a, first_b, dq_first, o_own, o_far, norm_late = line.region(
-            got_a, first_b, dq_first, o_own, o_far, norm_blocks, new=down_cuts[1:2]
-        )
+        o_part = token_sum(attn_late, dh_blocks)
+        qb_own, qb_far = token_grad(info, norm_late, dq_blocks)
+        got_a, first_b, dq_first, o_part, qb_own, qb_far, down_share = fence(
+            got_a, first_b, dq_first, o_part, qb_own, qb_far, down_share
+        )
+        down_sum = lax.all_gather(down_share, "ctx", axis_index_groups=line_groups, tiled=True)
+
 
         def line_start(part, got):
             whole = scatter_done(part, got).reshape(nz, -1, 2 * HD)
@@ -885,10 +864,9 @@
         line_a, sent_a = line_start(parts_a[0], got_a)
         got_b = scatter_second(parts_b, first_b)
         dq_got = scatter_second(dq_parts, dq_first)
-        o_back = core_swap(o_far)
-        qb_own, qb_far = token_grad(info, norm_late, dq_blocks)
-        sent_a, got_b, dq_got, o_back, qb_own, qb_far, normed_late, y_got = line.region(
-            sent_a, got_b, dq_got, o_back, qb_own, qb_far, normed, y_got, new=down_cuts[2:3]
+        qb_back = core_swap(qb_far)
+        sent_a, got_b, dq_got, qb_back, normed_late, y_got = fence(
+            sent_a, got_b, dq_got, qb_back, normed, y_got
         )
 
         line_b, sent_b = line_start(parts_b[0], got_b)
@@ -897,25 +875,16 @@
         d_query_low, grad_gain_q = norm_back(d_query_norm, query_low, scale_q, gain_q)
         d_query_low = d_query_low.astype(BF16)
         dql_got = gather_first(d_query_low)
-        qb_back = core_swap(qb_far)
         output = (hidden + scatter_done(y_parts[0].astype(F32), y_got)).astype(BF16)
         output = output.reshape(seqs, span, width)
         normed_cols = lax.all_to_all(normed_late, "fsdp", split_axis=1, concat_axis=0, tiled=True)
         normed_cols = normed_cols.reshape(nf, tokens, shard)
         normed_rel = [pick(normed_cols, f ^ j) for j in range(nf)]
-        o_cuts = cuts_of("o", o_own, o_back, 2)
-        qb_cuts = cuts_of("qb", qb_own, qb_back, 1)
-        sent_b, dql_got, qb_back, normed_rel = line.region(sent_b, dql_got, qb_back, normed_rel, new=o_cuts[:1])
-        qb_cuts = cuts_of("qb", qb_own, qb_back, 1)
+        sent_b, dql_got, normed_rel = fence(sent_b, dql_got, normed_rel)
 
         dql_more = gather_second(dql_got)
-        gu_done = jnp.concatenate([line.done["gu", i] for i in range(5)], axis=0)
-        gu_done = gu_done.reshape(nf, shard, hidden_cols)
-        if square:
-            gu_mine = [pick(gu_done, f)] + [swap(pick(gu_done, f ^ j), j) for j in (1, 2)]
-        else:
-            gu_done = lax.all_to_all(gu_done, "fsdp", split_axis=0, concat_axis=0, tiled=True)
-            gu_mine = [gu_done[j] for j in range(nf)]
+        qb_half = add_low(qb_own, qb_back).reshape(nf, rank // nf, head_cols // 2)
+        qb_rows = lax.all_to_all(qb_half, "fsdp", split_axis=0, concat_axis=0, tiled=True)
         dkv_total = jnp.concatenate([scatter_done(line_a, sent_a), scatter_done(line_b, sent_b)], axis=0)
         d_keys = rotary_back(dkv_total[:, :HD].reshape(seqs, span, HD), cosine, sine)
         d_keys = d_keys.astype(BF16).reshape(tokens, HD)
@@ -940,22 +909,16 @@
         gain_tail = gain_parts.reshape(nf * lines, 2 * HD).astype(BF16)
         gain_tail = jnp.pad(gain_tail, ((0, 16 - nf * lines), (0, 0)))
         last = jnp.concatenate([d_cat[:, rank:], gain_tail], axis=0)
-        last, dql_more = line.region(last, dql_more, new=qb_cuts)
+        last, dql_more = fence(last, dql_more)
 
         last_got = gather_first(last)
         dql_blocks = gather_done(d_query_low, dql_got, dql_more)
-        qa_own, qa_far = token_grad(info, normed_rel, dql_blocks)
-        last_got, qa_own, qa_far, gu_mine = line.region(last_got, qa_own, qa_far, gu_mine, new=o_cuts[1:])
+        qa_part = token_sum(normed_rel, dql_blocks)
+        last_got, qa_part, qb_rows = fence(last_got, qa_part, qb_rows)
 
         last_more = gather_second(last_got)
-        qa_back = core_swap(qa_far)
-        gu_far = [core_swap(x) for x in gu_mine]
-        down_done = jnp.concatenate([line.done["down", i] for i in range(3)], axis=0)
-        down_other = core_swap(down_done)
-        last_more, qa_back = line.region(last_more, qa_back)
-
-        if square:
-            gu_mine.append(swap(pick(gu_done, f ^ 3), 3))
+        last_more, gu_sum = fence(last_more, gu_sum)
+
         last_blocks = gather_done(last, last_got, last_more)
         kv_part = dot_rows(
             jnp.concatenate(normed_rel, axis=0), jnp.concatenate([b[:tokens] for b in last_blocks], axis=0)
@@ -965,39 +928,51 @@
         )
         gain_sum = jnp.pad(gain_sum, ((0, 16 - lines), (0, 0)))
         kv_part = jnp.concatenate([kv_part, gain_sum], axis=0)
-        kv_back = core_swap(half_of(kv_part, 1 - k).astype(BF16))
-        qa_cuts = cuts_of("qa", qa_own, qa_back, 1)
-        kv_back, down_done, down_other = line.region(kv_back, down_done, down_other, new=qa_cuts)
-
-        def columns_out(own, got):
-            both = jnp.where(k == 0, own, got), jnp.where(k == 0, got, own)
-            return jnp.concatenate(both, axis=1).astype(F32)
-
-        qb_done = line.done["qb", 0].reshape(nf, rank // nf, head_cols // 2)
-        qb_done = lax.all_to_all(qb_done, "fsdp", split_axis=0, concat_axis=0, tiled=True)
-        grad_down = columns_out(down_done, down_other)
-        kv_cuts = cuts_of("kv", half_of(kv_part, k), kv_back, 1)
-        qb_done, gu_mine = line.region(qb_done, gu_mine, new=kv_cuts)
-
-        qb_other = core_swap(qb_done)
-        o_done = jnp.concatenate([line.done["o", i] for i in range(2)], axis=0)
-        o_other = core_swap(o_done)
+        blank = jnp.zeros_like(qb_rows)
+        qb_full = jnp.where(
+            k == 0, jnp.concatenate([qb_rows, blank], axis=2), jnp.concatenate([blank, qb_rows], axis=2)
+        )
+        pieces_out = [o_part[:, i : i + rank] for i in range(0, o_part.shape[1], rank)]
+        pieces_out += [qb_full.reshape(-1, rank), qa_part]
+        kv_low = kv_part.astype(BF16)
+        wide = rank // (2 * HD)
+        kv_rows = kv_low.shape[0] // wide
+        pieces_out.append(
+            jnp.concatenate([kv_low[i * kv_rows : (i + 1) * kv_rows] for i in range(wide)], axis=1)
+        )
+        sizes = [p.shape[0] for p in pieces_out]
+        spare = -sum(sizes) % (16 * nc)
+        pieces_out.append(jnp.zeros((spare, rank), BF16))
+        buffer = jnp.concatenate(pieces_out, axis=0)
+        buffer, gu_sum = fence(buffer, gu_sum)
+        buffer_share = lax.psum_scatter(buffer, "ctx", scatter_dimension=0, tiled=True)
+
+        gu_done = gu_sum.reshape(nf, shard, hidden_cols)
         if square:
-            gu_far.append(core_swap(gu_mine[3]))
-        qb_other, o_other, gu_far = line.region(qb_other, o_other, gu_far)
+            gu_mine = [pick(gu_done, f)] + [swap(pick(gu_done, f ^ j), j) for j in range(1, nf)]
+        else:
+            gu_done = lax.all_to_all(gu_done, "fsdp", split_axis=0, concat_axis=0, tiled=True)
+            gu_mine = [gu_done[j] for j in range(nf)]
+        down_other = core_swap(down_sum)
+        gu_mine, down_sum, down_other, buffer_share = fence(gu_mine, down_sum, down_other, buffer_share)
+        buffer = lax.all_gather(buffer_share, "ctx", tiled=True)
+        gu_far = [core_swap(x) for x in gu_mine]
         grad_gate, grad_up = place_columns(info, gu_mine, gu_far, square)
-        grad_gate, grad_up, o_done, o_other = line.region(grad_gate, grad_up, o_done, o_other)
-        qa_done = line.done["qa", 0]
-        qa_other = core_swap(qa_done)
-        grad_o = columns_out(o_done, o_other)
-        grad_o, qa_other = line.region(grad_o, qa_other)
-        grad_qa = columns_out(qa_done, qa_other)
-        grad_qb = jnp.concatenate(
-            [jnp.where(k == 0, qb_done, qb_other), jnp.where(k == 0, qb_other, qb_done)], axis=2
-        )
-        grad_qb = grad_qb.transpose(1, 0, 2).reshape(rank // nf, nf * head_cols).astype(F32)
-        kv_done = line.done["kv", 0]
-        kv_grad = columns_out(kv_done, core_swap(kv_done))
+        both = jnp.where(k == 0, down_sum, down_other), jnp.where(k == 0, down_other, down_sum)
+        grad_down = jnp.concatenate(both, axis=1).astype(F32)
+        grad_gate, grad_up, grad_down, buffer = fence(grad_gate, grad_up, grad_down, buffer)
+        found, at = [], 0
+        for size in sizes:
+            found.append(buffer[at : at + size])
+            at += size
+        count_o = o_part.shape[1] // rank
+        grad_o = jnp.concatenate(found[:count_o], axis=1).astype(F32)
+        qb_rows = found[count_o].reshape(nf, rank // nf, head_cols)
+        grad_qb = qb_rows.transpose(1, 0, 2).reshape(rank // nf, nf * head_cols).astype(F32)
+        grad_qa = found[-2].astype(F32)
+        kv_grad = jnp.concatenate(
+            [found[-1][:, i * 2 * HD : (i + 1) * 2 * HD] for i in range(wide)], axis=0
+        ).astype(F32)
         gain_out = kv_grad[shard : shard + lines].reshape(lines * 2 * HD)
         return (
             output,

time: 1070 us -> 925 us (0.86)
  starting transfers between devices: 227 us -> 103 us
  other arithmetic: 177 us -> 93.7 us
  waiting for transfers between devices: 311 us -> 362 us
  local copies, waits for them, and re-layouts: 92.4 us -> 108 us
    ppermute x36 -> x0, starting transfers between devices: 126 us -> none  [the longest x12 92.7 us: inward(): return lax.ppermute(x, 'ctx', along([(0, 1), (3, 2)])) if staged else x]
    ppermute x36 -> x0, waiting for transfers between devices: 75.3 us -> none  [the longest x12 53.8 us: back(): return lax.ppermute(x, 'ctx', along([(1, 0), (2, 3)])) if staged else x]
    all_gather x0 -> x3, waiting for transfers between devices: none -> 54.2 us  [the longest x1 48.8 us: on_device(): buffer = lax.all_gather(buffer_share, 'ctx', tiled=True)]
    ppermute x56, waiting for transfers between devices: 178 us -> 230 us  [swap(): return lax.ppermute(x, 'fsdp', [(i, i ^ j) for i in range(nf)])]
    convert_element_type x39 -> x11, other arithmetic: 66.6 us -> 17.4 us  [add_low(): return (a.astype(F32) + b.astype(F32)).astype(BF16)]
    reduce_scatter x0 -> x3, waiting for transfers between devices: none -> 29.5 us  [the longest x1 17.3 us: on_device(): lax.psum_scatter(buffer, 'ctx', scatter_dimension=0, tiled=True)]
    select_n x17 -> x2, other arithmetic: 23.4 us -> 4.65 us  [the longest x1 2.51 us: on_device(): jnp.where(k == 0, down_sum, down_other)]
    pallas_call x5 -> x3, Pallas kernels: 62.6 us -> 45.5 us  [token_grad(): pl.pallas_call(kernel, grid_spec=pltpu.PrefetchScalarGridSpec(num_scalar_...]
  transfers between devices with their start and end apart: 128 -> 91, of which waited for: 43 -> 42; matrix products, arithmetic and copies ran while one was open for 25% -> 20% of each run, Pallas kernels for 19% -> 22%
where the time goes in v2:
time: 925 us; the launch traced here: 914 us
  waiting for transfers between devices  362 us (39%)
  Pallas kernels  197 us (21%)
  local copies, waits for them, and re-layouts  108 us (12%)
  starting transfers between devices  103 us (11%)
  other arithmetic  93.7 us (10%)
  matrix products  34.2 us (4%)
  between operations  16.3 us (2%)
    ppermute x56, waiting for transfers between devices, swap(): return lax.ppermute(x, 'fsdp', [(i, i ^ j) for i in range(nf)])  230 us
    pallas_call x4, Pallas kernels, feed_forward(): pl.pallas_call(kernel, grid=(steps,), in_specs=[whole, whole, lane_block(...  67.7 us
    ppermute x56, starting transfers between devices, swap(): return lax.ppermute(x, 'fsdp', [(i, i ^ j) for i in range(nf)])  64.8 us
    all_gather x1, waiting for transfers between devices, on_device(): buffer = lax.all_gather(buffer_share, 'ctx', tiled=True)  48.8 us
    pallas_call x3, Pallas kernels, token_grad(): pl.pallas_call(kernel, grid_spec=pltpu.PrefetchScalarGridSpec(num_scalar_...  45.5 us
    unnamed x199, local copies, waits for them, and re-layouts  36.6 us
    pallas_call x2, Pallas kernels, attend_backward(): pl.pallas_call(kernel, grid_spec=pltpu.PrefetchScalarGridSpec(num_scalar_...  26.8 us
    ppermute x6, waiting for transfers between devices, line_start(): lax.ppermute(low[s], 'ctx', [(i, i - 2 * s) for i in range(2 * s, nc)])  23.8 us
  transfers between devices with their start and end apart: 91, of which 42 were waited for; matrix products, arithmetic and copies ran while one was open for 20% of the time, Pallas kernels for 22%

profile of v2, /device:TPU:0, one launch (start us, length us, event | category | flops | bytes accessed | tf_op | source)
XLA Modules:
  0.0 914.3 jit_solution(7039800091163815191)
XLA Ops:
  9.5 5.2 all-to-all-start.1
  25.8 12.3 %collective-permute-done.1.refs_1_ = bf16[272,1536]{1,0:T(8,128)(2,1)} collective-permute-done((bf16[272,1536]{1,0:T(8,128)(2,1)}, bf16[272,1536]{1,0:T(8,128)(2,1)}, u32[]{:S(2)}, u32[]{:S(2)}) %collective-permute-start.1) | collective-permute-done | bytes 835616 | tf_op jit(solution)/shard_map/ppermute | solution.py:602
  44.1 7.0 collective-permute-done.2
  59.2 6.6 project.1
  67.0 3.7 all-to-all-start
  74.2 3.5 collective-permute-start.7
  77.7 4.5 collective-permute-start.8
  83.7 5.7 collective-permute-done.8
  89.4 4.3 collective-permute-done.9
  93.7 6.4 collective-permute-done.10.refs_1_
  113.4 22.4 %collective-permute-done.14 = bf16[128,1024]{1,0:T(8,128)(2,1)S(1)} collective-permute-done((bf16[128,1024]{1,0:T(8,128)(2,1)S(1)}, bf16[128,1024]{1,0:T(8,128)(2,1)S(1)}, u32[]{:S(2)}, u32[]{:S(2)}) %collective-permute-start.14) | collective-permute-done | bytes 262176 | tf_op jit(solution)/shard_map/ppermute | solution.py:602
  144.1 4.3 fusion.68.q_ref
  154.4 4.0 collective-permute-done.18
  158.4 17.3 %attend_forward.1 = (bf16[4,4,64,1024]{3,2,1,0:T(8,128)(2,1)}, bf16[4,4,64,1024]{3,2,1,0:T(8,128)(2,1)}, f32[4,1,1024]{2,1,0:T(1,128)}) custom-call(s32[7]{0:T(128)} %pad_add_fusion.info_ref, f32[4,4,64,1024]{3,2,1,0:T(8,128)} %fusion.68.q_ref, bf16[4,4,4,64,512]{4,3,2,1,0:T(8,128)(2,1)} %bitcast.14.near_ref, bf16[4,4,4,64,512]{4,3,2,1,0:T(8,128)(2,1)} %bitcast.15.far_ref, ...), custom_call_target="tpu_custom_call" | custom-call | flops 1 | bytes 1 | tf_op jit(solution)/shard_map/attend_forward/pallas_call | solution.py:152
  184.5 15.8 %collective-permute-done.23.s_ref.refs_7_ = bf16[256,2048]{1,0:T(8,128)(2,1)} collective-permute-done((bf16[256,2048]{1,0:T(8,128)(2,1)S(1)}, bf16[256,2048]{1,0:T(8,128)(2,1)}, u32[]{:S(2)}, u32[]{:S(2)}) %collective-permute-start.23) | collective-permute-done | bytes 1048608 | tf_op jit(solution)/shard_map/ppermute | solution.py:602
  200.2 10.0 %collective-permute-done.19 = bf16[128,2048]{1,0:T(8,128)(2,1)S(1)} collective-permute-done((bf16[128,2048]{1,0:T(8,128)(2,1)S(1)}, bf16[128,2048]{1,0:T(8,128)(2,1)S(1)}, u32[]{:S(2)}, u32[]{:S(2)}) %collective-permute-start.19) | collective-permute-done | bytes 524320 | tf_op jit(solution)/shard_map/ppermute | solution.py:602
  218.1 18.3 %collective-permute-done.24 = bf16[256,2048]{1,0:T(8,128)(2,1)S(1)} collective-permute-done((bf16[256,2048]{1,0:T(8,128)(2,1)S(1)}, bf16[256,2048]{1,0:T(8,128)(2,1)S(1)}, u32[]{:S(2)}, u32[]{:S(2)}) %collective-permute-start.24) | collective-permute-done | bytes 1048608 | tf_op jit(solution)/shard_map/ppermute | solution.py:602
  243.7 17.7 %feed_forward.4 = (bf16[256,1408]{1,0:T(8,128)(2,1)}, bf16[256,1408]{1,0:T(8,128)(2,1)}, bf16[256,1408]{1,0:T(8,128)(2,1)}, f32[256,2048]{1,0:T(8,128)}, f32[256,2048]{1,0:T(8,128)}) custom-call(bf16[256,2048]{1,0:T(8,128)(2,1)} %multiply_convert_fusion.x_ref.refs_0_, bf16[256,2048]{1,0:T(8,128)(2,1)} %copy-done.17, bf16[8,4,64,2816]{3,2,1,0:T(8,128)(2,1)} %bitcast.179, ...), custom_call_target="tpu_custom_call" | custom-call | flops 1 | bytes 1 | tf_op jit(solution)/shard_map/feed_forward/pallas_call | solution.py:355
  261.3 4.8 collective-permute-done.26.x_ref.refs_1_
  272.7 16.6 %feed_forward.5 = (bf16[256,1408]{1,0:T(8,128)(2,1)}, bf16[256,1408]{1,0:T(8,128)(2,1)}, bf16[256,1408]{1,0:T(8,128)(2,1)}, bf16[256,2048]{1,0:T(8,128)(2,1)}, bf16[256,2048]{1,0:T(8,128)(2,1)}) custom-call(bf16[256,2048]{1,0:T(8,128)(2,1)} %collective-permute-done.26.x_ref.refs_1_, bf16[256,2048]{1,0:T(8,128)(2,1)} %copy-done.47, ...), custom_call_target="tpu_custom_call" | custom-call | flops 1 | bytes 1 | tf_op jit(solution)/shard_map/feed_forward/pallas_call | solution.py:355
  290.1 16.8 %feed_forward.6 = (bf16[256,1408]{1,0:T(8,128)(2,1)}, bf16[256,1408]{1,0:T(8,128)(2,1)}, bf16[256,1408]{1,0:T(8,128)(2,1)}, bf16[256,2048]{1,0:T(8,128)(2,1)}, bf16[256,2048]{1,0:T(8,128)(2,1)}) custom-call(bf16[256,2048]{1,0:T(8,128)(2,1)} %collective-permute-done.27.x_ref.refs_2_, bf16[256,2048]{1,0:T(8,128)(2,1)} %collective-permute-done.22.s_ref.refs_6_, ...), custom_call_target="tpu_custom_call" | custom-call | flops 1 | bytes 1 | tf_op jit(solution)/shard_map/feed_forward/pallas_call | solution.py:355
  311.8 16.6 %feed_forward.7 = (bf16[256,1408]{1,0:T(8,128)(2,1)}, bf16[256,1408]{1,0:T(8,128)(2,1)}, bf16[256,1408]{1,0:T(8,128)(2,1)}, bf16[256,2048]{1,0:T(8,128)(2,1)}, bf16[256,2048]{1,0:T(8,128)(2,1)}) custom-call(bf16[256,2048]{1,0:T(8,128)(2,1)} %constant_dynamic-update-slice_fusion.22.x_ref.refs_3_, bf16[256,2048]{1,0:T(8,128)(2,1)} %collective-permute-done.23.s_ref.refs_7_, ...), custom_call_target="tpu_custom_call" | custom-call | flops 1 | bytes 1 | tf_op jit(solution)/shard_map/feed_forward/pallas_call | solution.py:355
  330.2 23.8 %token_grad.3 = (bf16[2048,1408]{1,0:T(8,128)(2,1)}, bf16[2048,1408]{1,0:T(8,128)(2,1)}) custom-call(s32[7]{0:T(128)} %pad_add_fusion.info_ref, bf16[256,2048]{1,0:T(8,128)(2,1)} %multiply_convert_fusion.x_ref.refs_0_, bf16[256,2048]{1,0:T(8,128)(2,1)} %collective-permute-done.26.x_ref.refs_1_, bf16[256,2048]{1,0:T(8,128)(2,1)} %collective-permute-done.27.x_ref.refs_2_, ...), custom_call_target="tpu_custom_call" | custom-call | flops 11811160064 | bytes 11534336 | tf_op jit(solution)/shard_map/token_grad/pallas_call | solution.py:425
  354.1 3.7 multiply_reduce_fusion
  360.2 3.7 collective-permute-done.33
  363.9 6.9 add_convert_fusion
  372.8 12.3 %token_grad.4 = (bf16[1408,1024]{1,0:T(8,128)(2,1)}, bf16[1408,1024]{1,0:T(8,128)(2,1)}) custom-call(s32[7]{0:T(128)} %pad_add_fusion.info_ref, bf16[256,1408]{1,0:T(8,128)(2,1)} %get-tuple-element.301.refs_0_, bf16[256,1408]{1,0:T(8,128)(2,1)} %get-tuple-element.302.refs_1_, bf16[256,1408]{1,0:T(8,128)(2,1)} %get-tuple-element.303.refs_2_, ...), custom_call_target="tpu_custom_call" | custom-call | flops 5905580032 | bytes 5767168 | tf_op jit(solution)/shard_map/token_grad/pallas_call | solution.py:425
  385.1 11.4 %collective-permute-done.34.refs_5_ = bf16[256,2048]{1,0:T(8,128)(2,1)} collective-permute-done((bf16[256,2048]{1,0:T(8,128)(2,1)}, bf16[256,2048]{1,0:T(8,128)(2,1)}, u32[]{:S(2)}, u32[]{:S(2)}) %collective-permute-start.34) | collective-permute-done | bytes 1048608 | tf_op jit(solution)/shard_map/ppermute | solution.py:602
  396.9 4.8 convolution_convert_fusion.5
  406.3 3.3 convolution_convert_fusion.4
  409.6 3.5 convolution_convert_fusion.3
  413.1 4.1 collective-permute-done.36
  420.1 3.0 add_convert_fusion.1
  426.5 3.7 convolution_convert_fusion.2
  431.7 13.5 %attend_backward.2 = (bf16[4,2,64,1024]{3,2,1,0:T(8,128)(2,1)}, bf16[4,4,2,64,512]{4,3,2,1,0:T(8,128)(2,1)}, bf16[4,4,2,64,512]{4,3,2,1,0:T(8,128)(2,1)}) custom-call(s32[7]{0:T(128)} %pad_add_fusion.info_ref, bf16[4,4,64,1024]{3,2,1,0:T(8,128)(2,1)} %get-tuple-element.319.q_ref, bf16[4,4,64,1024]{3,2,1,0:T(8,128)(2,1)} %get-tuple-element.240.o_ref, ...), custom_call_target="tpu_custom_call" | custom-call | flops 1 | bytes 1 | tf_op jit(solution)/shard_map/attend_backward/pallas_call | solution.py:252
  446.7 13.3 %attend_backward.3 = (bf16[4,2,64,1024]{3,2,1,0:T(8,128)(2,1)}, bf16[4,4,2,64,512]{4,3,2,1,0:T(8,128)(2,1)}, bf16[4,4,2,64,512]{4,3,2,1,0:T(8,128)(2,1)}) custom-call(s32[7]{0:T(128)} %pad_add_fusion.info_ref, bf16[4,4,64,1024]{3,2,1,0:T(8,128)(2,1)} %get-tuple-element.319.q_ref, bf16[4,4,64,1024]{3,2,1,0:T(8,128)(2,1)} %get-tuple-element.240.o_ref, ...), custom_call_target="tpu_custom_call" | custom-call | flops 1 | bytes 1 | tf_op jit(solution)/shard_map/attend_backward/pallas_call | solution.py:252
  460.0 12.2 %reduce-scatter.4.cloned.1.call-done = bf16[512,1408]{1,0:T(8,128)(2,1)} async-done(((bf16[2048,1408]{1,0:T(8,128)(2,1)}), bf16[512,1408]{1,0:T(8,128)(2,1)}) %reduce-scatter.4.cloned.1.call-update) | async-done | bytes 1441808 | tf_op jit(solution)/shard_map/reduce_scatter | solution.py:794
  495.9 3.0 convert_add_fusion
  504.2 9.1 token_sum.2
  516.2 9.4 %token_grad.5 = (bf16[1024,512]{1,0:T(8,128)(2,1)}, bf16[1024,512]{1,0:T(8,128)(2,1)}) custom-call(s32[7]{0:T(128)} %pad_add_fusion.info_ref, bf16[256,1024]{1,0:T(8,128)(2,1)} %get-tuple-element.348.refs_0_, bf16[256,1024]{1,0:T(8,128)(2,1)} %copy-done.45, bf16[256,1024]{1,0:T(8,128)(2,1)} %collective-permute-done.11.refs_2_, ...), custom_call_target="tpu_custom_call" | custom-call | flops 2147483648 | bytes 2097152 | tf_op jit(solution)/shard_map/token_grad/pallas_call | solution.py:425
  531.4 3.6 collective-permute-done.48
  547.0 7.7 collective-permute-done.57
  556.1 22.1 %collective-permute-done.58 = bf16[256,2048]{1,0:T(8,128)(2,1)} collective-permute-done((bf16[256,2048]{1,0:T(8,128)(2,1)}, bf16[256,2048]{1,0:T(8,128)(2,1)}, u32[]{:S(2)}, u32[]{:S(2)}) %collective-permute-start.58) | collective-permute-done | bytes 1048608 | tf_op jit(solution)/shard_map/ppermute | solution.py:602
  583.7 6.5 collective-permute-done.51
  593.2 3.2 slice_dynamic-update-slice_fusion.1
  597.7 7.0 collective-permute-done.54
  612.6 4.3 all-to-all-start.2
  628.8 4.0 all-to-all-done.2
  635.0 17.3 %collective-permute-done.61 = bf16[128,512]{1,0:T(8,128)(2,1)} collective-permute-done((bf16[128,512]{1,0:T(8,128)(2,1)}, bf16[128,512]{1,0:T(8,128)(2,1)}, u32[]{:S(2)}, u32[]{:S(2)}) %collective-permute-start.61) | collective-permute-done | bytes 131104 | tf_op jit(solution)/shard_map/ppermute | solution.py:860
  656.2 4.3 all-to-all-start.3
  660.5 6.3 project_back.1
  683.9 3.1 slice_dynamic-update-slice_fusion
  688.9 4.1 token_sum.3
  713.0 5.4 all-gather.10.cloned.1.call-done
  718.4 4.2 dynamic-slice_bitcast_fusion
  726.0 30.9 %collective-permute-done.71.refs_1_ = bf16[512,1408]{1,0:T(8,128)(2,1)S(1)} collective-permute-done((bf16[512,1408]{1,0:T(8,128)(2,1)S(1)}, bf16[512,1408]{1,0:T(8,128)(2,1)S(1)}, u32[]{:S(2)}, u32[]{:S(2)}) %collective-permute-start.71) | collective-permute-done | bytes 1441824 | tf_op jit(solution)/shard_map/ppermute | solution.py:602
  756.9 31.7 %collective-permute-done.72.refs_2_ = bf16[512,1408]{1,0:T(8,128)(2,1)S(1)} collective-permute-done((bf16[512,1408]{1,0:T(8,128)(2,1)S(1)}, bf16[512,1408]{1,0:T(8,128)(2,1)S(1)}, u32[]{:S(2)}, u32[]{:S(2)}) %collective-permute-start.72) | collective-permute-done | bytes 1441824 | tf_op jit(solution)/shard_map/ppermute | solution.py:602
  789.7 17.3 %reduce-scatter.8.cloned.1.call-done = bf16[496,1024]{1,0:T(8,128)(2,1)} async-done(((bf16[3968,1024]{1,0:T(8,128)(2,1)}), bf16[496,1024]{1,0:T(8,128)(2,1)}) %reduce-scatter.8.cloned.1.call-update) | async-done | bytes 1015824 | tf_op jit(solution)/shard_map/reduce_scatter | solution.py:948
  807.2 4.4 add_convert_fusion.3
  817.4 5.9 maximum_convert_fusion
  824.4 13.8 %place_columns.1 = (f32[512,5632]{1,0:T(8,128)}, f32[512,5632]{1,0:T(8,128)}) custom-call(s32[7]{0:T(128)} %pad_add_fusion.info_ref, bf16[512,1408]{1,0:T(8,128)(2,1)} %get-tuple-element.408.refs_0_, bf16[512,1408]{1,0:T(8,128)(2,1)} %copy-done.38, bf16[512,1408]{1,0:T(8,128)(2,1)} %copy-done.40, bf16[512,1408]{1,0:T(8,128)(2,1)} %collective-permute-done.73.refs_3_, ...), custom_call_target="tpu_custom_call" | custom-call | flops 1 | bytes 1 | tf_op jit(solution)/shard_map/place_columns/pallas_call | solution.py:586
  838.2 48.8 %all-gather.12.cloned.1.call-done = bf16[3968,1024]{1,0:T(8,128)(2,1)} async-done(((bf16[496,1024]{1,0:T(8,128)(2,1)}), bf16[3968,1024]{1,0:T(8,128)(2,1)}) %all-gather.12.cloned.1.call-update) | async-done | bytes 8126480 | tf_op jit(solution)/shard_map/all_gather | solution.py:958
  891.5 5.6 fusion.54
  902.6 4.4 maximum_convert_fusion.1
  (519 shorter events, 263.5 us)
Async XLA Ops:
  14.7 121.4 %all-gather.14.cloned.1.call-start = ((), (), s32[]{:S(2)}) async-start(), calls=%async_computation.13 | async-start | bytes 2359296 | tf_op jit(solution)/shard_map/all_gather | solution.py:695
  16.1 21.9 %collective-permute-start.1 = (bf16[272,1536]{1,0:T(8,128)(2,1)}, bf16[272,1536]{1,0:T(8,128)(2,1)}, u32[]{:S(2)}, u32[]{:S(2)}) collective-permute-start(bf16[272,1536]{1,0:T(8,128)(2,1)} %pad_maximum_fusion.5), channel_id=1, source_target_pairs={{0,2},{1,3},{2,0},{3,1},{4,6},{5,7},{6,4},{7,5},{8,10},{9,11},{10,... | collective-permute-start | bytes 2506760 | tf_op jit(solution)/shard_map/ppermute | solution.py:602
  18.1 23.6 %collective-permute-start = (bf16[272,1536]{1,0:T(8,128)(2,1)}, bf16[272,1536]{1,0:T(8,128)(2,1)}, u32[]{:S(2)}, u32[]{:S(2)}) collective-permute-start(bf16[272,1536]{1,0:T(8,128)(2,1)} %pad_maximum_fusion.5), channel_id=1, source_target_pairs={{0,1},{1,0},{2,3},{3,2},{4,5},{5,4},{6,7},{7,6},{8,9},{9,8},{10,11... | collective-permute-start | bytes 2506760 | tf_op jit(solution)/shard_map/ppermute | solution.py:602
  43.6 15.6 %collective-permute-start.4 = (bf16[272,1536]{1,0:T(8,128)(2,1)}, bf16[272,1536]{1,0:T(8,128)(2,1)}, u32[]{:S(2)}, u32[]{:S(2)}) collective-permute-start(bf16[272,1536]{1,0:T(8,128)(2,1)} %collective-permute-done.refs_0_), channel_id=1, source_target_pairs={{0,4},{4,0},{8,12},{12,8},{16,20},{20,16},{24,28},{28,24},{1,5},{5... | collective-permute-start | bytes 2506760 | tf_op jit(solution)/shard_map/core_swap/ppermute | solution.py:606
  43.6 15.6 %collective-permute-start.5 = (bf16[272,1536]{1,0:T(8,128)(2,1)}, bf16[272,1536]{1,0:T(8,128)(2,1)}, u32[]{:S(2)}, u32[]{:S(2)}) collective-permute-start(bf16[272,1536]{1,0:T(8,128)(2,1)} %collective-permute-done.1.refs_1_), channel_id=1, source_target_pairs={{0,4},{4,0},{8,12},{12,8},{16,20},{20,16},{24,28},{28,24},{1,5},{5... | collective-permute-start | bytes 2506760 | tf_op jit(solution)/shard_map/core_swap/ppermute | solution.py:606
  67.0 33.8 %all-to-all-start = ((bf16[64,4,2816]{2,0,1:T(8,128)(2,1)}), bf16[64,4,2816]{2,0,1:T(8,128)(2,1)S(1)}, u32[]{:S(2)}, u32[]{:S(2)}) async-start(bf16[64,4,2816]{2,0,1:T(8,128)(2,1)} %bitcast.176), calls=%async_computation | async-start | bytes 2883584 | tf_op jit(solution)/shard_map/all_to_all | solution.py:687
  70.7 166.7 %all-gather.16.cloned.1.call-start = ((), (), s32[]{:S(2)}) async-start(), calls=%async_computation.14 | async-start | bytes 12976128 | tf_op jit(solution)/shard_map/all_gather | solution.py:727
  70.8 29.3 %collective-permute-start.10 = (bf16[256,1024]{1,0:T(8,128)(2,1)S(1)}, bf16[256,1024]{1,0:T(8,128)(2,1)S(1)}, u32[]{:S(2)}, u32[]{:S(2)}) collective-permute-start(bf16[256,1024]{1,0:T(8,128)(2,1)S(1)} %copy-done.60), channel_id=1, source_target_pairs={{0,1},{1,0},{2,3},{3,2},{4,5},{5,4},{6,7},{7,6},{8,9},{9,8},{10,11... | collective-permute-start | bytes 1572872 | tf_op jit(solution)/shard_map/ppermute | solution.py:602
  72.7 28.2 %collective-permute-start.11 = (bf16[256,1024]{1,0:T(8,128)(2,1)S(1)}, bf16[256,1024]{1,0:T(8,128)(2,1)}, u32[]{:S(2)}, u32[]{:S(2)}) collective-permute-start(bf16[256,1024]{1,0:T(8,128)(2,1)S(1)} %copy-done.60), channel_id=1, source_target_pairs={{0,2},{1,3},{2,0},{3,1},{4,6},{5,7},{6,4},{7,5},{8,10},{9,11},{10,... | collective-permute-start | bytes 1572872 | tf_op jit(solution)/shard_map/ppermute | solution.py:602
  102.0 370.2 %reduce-scatter.4.cloned.1.call-start = ((), (), s32[]{:S(2)}) async-start(), calls=%async_computation.7 | async-start | bytes 7208960 | tf_op jit(solution)/shard_map/reduce_scatter | solution.py:794
  105.7 30.5 %collective-permute-start.12 = (bf16[1024,512]{1,0:T(8,128)(2,1)}, bf16[1024,512]{1,0:T(8,128)(2,1)S(1)}, u32[]{:S(2)}, u32[]{:S(2)}) collective-permute-start(bf16[1024,512]{1,0:T(8,128)(2,1)} %get-tuple-element.498), channel_id=1, source_target_pairs={{0,1},{1,0},{2,3},{3,2},{4,5},{5,4},{6,7},{7,6},{8,9},{9,8},{10,11... | collective-permute-start | bytes 3145736 | tf_op jit(solution)/shard_map/ppermute | solution.py:602
  106.4 29.7 %collective-permute-start.13 = (bf16[1024,512]{1,0:T(8,128)(2,1)}, bf16[1024,512]{1,0:T(8,128)(2,1)S(1)}, u32[]{:S(2)}, u32[]{:S(2)}) collective-permute-start(bf16[1024,512]{1,0:T(8,128)(2,1)} %get-tuple-element.498), channel_id=1, source_target_pairs={{0,2},{1,3},{2,0},{3,1},{4,6},{5,7},{6,4},{7,5},{8,10},{9,11},{10,... | collective-permute-start | bytes 3145736 | tf_op jit(solution)/shard_map/ppermute | solution.py:602
  109.9 25.8 %collective-permute-start.14 = (bf16[128,1024]{1,0:T(8,128)(2,1)S(1)}, bf16[128,1024]{1,0:T(8,128)(2,1)S(1)}, u32[]{:S(2)}, u32[]{:S(2)}) collective-permute-start(bf16[128,1024]{1,0:T(8,128)(2,1)S(1)} %slice.390), channel_id=1, source_target_pairs={{0,1},{1,0},{2,3},{3,2},{4,5},{5,4},{6,7},{7,6},{8,9},{9,8},{10,11... | collective-permute-start | bytes 786440 | tf_op jit(solution)/shard_map/ppermute | solution.py:602
  111.5 24.7 %collective-permute-start.15 = (bf16[128,1024]{1,0:T(8,128)(2,1)S(1)}, bf16[128,1024]{1,0:T(8,128)(2,1)}, u32[]{:S(2)}, u32[]{:S(2)}) collective-permute-start(bf16[128,1024]{1,0:T(8,128)(2,1)S(1)} %slice.391), channel_id=1, source_target_pairs={{0,2},{1,3},{2,0},{3,1},{4,6},{5,7},{6,4},{7,5},{8,10},{9,11},{10,... | collective-permute-start | bytes 786440 | tf_op jit(solution)/shard_map/ppermute | solution.py:602
  150.9 33.5 %collective-permute-start.21 = (bf16[256,2048]{1,0:T(8,128)(2,1)S(1)}, bf16[256,2048]{1,0:T(8,128)(2,1)S(1)}, u32[]{:S(2)}, u32[]{:S(2)}) collective-permute-start(bf16[256,2048]{1,0:T(8,128)(2,1)S(1)} %bitcast_convert_fusion.s_ref.refs_4_), channel_id=1, source_target_pairs={{0,1},{1,0},{2,3},{3,2},{4,5},{5,4},{6,7},{7,6},{8,9},{9,8},{10,11... | collective-permute-start | bytes 3145736 | tf_op jit(solution)/shard_map/ppermute | solution.py:602
  151.5 32.9 %collective-permute-start.22 = (bf16[256,2048]{1,0:T(8,128)(2,1)S(1)}, bf16[256,2048]{1,0:T(8,128)(2,1)}, u32[]{:S(2)}, u32[]{:S(2)}) collective-permute-start(bf16[256,2048]{1,0:T(8,128)(2,1)S(1)} %bitcast_convert_fusion.s_ref.refs_4_), channel_id=1, source_target_pairs={{0,2},{1,3},{2,0},{3,1},{4,6},{5,7},{6,4},{7,5},{8,10},{9,11},{10,... | collective-permute-start | bytes 3145736 | tf_op jit(solution)/shard_map/ppermute | solution.py:602
  152.9 47.3 %collective-permute-start.23 = (bf16[256,2048]{1,0:T(8,128)(2,1)S(1)}, bf16[256,2048]{1,0:T(8,128)(2,1)}, u32[]{:S(2)}, u32[]{:S(2)}) collective-permute-start(bf16[256,2048]{1,0:T(8,128)(2,1)S(1)} %bitcast_convert_fusion.s_ref.refs_4_), channel_id=1, source_target_pairs={{0,3},{1,2},{2,1},{3,0},{4,7},{5,6},{6,5},{7,4},{8,11},{9,10},{10,... | collective-permute-start | bytes 3145736 | tf_op jit(solution)/shard_map/ppermute | solution.py:602
  180.0 30.3 %collective-permute-start.19 = (bf16[128,2048]{1,0:T(8,128)(2,1)S(1)}, bf16[128,2048]{1,0:T(8,128)(2,1)S(1)}, u32[]{:S(2)}, u32[]{:S(2)}) collective-permute-start(bf16[128,2048]{1,0:T(8,128)(2,1)S(1)} %get-tuple-element.482), channel_id=1, source_target_pairs={{0,1},{1,0},{2,3},{3,2},{4,5},{5,4},{6,7},{7,6},{8,9},{9,8},{10,11... | collective-permute-start | bytes 1572872 | tf_op jit(solution)/shard_map/ppermute | solution.py:602
  180.5 30.3 %collective-permute-start.20 = (bf16[128,2048]{1,0:T(8,128)(2,1)S(1)}, bf16[128,2048]{1,0:T(8,128)(2,1)S(1)}, u32[]{:S(2)}, u32[]{:S(2)}) collective-permute-start(bf16[128,2048]{1,0:T(8,128)(2,1)S(1)} %get-tuple-element.481), channel_id=1, source_target_pairs={{0,2},{1,3},{2,0},{3,1},{4,6},{5,7},{6,4},{7,5},{8,10},{9,11},{10,... | collective-permute-start | bytes 1572872 | tf_op jit(solution)/shard_map/ppermute | solution.py:602
  211.1 25.2 %collective-permute-start.24 = (bf16[256,2048]{1,0:T(8,128)(2,1)S(1)}, bf16[256,2048]{1,0:T(8,128)(2,1)S(1)}, u32[]{:S(2)}, u32[]{:S(2)}) collective-permute-start(bf16[256,2048]{1,0:T(8,128)(2,1)S(1)} %pad_maximum_fusion.3), channel_id=1, source_target_pairs={{0,1},{1,0},{2,3},{3,2},{4,5},{5,4},{6,7},{7,6},{8,9},{9,8},{10,11... | collective-permute-start | bytes 3145736 | tf_op jit(solution)/shard_map/ppermute | solution.py:602
  212.6 24.9 %collective-permute-start.25 = (bf16[256,2048]{1,0:T(8,128)(2,1)S(1)}, bf16[256,2048]{1,0:T(8,128)(2,1)}, u32[]{:S(2)}, u32[]{:S(2)}) collective-permute-start(bf16[256,2048]{1,0:T(8,128)(2,1)S(1)} %pad_maximum_fusion.4), channel_id=1, source_target_pairs={{0,2},{1,3},{2,0},{3,1},{4,6},{5,7},{6,4},{7,5},{8,10},{9,11},{10,... | collective-permute-start | bytes 3145736 | tf_op jit(solution)/shard_map/ppermute | solution.py:602
  241.5 24.6 %collective-permute-start.26 = (bf16[256,2048]{1,0:T(8,128)(2,1)}, bf16[256,2048]{1,0:T(8,128)(2,1)}, u32[]{:S(2)}, u32[]{:S(2)}) collective-permute-start(bf16[256,2048]{1,0:T(8,128)(2,1)} %multiply_convert_fusion.x_ref.refs_0_), channel_id=1, source_target_pairs={{0,1},{1,0},{2,3},{3,2},{4,5},{5,4},{6,7},{7,6},{8,9},{9,8},{10,11... | collective-permute-start | bytes 3145736 | tf_op jit(solution)/shard_map/ppermute | solution.py:602
  242.6 24.1 %collective-permute-start.27 = (bf16[256,2048]{1,0:T(8,128)(2,1)}, bf16[256,2048]{1,0:T(8,128)(2,1)}, u32[]{:S(2)}, u32[]{:S(2)}) collective-permute-start(bf16[256,2048]{1,0:T(8,128)(2,1)} %multiply_convert_fusion.x_ref.refs_0_), channel_id=1, source_target_pairs={{0,2},{1,3},{2,0},{3,1},{4,6},{5,7},{6,4},{7,5},{8,10},{9,11},{10,... | collective-permute-start | bytes 3145736 | tf_op jit(solution)/shard_map/ppermute | solution.py:602
  268.6 38.3 %collective-permute-start.29 = (bf16[128,2048]{1,0:T(8,128)(2,1)}, bf16[128,2048]{1,0:T(8,128)(2,1)}, u32[]{:S(2)}, u32[]{:S(2)}) collective-permute-start(bf16[128,2048]{1,0:T(8,128)(2,1)} %slice.405), channel_id=1, source_target_pairs={{0,1},{1,0},{2,3},{3,2},{4,5},{5,4},{6,7},{7,6},{8,9},{9,8},{10,11... | collective-permute-start | bytes 1572872 | tf_op jit(solution)/shard_map/ppermute | solution.py:602
  271.7 35.2 %collective-permute-start.30 = (bf16[128,2048]{1,0:T(8,128)(2,1)}, bf16[128,2048]{1,0:T(8,128)(2,1)}, u32[]{:S(2)}, u32[]{:S(2)}) collective-permute-start(bf16[128,2048]{1,0:T(8,128)(2,1)} %slice.406), channel_id=1, source_target_pairs={{0,2},{1,3},{2,0},{3,1},{4,6},{5,7},{6,4},{7,5},{8,10},{9,11},{10,... | collective-permute-start | bytes 1572872 | tf_op jit(solution)/shard_map/ppermute | solution.py:602
  289.2 64.8 %collective-permute-start.28 = (bf16[256,2048]{1,0:T(8,128)(2,1)}, bf16[256,2048]{1,0:T(8,128)(2,1)}, u32[]{:S(2)}, u32[]{:S(2)}) collective-permute-start(bf16[256,2048]{1,0:T(8,128)(2,1)} %get-tuple-element.258), channel_id=1, source_target_pairs={{0,1},{1,0},{2,3},{3,2},{4,5},{5,4},{6,7},{7,6},{8,9},{9,8},{10,11... | collective-permute-start | bytes 3145736 | tf_op jit(solution)/shard_map/ppermute | solution.py:602
  306.9 47.1 %collective-permute-start.31 = (bf16[256,2048]{1,0:T(8,128)(2,1)}, bf16[256,2048]{1,0:T(8,128)(2,1)}, u32[]{:S(2)}, u32[]{:S(2)}) collective-permute-start(bf16[256,2048]{1,0:T(8,128)(2,1)} %get-tuple-element.262), channel_id=1, source_target_pairs={{0,2},{1,3},{2,0},{3,1},{4,6},{5,7},{6,4},{7,5},{8,10},{9,11},{10,... | collective-permute-start | bytes 3145736 | tf_op jit(solution)/shard_map/ppermute | solution.py:602
  328.5 25.5 %collective-permute-start.32 = (bf16[256,2048]{1,0:T(8,128)(2,1)}, bf16[256,2048]{1,0:T(8,128)(2,1)}, u32[]{:S(2)}, u32[]{:S(2)}) collective-permute-start(bf16[256,2048]{1,0:T(8,128)(2,1)} %get-tuple-element.275), channel_id=1, source_target_pairs={{0,3},{1,2},{2,1},{3,0},{4,7},{5,6},{6,5},{7,4},{8,11},{9,10},{10,... | collective-permute-start | bytes 3145736 | tf_op jit(solution)/shard_map/ppermute | solution.py:602
  370.8 165.8 %reduce-scatter.6.cloned.1.call-start = ((), (), s32[]{:S(2)}) async-start(), calls=%async_computation.8 | async-start | bytes 3604480 | tf_op jit(solution)/shard_map/reduce_scatter | solution.py:813
  370.8 25.6 %collective-permute-start.34 = (bf16[256,2048]{1,0:T(8,128)(2,1)}, bf16[256,2048]{1,0:T(8,128)(2,1)}, u32[]{:S(2)}, u32[]{:S(2)}) collective-permute-start(bf16[256,2048]{1,0:T(8,128)(2,1)} %get-tuple-element.294.refs_4_), channel_id=1, source_target_pairs={{0,1},{1,0},{2,3},{3,2},{4,5},{5,4},{6,7},{7,6},{8,9},{9,8},{10,11... | collective-permute-start | bytes 3145736 | tf_op jit(solution)/shard_map/ppermute | solution.py:602
  371.7 25.2 %collective-permute-start.35 = (bf16[256,2048]{1,0:T(8,128)(2,1)}, bf16[256,2048]{1,0:T(8,128)(2,1)}, u32[]{:S(2)}, u32[]{:S(2)}) collective-permute-start(bf16[256,2048]{1,0:T(8,128)(2,1)} %get-tuple-element.294.refs_4_), channel_id=1, source_target_pairs={{0,2},{1,3},{2,0},{3,1},{4,6},{5,7},{6,4},{7,5},{8,10},{9,11},{10,... | collective-permute-start | bytes 3145736 | tf_op jit(solution)/shard_map/ppermute | solution.py:602
  396.9 22.4 %collective-permute-start.38 = (bf16[1408,1024]{1,0:T(8,128)(2,1)}, bf16[1408,1024]{1,0:T(8,128)(2,1)S(1)}, u32[]{:S(2)}, u32[]{:S(2)}) collective-permute-start(bf16[1408,1024]{1,0:T(8,128)(2,1)} %get-tuple-element.313), channel_id=1, source_target_pairs={{0,4},{4,0},{8,12},{12,8},{16,20},{20,16},{24,28},{28,24},{1,5},{5... | collective-permute-start | bytes 8650760 | tf_op jit(solution)/shard_map/core_swap/ppermute | solution.py:606
  402.8 14.4 %collective-permute-start.36 = (bf16[128,2048]{1,0:T(8,128)(2,1)S(1)}, bf16[128,2048]{1,0:T(8,128)(2,1)S(1)}, u32[]{:S(2)}, u32[]{:S(2)}) collective-permute-start(bf16[128,2048]{1,0:T(8,128)(2,1)S(1)} %slice.407), channel_id=1, source_target_pairs={{0,1},{1,0},{2,3},{3,2},{4,5},{5,4},{6,7},{7,6},{8,9},{9,8},{10,11... | collective-permute-start | bytes 1572872 | tf_op jit(solution)/shard_map/ppermute | solution.py:602
  405.2 14.1 %collective-permute-start.37 = (bf16[128,2048]{1,0:T(8,128)(2,1)S(1)}, bf16[128,2048]{1,0:T(8,128)(2,1)S(1)}, u32[]{:S(2)}, u32[]{:S(2)}) collective-permute-start(bf16[128,2048]{1,0:T(8,128)(2,1)S(1)} %slice.408), channel_id=1, source_target_pairs={{0,2},{1,3},{2,0},{3,1},{4,6},{5,7},{6,4},{7,5},{8,10},{9,11},{10,... | collective-permute-start | bytes 1572872 | tf_op jit(solution)/shard_map/ppermute | solution.py:602
  423.2 284.9 %all-gather.8.cloned.1.call-start = ((), (), s32[]{:S(2)}) async-start(), calls=%async_computation.9 | async-start | bytes 7208960 | tf_op jit(solution)/shard_map/all_gather | solution.py:827
  445.2 14.8 %collective-permute-start.39 = (bf16[4,4,2,64,512]{4,3,2,1,0:T(8,128)(2,1)}, bf16[4,4,2,64,512]{4,3,2,1,0:T(8,128)(2,1)}, u32[]{:S(2)}, u32[]{:S(2)}) collective-permute-start(bf16[4,4,2,64,512]{4,3,2,1,0:T(8,128)(2,1)} %get-tuple-element.334), channel_id=1, source_target_pairs={{0,4},{4,0},{8,12},{12,8},{16,20},{20,16},{24,28},{28,24},{1,5},{5... | collective-permute-start | bytes 6291464 | tf_op jit(solution)/shard_map/core_swap/ppermute | solution.py:606
  472.3 246.1 %all-gather.10.cloned.1.call-start = ((), (), s32[]{:S(2)}) async-start(), calls=%async_computation.10 | async-start | bytes 3604480 | tf_op jit(solution)/shard_map/all_gather | solution.py:853
  493.9 42.7 %collective-permute-start.43 = (bf16[512,512]{1,0:T(8,128)(2,1)}, bf16[512,512]{1,0:T(8,128)(2,1)}, u32[]{:S(2)}, u32[]{:S(2)}) collective-permute-start(bf16[512,512]{1,0:T(8,128)(2,1)} %pad_maximum_fusion.12), channel_id=1, source_target_pairs={{0,1},{1,0},{2,3},{3,2},{4,5},{5,4},{6,7},{7,6},{8,9},{9,8},{10,11... | collective-permute-start | bytes 1572872 | tf_op jit(solution)/shard_map/ppermute | solution.py:602
  495.3 41.3 %collective-permute-start.44 = (bf16[512,512]{1,0:T(8,128)(2,1)}, bf16[512,512]{1,0:T(8,128)(2,1)}, u32[]{:S(2)}, u32[]{:S(2)}) collective-permute-start(bf16[512,512]{1,0:T(8,128)(2,1)} %pad_maximum_fusion.13), channel_id=1, source_target_pairs={{0,2},{1,3},{2,0},{3,1},{4,6},{5,7},{6,4},{7,5},{8,10},{9,11},{10,... | collective-permute-start | bytes 1572872 | tf_op jit(solution)/shard_map/ppermute | solution.py:602
  499.9 25.7 %collective-permute-start.45 = (bf16[256,512]{1,0:T(8,128)(2,1)}, bf16[256,512]{1,0:T(8,128)(2,1)}, u32[]{:S(2)}, u32[]{:S(2)}) collective-permute-start(bf16[256,512]{1,0:T(8,128)(2,1)} %bitcast.42), channel_id=1, source_target_pairs={{0,1},{1,0},{2,3},{3,2},{4,5},{5,4},{6,7},{7,6},{8,9},{9,8},{10,11... | collective-permute-start | bytes 786440 | tf_op jit(solution)/shard_map/ppermute | solution.py:602
  501.4 27.0 %collective-permute-start.46 = (bf16[256,512]{1,0:T(8,128)(2,1)}, bf16[256,512]{1,0:T(8,128)(2,1)}, u32[]{:S(2)}, u32[]{:S(2)}) collective-permute-start(bf16[256,512]{1,0:T(8,128)(2,1)} %bitcast.43), channel_id=1, source_target_pairs={{0,2},{1,3},{2,0},{3,1},{4,6},{5,7},{6,4},{7,5},{8,10},{9,11},{10,... | collective-permute-start | bytes 786440 | tf_op jit(solution)/shard_map/ppermute | solution.py:602
  503.7 26.2 %collective-permute-start.47 = (bf16[128,1024]{1,0:T(8,128)(2,1)}, bf16[128,1024]{1,0:T(8,128)(2,1)}, u32[]{:S(2)}, u32[]{:S(2)}) collective-permute-start(bf16[128,1024]{1,0:T(8,128)(2,1)} %get-tuple-element.494), channel_id=1, source_target_pairs={{0,1},{1,0},{2,3},{3,2},{4,5},{5,4},{6,7},{7,6},{8,9},{9,8},{10,11... | collective-permute-start | bytes 786440 | tf_op jit(solution)/shard_map/ppermute | solution.py:602
  528.3 26.4 %collective-permute-start.57 = (bf16[256,2048]{1,0:T(8,128)(2,1)}, bf16[256,2048]{1,0:T(8,128)(2,1)}, u32[]{:S(2)}, u32[]{:S(2)}) collective-permute-start(bf16[256,2048]{1,0:T(8,128)(2,1)} %get-tuple-element.366), channel_id=1, source_target_pairs={{0,1},{1,0},{2,3},{3,2},{4,5},{5,4},{6,7},{7,6},{8,9},{9,8},{10,11... | collective-permute-start | bytes 3145736 | tf_op jit(solution)/shard_map/ppermute | solution.py:602
  529.8 48.3 %collective-permute-start.58 = (bf16[256,2048]{1,0:T(8,128)(2,1)}, bf16[256,2048]{1,0:T(8,128)(2,1)}, u32[]{:S(2)}, u32[]{:S(2)}) collective-permute-start(bf16[256,2048]{1,0:T(8,128)(2,1)} %get-tuple-element.367), channel_id=1, source_target_pairs={{0,2},{1,3},{2,0},{3,1},{4,6},{5,7},{6,4},{7,5},{8,10},{9,11},{10,... | collective-permute-start | bytes 3145736 | tf_op jit(solution)/shard_map/ppermute | solution.py:602
  535.0 46.1 %collective-permute-start.59 = (bf16[256,2048]{1,0:T(8,128)(2,1)}, bf16[256,2048]{1,0:T(8,128)(2,1)}, u32[]{:S(2)}, u32[]{:S(2)}) collective-permute-start(bf16[256,2048]{1,0:T(8,128)(2,1)} %get-tuple-element.368), channel_id=1, source_target_pairs={{0,3},{1,2},{2,1},{3,0},{4,7},{5,6},{6,5},{7,4},{8,11},{9,10},{10,... | collective-permute-start | bytes 3145736 | tf_op jit(solution)/shard_map/ppermute | solution.py:602
  539.5 43.1 %collective-permute-start.49 = (bf16[128,512]{1,0:T(8,128)(2,1)S(1)}, bf16[128,512]{1,0:T(8,128)(2,1)}, u32[]{:S(2)}, u32[]{:S(2)}) collective-permute-start(bf16[128,512]{1,0:T(8,128)(2,1)S(1)} %get-tuple-element.492), channel_id=1, source_target_pairs={{8,0},{12,4},{16,8},{20,12},{24,16},{28,20},{9,1},{13,5},{17,9},{2... | collective-permute-start | bytes 393224 | tf_op jit(solution)/shard_map/ppermute | solution.py:860
  540.9 64.8 %collective-permute-start.56 = (bf16[1024,512]{1,0:T(8,128)(2,1)}, bf16[1024,512]{1,0:T(8,128)(2,1)}, u32[]{:S(2)}, u32[]{:S(2)}) collective-permute-start(bf16[1024,512]{1,0:T(8,128)(2,1)} %get-tuple-element.364), channel_id=1, source_target_pairs={{0,4},{4,0},{8,12},{12,8},{16,20},{20,16},{24,28},{28,24},{1,5},{5... | collective-permute-start | bytes 3145736 | tf_op jit(solution)/shard_map/core_swap/ppermute | solution.py:606
  554.8 28.4 %collective-permute-start.50 = (bf16[128,512]{1,0:T(8,128)(2,1)S(1)}, bf16[128,512]{1,0:T(8,128)(2,1)}, u32[]{:S(2)}, u32[]{:S(2)}) collective-permute-start(bf16[128,512]{1,0:T(8,128)(2,1)S(1)} %get-tuple-element.491), channel_id=1, source_target_pairs={{16,0},{20,4},{24,8},{28,12},{17,1},{21,5},{25,9},{29,13},{18,2},{... | collective-permute-start | bytes 393224 | tf_op jit(solution)/shard_map/ppermute | solution.py:860
  581.1 15.4 %collective-permute-start.52 = (bf16[512,512]{1,0:T(8,128)(2,1)}, bf16[512,512]{1,0:T(8,128)(2,1)}, u32[]{:S(2)}, u32[]{:S(2)}) collective-permute-start(bf16[512,512]{1,0:T(8,128)(2,1)} %pad_maximum_fusion.14), channel_id=1, source_target_pairs={{0,1},{1,0},{2,3},{3,2},{4,5},{5,4},{6,7},{7,6},{8,9},{9,8},{10,11... | collective-permute-start | bytes 1572872 | tf_op jit(solution)/shard_map/ppermute | solution.py:602
  582.6 15.2 %collective-permute-start.53 = (bf16[512,512]{1,0:T(8,128)(2,1)}, bf16[512,512]{1,0:T(8,128)(2,1)}, u32[]{:S(2)}, u32[]{:S(2)}) collective-permute-start(bf16[512,512]{1,0:T(8,128)(2,1)} %pad_maximum_fusion.15), channel_id=1, source_target_pairs={{0,2},{1,3},{2,0},{3,1},{4,6},{5,7},{6,4},{7,5},{8,10},{9,11},{10,... | collective-permute-start | bytes 1572872 | tf_op jit(solution)/shard_map/ppermute | solution.py:602
  583.2 21.6 %collective-permute-start.54 = (bf16[256,1024]{1,0:T(8,128)(2,1)}, bf16[256,1024]{1,0:T(8,128)(2,1)}, u32[]{:S(2)}, u32[]{:S(2)}) collective-permute-start(bf16[256,1024]{1,0:T(8,128)(2,1)} %pad_maximum_fusion.16), channel_id=1, source_target_pairs={{0,1},{1,0},{2,3},{3,2},{4,5},{5,4},{6,7},{7,6},{8,9},{9,8},{10,11... | collective-permute-start | bytes 1572872 | tf_op jit(solution)/shard_map/ppermute | solution.py:602
  590.2 15.5 %collective-permute-start.55 = (bf16[256,1024]{1,0:T(8,128)(2,1)}, bf16[256,1024]{1,0:T(8,128)(2,1)}, u32[]{:S(2)}, u32[]{:S(2)}) collective-permute-start(bf16[256,1024]{1,0:T(8,128)(2,1)} %pad_maximum_fusion.17), channel_id=1, source_target_pairs={{0,2},{1,3},{2,0},{3,1},{4,6},{5,7},{6,4},{7,5},{8,10},{9,11},{10,... | collective-permute-start | bytes 1572872 | tf_op jit(solution)/shard_map/ppermute | solution.py:602
  609.9 42.3 %collective-permute-start.63 = (bf16[256,1024]{1,0:T(8,128)(2,1)}, bf16[256,1024]{1,0:T(8,128)(2,1)}, u32[]{:S(2)}, u32[]{:S(2)}) collective-permute-start(bf16[256,1024]{1,0:T(8,128)(2,1)} %subtract_convert_fusion.refs_4_), channel_id=1, source_target_pairs={{0,1},{1,0},{2,3},{3,2},{4,5},{5,4},{6,7},{7,6},{8,9},{9,8},{10,11... | collective-permute-start | bytes 1572872 | tf_op jit(solution)/shard_map/ppermute | solution.py:602
  610.7 41.6 %collective-permute-start.64 = (bf16[256,1024]{1,0:T(8,128)(2,1)}, bf16[256,1024]{1,0:T(8,128)(2,1)}, u32[]{:S(2)}, u32[]{:S(2)}) collective-permute-start(bf16[256,1024]{1,0:T(8,128)(2,1)} %subtract_convert_fusion.refs_4_), channel_id=1, source_target_pairs={{0,2},{1,3},{2,0},{3,1},{4,6},{5,7},{6,4},{7,5},{8,10},{9,11},{10,... | collective-permute-start | bytes 1572872 | tf_op jit(solution)/shard_map/ppermute | solution.py:602
  612.6 20.3 %all-to-all-start.2 = ((bf16[256,4,512]{2,0,1:T(8,128)(2,1)}), bf16[256,4,512]{2,0,1:T(8,128)(2,1)}, u32[]{:S(2)}, u32[]{:S(2)}) async-start(bf16[256,4,512]{2,0,1:T(8,128)(2,1)} %bitcast.212), calls=%async_computation.4 | async-start | bytes 2097152 | tf_op jit(solution)/shard_map/all_to_all | solution.py:880
  620.3 14.6 %collective-permute-start.60 = (bf16[128,512]{1,0:T(8,128)(2,1)}, bf16[128,512]{1,0:T(8,128)(2,1)}, u32[]{:S(2)}, u32[]{:S(2)}) collective-permute-start(bf16[128,512]{1,0:T(8,128)(2,1)} %get-tuple-element.489), channel_id=1, source_target_pairs={{8,0},{12,4},{16,8},{20,12},{24,16},{28,20},{9,1},{13,5},{17,9},{2... | collective-permute-start | bytes 393224 | tf_op jit(solution)/shard_map/ppermute | solution.py:860
  621.6 30.6 %collective-permute-start.61 = (bf16[128,512]{1,0:T(8,128)(2,1)}, bf16[128,512]{1,0:T(8,128)(2,1)}, u32[]{:S(2)}, u32[]{:S(2)}) collective-permute-start(bf16[128,512]{1,0:T(8,128)(2,1)} %get-tuple-element.488), channel_id=1, source_target_pairs={{16,0},{20,4},{24,8},{28,12},{17,1},{21,5},{25,9},{29,13},{18,2},{... | collective-permute-start | bytes 393224 | tf_op jit(solution)/shard_map/ppermute | solution.py:860
  622.9 29.3 %collective-permute-start.62 = (bf16[128,512]{1,0:T(8,128)(2,1)}, bf16[128,512]{1,0:T(8,128)(2,1)}, u32[]{:S(2)}, u32[]{:S(2)}) collective-permute-start(bf16[128,512]{1,0:T(8,128)(2,1)} %get-tuple-element.487), channel_id=1, source_target_pairs={{24,0},{28,4},{25,1},{29,5},{26,2},{30,6},{27,3},{31,7}} | collective-permute-start | bytes 393224 | tf_op jit(solution)/shard_map/ppermute | solution.py:860
  656.2 39.2 %all-to-all-start.3 = ((bf16[4,256,512]{2,1,0:T(8,128)(2,1)}), bf16[4,256,512]{2,1,0:T(8,128)(2,1)}, u32[]{:S(2)}, u32[]{:S(2)}) async-start(bf16[4,256,512]{2,1,0:T(8,128)(2,1)} %bitcast.210), calls=%async_computation.5 | async-start | bytes 2097152 | tf_op jit(solution)/shard_map/all_to_all | solution.py:887
  660.5 146.6 %reduce-scatter.8.cloned.1.call-start = ((), (), s32[]{:S(2)}) async-start(), calls=%async_computation.11 | async-start | bytes 9142272 | tf_op jit(solution)/shard_map/reduce_scatter | solution.py:948
  712.7 174.3 %all-gather.12.cloned.1.call-start = ((), (), s32[]{:S(2)}) async-start(), calls=%async_computation.12 | async-start | bytes 9142272 | tf_op jit(solution)/shard_map/all_gather | solution.py:958
  722.5 34.4 %collective-permute-start.71 = (bf16[512,1408]{1,0:T(8,128)(2,1)S(1)}, bf16[512,1408]{1,0:T(8,128)(2,1)S(1)}, u32[]{:S(2)}, u32[]{:S(2)}) collective-permute-start(bf16[512,1408]{1,0:T(8,128)(2,1)S(1)} %get-tuple-element.445), channel_id=1, source_target_pairs={{0,1},{1,0},{2,3},{3,2},{4,5},{5,4},{6,7},{7,6},{8,9},{9,8},{10,11... | collective-permute-start | bytes 4325384 | tf_op jit(solution)/shard_map/ppermute | solution.py:602
  724.0 64.6 %collective-permute-start.72 = (bf16[512,1408]{1,0:T(8,128)(2,1)S(1)}, bf16[512,1408]{1,0:T(8,128)(2,1)S(1)}, u32[]{:S(2)}, u32[]{:S(2)}) collective-permute-start(bf16[512,1408]{1,0:T(8,128)(2,1)S(1)} %get-tuple-element.444), channel_id=1, source_target_pairs={{0,2},{1,3},{2,0},{3,1},{4,6},{5,7},{6,4},{7,5},{8,10},{9,11},{10,... | collective-permute-start | bytes 4325384 | tf_op jit(solution)/shard_map/ppermute | solution.py:602
  725.5 64.3 %collective-permute-start.73 = (bf16[512,1408]{1,0:T(8,128)(2,1)S(1)}, bf16[512,1408]{1,0:T(8,128)(2,1)}, u32[]{:S(2)}, u32[]{:S(2)}) collective-permute-start(bf16[512,1408]{1,0:T(8,128)(2,1)S(1)} %get-tuple-element.443), channel_id=1, source_target_pairs={{0,3},{1,2},{2,1},{3,0},{4,7},{5,6},{6,5},{7,4},{8,11},{9,10},{10,... | collective-permute-start | bytes 4325384 | tf_op jit(solution)/shard_map/ppermute | solution.py:602
  (117 other events, 926.4 us)
Sparse Core Ops, SparseCore 0:
  21.6 29.6 all-gather.13
  102.1 108.3 all-gather.15
  370.9 101.2 reduce-scatter.3
  475.0 56.6 reduce-scatter.5
  533.1 127.2 all-gather.7
  661.8 56.4 all-gather.9
  721.2 85.8 reduce-scatter.7
  808.7 78.2 all-gather.11

commit v3 on v2

--- a/solution.py
+++ b/solution.py
@@ -67,10 +67,9 @@
     return ((inside // span) ^ index) * span + lax.rem(inside, span)
 
 
-def key_block(info_ref, step, depth):
+def key_block(info_ref, step, near):
     place, core = info_ref[0], info_ref[2]
-    parity = jnp.where(step < depth, core, 1 - core)
-    return 2 * (place // 2 - lax.rem(step, depth)) + parity
+    return 2 * (place // 2 - step) + (core if near else 1 - core)
 
 
 def allowed_keys(keys_at, place, limit, rows, block, span, index):
@@ -88,7 +87,7 @@
     heads = columns // HD
     block = groups * span
     depth = kv_near.shape[1]
-    steps = 2 * depth
+    steps = depth
     rows = heads * block
     factor = HD ** (-0.5)
 
@@ -111,10 +110,7 @@
             l_s[...] = jnp.zeros((1, rows), F32)
             acc_s[...] = jnp.zeros((HD, rows), F32)
 
-        keys_at = key_block(info_ref, step, depth)
-        needed = (keys_at >= 0) & (keys_at <= place) & (keys_at * block < limit)
-
-        def work(kv_ref):
+        def work(kv_ref, keys_at):
             k = kv_ref[:, 0, 0, :, :HD].reshape(block, HD)
             v = kv_ref[:, 0, 0, :, HD:].reshape(block, HD)
             scores = dot_back(k, q_s[...])
@@ -127,13 +123,12 @@
             acc_s[...] = acc_s[...] * shrink + dot_rows(v, weights.astype(BF16))
             m_s[...] = best
 
-        @pl.when(needed & (step < depth))
-        def _():
-            work(near_ref)
-
-        @pl.when(needed & (step >= depth))
-        def _():
-            work(far_ref)
+        for near, kv_ref in ((True, near_ref), (False, far_ref)):
+            keys_at = key_block(info_ref, step, near)
+
+            @pl.when((keys_at >= 0) & (keys_at <= place) & (keys_at * block < limit))
+            def _(kv_ref=kv_ref, keys_at=keys_at):
+                work(kv_ref, keys_at)
 
         @pl.when(step == steps - 1)
         def _():
@@ -147,14 +142,13 @@
     tokens = pl.BlockSpec((groups, 1, span, columns), lambda s, t, i: (0, s, 0, 0))
     table = pl.BlockSpec((block, HALF), lambda s, t, i: (0, 0))
     shape = (groups, 1, 1, span, 2 * HD)
-    near = pl.BlockSpec(shape, lambda s, t, i: (0, jnp.minimum(jnp.minimum(t, depth - 1), i[0] // 2), s, 0, 0))
-    far = pl.BlockSpec(shape, lambda s, t, i: (0, jnp.minimum(jnp.maximum(t - depth, 0), i[0] // 2), s, 0, 0))
+    keys = pl.BlockSpec(shape, lambda s, t, i: (0, jnp.minimum(t, i[0] // 2), s, 0, 0))
     return pl.pallas_call(
         kernel,
         grid_spec=pltpu.PrefetchScalarGridSpec(
             num_scalar_prefetch=1,
             grid=(seqs, steps),
-            in_specs=[tokens, near, far, table, table],
+            in_specs=[tokens, keys, keys, table, table],
             out_specs=[tokens, tokens, pl.BlockSpec((1, 1, rows), lambda s, t, i: (s, 0, 0))],
             scratch_shapes=[
                 pltpu.VMEM((rows, HD), BF16),
@@ -179,7 +173,7 @@
     heads = columns // HD
     block = groups * span
     depth = kv_near.shape[1]
-    steps = 2 * depth
+    steps = depth
     rows = heads * block
     factor = HD ** (-0.5)
 
@@ -199,10 +193,7 @@
                 delta_s[:, part] = jnp.broadcast_to(both, (block, 128)).T[:1]
             acc_s[...] = jnp.zeros((HD, rows), F32)
 
-        keys_at = key_block(info_ref, lax.rem(step + depth, steps), depth)
-        needed = (keys_at >= 0) & (keys_at <= place) & (keys_at * block < limit)
-
-        def work(kv_ref, dkv_ref):
+        def work(kv_ref, dkv_ref, keys_at):
             k = kv_ref[:, 0, 0, :, :HD].reshape(block, HD)
             v = kv_ref[:, 0, 0, :, HD:].reshape(block, HD)
             q, grads = q_s[...], do_s[...]
@@ -217,14 +208,16 @@
                 dot(probs.astype(BF16), grads).astype(BF16).reshape(groups, span, HD)
             )
 
-        for turn, kv_ref, dkv_ref in ((step < depth, far_ref, dfar_ref), (step >= depth, near_ref, dnear_ref)):
-
-            @pl.when(needed & turn)
-            def _():
-                work(kv_ref, dkv_ref)
-
-            @pl.when(jnp.logical_not(needed) & turn)
-            def _():
+        for near, kv_ref, dkv_ref in ((True, near_ref, dnear_ref), (False, far_ref, dfar_ref)):
+            keys_at = key_block(info_ref, step, near)
+            needed = (keys_at >= 0) & (keys_at <= place) & (keys_at * block < limit)
+
+            @pl.when(needed)
+            def _(kv_ref=kv_ref, dkv_ref=dkv_ref, keys_at=keys_at):
+                work(kv_ref, dkv_ref, keys_at)
+
+            @pl.when(jnp.logical_not(needed))
+            def _(dkv_ref=dkv_ref):
                 dkv_ref[...] = jnp.zeros(dkv_ref.shape, BF16)
 
         @pl.when(step == steps - 1)
@@ -242,12 +235,8 @@
     tokens_out = pl.BlockSpec((groups, 1, span, columns), lambda s, t, i: (0, s, 0, 0))
     table = pl.BlockSpec((block, HALF), lambda s, t, i: (0, 0))
     shape = (groups, 1, 1, span, 2 * HD)
-    early = lambda t: jnp.minimum(t, depth - 1)
-    late = lambda t: jnp.maximum(t - depth, 0)
-    far = pl.BlockSpec(shape, lambda s, t, i: (0, jnp.minimum(early(t), i[0] // 2), s + first, 0, 0))
-    near = pl.BlockSpec(shape, lambda s, t, i: (0, jnp.minimum(late(t), i[0] // 2), s + first, 0, 0))
-    far_out = pl.BlockSpec(shape, lambda s, t, i: (0, early(t), s, 0, 0))
-    near_out = pl.BlockSpec(shape, lambda s, t, i: (0, late(t), s, 0, 0))
+    keys = pl.BlockSpec(shape, lambda s, t, i: (0, jnp.minimum(t, i[0] // 2), s + first, 0, 0))
+    keys_out = pl.BlockSpec(shape, lambda s, t, i: (0, t, s, 0, 0))
     dkv_shape = jax.ShapeDtypeStruct((groups, depth, count, span, 2 * HD), BF16)
     return pl.pallas_call(
         kernel,
@@ -259,12 +248,12 @@
                 tokens,
                 tokens,
                 pl.BlockSpec((1, 1, rows), lambda s, t, i: (s + first, 0, 0)),
-                near,
-                far,
+                keys,
+                keys,
                 table,
                 table,
             ],
-            out_specs=[tokens_out, near_out, far_out],
+            out_specs=[tokens_out, keys_out, keys_out],
             scratch_shapes=[
                 pltpu.VMEM((rows, HD), BF16),
                 pltpu.VMEM((rows, HD), BF16),
@@ -371,6 +360,64 @@
     )(x, signal, gu, gu, gu, gu, down_w)
 
 
+def hidden_units(x, gu, hidden):
+    tokens, width = x.shape
+    shares, blocks, share, columns = gu.shape
+    lanes = 128
+    up_at = columns // 2 // lanes
+    tile = 2 * lanes
+    steps = -(-hidden // tile)
+    tail = hidden - (steps - 1) * tile
+
+    def kernel(x_ref, ga_ref, gb_ref, ua_ref, ub_ref, inner_ref, g_s, u_s):
+        step = pl.program_id(0)
+
+        def work(size):
+            for s in range(shares):
+                for b in range(blocks):
+                    at = slice((b * shares + s) * share, (b * shares + s + 1) * share)
+                    g_s[at, :lanes] = ga_ref[s, b]
+                    u_s[at, :lanes] = ua_ref[s, b]
+                    if size > lanes:
+                        g_s[at, lanes:] = gb_ref[s, b]
+                        u_s[at, lanes:] = ub_ref[s, b]
+            rows = x_ref[...]
+            gate, upper = dot(rows, g_s[:, :size]), dot(rows, u_s[:, :size])
+            inner_ref[:, :size] = (gate * jax.nn.sigmoid(gate) * upper).astype(BF16)
+
+        @pl.when(step < steps - 1)
+        def _():
+            work(tile)
+
+        @pl.when(step == steps - 1)
+        def _():
+            work(tail)
+
+    def lane_block(base, second):
+        last = base + up_at - 1
+        return pl.BlockSpec(
+            (shares, blocks, share, lanes), lambda n: (0, 0, 0, jnp.minimum(base + 2 * n + second, last))
+        )
+
+    return pl.pallas_call(
+        kernel,
+        grid=(steps,),
+        in_specs=[
+            pl.BlockSpec((tokens, width), lambda n: (0, 0)),
+            lane_block(0, 0),
+            lane_block(0, 1),
+            lane_block(up_at, 0),
+            lane_block(up_at, 1),
+        ],
+        out_specs=pl.BlockSpec((tokens, tile), lambda n: (0, n)),
+        scratch_shapes=[pltpu.VMEM((width, tile), BF16), pltpu.VMEM((width, tile), BF16)],
+        out_shape=jax.ShapeDtypeStruct((tokens, hidden), BF16),
+        compiler_params=pltpu.CompilerParams(dimension_semantics=("arbitrary",)),
+        cost_estimate=cheap(),
+        name="hidden_units",
+    )(x, gu, gu, gu, gu)
+
+
 def token_grad(info, lefts, rights):
     paired = isinstance(rights, tuple)
     count = len(lefts)
@@ -442,25 +489,87 @@
     )(info, *lefts, *right_args)
 
 
-def token_sum(lefts, rights):
+def stack_rows(parts):
+    rows, columns = parts[0].shape
+
+    def kernel(*refs):
+        for j, ref in enumerate(refs[:-1]):
+            refs[-1][j * rows : (j + 1) * rows, :] = ref[...]
+
+    vmem = pl.BlockSpec(memory_space=pltpu.VMEM)
+    return pl.pallas_call(
+        kernel,
+        in_specs=[vmem] * len(parts),
+        out_specs=vmem,
+        out_shape=jax.ShapeDtypeStruct((len(parts) * rows, columns), parts[0].dtype),
+        cost_estimate=cheap(),
+        name="stack_rows",
+    )(*parts)
+
+
+def unpack(buffer, height, rank, groups):
+    steps = 4
+    o_tile, qb_tile, qa_tile = height // steps, rank // groups // steps, 2 * rank // groups // steps
+
+    def kernel(o0_ref, o1_ref, *refs):
+        qb_refs, (qa_ref, o_ref, qb_out, qa_out) = refs[:groups], refs[groups:]
+        o_ref[:, :rank] = o0_ref[...].astype(F32)
+        o_ref[:, rank:] = o1_ref[...].astype(F32)
+        for j, ref in enumerate(qb_refs):
+            qb_out[:, j * rank : (j + 1) * rank] = ref[...].astype(F32)
+        qa_out[...] = qa_ref[...].astype(F32)
+
+    def at(tile, start):
+        return pl.BlockSpec((tile, rank), lambda i: (start // tile + i, 0))
+
+    base = 2 * height
+    return pl.pallas_call(
+        kernel,
+        grid=(steps,),
+        in_specs=[at(o_tile, 0), at(o_tile, height)]
+        + [at(qb_tile, base + j * rank // groups) for j in range(groups)]
+        + [at(qa_tile, base + rank)],
+        out_specs=[
+            pl.BlockSpec((o_tile, 2 * rank), lambda i: (i, 0)),
+            pl.BlockSpec((qb_tile, groups * rank), lambda i: (i, 0)),
+            pl.BlockSpec((qa_tile, rank), lambda i: (i, 0)),
+        ],
+        out_shape=[
+            jax.ShapeDtypeStruct((height, 2 * rank), F32),
+            jax.ShapeDtypeStruct((rank // groups, groups * rank), F32),
+            jax.ShapeDtypeStruct((2 * rank // groups, rank), F32),
+        ],
+        cost_estimate=cheap(),
+        name="unpack",
+    )(*([buffer] * (3 + groups)))
+
+
+def token_sum(lefts, *rights):
     count = len(lefts)
     tokens, height = lefts[0].shape
-    width = rights[0].shape[1]
-    tile = min(height, 256)
+    width = rights[0][0].shape[1]
+    tile = next(t for t in (256, 128, height) if height % t == 0)
 
     def kernel(*refs):
-        refs[-1][...] = sum(dot_rows(l[...], r[...]) for l, r in zip(refs[:count], refs[count:-1])).astype(BF16)
+        for n in range(len(rights)):
+            right_refs = refs[(n + 1) * count : (n + 2) * count]
+            total = sum(dot_rows(l[...], r[...]) for l, r in zip(refs[:count], right_refs))
+            refs[-1][:, n * width : (n + 1) * width] = total.astype(BF16)
 
     return pl.pallas_call(
         kernel,
         grid=(height // tile,),
         in_specs=[pl.BlockSpec((tokens, tile), lambda m: (0, m))] * count
-        + [pl.BlockSpec((tokens, width), lambda m: (0, 0))] * count,
-        out_specs=pl.BlockSpec((tile, width), lambda m: (m, 0)),
-        out_shape=jax.ShapeDtypeStruct((height, width), BF16),
-        cost_estimate=cheap(),
+        + [pl.BlockSpec((tokens, width), lambda m: (0, 0))] * (count * len(rights)),
+        out_specs=pl.BlockSpec((tile, width * len(rights)), lambda m: (m, 0)),
+        out_shape=jax.ShapeDtypeStruct((height, width * len(rights)), BF16),
+        cost_estimate=pl.CostEstimate(
+            flops=2 * count * len(rights) * tokens * height * width,
+            bytes_accessed=2 * height * width,
+            transcendentals=0,
+        ),
         name="token_sum",
-    )(*lefts, *rights)
+    )(*lefts, *[r for part in rights for r in part])
 
 
 def project(info, inputs, own, pieces, others, cos_h, sin_h):
@@ -570,25 +679,26 @@
 def place_columns(info, mine, far, relative):
     groups = len(mine)
     rows, columns = mine[0].shape
+    width = columns // 2
     tile = min(rows, 64)
 
     def kernel(info_ref, *refs):
-        first_ref, second_ref = refs[-2:]
-        flag = info_ref[2] == 0
+        gate_ref, up_ref = refs[-2:]
+        flag = info_ref[2] == pl.program_id(0)
         for j in range(groups):
-            a, b = refs[j][...].astype(F32), refs[groups + j][...].astype(F32)
-            at = pl.ds(pl.multiple_of((info_ref[1] ^ j) * columns, 128), columns) if relative else slice(j * columns, (j + 1) * columns)
-            first_ref[:, at] = jnp.where(flag, a, b)
-            second_ref[:, at] = jnp.where(flag, b, a)
-
-    block = pl.BlockSpec((tile, columns), lambda r, i: (r, 0))
-    out = pl.BlockSpec((tile, groups * columns), lambda r, i: (r, 0))
+            block = jnp.where(flag, refs[j][...].astype(F32), refs[groups + j][...].astype(F32))
+            at = pl.ds(pl.multiple_of((info_ref[1] ^ j) * width, 128), width) if relative else slice(j * width, (j + 1) * width)
+            gate_ref[:, at] = block[:, :width]
+            up_ref[:, at] = block[:, width:]
+
+    block = pl.BlockSpec((tile, columns), lambda h, r, i: (r, 0))
+    out = pl.BlockSpec((tile, groups * width), lambda h, r, i: (h * (rows // tile) + r, 0))
     return pl.pallas_call(
         kernel,
         grid_spec=pltpu.PrefetchScalarGridSpec(
-            num_scalar_prefetch=1, grid=(rows // tile,), in_specs=[block] * (2 * groups), out_specs=[out, out]
+            num_scalar_prefetch=1, grid=(2, rows // tile), in_specs=[block] * (2 * groups), out_specs=[out, out]
         ),
-        out_shape=[jax.ShapeDtypeStruct((rows, groups * columns), F32)] * 2,
+        out_shape=[jax.ShapeDtypeStruct((2 * rows, groups * width), F32)] * 2,
         cost_estimate=cheap(),
         name="place_columns",
     )(info, *mine, *far)
@@ -725,7 +835,7 @@
         gu = turn(gu_share, gu_cols)
         kv_line, norm_got, gu = fence(kv_line, norm_got, gu)
         gu = lax.all_gather(gu, "ctx")
-        kv_mine = jnp.concatenate([kv_own] + kv_line, axis=0)
+        kv_mine = stack_rows([kv_own] + kv_line)
         kv_got = gather_first(kv_mine)
         norm_more = gather_second(norm_got)
         kv_got, norm_more, qb = fence(kv_got, norm_more, qb)
@@ -763,57 +873,48 @@
         ffn_got, first_dx = fence(ffn_got, done[0][4])
         ffn_more = gather_second(ffn_got)
         dffn_got = []
-        for j, x in enumerate(ffn_got):
-            done.append(feed_forward(x, signal_got[j], *weights, BF16))
-            if j + 1 < len(ffn_got):
-                ffn_got[j + 1], sent = fence(ffn_got[j + 1], done[-1][4])
-            elif square:
-                ffn_more, sent = fence(ffn_more, done[-1][4])
-            else:
-                sent = done[-1][4]
+        for j in range(len(ffn_got)):
+            done.append(feed_forward(ffn_got[j], signal_got[j], *weights, BF16))
+            sent, ffn_more, ffn_got[j + 1 :] = fence(done[-1][4], ffn_more, ffn_got[j + 1 :])
             dffn_got.append(swap(sent, j + 1))
         ffn_blocks = gather_done(ffn_in, ffn_got, ffn_more)
+        signal_blocks = [signal_low] + signal_got
+
+        inner_blocks = [d[0] for d in done]
         if square:
-            done.append(feed_forward(ffn_blocks[3], signal_got[2], *weights, BF16))
-        inner_blocks, gate_blocks, up_blocks, y_parts, dx = (list(t) for t in zip(*done))
-        late = fence(dx[nf - 1], ffn_blocks, gate_blocks, up_blocks)
+            inner_blocks.append(hidden_units(ffn_blocks[3], gu, hidden_cols))
+        dffn_got[0], inner_blocks, last_x = fence(dffn_got[0], inner_blocks, ffn_blocks[nf - 1])
+        down_part = token_sum(inner_blocks, signal_blocks)
+        down_part, last_x = fence(down_part, last_x)
+        down_share = lax.psum_scatter(down_part, "ctx", scatter_dimension=0, tiled=True)
+        if square:
+            done.append(feed_forward(last_x, signal_got[2], *weights, BF16))
+        _, gate_blocks, up_blocks, y_parts, dx = (list(t) for t in zip(*done))
+        late = fence(dx[nf - 1], ffn_blocks, gate_blocks, up_blocks, dffn_got)
+        dffn_got = late[4]
         if square:
             dffn_got.append(swap(late[0], 3))
 
-        gu_own, gu_far = token_grad(info, late[1], (late[2], late[3]))
-        dffn_got, gu_own, gu_far = fence(dffn_got, gu_own, gu_far)
-        gu_back = core_swap(gu_far)
+        gu_part = token_sum(late[1], late[2], late[3])
+        dffn_got, gu_part = fence(dffn_got, gu_part)
+        line_groups = [[2 * i + core for i in range(nz)] for core in range(2)]
+        gu_share = lax.psum_scatter(gu_part, "ctx", scatter_dimension=0, tiled=True)
         d_ffn = scatter_done(first_dx, dffn_got)
         d_norm_f, grad_gain_f = norm_back(d_ffn, hidden, scale_f, gain_f)
         d_hidden = signal + d_norm_f
         d_hidden_low = d_hidden.astype(BF16)
-        line_groups = [[2 * i + core for i in range(nz)] for core in range(2)]
-
-        d_hidden_low, gu_back = fence(d_hidden_low, gu_back)
-        gu_half = add_low(gu_own, gu_back)
-        gu_share = lax.psum_scatter(
-            gu_half, "ctx", scatter_dimension=0, axis_index_groups=line_groups, tiled=True
-        )
+        (d_hidden_low,) = fence(d_hidden_low)
+
         dh_got = gather_first(d_hidden_low)
-        signal_blocks = [signal_low] + signal_got
-        down_lefts, down_rights, _ = fence(inner_blocks, signal_blocks, gu_half)
-        down_own, down_far = token_grad(info, down_lefts, down_rights)
-
-        dh_got, down_own, down_far = fence(dh_got, down_own, down_far)
+        (dh_got,) = fence(dh_got)
         dh_more = gather_second(dh_got)
-        down_back = core_swap(down_far)
         d_attn = [dot_back(x, w_o).astype(BF16) for x in [d_hidden_low, *dh_got]]
 
-        dh_more, down_back, d_attn, y_parts = fence(dh_more, down_back, d_attn, y_parts)
+        dh_more, d_attn, y_parts = fence(dh_more, d_attn, y_parts)
         dh_blocks = gather_done(d_hidden_low, dh_got, dh_more)
         d_attn += [dot_back(x, w_o).astype(BF16) for x in dh_blocks[len(d_attn) :]]
         d_attn = jnp.concatenate(d_attn, axis=0).reshape(nf, seqs, span, head_cols)
         y_got = [swap(y_parts[j], j) for j in range(1, nf)]
-        down_half = add_low(down_own, down_back)
-        down_share = lax.psum_scatter(
-            down_half, "ctx", scatter_dimension=0, axis_index_groups=line_groups, tiled=True
-        )
-
         count = seqs // 2
         backward = (info, scaled, attn_out, d_attn, lse, kv_near, kv_far, cos_g, sin_g)
         dq_a, near_a, far_a = attend_backward(*backward, 0, count)
@@ -821,10 +922,10 @@
         back_a = core_swap(far_a)
         backward = (info, scaled, attn_out, d_attn, lse, kv_near, kv_far, cos_g, sin_g)
         dq_b, near_b, far_b = attend_backward(*backward, count, seqs - count)
-        dq_b, near_b, far_b, back_a, gu_share = fence(
-            dq_b, near_b, far_b, back_a, gu_share
-        )
-        gu_sum = lax.all_gather(gu_share, "ctx", axis_index_groups=line_groups, tiled=True)
+        dq_b, near_b, far_b, back_a, down_share = fence(
+            dq_b, near_b, far_b, back_a, down_share
+        )
+        down_sum = lax.all_gather(down_share, "ctx", tiled=True)
 
         def kv_parts(near, far):
             total = near.astype(F32) + far.astype(F32)
@@ -845,12 +946,11 @@
         parts_b = kv_parts(near_b, back_b)
         first_b = scatter_first(parts_b)
         dq_first = scatter_first(dq_parts)
-        o_part = token_sum(attn_late, dh_blocks)
         qb_own, qb_far = token_grad(info, norm_late, dq_blocks)
-        got_a, first_b, dq_first, o_part, qb_own, qb_far, down_share = fence(
-            got_a, first_b, dq_first, o_part, qb_own, qb_far, down_share
-        )
-        down_sum = lax.all_gather(down_share, "ctx", axis_index_groups=line_groups, tiled=True)
+        got_a, first_b, dq_first, qb_own, qb_far, gu_share = fence(
+            got_a, first_b, dq_first, qb_own, qb_far, gu_share
+        )
+        gu_sum = lax.all_gather(gu_share, "ctx", axis_index_groups=line_groups, tiled=True)
 
 
         def line_start(part, got):
@@ -914,10 +1014,11 @@
         last_got = gather_first(last)
         dql_blocks = gather_done(d_query_low, dql_got, dql_more)
         qa_part = token_sum(normed_rel, dql_blocks)
-        last_got, qa_part, qb_rows = fence(last_got, qa_part, qb_rows)
+        last_got, qa_part, qb_rows, attn_late = fence(last_got, qa_part, qb_rows, attn_late)
 
         last_more = gather_second(last_got)
-        last_more, gu_sum = fence(last_more, gu_sum)
+        o_part = token_sum(attn_late, dh_blocks)
+        last_more, o_part = fence(last_more, o_part)
 
         last_blocks = gather_done(last, last_got, last_more)
         kv_part = dot_rows(
@@ -944,32 +1045,33 @@
         spare = -sum(sizes) % (16 * nc)
         pieces_out.append(jnp.zeros((spare, rank), BF16))
         buffer = jnp.concatenate(pieces_out, axis=0)
-        buffer, gu_sum = fence(buffer, gu_sum)
+        buffer, down_sum = fence(buffer, down_sum)
         buffer_share = lax.psum_scatter(buffer, "ctx", scatter_dimension=0, tiled=True)
 
-        gu_done = gu_sum.reshape(nf, shard, hidden_cols)
+        gu_done = gu_sum.reshape(nf, -1, 2 * hidden_cols)
         if square:
             gu_mine = [pick(gu_done, f)] + [swap(pick(gu_done, f ^ j), j) for j in range(1, nf)]
         else:
             gu_done = lax.all_to_all(gu_done, "fsdp", split_axis=0, concat_axis=0, tiled=True)
             gu_mine = [gu_done[j] for j in range(nf)]
-        down_other = core_swap(down_sum)
-        gu_mine, down_sum, down_other, buffer_share = fence(gu_mine, down_sum, down_other, buffer_share)
+        gu_mine, down_sum, buffer_share = fence(gu_mine, down_sum, buffer_share)
         buffer = lax.all_gather(buffer_share, "ctx", tiled=True)
         gu_far = [core_swap(x) for x in gu_mine]
         grad_gate, grad_up = place_columns(info, gu_mine, gu_far, square)
-        both = jnp.where(k == 0, down_sum, down_other), jnp.where(k == 0, down_other, down_sum)
-        grad_down = jnp.concatenate(both, axis=1).astype(F32)
+        grad_down = down_sum.astype(F32)
         grad_gate, grad_up, grad_down, buffer = fence(grad_gate, grad_up, grad_down, buffer)
         found, at = [], 0
         for size in sizes:
             found.append(buffer[at : at + size])
             at += size
         count_o = o_part.shape[1] // rank
-        grad_o = jnp.concatenate(found[:count_o], axis=1).astype(F32)
-        qb_rows = found[count_o].reshape(nf, rank // nf, head_cols)
-        grad_qb = qb_rows.transpose(1, 0, 2).reshape(rank // nf, nf * head_cols).astype(F32)
-        grad_qa = found[-2].astype(F32)
+        if square and head_cols == rank and count_o == 2:
+            grad_o, grad_qb, grad_qa = unpack(buffer, o_part.shape[0], rank, nf)
+        else:
+            grad_o = jnp.concatenate(found[:count_o], axis=1).astype(F32)
+            qb_rows = found[count_o].reshape(nf, rank // nf, head_cols)
+            grad_qb = qb_rows.transpose(1, 0, 2).reshape(rank // nf, nf * head_cols).astype(F32)
+            grad_qa = found[-2].astype(F32)
         kv_grad = jnp.concatenate(
             [found[-1][:, i * 2 * HD : (i + 1) * 2 * HD] for i in range(wide)], axis=0
         ).astype(F32)

time: 925 us -> 910 us (0.984)
  other arithmetic: 93.7 us -> 77.6 us
  starting transfers between devices: 103 us -> 119 us
  Pallas kernels: 197 us -> 210 us
  matrix products: 34.2 us -> 23.3 us
    pallas_call x3 -> x1, Pallas kernels: 45.5 us -> 9.56 us  [token_grad(): pl.pallas_call(kernel, grid_spec=pltpu.PrefetchScalarGridSpec(num_scalar_...]
    pallas_call x2 -> x4, Pallas kernels: 13.2 us -> 45.5 us  [token_sum(): pl.pallas_call(kernel, grid=(height // tile,), in_specs=[pl.BlockSpec((to...]
    pallas_call x0 -> x3, Pallas kernels: none -> 20.4 us  [the longest x1 9.52 us: hidden_units(): pl.pallas_call(kernel, grid=(steps,), in_specs=[pl.BlockSpec((tokens, wid...]
    ppermute x56, starting transfers between devices: 64.8 us -> 79 us  [swap(): return lax.ppermute(x, 'fsdp', [(i, i ^ j) for i in range(nf)])]
    ppermute x56, waiting for transfers between devices: 230 us -> 218 us  [swap(): return lax.ppermute(x, 'fsdp', [(i, i ^ j) for i in range(nf)])]
    dot_general x8, matrix products: 21.3 us -> 9.21 us  [dot_back(): lax.dot_general(left, right, (((1,), (1,)), ((), ())), preferred_element_...]
    all_gather x1, waiting for transfers between devices: 0.01 us -> 9.54 us  [on_device(): lax.all_gather(gu_share, 'ctx', axis_index_groups=line_groups, tiled=True)]
    convert_element_type x11 -> x9, other arithmetic: 17.4 us -> 7.85 us  [add_low(): return (a.astype(F32) + b.astype(F32)).astype(BF16)]
  transfers between devices with their start and end apart: 91 -> 88, of which waited for: 42 -> 40; matrix products, arithmetic and copies ran while one was open for 20% -> 19% of each run, Pallas kernels for 22% -> 21%
where the time goes in v3:
time: 910 us; the launch traced here: 901 us
  waiting for transfers between devices  355 us (39%)
  Pallas kernels  210 us (23%)
  starting transfers between devices  119 us (13%)
  local copies, waits for them, and re-layouts  100 us (11%)
  other arithmetic  77.6 us (9%)
  matrix products  23.3 us (3%)
  between operations  16.1 us (2%)
    ppermute x56, waiting for transfers between devices, swap(): return lax.ppermute(x, 'fsdp', [(i, i ^ j) for i in range(nf)])  218 us
    ppermute x56, starting transfers between devices, swap(): return lax.ppermute(x, 'fsdp', [(i, i ^ j) for i in range(nf)])  79 us
    pallas_call x4, Pallas kernels, feed_forward(): pl.pallas_call(kernel, grid=(steps,), in_specs=[whole, whole, lane_block(...  68 us
    pallas_call x4, Pallas kernels, token_sum(): pl.pallas_call(kernel, grid=(height // tile,), in_specs=[pl.BlockSpec((to...  45.5 us
    all_gather x1, waiting for transfers between devices, on_device(): buffer = lax.all_gather(buffer_share, 'ctx', tiled=True)  45.4 us
    unnamed x224, local copies, waits for them, and re-layouts  39.4 us
    ppermute x6, waiting for transfers between devices, line_start(): lax.ppermute(low[s], 'ctx', [(i, i - 2 * s) for i in range(2 * s, nc)])  25.3 us
    pallas_call x2, Pallas kernels, attend_backward(): pl.pallas_call(kernel, grid_spec=pltpu.PrefetchScalarGridSpec(num_scalar_...  21.7 us
  transfers between devices with their start and end apart: 88, of which 40 were waited for; matrix products, arithmetic and copies ran while one was open for 19% of the time, Pallas kernels for 21%

profile of v3, /device:TPU:0, one launch (start us, length us, event | category | flops | bytes accessed | tf_op | source)
XLA Modules:
  0.0 900.9 jit_solution(5469133608199803260)
XLA Ops:
  9.5 5.2 all-to-all-start.1
  24.5 13.7 %collective-permute-done.1.refs_1_ = bf16[272,1536]{1,0:T(8,128)(2,1)} collective-permute-done((bf16[272,1536]{1,0:T(8,128)(2,1)}, bf16[272,1536]{1,0:T(8,128)(2,1)}, u32[]{:S(2)}, u32[]{:S(2)}) %collective-permute-start.1) | collective-permute-done | bytes 835616 | tf_op jit(solution)/shard_map/ppermute | solution.py:712
  47.3 3.5 collective-permute-done.2
  58.5 6.6 project.1
  66.3 3.7 all-to-all-start
  73.5 3.5 collective-permute-start.7
  77.0 4.5 collective-permute-start.8
  83.6 5.7 collective-permute-done.8.refs_2_
  89.3 4.3 collective-permute-done.9.refs_3_
  93.6 6.4 collective-permute-done.10.refs_1_
  115.3 19.1 %collective-permute-done.14 = bf16[128,1024]{1,0:T(8,128)(2,1)S(1)} collective-permute-done((bf16[128,1024]{1,0:T(8,128)(2,1)S(1)}, bf16[128,1024]{1,0:T(8,128)(2,1)S(1)}, u32[]{:S(2)}, u32[]{:S(2)}) %collective-permute-start.14) | collective-permute-done | bytes 262176 | tf_op jit(solution)/shard_map/ppermute | solution.py:712
  147.1 6.0 fusion.67.q_ref
  159.5 3.7 collective-permute-done.18
  165.2 14.6 %attend_forward.1 = (bf16[4,4,64,1024]{3,2,1,0:T(8,128)(2,1)}, bf16[4,4,64,1024]{3,2,1,0:T(8,128)(2,1)}, f32[4,1,1024]{2,1,0:T(1,128)}) custom-call(s32[7]{0:T(128)} %pad_add_fusion.info_ref, f32[4,4,64,1024]{3,2,1,0:T(8,128)} %fusion.67.q_ref, bf16[4,4,4,64,512]{4,3,2,1,0:T(8,128)(2,1)} %bitcast.193, bf16[4,4,4,64,512]{4,3,2,1,0:T(8,128)(2,1)} %bitcast.196, ...), custom_call_target="tpu_custom_call" | custom-call | flops 1 | bytes 1 | tf_op jit(solution)/shard_map/attend_forward/pallas_call | solution.py:146
  189.0 16.0 %collective-permute-done.22.s_ref.refs_6_ = bf16[256,2048]{1,0:T(8,128)(2,1)} collective-permute-done((bf16[256,2048]{1,0:T(8,128)(2,1)S(1)}, bf16[256,2048]{1,0:T(8,128)(2,1)}, u32[]{:S(2)}, u32[]{:S(2)}) %collective-permute-start.22) | collective-permute-done | bytes 1048608 | tf_op jit(solution)/shard_map/ppermute | solution.py:712
  205.2 10.1 %collective-permute-done.19 = bf16[128,2048]{1,0:T(8,128)(2,1)S(1)} collective-permute-done((bf16[128,2048]{1,0:T(8,128)(2,1)S(1)}, bf16[128,2048]{1,0:T(8,128)(2,1)S(1)}, u32[]{:S(2)}, u32[]{:S(2)}) %collective-permute-start.19) | collective-permute-done | bytes 524320 | tf_op jit(solution)/shard_map/ppermute | solution.py:712
  223.1 18.6 %collective-permute-done.25 = bf16[256,2048]{1,0:T(8,128)(2,1)S(1)} collective-permute-done((bf16[256,2048]{1,0:T(8,128)(2,1)S(1)}, bf16[256,2048]{1,0:T(8,128)(2,1)S(1)}, u32[]{:S(2)}, u32[]{:S(2)}) %collective-permute-start.25) | collective-permute-done | bytes 1048608 | tf_op jit(solution)/shard_map/ppermute | solution.py:712
  243.6 2.8 multiply_reduce_fusion.2
  249.6 17.5 %feed_forward.4 = (bf16[256,1408]{1,0:T(8,128)(2,1)}, bf16[256,1408]{1,0:T(8,128)(2,1)}, bf16[256,1408]{1,0:T(8,128)(2,1)}, f32[256,2048]{1,0:T(8,128)}, f32[256,2048]{1,0:T(8,128)}) custom-call(bf16[256,2048]{1,0:T(8,128)(2,1)} %multiply_convert_fusion.x_ref.refs_0_, bf16[256,2048]{1,0:T(8,128)(2,1)} %copy-done.18, bf16[8,4,64,2816]{3,2,1,0:T(8,128)(2,1)} %bitcast.173, ...), custom_call_target="tpu_custom_call" | custom-call | flops 1 | bytes 1 | tf_op jit(solution)/shard_map/feed_forward/pallas_call | solution.py:344
  267.1 5.1 collective-permute-done.26.x_ref.refs_1_
  278.5 16.6 %feed_forward.5 = (bf16[256,1408]{1,0:T(8,128)(2,1)}, bf16[256,1408]{1,0:T(8,128)(2,1)}, bf16[256,1408]{1,0:T(8,128)(2,1)}, bf16[256,2048]{1,0:T(8,128)(2,1)}, bf16[256,2048]{1,0:T(8,128)(2,1)}) custom-call(bf16[256,2048]{1,0:T(8,128)(2,1)} %collective-permute-done.26.x_ref.refs_1_, bf16[256,2048]{1,0:T(8,128)(2,1)} %copy-done.49, ...), custom_call_target="tpu_custom_call" | custom-call | flops 1 | bytes 1 | tf_op jit(solution)/shard_map/feed_forward/pallas_call | solution.py:344
  296.2 17.0 %feed_forward.6 = (bf16[256,1408]{1,0:T(8,128)(2,1)}, bf16[256,1408]{1,0:T(8,128)(2,1)}, bf16[256,1408]{1,0:T(8,128)(2,1)}, bf16[256,2048]{1,0:T(8,128)(2,1)}, bf16[256,2048]{1,0:T(8,128)(2,1)}) custom-call(bf16[256,2048]{1,0:T(8,128)(2,1)} %collective-permute-done.27.x_ref.refs_2_, bf16[256,2048]{1,0:T(8,128)(2,1)} %collective-permute-done.22.s_ref.refs_6_, ...), custom_call_target="tpu_custom_call" | custom-call | flops 1 | bytes 1 | tf_op jit(solution)/shard_map/feed_forward/pallas_call | solution.py:344
  317.0 9.5 %hidden_units.1.refs_3_ = bf16[256,1408]{1,0:T(8,128)(2,1)} custom-call(bf16[256,2048]{1,0:T(8,128)(2,1)} %constant_dynamic-update-slice_fusion.15.x_ref.refs_3_, bf16[8,4,64,2816]{3,2,1,0:T(8,128)(2,1)} %bitcast.185, bf16[8,4,64,2816]{3,2,1,0:T(8,128)(2,1)} %bitcast.186, bf16[8,4,64,2816]{3,2,1,0:T(8,128)(2,1)} %bitcast.187, bf16[8,4,64,2816]{3,2,1,0:T(8,128)(2,1)} %bitcast.188), custom_call_target="tpu_custom_call" | custom-call | flops 1 | bytes 1 | tf_op jit(solution)/shard_map/hidden_units/pallas_call | solution.py:402
  326.5 13.4 %token_sum.4 = bf16[1408,2048]{1,0:T(8,128)(2,1)} custom-call(bf16[256,1408]{1,0:T(8,128)(2,1)} %get-tuple-element.267.refs_0_, bf16[256,1408]{1,0:T(8,128)(2,1)} %get-tuple-element.268.refs_1_, bf16[256,1408]{1,0:T(8,128)(2,1)} %get-tuple-element.269.refs_2_, bf16[256,1408]{1,0:T(8,128)(2,1)} %hidden_units.1.refs_3_, bf16[256,2048]{1,0:T(8,128)(2,1)} %copy-done.18, ...), custom_call_target="tpu_custom_call" | custom-call | flops 5905580032 | bytes 5767168 | tf_op jit(solution)/shard_map/token_sum/pallas_call | solution.py:559
  340.8 17.0 %feed_forward.7 = (bf16[256,1408]{1,0:T(8,128)(2,1)}, bf16[256,1408]{1,0:T(8,128)(2,1)}, bf16[256,1408]{1,0:T(8,128)(2,1)}, bf16[256,2048]{1,0:T(8,128)(2,1)}, bf16[256,2048]{1,0:T(8,128)(2,1)}) custom-call(bf16[256,2048]{1,0:T(8,128)(2,1)} %constant_dynamic-update-slice_fusion.15.x_ref.refs_3_, bf16[256,2048]{1,0:T(8,128)(2,1)} %copy-done.48, ...), custom_call_target="tpu_custom_call" | custom-call | flops 1 | bytes 1 | tf_op jit(solution)/shard_map/feed_forward/pallas_call | solution.py:344
  357.9 4.6 collective-permute-done.31
  364.3 19.1 %token_sum.5 = bf16[2048,2816]{1,0:T(8,128)(2,1)} custom-call(bf16[256,2048]{1,0:T(8,128)(2,1)} %multiply_convert_fusion.x_ref.refs_0_, bf16[256,2048]{1,0:T(8,128)(2,1)} %collective-permute-done.26.x_ref.refs_1_, bf16[256,2048]{1,0:T(8,128)(2,1)} %collective-permute-done.27.x_ref.refs_2_, ...), custom_call_target="tpu_custom_call" | custom-call | flops 11811160064 | bytes 5767168 | tf_op jit(solution)/shard_map/token_sum/pallas_call | solution.py:559
  385.2 3.8 multiply_reduce_fusion
  391.0 8.7 collective-permute-start.33
  402.4 15.6 %collective-permute-done.33.refs_5_ = bf16[256,2048]{1,0:T(8,128)(2,1)S(1)} collective-permute-done((bf16[256,2048]{1,0:T(8,128)(2,1)S(1)}, bf16[256,2048]{1,0:T(8,128)(2,1)S(1)}, u32[]{:S(2)}, u32[]{:S(2)}) %collective-permute-start.33) | collective-permute-done | bytes 1048608 | tf_op jit(solution)/shard_map/ppermute | solution.py:712
  426.5 2.9 collective-permute-done.35
  434.8 11.2 %attend_backward.2 = (bf16[4,2,64,1024]{3,2,1,0:T(8,128)(2,1)}, bf16[4,4,2,64,512]{4,3,2,1,0:T(8,128)(2,1)}, bf16[4,4,2,64,512]{4,3,2,1,0:T(8,128)(2,1)}) custom-call(s32[7]{0:T(128)} %pad_add_fusion.info_ref, bf16[4,4,64,1024]{3,2,1,0:T(8,128)(2,1)} %get-tuple-element.310.q_ref, bf16[4,4,64,1024]{3,2,1,0:T(8,128)(2,1)} %get-tuple-element.238.o_ref, ...), custom_call_target="tpu_custom_call" | custom-call | flops 1 | bytes 1 | tf_op jit(solution)/shard_map/attend_backward/pallas_call | solution.py:241
  446.0 10.6 %attend_backward.3 = (bf16[4,2,64,1024]{3,2,1,0:T(8,128)(2,1)}, bf16[4,4,2,64,512]{4,3,2,1,0:T(8,128)(2,1)}, bf16[4,4,2,64,512]{4,3,2,1,0:T(8,128)(2,1)}) custom-call(s32[7]{0:T(128)} %pad_add_fusion.info_ref, bf16[4,4,64,1024]{3,2,1,0:T(8,128)(2,1)} %get-tuple-element.310.q_ref, bf16[4,4,64,1024]{3,2,1,0:T(8,128)(2,1)} %get-tuple-element.238.o_ref, ...), custom_call_target="tpu_custom_call" | custom-call | flops 1 | bytes 1 | tf_op jit(solution)/shard_map/attend_backward/pallas_call | solution.py:241
  459.1 2.6 collective-permute-start.40
  474.5 3.0 convert_add_fusion
  488.0 9.6 %token_grad.1 = (bf16[1024,512]{1,0:T(8,128)(2,1)}, bf16[1024,512]{1,0:T(8,128)(2,1)}) custom-call(s32[7]{0:T(128)} %pad_add_fusion.info_ref, bf16[256,1024]{1,0:T(8,128)(2,1)} %get-tuple-element.336.refs_0_, bf16[256,1024]{1,0:T(8,128)(2,1)} %copy-done.44, bf16[256,1024]{1,0:T(8,128)(2,1)} %collective-permute-done.11.refs_2_, ...), custom_call_target="tpu_custom_call" | custom-call | flops 2147483648 | bytes 2097152 | tf_op jit(solution)/shard_map/token_grad/pallas_call | solution.py:472
  500.9 4.2 collective-permute-done.45
  508.3 17.4 %reduce-scatter.6.cloned.1.call-done = bf16[256,2816]{1,0:T(8,128)(2,1)} async-done(((bf16[2048,2816]{1,0:T(8,128)(2,1)}), bf16[256,2816]{1,0:T(8,128)(2,1)}) %reduce-scatter.6.cloned.1.call-update) | async-done | bytes 1441808 | tf_op jit(solution)/shard_map/reduce_scatter | solution.py:901
  527.7 2.9 fusion.51
  538.3 14.3 %collective-permute-done.56 = bf16[256,2048]{1,0:T(8,128)(2,1)} collective-permute-done((bf16[256,2048]{1,0:T(8,128)(2,1)}, bf16[256,2048]{1,0:T(8,128)(2,1)}, u32[]{:S(2)}, u32[]{:S(2)}) %collective-permute-start.56) | collective-permute-done | bytes 1048608 | tf_op jit(solution)/shard_map/ppermute | solution.py:712
  559.5 13.8 %collective-permute-done.49 = bf16[128,512]{1,0:T(8,128)(2,1)S(1)} collective-permute-done((bf16[128,512]{1,0:T(8,128)(2,1)S(1)}, bf16[128,512]{1,0:T(8,128)(2,1)S(1)}, u32[]{:S(2)}, u32[]{:S(2)}) %collective-permute-start.49) | collective-permute-done | bytes 131104 | tf_op jit(solution)/shard_map/ppermute | solution.py:960
  580.1 5.8 collective-permute-done.50
  593.1 4.2 all-to-all-start.2
  597.4 2.9 fusion.49
  608.5 5.6 all-to-all-done.2
  614.1 4.3 all-to-all-start.3
  620.6 11.5 %collective-permute-done.59 = bf16[128,512]{1,0:T(8,128)(2,1)} collective-permute-done((bf16[128,512]{1,0:T(8,128)(2,1)}, bf16[128,512]{1,0:T(8,128)(2,1)}, u32[]{:S(2)}, u32[]{:S(2)}) %collective-permute-start.59) | collective-permute-done | bytes 131104 | tf_op jit(solution)/shard_map/ppermute | solution.py:960
  636.0 6.3 project_back.1
  642.3 2.7 fusion.7
  646.8 5.4 collective-permute-start.66
  656.1 2.8 collective-permute-done.66
  668.5 4.2 token_sum.6
  678.3 8.8 token_sum.7
  690.0 3.2 slice_dynamic-update-slice_fusion.1
  701.8 9.5 %all-gather.8.cloned.1.call-done = bf16[1024,2816]{1,0:T(8,128)(2,1)} async-done(((bf16[256,2816]{1,0:T(8,128)(2,1)}), bf16[1024,2816]{1,0:T(8,128)(2,1)}) %all-gather.8.cloned.1.call-update) | async-done | bytes 5767184 | tf_op jit(solution)/shard_map/all_gather | solution.py:953
  711.3 4.1 dynamic-slice_bitcast_fusion
  719.0 31.0 %collective-permute-done.63.refs_1_ = bf16[256,2816]{1,0:T(8,128)(2,1)S(1)} collective-permute-done((bf16[256,2816]{1,0:T(8,128)(2,1)S(1)}, bf16[256,2816]{1,0:T(8,128)(2,1)S(1)}, u32[]{:S(2)}, u32[]{:S(2)}) %collective-permute-start.63) | collective-permute-done | bytes 1441824 | tf_op jit(solution)/shard_map/ppermute | solution.py:712
  749.9 31.4 %collective-permute-done.64.refs_2_ = bf16[256,2816]{1,0:T(8,128)(2,1)S(1)} collective-permute-done((bf16[256,2816]{1,0:T(8,128)(2,1)S(1)}, bf16[256,2816]{1,0:T(8,128)(2,1)S(1)}, u32[]{:S(2)}, u32[]{:S(2)}) %collective-permute-start.64) | collective-permute-done | bytes 1441824 | tf_op jit(solution)/shard_map/ppermute | solution.py:712
  782.4 17.3 %reduce-scatter.8.cloned.1.call-done = bf16[496,1024]{1,0:T(8,128)(2,1)} async-done(((bf16[3968,1024]{1,0:T(8,128)(2,1)}), bf16[496,1024]{1,0:T(8,128)(2,1)}) %reduce-scatter.8.cloned.1.call-update) | async-done | bytes 1015824 | tf_op jit(solution)/shard_map/reduce_scatter | solution.py:1049
  800.9 4.4 add_convert_fusion.1
  806.9 9.5 %convert_element_type.344 = f32[1408,2048]{1,0:T(8,128)} convert(bf16[1408,2048]{1,0:T(8,128)(2,1)} %all-gather.10.cloned.1.call-done) | non-fusion elementwise | flops 2883584 | bytes 17301504 | tf_op jit(solution)/shard_map/convert_element_type | solution.py:1061
  816.4 17.8 %place_columns.1 = (f32[512,5632]{1,0:T(8,128)}, f32[512,5632]{1,0:T(8,128)}) custom-call(s32[7]{0:T(128)} %pad_add_fusion.info_ref, bf16[256,2816]{1,0:T(8,128)(2,1)} %get-tuple-element.402.refs_0_, bf16[256,2816]{1,0:T(8,128)(2,1)} %copy-done.40, bf16[256,2816]{1,0:T(8,128)(2,1)} %copy-done.41, bf16[256,2816]{1,0:T(8,128)(2,1)} %collective-permute-done.65.refs_3_, ...), custom_call_target="tpu_custom_call" | custom-call | flops 1 | bytes 1 | tf_op jit(solution)/shard_map/place_columns/pallas_call | solution.py:696
  834.2 45.4 %all-gather.12.cloned.1.call-done.o0_ref.o1_ref.refs_0_.refs_1_.refs_2_.refs_3_.refs_4_ = bf16[3968,1024]{1,0:T(8,128)(2,1)} async-done(((bf16[496,1024]{1,0:T(8,128)(2,1)}), bf16[3968,1024]{1,0:T(8,128)(2,1)}) %all-gather.12.cloned.1.call-update) | async-done | bytes 8126480 | tf_op jit(solution)/shard_map/all_gather | solution.py:1058
  881.8 8.6 unpack.1
  (532 shorter events, 249.7 us)
Async XLA Ops:
  14.7 120.8 %all-gather.14.cloned.1.call-start = ((), (), s32[]{:S(2)}) async-start(), calls=%async_computation.13 | async-start | bytes 2359296 | tf_op jit(solution)/shard_map/all_gather | solution.py:805
  16.1 25.2 %collective-permute-start = (bf16[272,1536]{1,0:T(8,128)(2,1)}, bf16[272,1536]{1,0:T(8,128)(2,1)S(1)}, u32[]{:S(2)}, u32[]{:S(2)}) collective-permute-start(bf16[272,1536]{1,0:T(8,128)(2,1)} %pad_maximum_fusion.5), channel_id=1, source_target_pairs={{0,1},{1,0},{2,3},{3,2},{4,5},{5,4},{6,7},{7,6},{8,9},{9,8},{10,11... | collective-permute-start | bytes 2506760 | tf_op jit(solution)/shard_map/ppermute | solution.py:712
  18.1 20.1 %collective-permute-start.1 = (bf16[272,1536]{1,0:T(8,128)(2,1)}, bf16[272,1536]{1,0:T(8,128)(2,1)}, u32[]{:S(2)}, u32[]{:S(2)}) collective-permute-start(bf16[272,1536]{1,0:T(8,128)(2,1)} %pad_maximum_fusion.5), channel_id=1, source_target_pairs={{0,2},{1,3},{2,0},{3,1},{4,6},{5,7},{6,4},{7,5},{8,10},{9,11},{10,... | collective-permute-start | bytes 2506760 | tf_op jit(solution)/shard_map/ppermute | solution.py:712
  66.3 33.7 %all-to-all-start = ((bf16[64,4,2816]{2,0,1:T(8,128)(2,1)}), bf16[64,4,2816]{2,0,1:T(8,128)(2,1)S(1)}, u32[]{:S(2)}, u32[]{:S(2)}) async-start(bf16[64,4,2816]{2,0,1:T(8,128)(2,1)} %bitcast.170), calls=%async_computation | async-start | bytes 2883584 | tf_op jit(solution)/shard_map/all_to_all | solution.py:797
  70.0 172.6 %all-gather.16.cloned.1.call-start = ((), (), s32[]{:S(2)}) async-start(), calls=%async_computation.14 | async-start | bytes 12976128 | tf_op jit(solution)/shard_map/all_gather | solution.py:837
  70.1 29.9 %collective-permute-start.10 = (bf16[256,1024]{1,0:T(8,128)(2,1)}, bf16[256,1024]{1,0:T(8,128)(2,1)S(1)}, u32[]{:S(2)}, u32[]{:S(2)}) collective-permute-start(bf16[256,1024]{1,0:T(8,128)(2,1)} %get-tuple-element.336.refs_0_), channel_id=1, source_target_pairs={{0,1},{1,0},{2,3},{3,2},{4,5},{5,4},{6,7},{7,6},{8,9},{9,8},{10,11... | collective-permute-start | bytes 1572872 | tf_op jit(solution)/shard_map/ppermute | solution.py:712
  72.0 28.0 %collective-permute-start.11 = (bf16[256,1024]{1,0:T(8,128)(2,1)}, bf16[256,1024]{1,0:T(8,128)(2,1)}, u32[]{:S(2)}, u32[]{:S(2)}) collective-permute-start(bf16[256,1024]{1,0:T(8,128)(2,1)} %get-tuple-element.336.refs_0_), channel_id=1, source_target_pairs={{0,2},{1,3},{2,0},{3,1},{4,6},{5,7},{6,4},{7,5},{8,10},{9,11},{10,... | collective-permute-start | bytes 1572872 | tf_op jit(solution)/shard_map/ppermute | solution.py:712
  101.3 355.3 %reduce-scatter.4.cloned.1.call-start = ((), (), s32[]{:S(2)}) async-start(), calls=%async_computation.7 | async-start | bytes 6488064 | tf_op jit(solution)/shard_map/reduce_scatter | solution.py:889
  103.8 31.7 %collective-permute-start.12 = (bf16[1024,512]{1,0:T(8,128)(2,1)}, bf16[1024,512]{1,0:T(8,128)(2,1)}, u32[]{:S(2)}, u32[]{:S(2)}) collective-permute-start(bf16[1024,512]{1,0:T(8,128)(2,1)} %stack_rows.1), channel_id=1, source_target_pairs={{0,1},{1,0},{2,3},{3,2},{4,5},{5,4},{6,7},{7,6},{8,9},{9,8},{10,11... | collective-permute-start | bytes 3145736 | tf_op jit(solution)/shard_map/ppermute | solution.py:712
  105.2 30.3 %collective-permute-start.13 = (bf16[1024,512]{1,0:T(8,128)(2,1)}, bf16[1024,512]{1,0:T(8,128)(2,1)}, u32[]{:S(2)}, u32[]{:S(2)}) collective-permute-start(bf16[1024,512]{1,0:T(8,128)(2,1)} %stack_rows.1), channel_id=1, source_target_pairs={{0,2},{1,3},{2,0},{3,1},{4,6},{5,7},{6,4},{7,5},{8,10},{9,11},{10,... | collective-permute-start | bytes 3145736 | tf_op jit(solution)/shard_map/ppermute | solution.py:712
  109.4 25.0 %collective-permute-start.14 = (bf16[128,1024]{1,0:T(8,128)(2,1)S(1)}, bf16[128,1024]{1,0:T(8,128)(2,1)S(1)}, u32[]{:S(2)}, u32[]{:S(2)}) collective-permute-start(bf16[128,1024]{1,0:T(8,128)(2,1)S(1)} %slice.378), channel_id=1, source_target_pairs={{0,1},{1,0},{2,3},{3,2},{4,5},{5,4},{6,7},{7,6},{8,9},{9,8},{10,11... | collective-permute-start | bytes 786440 | tf_op jit(solution)/shard_map/ppermute | solution.py:712
  110.9 24.6 %collective-permute-start.15 = (bf16[128,1024]{1,0:T(8,128)(2,1)S(1)}, bf16[128,1024]{1,0:T(8,128)(2,1)S(1)}, u32[]{:S(2)}, u32[]{:S(2)}) collective-permute-start(bf16[128,1024]{1,0:T(8,128)(2,1)S(1)} %slice.379), channel_id=1, source_target_pairs={{0,2},{1,3},{2,0},{3,1},{4,6},{5,7},{6,4},{7,5},{8,10},{9,11},{10,... | collective-permute-start | bytes 786440 | tf_op jit(solution)/shard_map/ppermute | solution.py:712
  139.8 13.3 %collective-permute-start.16 = (bf16[512,512]{1,0:T(8,128)(2,1)S(1)}, bf16[512,512]{1,0:T(8,128)(2,1)S(1)}, u32[]{:S(2)}, u32[]{:S(2)}) collective-permute-start(bf16[512,512]{1,0:T(8,128)(2,1)S(1)} %slice.380), channel_id=1, source_target_pairs={{0,1},{1,0},{2,3},{3,2},{4,5},{5,4},{6,7},{7,6},{8,9},{9,8},{10,11... | collective-permute-start | bytes 1572872 | tf_op jit(solution)/shard_map/ppermute | solution.py:712
  156.0 32.9 %collective-permute-start.21 = (bf16[256,2048]{1,0:T(8,128)(2,1)S(1)}, bf16[256,2048]{1,0:T(8,128)(2,1)S(1)}, u32[]{:S(2)}, u32[]{:S(2)}) collective-permute-start(bf16[256,2048]{1,0:T(8,128)(2,1)S(1)} %bitcast_convert_fusion.s_ref.refs_4_), channel_id=1, source_target_pairs={{0,1},{1,0},{2,3},{3,2},{4,5},{5,4},{6,7},{7,6},{8,9},{9,8},{10,11... | collective-permute-start | bytes 3145736 | tf_op jit(solution)/shard_map/ppermute | solution.py:712
  157.2 47.7 %collective-permute-start.22 = (bf16[256,2048]{1,0:T(8,128)(2,1)S(1)}, bf16[256,2048]{1,0:T(8,128)(2,1)}, u32[]{:S(2)}, u32[]{:S(2)}) collective-permute-start(bf16[256,2048]{1,0:T(8,128)(2,1)S(1)} %bitcast_convert_fusion.s_ref.refs_4_), channel_id=1, source_target_pairs={{0,2},{1,3},{2,0},{3,1},{4,6},{5,7},{6,4},{7,5},{8,10},{9,11},{10,... | collective-permute-start | bytes 3145736 | tf_op jit(solution)/shard_map/ppermute | solution.py:712
  158.0 47.2 %collective-permute-start.23 = (bf16[256,2048]{1,0:T(8,128)(2,1)S(1)}, bf16[256,2048]{1,0:T(8,128)(2,1)S(1)}, u32[]{:S(2)}, u32[]{:S(2)}) collective-permute-start(bf16[256,2048]{1,0:T(8,128)(2,1)S(1)} %bitcast_convert_fusion.s_ref.refs_4_), channel_id=1, source_target_pairs={{0,3},{1,2},{2,1},{3,0},{4,7},{5,6},{6,5},{7,4},{8,11},{9,10},{10,... | collective-permute-start | bytes 3145736 | tf_op jit(solution)/shard_map/ppermute | solution.py:712
  184.0 31.3 %collective-permute-start.19 = (bf16[128,2048]{1,0:T(8,128)(2,1)S(1)}, bf16[128,2048]{1,0:T(8,128)(2,1)S(1)}, u32[]{:S(2)}, u32[]{:S(2)}) collective-permute-start(bf16[128,2048]{1,0:T(8,128)(2,1)S(1)} %get-tuple-element.473), channel_id=1, source_target_pairs={{0,1},{1,0},{2,3},{3,2},{4,5},{5,4},{6,7},{7,6},{8,9},{9,8},{10,11... | collective-permute-start | bytes 1572872 | tf_op jit(solution)/shard_map/ppermute | solution.py:712
  185.4 30.8 %collective-permute-start.20 = (bf16[128,2048]{1,0:T(8,128)(2,1)S(1)}, bf16[128,2048]{1,0:T(8,128)(2,1)S(1)}, u32[]{:S(2)}, u32[]{:S(2)}) collective-permute-start(bf16[128,2048]{1,0:T(8,128)(2,1)S(1)} %get-tuple-element.472), channel_id=1, source_target_pairs={{0,2},{1,3},{2,0},{3,1},{4,6},{5,7},{6,4},{7,5},{8,10},{9,11},{10,... | collective-permute-start | bytes 1572872 | tf_op jit(solution)/shard_map/ppermute | solution.py:712
  216.5 25.2 %collective-permute-start.25 = (bf16[256,2048]{1,0:T(8,128)(2,1)S(1)}, bf16[256,2048]{1,0:T(8,128)(2,1)S(1)}, u32[]{:S(2)}, u32[]{:S(2)}) collective-permute-start(bf16[256,2048]{1,0:T(8,128)(2,1)S(1)} %pad_maximum_fusion.4), channel_id=1, source_target_pairs={{0,2},{1,3},{2,0},{3,1},{4,6},{5,7},{6,4},{7,5},{8,10},{9,11},{10,... | collective-permute-start | bytes 3145736 | tf_op jit(solution)/shard_map/ppermute | solution.py:712
  217.6 25.1 %collective-permute-start.24 = (bf16[256,2048]{1,0:T(8,128)(2,1)S(1)}, bf16[256,2048]{1,0:T(8,128)(2,1)S(1)}, u32[]{:S(2)}, u32[]{:S(2)}) collective-permute-start(bf16[256,2048]{1,0:T(8,128)(2,1)S(1)} %pad_maximum_fusion.3), channel_id=1, source_target_pairs={{0,1},{1,0},{2,3},{3,2},{4,5},{5,4},{6,7},{7,6},{8,9},{9,8},{10,11... | collective-permute-start | bytes 3145736 | tf_op jit(solution)/shard_map/ppermute | solution.py:712
  247.6 24.6 %collective-permute-start.26 = (bf16[256,2048]{1,0:T(8,128)(2,1)}, bf16[256,2048]{1,0:T(8,128)(2,1)}, u32[]{:S(2)}, u32[]{:S(2)}) collective-permute-start(bf16[256,2048]{1,0:T(8,128)(2,1)} %multiply_convert_fusion.x_ref.refs_0_), channel_id=1, source_target_pairs={{0,1},{1,0},{2,3},{3,2},{4,5},{5,4},{6,7},{7,6},{8,9},{9,8},{10,11... | collective-permute-start | bytes 3145736 | tf_op jit(solution)/shard_map/ppermute | solution.py:712
  248.7 23.9 %collective-permute-start.27 = (bf16[256,2048]{1,0:T(8,128)(2,1)}, bf16[256,2048]{1,0:T(8,128)(2,1)}, u32[]{:S(2)}, u32[]{:S(2)}) collective-permute-start(bf16[256,2048]{1,0:T(8,128)(2,1)} %multiply_convert_fusion.x_ref.refs_0_), channel_id=1, source_target_pairs={{0,2},{1,3},{2,0},{3,1},{4,6},{5,7},{6,4},{7,5},{8,10},{9,11},{10,... | collective-permute-start | bytes 3145736 | tf_op jit(solution)/shard_map/ppermute | solution.py:712
  274.4 20.7 %collective-permute-start.28 = (bf16[128,2048]{1,0:T(8,128)(2,1)}, bf16[128,2048]{1,0:T(8,128)(2,1)}, u32[]{:S(2)}, u32[]{:S(2)}) collective-permute-start(bf16[128,2048]{1,0:T(8,128)(2,1)} %slice.393), channel_id=1, source_target_pairs={{0,1},{1,0},{2,3},{3,2},{4,5},{5,4},{6,7},{7,6},{8,9},{9,8},{10,11... | collective-permute-start | bytes 1572872 | tf_op jit(solution)/shard_map/ppermute | solution.py:712
  277.8 17.4 %collective-permute-start.29 = (bf16[128,2048]{1,0:T(8,128)(2,1)}, bf16[128,2048]{1,0:T(8,128)(2,1)}, u32[]{:S(2)}, u32[]{:S(2)}) collective-permute-start(bf16[128,2048]{1,0:T(8,128)(2,1)} %slice.394), channel_id=1, source_target_pairs={{0,2},{1,3},{2,0},{3,1},{4,6},{5,7},{6,4},{7,5},{8,10},{9,11},{10,... | collective-permute-start | bytes 1572872 | tf_op jit(solution)/shard_map/ppermute | solution.py:712
  295.1 31.4 %collective-permute-start.30 = (bf16[256,2048]{1,0:T(8,128)(2,1)}, bf16[256,2048]{1,0:T(8,128)(2,1)}, u32[]{:S(2)}, u32[]{:S(2)}) collective-permute-start(bf16[256,2048]{1,0:T(8,128)(2,1)} %get-tuple-element.256), channel_id=1, source_target_pairs={{0,1},{1,0},{2,3},{3,2},{4,5},{5,4},{6,7},{7,6},{8,9},{9,8},{10,11... | collective-permute-start | bytes 3145736 | tf_op jit(solution)/shard_map/ppermute | solution.py:712
  339.9 185.8 %reduce-scatter.6.cloned.1.call-start = ((), (), s32[]{:S(2)}) async-start(), calls=%async_computation.8 | async-start | bytes 12976128 | tf_op jit(solution)/shard_map/reduce_scatter | solution.py:901
  340.0 22.5 %collective-permute-start.31 = (bf16[256,2048]{1,0:T(8,128)(2,1)}, bf16[256,2048]{1,0:T(8,128)(2,1)}, u32[]{:S(2)}, u32[]{:S(2)}) collective-permute-start(bf16[256,2048]{1,0:T(8,128)(2,1)} %get-tuple-element.284), channel_id=1, source_target_pairs={{0,2},{1,3},{2,0},{3,1},{4,6},{5,7},{6,4},{7,5},{8,10},{9,11},{10,... | collective-permute-start | bytes 3145736 | tf_op jit(solution)/shard_map/ppermute | solution.py:712
  362.5 22.5 %collective-permute-start.32 = (bf16[256,2048]{1,0:T(8,128)(2,1)}, bf16[256,2048]{1,0:T(8,128)(2,1)}, u32[]{:S(2)}, u32[]{:S(2)}) collective-permute-start(bf16[256,2048]{1,0:T(8,128)(2,1)} %get-tuple-element.287), channel_id=1, source_target_pairs={{0,3},{1,2},{2,1},{3,0},{4,7},{5,6},{6,5},{7,4},{8,11},{9,10},{10,... | collective-permute-start | bytes 3145736 | tf_op jit(solution)/shard_map/ppermute | solution.py:712
  384.9 316.6 %all-gather.10.cloned.1.call-start = ((), (), s32[]{:S(2)}) async-start(), calls=%async_computation.10 | async-start | bytes 6488064 | tf_op jit(solution)/shard_map/all_gather | solution.py:928
  391.0 27.1 %collective-permute-start.33 = (bf16[256,2048]{1,0:T(8,128)(2,1)S(1)}, bf16[256,2048]{1,0:T(8,128)(2,1)S(1)}, u32[]{:S(2)}, u32[]{:S(2)}) collective-permute-start(bf16[256,2048]{1,0:T(8,128)(2,1)S(1)} %get-tuple-element.427.refs_4_), channel_id=1, source_target_pairs={{0,1},{1,0},{2,3},{3,2},{4,5},{5,4},{6,7},{7,6},{8,9},{9,8},{10,11... | collective-permute-start | bytes 3145736 | tf_op jit(solution)/shard_map/ppermute | solution.py:712
  399.7 20.4 %collective-permute-start.34 = (bf16[256,2048]{1,0:T(8,128)(2,1)S(1)}, bf16[256,2048]{1,0:T(8,128)(2,1)S(1)}, u32[]{:S(2)}, u32[]{:S(2)}) collective-permute-start(bf16[256,2048]{1,0:T(8,128)(2,1)S(1)} %get-tuple-element.427.refs_4_), channel_id=1, source_target_pairs={{0,2},{1,3},{2,0},{3,1},{4,6},{5,7},{6,4},{7,5},{8,10},{9,11},{10,... | collective-permute-start | bytes 3145736 | tf_op jit(solution)/shard_map/ppermute | solution.py:712
  456.6 254.7 %all-gather.8.cloned.1.call-start = ((), (), s32[]{:S(2)}) async-start(), calls=%async_computation.9 | async-start | bytes 7208960 | tf_op jit(solution)/shard_map/all_gather | solution.py:953
  459.1 14.9 %collective-permute-start.40 = (bf16[4,4,2,64,512]{4,3,2,1,0:T(8,128)(2,1)S(1)}, bf16[4,4,2,64,512]{4,3,2,1,0:T(8,128)(2,1)S(1)}, u32[]{:S(2)}, u32[]{:S(2)}) collective-permute-start(bf16[4,4,2,64,512]{4,3,2,1,0:T(8,128)(2,1)S(1)} %copy-done.102), channel_id=1, source_target_pairs={{0,4},{4,0},{8,12},{12,8},{16,20},{20,16},{24,28},{28,24},{1,5},{5... | collective-permute-start | bytes 6291464 | tf_op jit(solution)/shard_map/core_swap/ppermute | solution.py:716
  478.6 19.0 %collective-permute-start.43 = (bf16[256,512]{1,0:T(8,128)(2,1)}, bf16[256,512]{1,0:T(8,128)(2,1)}, u32[]{:S(2)}, u32[]{:S(2)}) collective-permute-start(bf16[256,512]{1,0:T(8,128)(2,1)} %bitcast.42), channel_id=1, source_target_pairs={{0,1},{1,0},{2,3},{3,2},{4,5},{5,4},{6,7},{7,6},{8,9},{9,8},{10,11... | collective-permute-start | bytes 786440 | tf_op jit(solution)/shard_map/ppermute | solution.py:712
  480.5 20.4 %collective-permute-start.44 = (bf16[256,512]{1,0:T(8,128)(2,1)}, bf16[256,512]{1,0:T(8,128)(2,1)}, u32[]{:S(2)}, u32[]{:S(2)}) collective-permute-start(bf16[256,512]{1,0:T(8,128)(2,1)} %bitcast.43), channel_id=1, source_target_pairs={{0,2},{1,3},{2,0},{3,1},{4,6},{5,7},{6,4},{7,5},{8,10},{9,11},{10,... | collective-permute-start | bytes 786440 | tf_op jit(solution)/shard_map/ppermute | solution.py:712
  482.4 25.9 %collective-permute-start.42 = (bf16[512,512]{1,0:T(8,128)(2,1)}, bf16[512,512]{1,0:T(8,128)(2,1)}, u32[]{:S(2)}, u32[]{:S(2)}) collective-permute-start(bf16[512,512]{1,0:T(8,128)(2,1)} %pad_maximum_fusion.13), channel_id=1, source_target_pairs={{0,2},{1,3},{2,0},{3,1},{4,6},{5,7},{6,4},{7,5},{8,10},{9,11},{10,... | collective-permute-start | bytes 1572872 | tf_op jit(solution)/shard_map/ppermute | solution.py:712
  484.4 24.0 %collective-permute-start.41 = (bf16[512,512]{1,0:T(8,128)(2,1)}, bf16[512,512]{1,0:T(8,128)(2,1)}, u32[]{:S(2)}, u32[]{:S(2)}) collective-permute-start(bf16[512,512]{1,0:T(8,128)(2,1)} %pad_maximum_fusion.12), channel_id=1, source_target_pairs={{0,1},{1,0},{2,3},{3,2},{4,5},{5,4},{6,7},{7,6},{8,9},{9,8},{10,11... | collective-permute-start | bytes 1572872 | tf_op jit(solution)/shard_map/ppermute | solution.py:712
  485.3 19.9 %collective-permute-start.45 = (bf16[128,1024]{1,0:T(8,128)(2,1)}, bf16[128,1024]{1,0:T(8,128)(2,1)}, u32[]{:S(2)}, u32[]{:S(2)}) collective-permute-start(bf16[128,1024]{1,0:T(8,128)(2,1)} %get-tuple-element.485), channel_id=1, source_target_pairs={{0,1},{1,0},{2,3},{3,2},{4,5},{5,4},{6,7},{7,6},{8,9},{9,8},{10,11... | collective-permute-start | bytes 786440 | tf_op jit(solution)/shard_map/ppermute | solution.py:712
  500.9 36.1 %collective-permute-start.55 = (bf16[256,2048]{1,0:T(8,128)(2,1)}, bf16[256,2048]{1,0:T(8,128)(2,1)}, u32[]{:S(2)}, u32[]{:S(2)}) collective-permute-start(bf16[256,2048]{1,0:T(8,128)(2,1)} %get-tuple-element.353), channel_id=1, source_target_pairs={{0,1},{1,0},{2,3},{3,2},{4,5},{5,4},{6,7},{7,6},{8,9},{9,8},{10,11... | collective-permute-start | bytes 3145736 | tf_op jit(solution)/shard_map/ppermute | solution.py:712
  505.2 47.5 %collective-permute-start.56 = (bf16[256,2048]{1,0:T(8,128)(2,1)}, bf16[256,2048]{1,0:T(8,128)(2,1)}, u32[]{:S(2)}, u32[]{:S(2)}) collective-permute-start(bf16[256,2048]{1,0:T(8,128)(2,1)} %get-tuple-element.354), channel_id=1, source_target_pairs={{0,2},{1,3},{2,0},{3,1},{4,6},{5,7},{6,4},{7,5},{8,10},{9,11},{10,... | collective-permute-start | bytes 3145736 | tf_op jit(solution)/shard_map/ppermute | solution.py:712
  506.4 49.2 %collective-permute-start.57 = (bf16[256,2048]{1,0:T(8,128)(2,1)}, bf16[256,2048]{1,0:T(8,128)(2,1)}, u32[]{:S(2)}, u32[]{:S(2)}) collective-permute-start(bf16[256,2048]{1,0:T(8,128)(2,1)} %get-tuple-element.355), channel_id=1, source_target_pairs={{0,3},{1,2},{2,1},{3,0},{4,7},{5,6},{6,5},{7,4},{8,11},{9,10},{10,... | collective-permute-start | bytes 3145736 | tf_op jit(solution)/shard_map/ppermute | solution.py:712
  531.7 24.2 %collective-permute-start.47 = (bf16[128,512]{1,0:T(8,128)(2,1)S(1)}, bf16[128,512]{1,0:T(8,128)(2,1)S(1)}, u32[]{:S(2)}, u32[]{:S(2)}) collective-permute-start(bf16[128,512]{1,0:T(8,128)(2,1)S(1)} %get-tuple-element.483), channel_id=1, source_target_pairs={{8,0},{12,4},{16,8},{20,12},{24,16},{28,20},{9,1},{13,5},{17,9},{2... | collective-permute-start | bytes 393224 | tf_op jit(solution)/shard_map/ppermute | solution.py:960
  533.1 52.7 %collective-permute-start.54 = (bf16[1024,512]{1,0:T(8,128)(2,1)}, bf16[1024,512]{1,0:T(8,128)(2,1)}, u32[]{:S(2)}, u32[]{:S(2)}) collective-permute-start(bf16[1024,512]{1,0:T(8,128)(2,1)} %get-tuple-element.351), channel_id=1, source_target_pairs={{0,4},{4,0},{8,12},{12,8},{16,20},{20,16},{24,28},{28,24},{1,5},{5... | collective-permute-start | bytes 3145736 | tf_op jit(solution)/shard_map/core_swap/ppermute | solution.py:716
  537.0 20.8 %collective-permute-start.48 = (bf16[128,512]{1,0:T(8,128)(2,1)S(1)}, bf16[128,512]{1,0:T(8,128)(2,1)S(1)}, u32[]{:S(2)}, u32[]{:S(2)}) collective-permute-start(bf16[128,512]{1,0:T(8,128)(2,1)S(1)} %get-tuple-element.482), channel_id=1, source_target_pairs={{16,0},{20,4},{24,8},{28,12},{17,1},{21,5},{25,9},{29,13},{18,2},{... | collective-permute-start | bytes 393224 | tf_op jit(solution)/shard_map/ppermute | solution.py:960
  552.6 20.7 %collective-permute-start.49 = (bf16[128,512]{1,0:T(8,128)(2,1)S(1)}, bf16[128,512]{1,0:T(8,128)(2,1)S(1)}, u32[]{:S(2)}, u32[]{:S(2)}) collective-permute-start(bf16[128,512]{1,0:T(8,128)(2,1)S(1)} %get-tuple-element.481), channel_id=1, source_target_pairs={{24,0},{28,4},{25,1},{29,5},{26,2},{30,6},{27,3},{31,7}} | collective-permute-start | bytes 393224 | tf_op jit(solution)/shard_map/ppermute | solution.py:960
  555.6 24.5 %collective-permute-start.53 = (bf16[256,1024]{1,0:T(8,128)(2,1)}, bf16[256,1024]{1,0:T(8,128)(2,1)}, u32[]{:S(2)}, u32[]{:S(2)}) collective-permute-start(bf16[256,1024]{1,0:T(8,128)(2,1)} %pad_maximum_fusion.17), channel_id=1, source_target_pairs={{0,2},{1,3},{2,0},{3,1},{4,6},{5,7},{6,4},{7,5},{8,10},{9,11},{10,... | collective-permute-start | bytes 1572872 | tf_op jit(solution)/shard_map/ppermute | solution.py:712
  555.9 24.2 %collective-permute-start.52 = (bf16[256,1024]{1,0:T(8,128)(2,1)}, bf16[256,1024]{1,0:T(8,128)(2,1)}, u32[]{:S(2)}, u32[]{:S(2)}) collective-permute-start(bf16[256,1024]{1,0:T(8,128)(2,1)} %pad_maximum_fusion.16), channel_id=1, source_target_pairs={{0,1},{1,0},{2,3},{3,2},{4,5},{5,4},{6,7},{7,6},{8,9},{9,8},{10,11... | collective-permute-start | bytes 1572872 | tf_op jit(solution)/shard_map/ppermute | solution.py:712
  557.8 22.3 %collective-permute-start.51 = (bf16[512,512]{1,0:T(8,128)(2,1)}, bf16[512,512]{1,0:T(8,128)(2,1)}, u32[]{:S(2)}, u32[]{:S(2)}) collective-permute-start(bf16[512,512]{1,0:T(8,128)(2,1)} %pad_maximum_fusion.15), channel_id=1, source_target_pairs={{0,2},{1,3},{2,0},{3,1},{4,6},{5,7},{6,4},{7,5},{8,10},{9,11},{10,... | collective-permute-start | bytes 1572872 | tf_op jit(solution)/shard_map/ppermute | solution.py:712
  590.1 42.0 %collective-permute-start.61 = (bf16[256,1024]{1,0:T(8,128)(2,1)}, bf16[256,1024]{1,0:T(8,128)(2,1)}, u32[]{:S(2)}, u32[]{:S(2)}) collective-permute-start(bf16[256,1024]{1,0:T(8,128)(2,1)} %subtract_convert_fusion.refs_4_), channel_id=1, source_target_pairs={{0,1},{1,0},{2,3},{3,2},{4,5},{5,4},{6,7},{7,6},{8,9},{9,8},{10,11... | collective-permute-start | bytes 1572872 | tf_op jit(solution)/shard_map/ppermute | solution.py:712
  591.8 40.3 %collective-permute-start.62 = (bf16[256,1024]{1,0:T(8,128)(2,1)}, bf16[256,1024]{1,0:T(8,128)(2,1)}, u32[]{:S(2)}, u32[]{:S(2)}) collective-permute-start(bf16[256,1024]{1,0:T(8,128)(2,1)} %subtract_convert_fusion.refs_4_), channel_id=1, source_target_pairs={{0,2},{1,3},{2,0},{3,1},{4,6},{5,7},{6,4},{7,5},{8,10},{9,11},{10,... | collective-permute-start | bytes 1572872 | tf_op jit(solution)/shard_map/ppermute | solution.py:712
  593.1 21.0 %all-to-all-start.2 = ((bf16[256,4,512]{2,0,1:T(8,128)(2,1)}), bf16[256,4,512]{2,0,1:T(8,128)(2,1)}, u32[]{:S(2)}, u32[]{:S(2)}) async-start(bf16[256,4,512]{2,0,1:T(8,128)(2,1)} %bitcast.212), calls=%async_computation.4 | async-start | bytes 2097152 | tf_op jit(solution)/shard_map/all_to_all | solution.py:980
  601.0 19.6 %collective-permute-start.58 = (bf16[128,512]{1,0:T(8,128)(2,1)}, bf16[128,512]{1,0:T(8,128)(2,1)}, u32[]{:S(2)}, u32[]{:S(2)}) collective-permute-start(bf16[128,512]{1,0:T(8,128)(2,1)} %get-tuple-element.480), channel_id=1, source_target_pairs={{8,0},{12,4},{16,8},{20,12},{24,16},{28,20},{9,1},{13,5},{17,9},{2... | collective-permute-start | bytes 393224 | tf_op jit(solution)/shard_map/ppermute | solution.py:960
  602.3 29.8 %collective-permute-start.59 = (bf16[128,512]{1,0:T(8,128)(2,1)}, bf16[128,512]{1,0:T(8,128)(2,1)}, u32[]{:S(2)}, u32[]{:S(2)}) collective-permute-start(bf16[128,512]{1,0:T(8,128)(2,1)} %get-tuple-element.479), channel_id=1, source_target_pairs={{16,0},{20,4},{24,8},{28,12},{17,1},{21,5},{25,9},{29,13},{18,2},{... | collective-permute-start | bytes 393224 | tf_op jit(solution)/shard_map/ppermute | solution.py:960
  603.6 28.5 %collective-permute-start.60 = (bf16[128,512]{1,0:T(8,128)(2,1)}, bf16[128,512]{1,0:T(8,128)(2,1)}, u32[]{:S(2)}, u32[]{:S(2)}) collective-permute-start(bf16[128,512]{1,0:T(8,128)(2,1)} %get-tuple-element.478), channel_id=1, source_target_pairs={{24,0},{28,4},{25,1},{29,5},{26,2},{30,6},{27,3},{31,7}} | collective-permute-start | bytes 393224 | tf_op jit(solution)/shard_map/ppermute | solution.py:960
  614.1 58.6 %all-to-all-start.3 = ((bf16[4,256,512]{2,1,0:T(8,128)(2,1)}), bf16[4,256,512]{2,1,0:T(8,128)(2,1)}, u32[]{:S(2)}, u32[]{:S(2)}) async-start(bf16[4,256,512]{2,1,0:T(8,128)(2,1)} %bitcast.211), calls=%async_computation.5 | async-start | bytes 2097152 | tf_op jit(solution)/shard_map/all_to_all | solution.py:987
  618.4 181.4 %reduce-scatter.8.cloned.1.call-start = ((), (), s32[]{:S(2)}) async-start(), calls=%async_computation.11 | async-start | bytes 9142272 | tf_op jit(solution)/shard_map/reduce_scatter | solution.py:1049
  701.5 178.1 %all-gather.12.cloned.1.call-start = ((), (), s32[]{:S(2)}) async-start(), calls=%async_computation.12 | async-start | bytes 9142272 | tf_op jit(solution)/shard_map/all_gather | solution.py:1058
  715.5 34.4 %collective-permute-start.63 = (bf16[256,2816]{1,0:T(8,128)(2,1)S(1)}, bf16[256,2816]{1,0:T(8,128)(2,1)S(1)}, u32[]{:S(2)}, u32[]{:S(2)}) collective-permute-start(bf16[256,2816]{1,0:T(8,128)(2,1)S(1)} %get-tuple-element.436), channel_id=1, source_target_pairs={{0,1},{1,0},{2,3},{3,2},{4,5},{5,4},{6,7},{7,6},{8,9},{9,8},{10,11... | collective-permute-start | bytes 4325384 | tf_op jit(solution)/shard_map/ppermute | solution.py:712
  717.1 64.2 %collective-permute-start.64 = (bf16[256,2816]{1,0:T(8,128)(2,1)S(1)}, bf16[256,2816]{1,0:T(8,128)(2,1)S(1)}, u32[]{:S(2)}, u32[]{:S(2)}) collective-permute-start(bf16[256,2816]{1,0:T(8,128)(2,1)S(1)} %get-tuple-element.435), channel_id=1, source_target_pairs={{0,2},{1,3},{2,0},{3,1},{4,6},{5,7},{6,4},{7,5},{8,10},{9,11},{10,... | collective-permute-start | bytes 4325384 | tf_op jit(solution)/shard_map/ppermute | solution.py:712
  718.6 63.8 %collective-permute-start.65 = (bf16[256,2816]{1,0:T(8,128)(2,1)S(1)}, bf16[256,2816]{1,0:T(8,128)(2,1)}, u32[]{:S(2)}, u32[]{:S(2)}) collective-permute-start(bf16[256,2816]{1,0:T(8,128)(2,1)S(1)} %get-tuple-element.434), channel_id=1, source_target_pairs={{0,3},{1,2},{2,1},{3,0},{4,7},{5,6},{6,5},{7,4},{8,11},{9,10},{10,... | collective-permute-start | bytes 4325384 | tf_op jit(solution)/shard_map/ppermute | solution.py:712
  799.8 16.6 %collective-permute-start.72 = (bf16[256,2816]{1,0:T(8,128)(2,1)}, bf16[256,2816]{1,0:T(8,128)(2,1)}, u32[]{:S(2)}, u32[]{:S(2)}) collective-permute-start(bf16[256,2816]{1,0:T(8,128)(2,1)} %get-tuple-element.402.refs_0_), channel_id=1, source_target_pairs={{0,4},{4,0},{8,12},{12,8},{16,20},{20,16},{24,28},{28,24},{1,5},{5... | collective-permute-start | bytes 4325384 | tf_op jit(solution)/shard_map/core_swap/ppermute | solution.py:716
  799.9 16.5 %collective-permute-start.73 = (bf16[256,2816]{1,0:T(8,128)(2,1)}, bf16[256,2816]{1,0:T(8,128)(2,1)}, u32[]{:S(2)}, u32[]{:S(2)}) collective-permute-start(bf16[256,2816]{1,0:T(8,128)(2,1)} %copy-done.40), channel_id=1, source_target_pairs={{0,4},{4,0},{8,12},{12,8},{16,20},{20,16},{24,28},{28,24},{1,5},{5... | collective-permute-start | bytes 4325384 | tf_op jit(solution)/shard_map/core_swap/ppermute | solution.py:716
  800.4 16.0 %collective-permute-start.74 = (bf16[256,2816]{1,0:T(8,128)(2,1)}, bf16[256,2816]{1,0:T(8,128)(2,1)}, u32[]{:S(2)}, u32[]{:S(2)}) collective-permute-start(bf16[256,2816]{1,0:T(8,128)(2,1)} %copy-done.41), channel_id=1, source_target_pairs={{0,4},{4,0},{8,12},{12,8},{16,20},{20,16},{24,28},{28,24},{1,5},{5... | collective-permute-start | bytes 4325384 | tf_op jit(solution)/shard_map/core_swap/ppermute | solution.py:716
  800.5 15.9 %collective-permute-start.75 = (bf16[256,2816]{1,0:T(8,128)(2,1)}, bf16[256,2816]{1,0:T(8,128)(2,1)}, u32[]{:S(2)}, u32[]{:S(2)}) collective-permute-start(bf16[256,2816]{1,0:T(8,128)(2,1)} %collective-permute-done.65.refs_3_), channel_id=1, source_target_pairs={{0,4},{4,0},{8,12},{12,8},{16,20},{20,16},{24,28},{28,24},{1,5},{5... | collective-permute-start | bytes 4325384 | tf_op jit(solution)/shard_map/core_swap/ppermute | solution.py:716
  (128 other events, 1115.6 us)
Sparse Core Ops, SparseCore 0:
  22.1 29.0 all-gather.13
  101.4 108.3 all-gather.15
  340.0 65.2 reduce-scatter.3
  408.1 117.6 reduce-scatter.5
  527.2 67.5 all-gather.9
  596.3 114.9 all-gather.7
  714.2 85.4 reduce-scatter.7
  801.4 78.2 all-gather.11

commit v4 on v3

--- a/solution.py
+++ b/solution.py
@@ -268,8 +268,9 @@
     )(info, scaled, attn_out, d_attn, lse, kv_near, kv_far, cosine, sine)
 
 
-def feed_forward(x, signal, gu, down_w, last_kind):
-    tokens, width = x.shape
+def feed_forward(xs, signals, gu, down_w, last_kind):
+    count = len(xs)
+    tokens, width = xs[0].shape
     hidden = down_w.shape[0]
     shares, blocks, share, columns = gu.shape
     lanes = 128
@@ -278,8 +279,28 @@
     steps = -(-hidden // tile)
     tail = hidden - (steps - 1) * tile
 
-    def kernel(x_ref, s_ref, ga_ref, gb_ref, ua_ref, ub_ref, d_ref, inner_ref, dg_ref, du_ref, y_ref, dx_ref, g_s, u_s, y_s, dx_s):
+    def kernel(*refs):
+        x_refs, s_refs, refs = refs[:count], refs[count : 2 * count], refs[2 * count :]
+        ga_ref, gb_ref, ua_ref, ub_ref, d_ref, refs = *refs[:5], refs[5:]
+        outs, scratch = [refs[n * count : (n + 1) * count] for n in range(5)], refs[5 * count :]
+        inner_refs, dg_refs, du_refs, y_refs, dx_refs = outs
+        g_s, u_s, y_s, dx_s = scratch[:4]
         step = pl.program_id(0)
+        if count > 1:
+            x_s, s_s = scratch[4:]
+
+            @pl.when(step == 0)
+            def _():
+                for n in range(count):
+                    x_s[n * tokens : (n + 1) * tokens] = x_refs[n][...]
+                    s_s[n * tokens : (n + 1) * tokens] = s_refs[n][...]
+
+        else:
+            x_s, s_s = x_refs[0], s_refs[0]
+
+        def spread(targets, value, size):
+            for n, ref in enumerate(targets):
+                ref[:, :size] = value[n * tokens : (n + 1) * tokens].astype(ref.dtype)
 
         def work(size, start):
             for s in range(shares):
@@ -291,7 +312,7 @@
                         g_s[at, lanes:] = gb_ref[s, b]
                         u_s[at, lanes:] = ub_ref[s, b]
             gate_tile, up_tile, down_tile = g_s[:, :size], u_s[:, :size], d_ref[:size, :]
-            rows, grads = x_ref[...], s_ref[...]
+            rows, grads = x_s[...], s_s[...]
             gate, upper = dot(rows, gate_tile), dot(rows, up_tile)
             d_inner = dot_back(grads, down_tile)
             sigma = jax.nn.sigmoid(gate)
@@ -299,9 +320,9 @@
             inner = (swish * upper).astype(BF16)
             d_gate = (d_inner * upper * sigma * (1.0 + gate * (1.0 - sigma))).astype(BF16)
             d_upper = (d_inner * swish).astype(BF16)
-            inner_ref[:, :size] = inner
-            dg_ref[:, :size] = d_gate
-            du_ref[:, :size] = d_upper
+            spread(inner_refs, inner, size)
+            spread(dg_refs, d_gate, size)
+            spread(du_refs, d_upper, size)
             y = dot(inner, down_tile)
             dx = dot_back(d_gate, gate_tile) + dot_back(d_upper, up_tile)
             if start:
@@ -329,8 +350,8 @@
 
         @pl.when(step == steps - 1)
         def _():
-            y_ref[...] = y_s[...].astype(y_ref.dtype)
-            dx_ref[...] = dx_s[...].astype(dx_ref.dtype)
+            spread(y_refs, y_s[...], width)
+            spread(dx_refs, dx_s[...], width)
 
     def lane_block(base, second):
         last = base + up_at - 1
@@ -341,23 +362,27 @@
     whole = pl.BlockSpec((tokens, width), lambda n: (0, 0))
     rows = pl.BlockSpec((tile, width), lambda n: (n, 0))
     out = pl.BlockSpec((tokens, tile), lambda n: (0, n))
-    return pl.pallas_call(
+    extra = [pltpu.VMEM((count * tokens, width), BF16)] * 2 if count > 1 else []
+    found = pl.pallas_call(
         kernel,
         grid=(steps,),
-        in_specs=[whole, whole, lane_block(0, 0), lane_block(0, 1), lane_block(up_at, 0), lane_block(up_at, 1), rows],
-        out_specs=[out, out, out, whole, whole],
+        in_specs=[whole] * (2 * count)
+        + [lane_block(0, 0), lane_block(0, 1), lane_block(up_at, 0), lane_block(up_at, 1), rows],
+        out_specs=[out] * (3 * count) + [whole] * (2 * count),
         scratch_shapes=[
             pltpu.VMEM((width, tile), BF16),
             pltpu.VMEM((width, tile), BF16),
-            pltpu.VMEM((tokens, width), F32),
-            pltpu.VMEM((tokens, width), F32),
+            pltpu.VMEM((count * tokens, width), F32),
+            pltpu.VMEM((count * tokens, width), F32),
+            *extra,
         ],
-        out_shape=[jax.ShapeDtypeStruct((tokens, hidden), BF16)] * 3
-        + [jax.ShapeDtypeStruct((tokens, width), last_kind)] * 2,
+        out_shape=[jax.ShapeDtypeStruct((tokens, hidden), BF16)] * (3 * count)
+        + [jax.ShapeDtypeStruct((tokens, width), last_kind)] * (2 * count),
         compiler_params=pltpu.CompilerParams(dimension_semantics=("arbitrary",)),
         cost_estimate=cheap(),
         name="feed_forward",
-    )(x, signal, gu, gu, gu, gu, down_w)
+    )(*xs, *signals, gu, gu, gu, gu, down_w)
+    return [[found[n * count + b] for n in range(5)] for b in range(count)]
 
 
 def hidden_units(x, gu, hidden):
@@ -869,26 +894,27 @@
 
         weights = (gu, w_down)
         ffn_got = gather_first(ffn_in)
-        done = [feed_forward(ffn_in, signal_low, *weights, F32)]
+        done = feed_forward([ffn_in], [signal_low], *weights, F32)
         ffn_got, first_dx = fence(ffn_got, done[0][4])
         ffn_more = gather_second(ffn_got)
         dffn_got = []
-        for j in range(len(ffn_got)):
-            done.append(feed_forward(ffn_got[j], signal_got[j], *weights, BF16))
-            sent, ffn_more, ffn_got[j + 1 :] = fence(done[-1][4], ffn_more, ffn_got[j + 1 :])
-            dffn_got.append(swap(sent, j + 1))
+        pair = 2 if square else 1
+        for j in range(0, len(ffn_got), pair):
+            done += feed_forward(ffn_got[j : j + pair], signal_got[j : j + pair], *weights, BF16)
+            sent, ffn_more, ffn_got[j + pair :] = fence([d[4] for d in done[-pair:]], ffn_more, ffn_got[j + pair :])
+            dffn_got += [swap(x, j + 1 + n) for n, x in enumerate(sent)]
         ffn_blocks = gather_done(ffn_in, ffn_got, ffn_more)
         signal_blocks = [signal_low] + signal_got
 
         inner_blocks = [d[0] for d in done]
         if square:
             inner_blocks.append(hidden_units(ffn_blocks[3], gu, hidden_cols))
-        dffn_got[0], inner_blocks, last_x = fence(dffn_got[0], inner_blocks, ffn_blocks[nf - 1])
+        inner_blocks, last_x = fence(inner_blocks, ffn_blocks[nf - 1])
         down_part = token_sum(inner_blocks, signal_blocks)
         down_part, last_x = fence(down_part, last_x)
         down_share = lax.psum_scatter(down_part, "ctx", scatter_dimension=0, tiled=True)
         if square:
-            done.append(feed_forward(last_x, signal_got[2], *weights, BF16))
+            done += feed_forward([last_x], [signal_got[2]], *weights, BF16)
         _, gate_blocks, up_blocks, y_parts, dx = (list(t) for t in zip(*done))
         late = fence(dx[nf - 1], ffn_blocks, gate_blocks, up_blocks, dffn_got)
         dffn_got = late[4]

time: 910 us -> 903 us (level)
    pallas_call x4 -> x3, Pallas kernels: 68 us -> 62.8 us  [feed_forward(): pl.pallas_call(kernel, grid=(steps,), in_specs=[whole] * (2 * count) + [l...]
    unnamed x224 -> x222, local copies, waits for them, and re-layouts: 39.4 us -> 39.8 us
  transfers between devices with their start and end apart: 88 -> 88, of which waited for: 40 -> 42; matrix products, arithmetic and copies ran while one was open for 19% -> 18% of each run, Pallas kernels for 21% -> 19%
where the time goes in v4:
time: 903 us; the launch traced here: 893 us
  waiting for transfers between devices  356 us (39%)
  Pallas kernels  205 us (23%)
  starting transfers between devices  114 us (13%)
  local copies, waits for them, and re-layouts  101 us (11%)
  other arithmetic  77 us (9%)
  matrix products  23.3 us (3%)
  between operations  16.1 us (2%)
    ppermute x56, waiting for transfers between devices, swap(): return lax.ppermute(x, 'fsdp', [(i, i ^ j) for i in range(nf)])  218 us
    ppermute x56, starting transfers between devices, swap(): return lax.ppermute(x, 'fsdp', [(i, i ^ j) for i in range(nf)])  74.9 us
    pallas_call x3, Pallas kernels, feed_forward(): pl.pallas_call(kernel, grid=(steps,), in_specs=[whole] * (2 * count) + [l...  62.8 us
    all_gather x1, waiting for transfers between devices, on_device(): buffer = lax.all_gather(buffer_share, 'ctx', tiled=True)  45.5 us
    pallas_call x4, Pallas kernels, token_sum(): pl.pallas_call(kernel, grid=(height // tile,), in_specs=[pl.BlockSpec((to...  45.5 us
    unnamed x222, local copies, waits for them, and re-layouts  39.8 us
    ppermute x6, waiting for transfers between devices, line_start(): lax.ppermute(low[s], 'ctx', [(i, i - 2 * s) for i in range(2 * s, nc)])  22.7 us
    pallas_call x2, Pallas kernels, attend_backward(): pl.pallas_call(kernel, grid_spec=pltpu.PrefetchScalarGridSpec(num_scalar_...  21.7 us
  transfers between devices with their start and end apart: 88, of which 42 were waited for; matrix products, arithmetic and copies ran while one was open for 18% of the time, Pallas kernels for 19%

profile of v4, /device:TPU:0, one launch (start us, length us, event | category | flops | bytes accessed | tf_op | source)
XLA Modules:
  0.0 892.6 jit_solution(4853177247001712414)
XLA Ops:
  9.5 5.2 all-to-all-start.1
  22.0 2.5 constant_dynamic-slice_fusion.2
  24.5 13.7 %collective-permute-done.1.refs_1_ = bf16[272,1536]{1,0:T(8,128)(2,1)} collective-permute-done((bf16[272,1536]{1,0:T(8,128)(2,1)}, bf16[272,1536]{1,0:T(8,128)(2,1)}, u32[]{:S(2)}, u32[]{:S(2)}) %collective-permute-start.1) | collective-permute-done | bytes 835616 | tf_op jit(solution)/shard_map/ppermute | solution.py:737
  47.3 3.5 collective-permute-done.2
  58.5 6.6 project.1
  66.3 3.7 all-to-all-start
  73.4 3.5 collective-permute-start.7
  76.9 4.5 collective-permute-start.8
  83.5 5.7 collective-permute-done.8.refs_2_
  89.2 4.3 collective-permute-done.9.refs_3_
  93.5 6.4 collective-permute-done.10.refs_1_
  115.3 19.1 %collective-permute-done.14 = bf16[128,1024]{1,0:T(8,128)(2,1)S(1)} collective-permute-done((bf16[128,1024]{1,0:T(8,128)(2,1)S(1)}, bf16[128,1024]{1,0:T(8,128)(2,1)S(1)}, u32[]{:S(2)}, u32[]{:S(2)}) %collective-permute-start.14) | collective-permute-done | bytes 262176 | tf_op jit(solution)/shard_map/ppermute | solution.py:737
  147.0 6.0 fusion.67.q_ref
  159.4 3.7 collective-permute-done.18
  165.1 14.6 %attend_forward.1 = (bf16[4,4,64,1024]{3,2,1,0:T(8,128)(2,1)}, bf16[4,4,64,1024]{3,2,1,0:T(8,128)(2,1)}, f32[4,1,1024]{2,1,0:T(1,128)}) custom-call(s32[7]{0:T(128)} %pad_add_fusion.info_ref, f32[4,4,64,1024]{3,2,1,0:T(8,128)} %fusion.67.q_ref, bf16[4,4,4,64,512]{4,3,2,1,0:T(8,128)(2,1)} %bitcast.189, bf16[4,4,4,64,512]{4,3,2,1,0:T(8,128)(2,1)} %bitcast.192, ...), custom_call_target="tpu_custom_call" | custom-call | flops 1 | bytes 1 | tf_op jit(solution)/shard_map/attend_forward/pallas_call | solution.py:146
  188.9 16.0 %collective-permute-done.22.refs_3_.refs_6_ = bf16[256,2048]{1,0:T(8,128)(2,1)} collective-permute-done((bf16[256,2048]{1,0:T(8,128)(2,1)S(1)}, bf16[256,2048]{1,0:T(8,128)(2,1)}, u32[]{:S(2)}, u32[]{:S(2)}) %collective-permute-start.22) | collective-permute-done | bytes 1048608 | tf_op jit(solution)/shard_map/ppermute | solution.py:737
  205.2 10.1 %collective-permute-done.19 = bf16[128,2048]{1,0:T(8,128)(2,1)S(1)} collective-permute-done((bf16[128,2048]{1,0:T(8,128)(2,1)S(1)}, bf16[128,2048]{1,0:T(8,128)(2,1)S(1)}, u32[]{:S(2)}, u32[]{:S(2)}) %collective-permute-start.19) | collective-permute-done | bytes 524320 | tf_op jit(solution)/shard_map/ppermute | solution.py:737
  219.9 2.6 fusion.70
  222.5 19.2 %collective-permute-done.25 = bf16[256,2048]{1,0:T(8,128)(2,1)S(1)} collective-permute-done((bf16[256,2048]{1,0:T(8,128)(2,1)S(1)}, bf16[256,2048]{1,0:T(8,128)(2,1)S(1)}, u32[]{:S(2)}, u32[]{:S(2)}) %collective-permute-start.25) | collective-permute-done | bytes 1048608 | tf_op jit(solution)/shard_map/ppermute | solution.py:737
  243.6 2.8 multiply_reduce_fusion.2
  249.6 17.7 %feed_forward.3 = (bf16[256,1408]{1,0:T(8,128)(2,1)}, bf16[256,1408]{1,0:T(8,128)(2,1)}, bf16[256,1408]{1,0:T(8,128)(2,1)}, f32[256,2048]{1,0:T(8,128)}, f32[256,2048]{1,0:T(8,128)}) custom-call(bf16[256,2048]{1,0:T(8,128)(2,1)} %multiply_convert_fusion.refs_0_, bf16[256,2048]{1,0:T(8,128)(2,1)} %copy-done.18, bf16[8,4,64,2816]{3,2,1,0:T(8,128)(2,1)} %bitcast.173, ...), custom_call_target="tpu_custom_call" | custom-call | flops 1 | bytes 1 | tf_op jit(solution)/shard_map/feed_forward/pallas_call | solution.py:366
  267.3 5.0 collective-permute-done.26.refs_0_.refs_1_
  278.5 28.4 %feed_forward.4 = (bf16[256,1408]{1,0:T(8,128)(2,1)}, bf16[256,1408]{1,0:T(8,128)(2,1)}, bf16[256,1408]{1,0:T(8,128)(2,1)}, bf16[256,1408]{1,0:T(8,128)(2,1)}, b...) custom-call(bf16[256,2048]{1,0:T(8,128)(2,1)} %collective-permute-do, ...), custom_call_target="tpu_custom_call" | custom-call | flops 1 | bytes 1 | tf_op jit(solution)/shard_map/feed_forward/pallas_call | solution.py:366
  310.7 9.5 %hidden_units.1.refs_3_ = bf16[256,1408]{1,0:T(8,128)(2,1)} custom-call(bf16[256,2048]{1,0:T(8,128)(2,1)} %constant_dynamic-update-slice_fusion.15.x_ref.refs_0_.refs_3_, bf16[8,4,64,2816]{3,2,1,0:T(8,128)(2,1)} %bitcast.181, bf16[8,4,64,2816]{3,2,1,0:T(8,128)(2,1)} %bitcast.182, bf16[8,4,64,2816]{3,2,1,0:T(8,128)(2,1)} %bitcast.183, ...), custom_call_target="tpu_custom_call" | custom-call | flops 1 | bytes 1 | tf_op jit(solution)/shard_map/hidden_units/pallas_call | solution.py:427
  320.2 13.4 %token_sum.4 = bf16[1408,2048]{1,0:T(8,128)(2,1)} custom-call(bf16[256,1408]{1,0:T(8,128)(2,1)} %get-tuple-element.259.refs_0_, bf16[256,1408]{1,0:T(8,128)(2,1)} %get-tuple-element.260.refs_1_, bf16[256,1408]{1,0:T(8,128)(2,1)} %get-tuple-element.261.refs_2_, bf16[256,1408]{1,0:T(8,128)(2,1)} %hidden_units.1.refs_3_, bf16[256,2048]{1,0:T(8,128)(2,1)} %copy-done.18, ...), custom_call_target="tpu_custom_call" | custom-call | flops 5905580032 | bytes 5767168 | tf_op jit(solution)/shard_map/token_sum/pallas_call | solution.py:584
  335.6 16.8 %feed_forward.5 = (bf16[256,1408]{1,0:T(8,128)(2,1)}, bf16[256,1408]{1,0:T(8,128)(2,1)}, bf16[256,1408]{1,0:T(8,128)(2,1)}, bf16[256,2048]{1,0:T(8,128)(2,1)}, bf16[256,2048]{1,0:T(8,128)(2,1)}) custom-call(bf16[256,2048]{1,0:T(8,128)(2,1)} %constant_dynamic-update-slice_fusion.15.x_ref.refs_0_.refs_3_, bf16[256,2048]{1,0:T(8,128)(2,1)} %copy-done.48, ...), custom_call_target="tpu_custom_call" | custom-call | flops 1 | bytes 1 | tf_op jit(solution)/shard_map/feed_forward/pallas_call | solution.py:366
  352.4 3.9 collective-permute-done.30
  359.0 19.1 %token_sum.5 = bf16[2048,2816]{1,0:T(8,128)(2,1)} custom-call(bf16[256,2048]{1,0:T(8,128)(2,1)} %multiply_convert_fusion.refs_0_, bf16[256,2048]{1,0:T(8,128)(2,1)} %collective-permute-done.26.refs_0_.refs_1_, bf16[256,2048]{1,0:T(8,128)(2,1)} %collective-permute-done.27.refs_1_.refs_2_, ...), custom_call_target="tpu_custom_call" | custom-call | flops 11811160064 | bytes 5767168 | tf_op jit(solution)/shard_map/token_sum/pallas_call | solution.py:584
  379.8 3.8 multiply_reduce_fusion
  385.6 8.6 collective-permute-start.33
  397.0 15.6 %collective-permute-done.33.refs_5_ = bf16[256,2048]{1,0:T(8,128)(2,1)S(1)} collective-permute-done((bf16[256,2048]{1,0:T(8,128)(2,1)S(1)}, bf16[256,2048]{1,0:T(8,128)(2,1)S(1)}, u32[]{:S(2)}, u32[]{:S(2)}) %collective-permute-start.33) | collective-permute-done | bytes 1048608 | tf_op jit(solution)/shard_map/ppermute | solution.py:737
  421.0 2.9 collective-permute-done.35
  429.3 10.9 %attend_backward.2 = (bf16[4,2,64,1024]{3,2,1,0:T(8,128)(2,1)}, bf16[4,4,2,64,512]{4,3,2,1,0:T(8,128)(2,1)}, bf16[4,4,2,64,512]{4,3,2,1,0:T(8,128)(2,1)}) custom-call(s32[7]{0:T(128)} %pad_add_fusion.info_ref, bf16[4,4,64,1024]{3,2,1,0:T(8,128)(2,1)} %get-tuple-element.302.q_ref, bf16[4,4,64,1024]{3,2,1,0:T(8,128)(2,1)} %get-tuple-element.234.o_ref, ...), custom_call_target="tpu_custom_call" | custom-call | flops 1 | bytes 1 | tf_op jit(solution)/shard_map/attend_backward/pallas_call | solution.py:241
  440.3 10.7 %attend_backward.3 = (bf16[4,2,64,1024]{3,2,1,0:T(8,128)(2,1)}, bf16[4,4,2,64,512]{4,3,2,1,0:T(8,128)(2,1)}, bf16[4,4,2,64,512]{4,3,2,1,0:T(8,128)(2,1)}) custom-call(s32[7]{0:T(128)} %pad_add_fusion.info_ref, bf16[4,4,64,1024]{3,2,1,0:T(8,128)(2,1)} %get-tuple-element.302.q_ref, bf16[4,4,64,1024]{3,2,1,0:T(8,128)(2,1)} %get-tuple-element.234.o_ref, ...), custom_call_target="tpu_custom_call" | custom-call | flops 1 | bytes 1 | tf_op jit(solution)/shard_map/attend_backward/pallas_call | solution.py:241
  455.9 2.5 fusion.47
  469.0 3.0 convert_add_fusion
  482.4 9.6 %token_grad.1 = (bf16[1024,512]{1,0:T(8,128)(2,1)}, bf16[1024,512]{1,0:T(8,128)(2,1)}) custom-call(s32[7]{0:T(128)} %pad_add_fusion.info_ref, bf16[256,1024]{1,0:T(8,128)(2,1)} %get-tuple-element.328.refs_0_, bf16[256,1024]{1,0:T(8,128)(2,1)} %copy-done.44, bf16[256,1024]{1,0:T(8,128)(2,1)} %collective-permute-done.11.refs_2_, ...), custom_call_target="tpu_custom_call" | custom-call | flops 2147483648 | bytes 2097152 | tf_op jit(solution)/shard_map/token_grad/pallas_call | solution.py:497
  495.5 4.1 collective-permute-done.45
  502.7 16.5 %reduce-scatter.6.cloned.1.call-done = bf16[256,2816]{1,0:T(8,128)(2,1)} async-done(((bf16[2048,2816]{1,0:T(8,128)(2,1)}), bf16[256,2816]{1,0:T(8,128)(2,1)}) %reduce-scatter.6.cloned.1.call-update) | async-done | bytes 1441808 | tf_op jit(solution)/shard_map/reduce_scatter | solution.py:927
  521.2 2.9 fusion.51
  531.8 15.5 %collective-permute-done.56 = bf16[256,2048]{1,0:T(8,128)(2,1)} collective-permute-done((bf16[256,2048]{1,0:T(8,128)(2,1)}, bf16[256,2048]{1,0:T(8,128)(2,1)}, u32[]{:S(2)}, u32[]{:S(2)}) %collective-permute-start.56) | collective-permute-done | bytes 1048608 | tf_op jit(solution)/shard_map/ppermute | solution.py:737
  554.0 9.8 %collective-permute-done.49 = bf16[128,512]{1,0:T(8,128)(2,1)S(1)} collective-permute-done((bf16[128,512]{1,0:T(8,128)(2,1)S(1)}, bf16[128,512]{1,0:T(8,128)(2,1)S(1)}, u32[]{:S(2)}, u32[]{:S(2)}) %collective-permute-start.49) | collective-permute-done | bytes 131104 | tf_op jit(solution)/shard_map/ppermute | solution.py:986
  569.7 4.9 collective-permute-done.51
  583.3 4.3 all-to-all-start.2
  587.6 2.9 fusion.49
  596.2 2.6 add_convert_fusion
  598.8 4.9 all-to-all-done.2
  603.7 4.3 all-to-all-start.3
  610.2 12.9 %collective-permute-done.59 = bf16[128,512]{1,0:T(8,128)(2,1)} collective-permute-done((bf16[128,512]{1,0:T(8,128)(2,1)}, bf16[128,512]{1,0:T(8,128)(2,1)}, u32[]{:S(2)}, u32[]{:S(2)}) %collective-permute-start.59) | collective-permute-done | bytes 131104 | tf_op jit(solution)/shard_map/ppermute | solution.py:986
  627.1 6.3 project_back.1
  643.9 3.3 collective-permute-done.67
  653.6 4.2 token_sum.6
  664.5 8.8 token_sum.7
  676.2 3.3 slice_dynamic-update-slice_fusion.1
  688.0 15.0 %all-gather.8.cloned.1.call-done = bf16[1024,2816]{1,0:T(8,128)(2,1)} async-done(((bf16[256,2816]{1,0:T(8,128)(2,1)}), bf16[1024,2816]{1,0:T(8,128)(2,1)}) %all-gather.8.cloned.1.call-update) | async-done | bytes 5767184 | tf_op jit(solution)/shard_map/all_gather | solution.py:979
  703.0 4.1 dynamic-slice_bitcast_fusion
  710.7 30.9 %collective-permute-done.63.refs_1_ = bf16[256,2816]{1,0:T(8,128)(2,1)S(1)} collective-permute-done((bf16[256,2816]{1,0:T(8,128)(2,1)S(1)}, bf16[256,2816]{1,0:T(8,128)(2,1)S(1)}, u32[]{:S(2)}, u32[]{:S(2)}) %collective-permute-start.63) | collective-permute-done | bytes 1441824 | tf_op jit(solution)/shard_map/ppermute | solution.py:737
  741.6 31.4 %collective-permute-done.64.refs_2_ = bf16[256,2816]{1,0:T(8,128)(2,1)S(1)} collective-permute-done((bf16[256,2816]{1,0:T(8,128)(2,1)S(1)}, bf16[256,2816]{1,0:T(8,128)(2,1)S(1)}, u32[]{:S(2)}, u32[]{:S(2)}) %collective-permute-start.64) | collective-permute-done | bytes 1441824 | tf_op jit(solution)/shard_map/ppermute | solution.py:737
  774.1 17.3 %reduce-scatter.8.cloned.1.call-done = bf16[496,1024]{1,0:T(8,128)(2,1)} async-done(((bf16[3968,1024]{1,0:T(8,128)(2,1)}), bf16[496,1024]{1,0:T(8,128)(2,1)}) %reduce-scatter.8.cloned.1.call-update) | async-done | bytes 1015824 | tf_op jit(solution)/shard_map/reduce_scatter | solution.py:1075
  792.6 4.4 add_convert_fusion.1
  798.6 9.5 %convert_element_type.344 = f32[1408,2048]{1,0:T(8,128)} convert(bf16[1408,2048]{1,0:T(8,128)(2,1)} %all-gather.10.cloned.1.call-done) | non-fusion elementwise | flops 2883584 | bytes 17301504 | tf_op jit(solution)/shard_map/convert_element_type | solution.py:1087
  808.1 17.8 %place_columns.1 = (f32[512,5632]{1,0:T(8,128)}, f32[512,5632]{1,0:T(8,128)}) custom-call(s32[7]{0:T(128)} %pad_add_fusion.info_ref, bf16[256,2816]{1,0:T(8,128)(2,1)} %get-tuple-element.394.refs_0_, bf16[256,2816]{1,0:T(8,128)(2,1)} %copy-done.40, bf16[256,2816]{1,0:T(8,128)(2,1)} %copy-done.41, bf16[256,2816]{1,0:T(8,128)(2,1)} %collective-permute-done.65.refs_3_, ...), custom_call_target="tpu_custom_call" | custom-call | flops 1 | bytes 1 | tf_op jit(solution)/shard_map/place_columns/pallas_call | solution.py:721
  825.9 45.5 %all-gather.12.cloned.1.call-done.o0_ref.o1_ref.refs_0_.refs_1_.refs_2_.refs_3_.refs_4_ = bf16[3968,1024]{1,0:T(8,128)(2,1)} async-done(((bf16[496,1024]{1,0:T(8,128)(2,1)}), bf16[3968,1024]{1,0:T(8,128)(2,1)}) %all-gather.12.cloned.1.call-update) | async-done | bytes 8126480 | tf_op jit(solution)/shard_map/all_gather | solution.py:1084
  873.6 8.6 unpack.1
  (529 shorter events, 245.6 us)
Async XLA Ops:
  14.7 120.7 %all-gather.14.cloned.1.call-start = ((), (), s32[]{:S(2)}) async-start(), calls=%async_computation.13 | async-start | bytes 2359296 | tf_op jit(solution)/shard_map/all_gather | solution.py:830
  16.1 25.2 %collective-permute-start = (bf16[272,1536]{1,0:T(8,128)(2,1)}, bf16[272,1536]{1,0:T(8,128)(2,1)S(1)}, u32[]{:S(2)}, u32[]{:S(2)}) collective-permute-start(bf16[272,1536]{1,0:T(8,128)(2,1)} %pad_maximum_fusion.5), channel_id=1, source_target_pairs={{0,1},{1,0},{2,3},{3,2},{4,5},{5,4},{6,7},{7,6},{8,9},{9,8},{10,11... | collective-permute-start | bytes 2506760 | tf_op jit(solution)/shard_map/ppermute | solution.py:737
  18.1 20.1 %collective-permute-start.1 = (bf16[272,1536]{1,0:T(8,128)(2,1)}, bf16[272,1536]{1,0:T(8,128)(2,1)}, u32[]{:S(2)}, u32[]{:S(2)}) collective-permute-start(bf16[272,1536]{1,0:T(8,128)(2,1)} %pad_maximum_fusion.5), channel_id=1, source_target_pairs={{0,2},{1,3},{2,0},{3,1},{4,6},{5,7},{6,4},{7,5},{8,10},{9,11},{10,... | collective-permute-start | bytes 2506760 | tf_op jit(solution)/shard_map/ppermute | solution.py:737
  66.3 33.7 %all-to-all-start = ((bf16[64,4,2816]{2,0,1:T(8,128)(2,1)}), bf16[64,4,2816]{2,0,1:T(8,128)(2,1)S(1)}, u32[]{:S(2)}, u32[]{:S(2)}) async-start(bf16[64,4,2816]{2,0,1:T(8,128)(2,1)} %bitcast.170), calls=%async_computation | async-start | bytes 2883584 | tf_op jit(solution)/shard_map/all_to_all | solution.py:822
  70.0 172.6 %all-gather.16.cloned.1.call-start = ((), (), s32[]{:S(2)}) async-start(), calls=%async_computation.14 | async-start | bytes 12976128 | tf_op jit(solution)/shard_map/all_gather | solution.py:862
  70.0 29.9 %collective-permute-start.10 = (bf16[256,1024]{1,0:T(8,128)(2,1)}, bf16[256,1024]{1,0:T(8,128)(2,1)S(1)}, u32[]{:S(2)}, u32[]{:S(2)}) collective-permute-start(bf16[256,1024]{1,0:T(8,128)(2,1)} %get-tuple-element.328.refs_0_), channel_id=1, source_target_pairs={{0,1},{1,0},{2,3},{3,2},{4,5},{5,4},{6,7},{7,6},{8,9},{9,8},{10,11... | collective-permute-start | bytes 1572872 | tf_op jit(solution)/shard_map/ppermute | solution.py:737
  72.0 28.0 %collective-permute-start.11 = (bf16[256,1024]{1,0:T(8,128)(2,1)}, bf16[256,1024]{1,0:T(8,128)(2,1)}, u32[]{:S(2)}, u32[]{:S(2)}) collective-permute-start(bf16[256,1024]{1,0:T(8,128)(2,1)} %get-tuple-element.328.refs_0_), channel_id=1, source_target_pairs={{0,2},{1,3},{2,0},{3,1},{4,6},{5,7},{6,4},{7,5},{8,10},{9,11},{10,... | collective-permute-start | bytes 1572872 | tf_op jit(solution)/shard_map/ppermute | solution.py:737
  101.2 349.8 %reduce-scatter.4.cloned.1.call-start = ((), (), s32[]{:S(2)}) async-start(), calls=%async_computation.7 | async-start | bytes 6488064 | tf_op jit(solution)/shard_map/reduce_scatter | solution.py:915
  103.8 31.7 %collective-permute-start.12 = (bf16[1024,512]{1,0:T(8,128)(2,1)}, bf16[1024,512]{1,0:T(8,128)(2,1)}, u32[]{:S(2)}, u32[]{:S(2)}) collective-permute-start(bf16[1024,512]{1,0:T(8,128)(2,1)} %stack_rows.1), channel_id=1, source_target_pairs={{0,1},{1,0},{2,3},{3,2},{4,5},{5,4},{6,7},{7,6},{8,9},{9,8},{10,11... | collective-permute-start | bytes 3145736 | tf_op jit(solution)/shard_map/ppermute | solution.py:737
  105.1 30.3 %collective-permute-start.13 = (bf16[1024,512]{1,0:T(8,128)(2,1)}, bf16[1024,512]{1,0:T(8,128)(2,1)}, u32[]{:S(2)}, u32[]{:S(2)}) collective-permute-start(bf16[1024,512]{1,0:T(8,128)(2,1)} %stack_rows.1), channel_id=1, source_target_pairs={{0,2},{1,3},{2,0},{3,1},{4,6},{5,7},{6,4},{7,5},{8,10},{9,11},{10,... | collective-permute-start | bytes 3145736 | tf_op jit(solution)/shard_map/ppermute | solution.py:737
  109.4 25.0 %collective-permute-start.14 = (bf16[128,1024]{1,0:T(8,128)(2,1)S(1)}, bf16[128,1024]{1,0:T(8,128)(2,1)S(1)}, u32[]{:S(2)}, u32[]{:S(2)}) collective-permute-start(bf16[128,1024]{1,0:T(8,128)(2,1)S(1)} %slice.378), channel_id=1, source_target_pairs={{0,1},{1,0},{2,3},{3,2},{4,5},{5,4},{6,7},{7,6},{8,9},{9,8},{10,11... | collective-permute-start | bytes 786440 | tf_op jit(solution)/shard_map/ppermute | solution.py:737
  110.9 24.6 %collective-permute-start.15 = (bf16[128,1024]{1,0:T(8,128)(2,1)S(1)}, bf16[128,1024]{1,0:T(8,128)(2,1)S(1)}, u32[]{:S(2)}, u32[]{:S(2)}) collective-permute-start(bf16[128,1024]{1,0:T(8,128)(2,1)S(1)} %slice.379), channel_id=1, source_target_pairs={{0,2},{1,3},{2,0},{3,1},{4,6},{5,7},{6,4},{7,5},{8,10},{9,11},{10,... | collective-permute-start | bytes 786440 | tf_op jit(solution)/shard_map/ppermute | solution.py:737
  139.7 13.3 %collective-permute-start.16 = (bf16[512,512]{1,0:T(8,128)(2,1)S(1)}, bf16[512,512]{1,0:T(8,128)(2,1)S(1)}, u32[]{:S(2)}, u32[]{:S(2)}) collective-permute-start(bf16[512,512]{1,0:T(8,128)(2,1)S(1)} %slice.380), channel_id=1, source_target_pairs={{0,1},{1,0},{2,3},{3,2},{4,5},{5,4},{6,7},{7,6},{8,9},{9,8},{10,11... | collective-permute-start | bytes 1572872 | tf_op jit(solution)/shard_map/ppermute | solution.py:737
  156.0 32.9 %collective-permute-start.21 = (bf16[256,2048]{1,0:T(8,128)(2,1)S(1)}, bf16[256,2048]{1,0:T(8,128)(2,1)S(1)}, u32[]{:S(2)}, u32[]{:S(2)}) collective-permute-start(bf16[256,2048]{1,0:T(8,128)(2,1)S(1)} %bitcast_convert_fusion.refs_1_.refs_4_), channel_id=1, source_target_pairs={{0,1},{1,0},{2,3},{3,2},{4,5},{5,4},{6,7},{7,6},{8,9},{9,8},{10,11... | collective-permute-start | bytes 3145736 | tf_op jit(solution)/shard_map/ppermute | solution.py:737
  157.2 47.7 %collective-permute-start.22 = (bf16[256,2048]{1,0:T(8,128)(2,1)S(1)}, bf16[256,2048]{1,0:T(8,128)(2,1)}, u32[]{:S(2)}, u32[]{:S(2)}) collective-permute-start(bf16[256,2048]{1,0:T(8,128)(2,1)S(1)} %bitcast_convert_fusion.refs_1_.refs_4_), channel_id=1, source_target_pairs={{0,2},{1,3},{2,0},{3,1},{4,6},{5,7},{6,4},{7,5},{8,10},{9,11},{10,... | collective-permute-start | bytes 3145736 | tf_op jit(solution)/shard_map/ppermute | solution.py:737
  158.0 47.2 %collective-permute-start.23 = (bf16[256,2048]{1,0:T(8,128)(2,1)S(1)}, bf16[256,2048]{1,0:T(8,128)(2,1)S(1)}, u32[]{:S(2)}, u32[]{:S(2)}) collective-permute-start(bf16[256,2048]{1,0:T(8,128)(2,1)S(1)} %bitcast_convert_fusion.refs_1_.refs_4_), channel_id=1, source_target_pairs={{0,3},{1,2},{2,1},{3,0},{4,7},{5,6},{6,5},{7,4},{8,11},{9,10},{10,... | collective-permute-start | bytes 3145736 | tf_op jit(solution)/shard_map/ppermute | solution.py:737
  183.9 31.4 %collective-permute-start.19 = (bf16[128,2048]{1,0:T(8,128)(2,1)S(1)}, bf16[128,2048]{1,0:T(8,128)(2,1)S(1)}, u32[]{:S(2)}, u32[]{:S(2)}) collective-permute-start(bf16[128,2048]{1,0:T(8,128)(2,1)S(1)} %get-tuple-element.465), channel_id=1, source_target_pairs={{0,1},{1,0},{2,3},{3,2},{4,5},{5,4},{6,7},{7,6},{8,9},{9,8},{10,11... | collective-permute-start | bytes 1572872 | tf_op jit(solution)/shard_map/ppermute | solution.py:737
  185.4 30.8 %collective-permute-start.20 = (bf16[128,2048]{1,0:T(8,128)(2,1)S(1)}, bf16[128,2048]{1,0:T(8,128)(2,1)S(1)}, u32[]{:S(2)}, u32[]{:S(2)}) collective-permute-start(bf16[128,2048]{1,0:T(8,128)(2,1)S(1)} %get-tuple-element.464), channel_id=1, source_target_pairs={{0,2},{1,3},{2,0},{3,1},{4,6},{5,7},{6,4},{7,5},{8,10},{9,11},{10,... | collective-permute-start | bytes 1572872 | tf_op jit(solution)/shard_map/ppermute | solution.py:737
  216.4 25.2 %collective-permute-start.25 = (bf16[256,2048]{1,0:T(8,128)(2,1)S(1)}, bf16[256,2048]{1,0:T(8,128)(2,1)S(1)}, u32[]{:S(2)}, u32[]{:S(2)}) collective-permute-start(bf16[256,2048]{1,0:T(8,128)(2,1)S(1)} %pad_maximum_fusion.4), channel_id=1, source_target_pairs={{0,2},{1,3},{2,0},{3,1},{4,6},{5,7},{6,4},{7,5},{8,10},{9,11},{10,... | collective-permute-start | bytes 3145736 | tf_op jit(solution)/shard_map/ppermute | solution.py:737
  217.5 25.1 %collective-permute-start.24 = (bf16[256,2048]{1,0:T(8,128)(2,1)S(1)}, bf16[256,2048]{1,0:T(8,128)(2,1)S(1)}, u32[]{:S(2)}, u32[]{:S(2)}) collective-permute-start(bf16[256,2048]{1,0:T(8,128)(2,1)S(1)} %pad_maximum_fusion.3), channel_id=1, source_target_pairs={{0,1},{1,0},{2,3},{3,2},{4,5},{5,4},{6,7},{7,6},{8,9},{9,8},{10,11... | collective-permute-start | bytes 3145736 | tf_op jit(solution)/shard_map/ppermute | solution.py:737
  247.6 24.6 %collective-permute-start.26 = (bf16[256,2048]{1,0:T(8,128)(2,1)}, bf16[256,2048]{1,0:T(8,128)(2,1)}, u32[]{:S(2)}, u32[]{:S(2)}) collective-permute-start(bf16[256,2048]{1,0:T(8,128)(2,1)} %multiply_convert_fusion.refs_0_), channel_id=1, source_target_pairs={{0,1},{1,0},{2,3},{3,2},{4,5},{5,4},{6,7},{7,6},{8,9},{9,8},{10,11... | collective-permute-start | bytes 3145736 | tf_op jit(solution)/shard_map/ppermute | solution.py:737
  248.6 23.9 %collective-permute-start.27 = (bf16[256,2048]{1,0:T(8,128)(2,1)}, bf16[256,2048]{1,0:T(8,128)(2,1)}, u32[]{:S(2)}, u32[]{:S(2)}) collective-permute-start(bf16[256,2048]{1,0:T(8,128)(2,1)} %multiply_convert_fusion.refs_0_), channel_id=1, source_target_pairs={{0,2},{1,3},{2,0},{3,1},{4,6},{5,7},{6,4},{7,5},{8,10},{9,11},{10,... | collective-permute-start | bytes 3145736 | tf_op jit(solution)/shard_map/ppermute | solution.py:737
  274.4 32.5 %collective-permute-start.28 = (bf16[128,2048]{1,0:T(8,128)(2,1)}, bf16[128,2048]{1,0:T(8,128)(2,1)}, u32[]{:S(2)}, u32[]{:S(2)}) collective-permute-start(bf16[128,2048]{1,0:T(8,128)(2,1)} %slice.393), channel_id=1, source_target_pairs={{0,1},{1,0},{2,3},{3,2},{4,5},{5,4},{6,7},{7,6},{8,9},{9,8},{10,11... | collective-permute-start | bytes 1572872 | tf_op jit(solution)/shard_map/ppermute | solution.py:737
  277.7 29.2 %collective-permute-start.29 = (bf16[128,2048]{1,0:T(8,128)(2,1)}, bf16[128,2048]{1,0:T(8,128)(2,1)}, u32[]{:S(2)}, u32[]{:S(2)}) collective-permute-start(bf16[128,2048]{1,0:T(8,128)(2,1)} %slice.394), channel_id=1, source_target_pairs={{0,2},{1,3},{2,0},{3,1},{4,6},{5,7},{6,4},{7,5},{8,10},{9,11},{10,... | collective-permute-start | bytes 1572872 | tf_op jit(solution)/shard_map/ppermute | solution.py:737
  333.6 185.6 %reduce-scatter.6.cloned.1.call-start = ((), (), s32[]{:S(2)}) async-start(), calls=%async_computation.8 | async-start | bytes 12976128 | tf_op jit(solution)/shard_map/reduce_scatter | solution.py:927
  333.7 22.6 %collective-permute-start.30 = (bf16[256,2048]{1,0:T(8,128)(2,1)}, bf16[256,2048]{1,0:T(8,128)(2,1)}, u32[]{:S(2)}, u32[]{:S(2)}) collective-permute-start(bf16[256,2048]{1,0:T(8,128)(2,1)} %get-tuple-element.275), channel_id=1, source_target_pairs={{0,1},{1,0},{2,3},{3,2},{4,5},{5,4},{6,7},{7,6},{8,9},{9,8},{10,11... | collective-permute-start | bytes 3145736 | tf_op jit(solution)/shard_map/ppermute | solution.py:737
  334.8 22.4 %collective-permute-start.31 = (bf16[256,2048]{1,0:T(8,128)(2,1)}, bf16[256,2048]{1,0:T(8,128)(2,1)}, u32[]{:S(2)}, u32[]{:S(2)}) collective-permute-start(bf16[256,2048]{1,0:T(8,128)(2,1)} %get-tuple-element.276), channel_id=1, source_target_pairs={{0,2},{1,3},{2,0},{3,1},{4,6},{5,7},{6,4},{7,5},{8,10},{9,11},{10,... | collective-permute-start | bytes 3145736 | tf_op jit(solution)/shard_map/ppermute | solution.py:737
  357.2 22.5 %collective-permute-start.32 = (bf16[256,2048]{1,0:T(8,128)(2,1)}, bf16[256,2048]{1,0:T(8,128)(2,1)}, u32[]{:S(2)}, u32[]{:S(2)}) collective-permute-start(bf16[256,2048]{1,0:T(8,128)(2,1)} %get-tuple-element.279), channel_id=1, source_target_pairs={{0,3},{1,2},{2,1},{3,0},{4,7},{5,6},{6,5},{7,4},{8,11},{9,10},{10,... | collective-permute-start | bytes 3145736 | tf_op jit(solution)/shard_map/ppermute | solution.py:737
  379.7 308.0 %all-gather.10.cloned.1.call-start = ((), (), s32[]{:S(2)}) async-start(), calls=%async_computation.10 | async-start | bytes 6488064 | tf_op jit(solution)/shard_map/all_gather | solution.py:954
  385.6 27.0 %collective-permute-start.33 = (bf16[256,2048]{1,0:T(8,128)(2,1)S(1)}, bf16[256,2048]{1,0:T(8,128)(2,1)S(1)}, u32[]{:S(2)}, u32[]{:S(2)}) collective-permute-start(bf16[256,2048]{1,0:T(8,128)(2,1)S(1)} %get-tuple-element.419.refs_4_), channel_id=1, source_target_pairs={{0,1},{1,0},{2,3},{3,2},{4,5},{5,4},{6,7},{7,6},{8,9},{9,8},{10,11... | collective-permute-start | bytes 3145736 | tf_op jit(solution)/shard_map/ppermute | solution.py:737
  394.2 20.4 %collective-permute-start.34 = (bf16[256,2048]{1,0:T(8,128)(2,1)S(1)}, bf16[256,2048]{1,0:T(8,128)(2,1)S(1)}, u32[]{:S(2)}, u32[]{:S(2)}) collective-permute-start(bf16[256,2048]{1,0:T(8,128)(2,1)S(1)} %get-tuple-element.419.refs_4_), channel_id=1, source_target_pairs={{0,2},{1,3},{2,0},{3,1},{4,6},{5,7},{6,4},{7,5},{8,10},{9,11},{10,... | collective-permute-start | bytes 3145736 | tf_op jit(solution)/shard_map/ppermute | solution.py:737
  451.1 252.0 %all-gather.8.cloned.1.call-start = ((), (), s32[]{:S(2)}) async-start(), calls=%async_computation.9 | async-start | bytes 7208960 | tf_op jit(solution)/shard_map/all_gather | solution.py:979
  453.5 15.0 %collective-permute-start.40 = (bf16[4,4,2,64,512]{4,3,2,1,0:T(8,128)(2,1)S(1)}, bf16[4,4,2,64,512]{4,3,2,1,0:T(8,128)(2,1)S(1)}, u32[]{:S(2)}, u32[]{:S(2)}) collective-permute-start(bf16[4,4,2,64,512]{4,3,2,1,0:T(8,128)(2,1)S(1)} %copy-done.101), channel_id=1, source_target_pairs={{0,4},{4,0},{8,12},{12,8},{16,20},{20,16},{24,28},{28,24},{1,5},{5... | collective-permute-start | bytes 6291464 | tf_op jit(solution)/shard_map/core_swap/ppermute | solution.py:741
  473.1 18.9 %collective-permute-start.43 = (bf16[256,512]{1,0:T(8,128)(2,1)}, bf16[256,512]{1,0:T(8,128)(2,1)}, u32[]{:S(2)}, u32[]{:S(2)}) collective-permute-start(bf16[256,512]{1,0:T(8,128)(2,1)} %bitcast.42), channel_id=1, source_target_pairs={{0,1},{1,0},{2,3},{3,2},{4,5},{5,4},{6,7},{7,6},{8,9},{9,8},{10,11... | collective-permute-start | bytes 786440 | tf_op jit(solution)/shard_map/ppermute | solution.py:737
  474.9 20.4 %collective-permute-start.44 = (bf16[256,512]{1,0:T(8,128)(2,1)}, bf16[256,512]{1,0:T(8,128)(2,1)}, u32[]{:S(2)}, u32[]{:S(2)}) collective-permute-start(bf16[256,512]{1,0:T(8,128)(2,1)} %bitcast.43), channel_id=1, source_target_pairs={{0,2},{1,3},{2,0},{3,1},{4,6},{5,7},{6,4},{7,5},{8,10},{9,11},{10,... | collective-permute-start | bytes 786440 | tf_op jit(solution)/shard_map/ppermute | solution.py:737
  476.8 25.9 %collective-permute-start.42 = (bf16[512,512]{1,0:T(8,128)(2,1)}, bf16[512,512]{1,0:T(8,128)(2,1)}, u32[]{:S(2)}, u32[]{:S(2)}) collective-permute-start(bf16[512,512]{1,0:T(8,128)(2,1)} %pad_maximum_fusion.13), channel_id=1, source_target_pairs={{0,2},{1,3},{2,0},{3,1},{4,6},{5,7},{6,4},{7,5},{8,10},{9,11},{10,... | collective-permute-start | bytes 1572872 | tf_op jit(solution)/shard_map/ppermute | solution.py:737
  478.8 23.9 %collective-permute-start.41 = (bf16[512,512]{1,0:T(8,128)(2,1)}, bf16[512,512]{1,0:T(8,128)(2,1)}, u32[]{:S(2)}, u32[]{:S(2)}) collective-permute-start(bf16[512,512]{1,0:T(8,128)(2,1)} %pad_maximum_fusion.12), channel_id=1, source_target_pairs={{0,1},{1,0},{2,3},{3,2},{4,5},{5,4},{6,7},{7,6},{8,9},{9,8},{10,11... | collective-permute-start | bytes 1572872 | tf_op jit(solution)/shard_map/ppermute | solution.py:737
  479.9 19.7 %collective-permute-start.45 = (bf16[128,1024]{1,0:T(8,128)(2,1)}, bf16[128,1024]{1,0:T(8,128)(2,1)}, u32[]{:S(2)}, u32[]{:S(2)}) collective-permute-start(bf16[128,1024]{1,0:T(8,128)(2,1)} %get-tuple-element.477), channel_id=1, source_target_pairs={{0,1},{1,0},{2,3},{3,2},{4,5},{5,4},{6,7},{7,6},{8,9},{9,8},{10,11... | collective-permute-start | bytes 786440 | tf_op jit(solution)/shard_map/ppermute | solution.py:737
  495.3 35.2 %collective-permute-start.55 = (bf16[256,2048]{1,0:T(8,128)(2,1)}, bf16[256,2048]{1,0:T(8,128)(2,1)}, u32[]{:S(2)}, u32[]{:S(2)}) collective-permute-start(bf16[256,2048]{1,0:T(8,128)(2,1)} %get-tuple-element.345), channel_id=1, source_target_pairs={{0,1},{1,0},{2,3},{3,2},{4,5},{5,4},{6,7},{7,6},{8,9},{9,8},{10,11... | collective-permute-start | bytes 3145736 | tf_op jit(solution)/shard_map/ppermute | solution.py:737
  499.6 47.7 %collective-permute-start.56 = (bf16[256,2048]{1,0:T(8,128)(2,1)}, bf16[256,2048]{1,0:T(8,128)(2,1)}, u32[]{:S(2)}, u32[]{:S(2)}) collective-permute-start(bf16[256,2048]{1,0:T(8,128)(2,1)} %get-tuple-element.346), channel_id=1, source_target_pairs={{0,2},{1,3},{2,0},{3,1},{4,6},{5,7},{6,4},{7,5},{8,10},{9,11},{10,... | collective-permute-start | bytes 3145736 | tf_op jit(solution)/shard_map/ppermute | solution.py:737
  500.9 49.4 %collective-permute-start.57 = (bf16[256,2048]{1,0:T(8,128)(2,1)}, bf16[256,2048]{1,0:T(8,128)(2,1)}, u32[]{:S(2)}, u32[]{:S(2)}) collective-permute-start(bf16[256,2048]{1,0:T(8,128)(2,1)} %get-tuple-element.347), channel_id=1, source_target_pairs={{0,3},{1,2},{2,1},{3,0},{4,7},{5,6},{6,5},{7,4},{8,11},{9,10},{10,... | collective-permute-start | bytes 3145736 | tf_op jit(solution)/shard_map/ppermute | solution.py:737
  525.2 25.3 %collective-permute-start.47 = (bf16[128,512]{1,0:T(8,128)(2,1)S(1)}, bf16[128,512]{1,0:T(8,128)(2,1)S(1)}, u32[]{:S(2)}, u32[]{:S(2)}) collective-permute-start(bf16[128,512]{1,0:T(8,128)(2,1)S(1)} %get-tuple-element.475), channel_id=1, source_target_pairs={{8,0},{12,4},{16,8},{20,12},{24,16},{28,20},{9,1},{13,5},{17,9},{2... | collective-permute-start | bytes 393224 | tf_op jit(solution)/shard_map/ppermute | solution.py:986
  526.6 48.1 %collective-permute-start.54 = (bf16[1024,512]{1,0:T(8,128)(2,1)}, bf16[1024,512]{1,0:T(8,128)(2,1)}, u32[]{:S(2)}, u32[]{:S(2)}) collective-permute-start(bf16[1024,512]{1,0:T(8,128)(2,1)} %get-tuple-element.343), channel_id=1, source_target_pairs={{0,4},{4,0},{8,12},{12,8},{16,20},{20,16},{24,28},{28,24},{1,5},{5... | collective-permute-start | bytes 3145736 | tf_op jit(solution)/shard_map/core_swap/ppermute | solution.py:741
  530.5 21.8 %collective-permute-start.48 = (bf16[128,512]{1,0:T(8,128)(2,1)S(1)}, bf16[128,512]{1,0:T(8,128)(2,1)S(1)}, u32[]{:S(2)}, u32[]{:S(2)}) collective-permute-start(bf16[128,512]{1,0:T(8,128)(2,1)S(1)} %get-tuple-element.474), channel_id=1, source_target_pairs={{16,0},{20,4},{24,8},{28,12},{17,1},{21,5},{25,9},{29,13},{18,2},{... | collective-permute-start | bytes 393224 | tf_op jit(solution)/shard_map/ppermute | solution.py:986
  547.3 16.5 %collective-permute-start.49 = (bf16[128,512]{1,0:T(8,128)(2,1)S(1)}, bf16[128,512]{1,0:T(8,128)(2,1)S(1)}, u32[]{:S(2)}, u32[]{:S(2)}) collective-permute-start(bf16[128,512]{1,0:T(8,128)(2,1)S(1)} %get-tuple-element.473), channel_id=1, source_target_pairs={{24,0},{28,4},{25,1},{29,5},{26,2},{30,6},{27,3},{31,7}} | collective-permute-start | bytes 393224 | tf_op jit(solution)/shard_map/ppermute | solution.py:986
  550.3 19.5 %collective-permute-start.53 = (bf16[256,1024]{1,0:T(8,128)(2,1)}, bf16[256,1024]{1,0:T(8,128)(2,1)}, u32[]{:S(2)}, u32[]{:S(2)}) collective-permute-start(bf16[256,1024]{1,0:T(8,128)(2,1)} %pad_maximum_fusion.17), channel_id=1, source_target_pairs={{0,2},{1,3},{2,0},{3,1},{4,6},{5,7},{6,4},{7,5},{8,10},{9,11},{10,... | collective-permute-start | bytes 1572872 | tf_op jit(solution)/shard_map/ppermute | solution.py:737
  550.5 19.2 %collective-permute-start.52 = (bf16[256,1024]{1,0:T(8,128)(2,1)}, bf16[256,1024]{1,0:T(8,128)(2,1)}, u32[]{:S(2)}, u32[]{:S(2)}) collective-permute-start(bf16[256,1024]{1,0:T(8,128)(2,1)} %pad_maximum_fusion.16), channel_id=1, source_target_pairs={{0,1},{1,0},{2,3},{3,2},{4,5},{5,4},{6,7},{7,6},{8,9},{9,8},{10,11... | collective-permute-start | bytes 1572872 | tf_op jit(solution)/shard_map/ppermute | solution.py:737
  552.3 22.4 %collective-permute-start.51 = (bf16[512,512]{1,0:T(8,128)(2,1)}, bf16[512,512]{1,0:T(8,128)(2,1)}, u32[]{:S(2)}, u32[]{:S(2)}) collective-permute-start(bf16[512,512]{1,0:T(8,128)(2,1)} %pad_maximum_fusion.15), channel_id=1, source_target_pairs={{0,2},{1,3},{2,0},{3,1},{4,6},{5,7},{6,4},{7,5},{8,10},{9,11},{10,... | collective-permute-start | bytes 1572872 | tf_op jit(solution)/shard_map/ppermute | solution.py:737
  578.8 44.3 %collective-permute-start.61 = (bf16[256,1024]{1,0:T(8,128)(2,1)}, bf16[256,1024]{1,0:T(8,128)(2,1)}, u32[]{:S(2)}, u32[]{:S(2)}) collective-permute-start(bf16[256,1024]{1,0:T(8,128)(2,1)} %subtract_convert_fusion.refs_4_), channel_id=1, source_target_pairs={{0,1},{1,0},{2,3},{3,2},{4,5},{5,4},{6,7},{7,6},{8,9},{9,8},{10,11... | collective-permute-start | bytes 1572872 | tf_op jit(solution)/shard_map/ppermute | solution.py:737
  580.6 42.6 %collective-permute-start.62 = (bf16[256,1024]{1,0:T(8,128)(2,1)}, bf16[256,1024]{1,0:T(8,128)(2,1)}, u32[]{:S(2)}, u32[]{:S(2)}) collective-permute-start(bf16[256,1024]{1,0:T(8,128)(2,1)} %subtract_convert_fusion.refs_4_), channel_id=1, source_target_pairs={{0,2},{1,3},{2,0},{3,1},{4,6},{5,7},{6,4},{7,5},{8,10},{9,11},{10,... | collective-permute-start | bytes 1572872 | tf_op jit(solution)/shard_map/ppermute | solution.py:737
  583.3 20.4 %all-to-all-start.2 = ((bf16[256,4,512]{2,0,1:T(8,128)(2,1)}), bf16[256,4,512]{2,0,1:T(8,128)(2,1)}, u32[]{:S(2)}, u32[]{:S(2)}) async-start(bf16[256,4,512]{2,0,1:T(8,128)(2,1)} %bitcast.208), calls=%async_computation.4 | async-start | bytes 2097152 | tf_op jit(solution)/shard_map/all_to_all | solution.py:1006
  591.3 19.0 %collective-permute-start.58 = (bf16[128,512]{1,0:T(8,128)(2,1)}, bf16[128,512]{1,0:T(8,128)(2,1)}, u32[]{:S(2)}, u32[]{:S(2)}) collective-permute-start(bf16[128,512]{1,0:T(8,128)(2,1)} %get-tuple-element.472), channel_id=1, source_target_pairs={{8,0},{12,4},{16,8},{20,12},{24,16},{28,20},{9,1},{13,5},{17,9},{2... | collective-permute-start | bytes 393224 | tf_op jit(solution)/shard_map/ppermute | solution.py:986
  592.5 30.6 %collective-permute-start.59 = (bf16[128,512]{1,0:T(8,128)(2,1)}, bf16[128,512]{1,0:T(8,128)(2,1)}, u32[]{:S(2)}, u32[]{:S(2)}) collective-permute-start(bf16[128,512]{1,0:T(8,128)(2,1)} %get-tuple-element.471), channel_id=1, source_target_pairs={{16,0},{20,4},{24,8},{28,12},{17,1},{21,5},{25,9},{29,13},{18,2},{... | collective-permute-start | bytes 393224 | tf_op jit(solution)/shard_map/ppermute | solution.py:986
  593.8 29.3 %collective-permute-start.60 = (bf16[128,512]{1,0:T(8,128)(2,1)}, bf16[128,512]{1,0:T(8,128)(2,1)}, u32[]{:S(2)}, u32[]{:S(2)}) collective-permute-start(bf16[128,512]{1,0:T(8,128)(2,1)} %get-tuple-element.470), channel_id=1, source_target_pairs={{24,0},{28,4},{25,1},{29,5},{26,2},{30,6},{27,3},{31,7}} | collective-permute-start | bytes 393224 | tf_op jit(solution)/shard_map/ppermute | solution.py:986
  603.7 54.0 %all-to-all-start.3 = ((bf16[4,256,512]{2,1,0:T(8,128)(2,1)}), bf16[4,256,512]{2,1,0:T(8,128)(2,1)}, u32[]{:S(2)}, u32[]{:S(2)}) async-start(bf16[4,256,512]{2,1,0:T(8,128)(2,1)} %bitcast.207), calls=%async_computation.5 | async-start | bytes 2097152 | tf_op jit(solution)/shard_map/all_to_all | solution.py:1013
  608.0 183.5 %reduce-scatter.8.cloned.1.call-start = ((), (), s32[]{:S(2)}) async-start(), calls=%async_computation.11 | async-start | bytes 9142272 | tf_op jit(solution)/shard_map/reduce_scatter | solution.py:1075
  687.7 183.6 %all-gather.12.cloned.1.call-start = ((), (), s32[]{:S(2)}) async-start(), calls=%async_computation.12 | async-start | bytes 9142272 | tf_op jit(solution)/shard_map/all_gather | solution.py:1084
  707.2 34.4 %collective-permute-start.63 = (bf16[256,2816]{1,0:T(8,128)(2,1)S(1)}, bf16[256,2816]{1,0:T(8,128)(2,1)S(1)}, u32[]{:S(2)}, u32[]{:S(2)}) collective-permute-start(bf16[256,2816]{1,0:T(8,128)(2,1)S(1)} %get-tuple-element.428), channel_id=1, source_target_pairs={{0,1},{1,0},{2,3},{3,2},{4,5},{5,4},{6,7},{7,6},{8,9},{9,8},{10,11... | collective-permute-start | bytes 4325384 | tf_op jit(solution)/shard_map/ppermute | solution.py:737
  708.9 64.2 %collective-permute-start.64 = (bf16[256,2816]{1,0:T(8,128)(2,1)S(1)}, bf16[256,2816]{1,0:T(8,128)(2,1)S(1)}, u32[]{:S(2)}, u32[]{:S(2)}) collective-permute-start(bf16[256,2816]{1,0:T(8,128)(2,1)S(1)} %get-tuple-element.427), channel_id=1, source_target_pairs={{0,2},{1,3},{2,0},{3,1},{4,6},{5,7},{6,4},{7,5},{8,10},{9,11},{10,... | collective-permute-start | bytes 4325384 | tf_op jit(solution)/shard_map/ppermute | solution.py:737
  710.3 63.8 %collective-permute-start.65 = (bf16[256,2816]{1,0:T(8,128)(2,1)S(1)}, bf16[256,2816]{1,0:T(8,128)(2,1)}, u32[]{:S(2)}, u32[]{:S(2)}) collective-permute-start(bf16[256,2816]{1,0:T(8,128)(2,1)S(1)} %get-tuple-element.426), channel_id=1, source_target_pairs={{0,3},{1,2},{2,1},{3,0},{4,7},{5,6},{6,5},{7,4},{8,11},{9,10},{10,... | collective-permute-start | bytes 4325384 | tf_op jit(solution)/shard_map/ppermute | solution.py:737
  791.5 16.6 %collective-permute-start.72 = (bf16[256,2816]{1,0:T(8,128)(2,1)}, bf16[256,2816]{1,0:T(8,128)(2,1)}, u32[]{:S(2)}, u32[]{:S(2)}) collective-permute-start(bf16[256,2816]{1,0:T(8,128)(2,1)} %get-tuple-element.394.refs_0_), channel_id=1, source_target_pairs={{0,4},{4,0},{8,12},{12,8},{16,20},{20,16},{24,28},{28,24},{1,5},{5... | collective-permute-start | bytes 4325384 | tf_op jit(solution)/shard_map/core_swap/ppermute | solution.py:741
  791.6 16.5 %collective-permute-start.73 = (bf16[256,2816]{1,0:T(8,128)(2,1)}, bf16[256,2816]{1,0:T(8,128)(2,1)}, u32[]{:S(2)}, u32[]{:S(2)}) collective-permute-start(bf16[256,2816]{1,0:T(8,128)(2,1)} %copy-done.40), channel_id=1, source_target_pairs={{0,4},{4,0},{8,12},{12,8},{16,20},{20,16},{24,28},{28,24},{1,5},{5... | collective-permute-start | bytes 4325384 | tf_op jit(solution)/shard_map/core_swap/ppermute | solution.py:741
  792.1 16.0 %collective-permute-start.74 = (bf16[256,2816]{1,0:T(8,128)(2,1)}, bf16[256,2816]{1,0:T(8,128)(2,1)}, u32[]{:S(2)}, u32[]{:S(2)}) collective-permute-start(bf16[256,2816]{1,0:T(8,128)(2,1)} %copy-done.41), channel_id=1, source_target_pairs={{0,4},{4,0},{8,12},{12,8},{16,20},{20,16},{24,28},{28,24},{1,5},{5... | collective-permute-start | bytes 4325384 | tf_op jit(solution)/shard_map/core_swap/ppermute | solution.py:741
  792.2 15.9 %collective-permute-start.75 = (bf16[256,2816]{1,0:T(8,128)(2,1)}, bf16[256,2816]{1,0:T(8,128)(2,1)}, u32[]{:S(2)}, u32[]{:S(2)}) collective-permute-start(bf16[256,2816]{1,0:T(8,128)(2,1)} %collective-permute-done.65.refs_3_), channel_id=1, source_target_pairs={{0,4},{4,0},{8,12},{12,8},{16,20},{20,16},{24,28},{28,24},{1,5},{5... | collective-permute-start | bytes 4325384 | tf_op jit(solution)/shard_map/core_swap/ppermute | solution.py:741
  (127 other events, 1082.7 us)
Sparse Core Ops, SparseCore 0:
  22.1 29.0 all-gather.13
  101.3 108.3 all-gather.15
  333.7 65.0 reduce-scatter.3
  401.5 117.6 reduce-scatter.5
  520.7 67.5 all-gather.9
  589.7 113.2 all-gather.7
  705.9 85.4 reduce-scatter.7
  793.1 78.2 all-gather.11

commit v5 on v4

--- a/solution.py
+++ b/solution.py
@@ -91,7 +91,8 @@
     rows = heads * block
     factor = HD ** (-0.5)
 
-    def kernel(info_ref, q_ref, near_ref, far_ref, cos_ref, sin_ref, out_ref, scaled_ref, lse_ref, q_s, m_s, l_s, acc_s):
+    def kernel(info_ref, q_ref, near_ref, far_ref, cos_ref, sin_ref, *refs):
+        out_refs, (scaled_ref, lse_ref, q_s, m_s, l_s, acc_s) = refs[:groups], refs[groups:]
         seq, step = pl.program_id(0), pl.program_id(1)
         place, index, limit = info_ref[0], info_ref[1], info_ref[3 + seq]
 
@@ -136,7 +137,8 @@
             for h in range(heads):
                 part = slice(h * block, (h + 1) * block)
                 out = (acc_s[:, part] * inverse[:, part]).T.astype(BF16)
-                out_ref[:, 0, :, h * HD : (h + 1) * HD] = out.reshape(groups, span, HD)
+                for j, out_ref in enumerate(out_refs):
+                    out_ref[0, :, h * HD : (h + 1) * HD] = out[j * span : (j + 1) * span]
             lse_ref[0] = m_s[...] + jnp.log(l_s[...])
 
     tokens = pl.BlockSpec((groups, 1, span, columns), lambda s, t, i: (0, s, 0, 0))
@@ -149,7 +151,8 @@
             num_scalar_prefetch=1,
             grid=(seqs, steps),
             in_specs=[tokens, keys, keys, table, table],
-            out_specs=[tokens, tokens, pl.BlockSpec((1, 1, rows), lambda s, t, i: (s, 0, 0))],
+            out_specs=[pl.BlockSpec((1, span, columns), lambda s, t, i: (s, 0, 0))] * groups
+            + [tokens, pl.BlockSpec((1, 1, rows), lambda s, t, i: (s, 0, 0))],
             scratch_shapes=[
                 pltpu.VMEM((rows, HD), BF16),
                 pltpu.VMEM((1, rows), F32),
@@ -157,11 +160,8 @@
                 pltpu.VMEM((HD, rows), F32),
             ],
         ),
-        out_shape=[
-            jax.ShapeDtypeStruct(queries.shape, BF16),
-            jax.ShapeDtypeStruct(queries.shape, BF16),
-            jax.ShapeDtypeStruct((seqs, 1, rows), F32),
-        ],
+        out_shape=[jax.ShapeDtypeStruct((seqs, span, columns), BF16)] * groups
+        + [jax.ShapeDtypeStruct(queries.shape, BF16), jax.ShapeDtypeStruct((seqs, 1, rows), F32)],
         compiler_params=pltpu.CompilerParams(dimension_semantics=("arbitrary", "arbitrary")),
         cost_estimate=cheap(),
         name="attend_forward",
@@ -177,7 +177,11 @@
     rows = heads * block
     factor = HD ** (-0.5)
 
-    def kernel(info_ref, q_ref, o_ref, do_ref, lse_ref, near_ref, far_ref, cos_ref, sin_ref, dq_ref, dnear_ref, dfar_ref, q_s, do_s, delta_s, acc_s):
+    def kernel(info_ref, *refs):
+        o_refs, refs = refs[:groups], refs[groups:]
+        body(info_ref, o_refs, *refs)
+
+    def body(info_ref, o_refs, q_ref, do_ref, lse_ref, near_ref, far_ref, cos_ref, sin_ref, dq_ref, dnear_ref, dfar_ref, q_s, do_s, delta_s, acc_s):
         seq, step = pl.program_id(0) + first, pl.program_id(1)
         place, index, limit = info_ref[0], info_ref[1], info_ref[3 + seq]
 
@@ -188,7 +192,7 @@
                 q_s[part, :] = q_ref[:, 0, :, lanes].reshape(block, HD)
                 grads = do_ref[:, 0, :, lanes].reshape(block, HD)
                 do_s[part, :] = grads
-                out = o_ref[:, 0, :, lanes].reshape(block, HD)
+                out = jnp.concatenate([o_ref[0, :, lanes] for o_ref in o_refs], axis=0)
                 both = jnp.sum(grads.astype(F32) * out.astype(F32), axis=1, keepdims=True)
                 delta_s[:, part] = jnp.broadcast_to(both, (block, 128)).T[:1]
             acc_s[...] = jnp.zeros((HD, rows), F32)
@@ -243,8 +247,8 @@
         grid_spec=pltpu.PrefetchScalarGridSpec(
             num_scalar_prefetch=1,
             grid=(count, steps),
-            in_specs=[
-                tokens,
+            in_specs=[pl.BlockSpec((1, span, columns), lambda s, t, i: (s + first, 0, 0))] * groups
+            + [
                 tokens,
                 tokens,
                 pl.BlockSpec((1, 1, rows), lambda s, t, i: (s + first, 0, 0)),
@@ -265,12 +269,13 @@
         compiler_params=pltpu.CompilerParams(dimension_semantics=("arbitrary", "arbitrary")),
         cost_estimate=cheap(),
         name="attend_backward",
-    )(info, scaled, attn_out, d_attn, lse, kv_near, kv_far, cosine, sine)
+    )(info, *attn_out, scaled, d_attn, lse, kv_near, kv_far, cosine, sine)
 
 
 def feed_forward(xs, signals, gu, down_w, last_kind):
-    count = len(xs)
-    tokens, width = xs[0].shape
+    count, pieces = len(signals), len(xs)
+    tokens, width = signals[0].shape
+    step_rows = xs[0].shape[0]
     hidden = down_w.shape[0]
     shares, blocks, share, columns = gu.shape
     lanes = 128
@@ -280,23 +285,21 @@
     tail = hidden - (steps - 1) * tile
 
     def kernel(*refs):
-        x_refs, s_refs, refs = refs[:count], refs[count : 2 * count], refs[2 * count :]
+        x_refs, s_refs, refs = refs[:pieces], refs[pieces : pieces + count], refs[pieces + count :]
         ga_ref, gb_ref, ua_ref, ub_ref, d_ref, refs = *refs[:5], refs[5:]
-        outs, scratch = [refs[n * count : (n + 1) * count] for n in range(5)], refs[5 * count :]
-        inner_refs, dg_refs, du_refs, y_refs, dx_refs = outs
+        outs, scratch = [refs[n * count : (n + 1) * count] for n in range(6)], refs[6 * count :]
+        inner_refs, dg_refs, du_refs, y_refs, dx_refs, joined_refs = outs
         g_s, u_s, y_s, dx_s = scratch[:4]
         step = pl.program_id(0)
-        if count > 1:
-            x_s, s_s = scratch[4:]
-
-            @pl.when(step == 0)
-            def _():
-                for n in range(count):
-                    x_s[n * tokens : (n + 1) * tokens] = x_refs[n][...]
-                    s_s[n * tokens : (n + 1) * tokens] = s_refs[n][...]
-
-        else:
-            x_s, s_s = x_refs[0], s_refs[0]
+        x_s, s_s = scratch[4:]
+
+        @pl.when(step == 0)
+        def _():
+            for n in range(pieces):
+                x_s[n * step_rows : (n + 1) * step_rows] = x_refs[n][...]
+            for n in range(count):
+                s_s[n * tokens : (n + 1) * tokens] = s_refs[n][...]
+                joined_refs[n][...] = x_s[n * tokens : (n + 1) * tokens]
 
         def spread(targets, value, size):
             for n, ref in enumerate(targets):
@@ -362,13 +365,15 @@
     whole = pl.BlockSpec((tokens, width), lambda n: (0, 0))
     rows = pl.BlockSpec((tile, width), lambda n: (n, 0))
     out = pl.BlockSpec((tokens, tile), lambda n: (0, n))
-    extra = [pltpu.VMEM((count * tokens, width), BF16)] * 2 if count > 1 else []
+    piece = pl.BlockSpec((step_rows, width), lambda n: (0, 0))
+    extra = [pltpu.VMEM((count * tokens, width), BF16)] * 2
     found = pl.pallas_call(
         kernel,
         grid=(steps,),
-        in_specs=[whole] * (2 * count)
+        in_specs=[piece] * pieces
+        + [whole] * count
         + [lane_block(0, 0), lane_block(0, 1), lane_block(up_at, 0), lane_block(up_at, 1), rows],
-        out_specs=[out] * (3 * count) + [whole] * (2 * count),
+        out_specs=[out] * (3 * count) + [whole] * (3 * count),
         scratch_shapes=[
             pltpu.VMEM((width, tile), BF16),
             pltpu.VMEM((width, tile), BF16),
@@ -377,16 +382,19 @@
             *extra,
         ],
         out_shape=[jax.ShapeDtypeStruct((tokens, hidden), BF16)] * (3 * count)
-        + [jax.ShapeDtypeStruct((tokens, width), last_kind)] * (2 * count),
+        + [jax.ShapeDtypeStruct((tokens, width), last_kind)] * (2 * count)
+        + [jax.ShapeDtypeStruct((tokens, width), BF16)] * count,
         compiler_params=pltpu.CompilerParams(dimension_semantics=("arbitrary",)),
         cost_estimate=cheap(),
         name="feed_forward",
     )(*xs, *signals, gu, gu, gu, gu, down_w)
-    return [[found[n * count + b] for n in range(5)] for b in range(count)]
-
-
-def hidden_units(x, gu, hidden):
-    tokens, width = x.shape
+    return [[found[n * count + b] for n in range(6)] for b in range(count)]
+
+
+def hidden_units(xs, gu, hidden):
+    pieces = len(xs)
+    step_rows, width = xs[0].shape
+    tokens = pieces * step_rows
     shares, blocks, share, columns = gu.shape
     lanes = 128
     up_at = columns // 2 // lanes
@@ -394,8 +402,16 @@
     steps = -(-hidden // tile)
     tail = hidden - (steps - 1) * tile
 
-    def kernel(x_ref, ga_ref, gb_ref, ua_ref, ub_ref, inner_ref, g_s, u_s):
+    def kernel(*refs):
+        x_refs, refs = refs[:pieces], refs[pieces:]
+        ga_ref, gb_ref, ua_ref, ub_ref, inner_ref, joined_ref, g_s, u_s, x_s = refs
         step = pl.program_id(0)
+
+        @pl.when(step == 0)
+        def _():
+            for n in range(pieces):
+                x_s[n * step_rows : (n + 1) * step_rows] = x_refs[n][...]
+            joined_ref[...] = x_s[...]
 
         def work(size):
             for s in range(shares):
@@ -406,7 +422,7 @@
                     if size > lanes:
                         g_s[at, lanes:] = gb_ref[s, b]
                         u_s[at, lanes:] = ub_ref[s, b]
-            rows = x_ref[...]
+            rows = x_s[...]
             gate, upper = dot(rows, g_s[:, :size]), dot(rows, u_s[:, :size])
             inner_ref[:, :size] = (gate * jax.nn.sigmoid(gate) * upper).astype(BF16)
 
@@ -427,20 +443,30 @@
     return pl.pallas_call(
         kernel,
         grid=(steps,),
-        in_specs=[
-            pl.BlockSpec((tokens, width), lambda n: (0, 0)),
+        in_specs=[pl.BlockSpec((step_rows, width), lambda n: (0, 0))] * pieces
+        + [
             lane_block(0, 0),
             lane_block(0, 1),
             lane_block(up_at, 0),
             lane_block(up_at, 1),
         ],
-        out_specs=pl.BlockSpec((tokens, tile), lambda n: (0, n)),
-        scratch_shapes=[pltpu.VMEM((width, tile), BF16), pltpu.VMEM((width, tile), BF16)],
-        out_shape=jax.ShapeDtypeStruct((tokens, hidden), BF16),
+        out_specs=[
+            pl.BlockSpec((tokens, tile), lambda n: (0, n)),
+            pl.BlockSpec((tokens, width), lambda n: (0, 0)),
+        ],
+        scratch_shapes=[
+            pltpu.VMEM((width, tile), BF16),
+            pltpu.VMEM((width, tile), BF16),
+            pltpu.VMEM((tokens, width), BF16),
+        ],
+        out_shape=[
+            jax.ShapeDtypeStruct((tokens, hidden), BF16),
+            jax.ShapeDtypeStruct((tokens, width), BF16),
+        ],
         compiler_params=pltpu.CompilerParams(dimension_semantics=("arbitrary",)),
         cost_estimate=cheap(),
         name="hidden_units",
-    )(x, gu, gu, gu, gu)
+    )(*xs, gu, gu, gu, gu)
 
 
 def token_grad(info, lefts, rights):
@@ -874,9 +900,9 @@
         signal_got = [swap(signal_low, j) for j in range(1, nf)]
         kv_near = kv_near.reshape(nf, nz, seqs, span, 2 * HD)
         kv_far = kv_far.reshape(nf, nz, seqs, span, 2 * HD)
-        attn_out, scaled, lse = attend_forward(info, queries, kv_near, kv_far, cos_g, sin_g)
-
-        attn_blocks = [attn_out[j].reshape(tokens, head_cols) for j in range(nf)]
+        *attn_out, scaled, lse = attend_forward(info, queries, kv_near, kv_far, cos_g, sin_g)
+
+        attn_blocks = [x.reshape(tokens, head_cols) for x in attn_out]
         o_parts = [None] * nf
         o_parts[nf - 1] = dot(attn_blocks[nf - 1], w_o).astype(BF16)
         if square:
@@ -893,29 +919,37 @@
         ffn_in = (hidden * scale_f * gain_f).astype(BF16)
 
         weights = (gu, w_down)
-        ffn_got = gather_first(ffn_in)
-        done = feed_forward([ffn_in], [signal_low], *weights, F32)
+        if square:
+            halves = [ffn_in[: tokens // 2], ffn_in[tokens // 2 :]]
+            ffn_got = [[swap(x, j) for x in halves] for j in (1, 2)]
+        else:
+            halves = [ffn_in]
+            ffn_got = [[swap(ffn_in, j)] for j in range(1, nf)]
+        done = feed_forward(halves, [signal_low], *weights, F32)
         ffn_got, first_dx = fence(ffn_got, done[0][4])
-        ffn_more = gather_second(ffn_got)
+        ffn_more = [swap(ffn_got[1][0], 1), swap(ffn_got[0][1], 2)] if square else []
         dffn_got = []
         pair = 2 if square else 1
         for j in range(0, len(ffn_got), pair):
-            done += feed_forward(ffn_got[j : j + pair], signal_got[j : j + pair], *weights, BF16)
+            xs = [x for got in ffn_got[j : j + pair] for x in got]
+            done += feed_forward(xs, signal_got[j : j + pair], *weights, BF16)
             sent, ffn_more, ffn_got[j + pair :] = fence([d[4] for d in done[-pair:]], ffn_more, ffn_got[j + pair :])
             dffn_got += [swap(x, j + 1 + n) for n, x in enumerate(sent)]
-        ffn_blocks = gather_done(ffn_in, ffn_got, ffn_more)
         signal_blocks = [signal_low] + signal_got
 
         inner_blocks = [d[0] for d in done]
         if square:
-            inner_blocks.append(hidden_units(ffn_blocks[3], gu, hidden_cols))
-        inner_blocks, last_x = fence(inner_blocks, ffn_blocks[nf - 1])
+            last_inner, last_x = hidden_units(ffn_more, gu, hidden_cols)
+            inner_blocks.append(last_inner)
+        else:
+            last_x = ffn_in
+        inner_blocks, last_x = fence(inner_blocks, last_x)
         down_part = token_sum(inner_blocks, signal_blocks)
         down_part, last_x = fence(down_part, last_x)
         down_share = lax.psum_scatter(down_part, "ctx", scatter_dimension=0, tiled=True)
         if square:
             done += feed_forward([last_x], [signal_got[2]], *weights, BF16)
-        _, gate_blocks, up_blocks, y_parts, dx = (list(t) for t in zip(*done))
+        _, gate_blocks, up_blocks, y_parts, dx, ffn_blocks = (list(t) for t in zip(*done))
         late = fence(dx[nf - 1], ffn_blocks, gate_blocks, up_blocks, dffn_got)
         dffn_got = late[4]
         if square:

time: 903 us -> 899 us (level)
  waiting for transfers between devices: 356 us -> 369 us
  local copies, waits for them, and re-layouts: 101 us -> 90.7 us
    ppermute x56 -> x58, waiting for transfers between devices: 218 us -> 228 us  [swap(): return lax.ppermute(x, 'fsdp', [(i, i ^ j) for i in range(nf)])]
    ppermute x56 -> x58, starting transfers between devices: 74.9 us -> 65.7 us  [swap(): return lax.ppermute(x, 'fsdp', [(i, i ^ j) for i in range(nf)])]
    unnamed x222 -> x217, local copies, waits for them, and re-layouts: 39.8 us -> 36.4 us
  transfers between devices with their start and end apart: 88 -> 90, of which waited for: 42 -> 41; matrix products, arithmetic and copies ran while one was open for 18% -> 18% of each run, Pallas kernels for 19% -> 20%
where the time goes in v5:
time: 899 us; the launch traced here: 890 us
  waiting for transfers between devices  369 us (41%)
  Pallas kernels  207 us (23%)
  starting transfers between devices  105 us (12%)
  local copies, waits for them, and re-layouts  90.7 us (10%)
  other arithmetic  76.1 us (8%)
  matrix products  25.8 us (3%)
  between operations  16.1 us (2%)
    ppermute x58, waiting for transfers between devices, swap(): return lax.ppermute(x, 'fsdp', [(i, i ^ j) for i in range(nf)])  228 us
    ppermute x58, starting transfers between devices, swap(): return lax.ppermute(x, 'fsdp', [(i, i ^ j) for i in range(nf)])  65.7 us
    pallas_call x3, Pallas kernels, feed_forward(): pl.pallas_call(kernel, grid=(steps,), in_specs=[piece] * pieces + [whole]...  64.2 us
    all_gather x1, waiting for transfers between devices, on_device(): buffer = lax.all_gather(buffer_share, 'ctx', tiled=True)  45.5 us
    pallas_call x4, Pallas kernels, token_sum(): pl.pallas_call(kernel, grid=(height // tile,), in_specs=[pl.BlockSpec((to...  45.5 us
    unnamed x217, local copies, waits for them, and re-layouts  36.4 us
    ppermute x6, waiting for transfers between devices, line_start(): lax.ppermute(low[s], 'ctx', [(i, i - 2 * s) for i in range(2 * s, nc)])  30.4 us
    pallas_call x2, Pallas kernels, attend_backward(): pl.pallas_call(kernel, grid_spec=pltpu.PrefetchScalarGridSpec(num_scalar_...  22 us
  transfers between devices with their start and end apart: 90, of which 41 were waited for; matrix products, arithmetic and copies ran while one was open for 18% of the time, Pallas kernels for 20%

profile of v5, /device:TPU:0, one launch (start us, length us, event | category | flops | bytes accessed | tf_op | source)
XLA Modules:
  0.0 890.0 jit_solution(2884434116615634195)
XLA Ops:
  9.5 5.2 all-to-all-start.1
  22.0 2.5 constant_dynamic-slice_fusion.2
  24.5 13.7 %collective-permute-done.1.refs_1_ = bf16[272,1536]{1,0:T(8,128)(2,1)} collective-permute-done((bf16[272,1536]{1,0:T(8,128)(2,1)}, bf16[272,1536]{1,0:T(8,128)(2,1)}, u32[]{:S(2)}, u32[]{:S(2)}) %collective-permute-start.1) | collective-permute-done | bytes 835616 | tf_op jit(solution)/shard_map/ppermute | solution.py:763
  47.3 3.5 collective-permute-done.2
  58.4 6.6 project.1
  66.2 3.7 all-to-all-start
  73.4 3.5 collective-permute-start.7
  76.9 4.5 collective-permute-start.8
  83.6 5.7 collective-permute-done.8.refs_2_
  89.2 4.2 collective-permute-done.9.refs_3_
  93.5 6.4 collective-permute-done.10.refs_1_
  115.2 19.1 %collective-permute-done.14 = bf16[128,1024]{1,0:T(8,128)(2,1)S(1)} collective-permute-done((bf16[128,1024]{1,0:T(8,128)(2,1)S(1)}, bf16[128,1024]{1,0:T(8,128)(2,1)S(1)}, u32[]{:S(2)}, u32[]{:S(2)}) %collective-permute-start.14) | collective-permute-done | bytes 262176 | tf_op jit(solution)/shard_map/ppermute | solution.py:763
  147.0 6.0 fusion.67.q_ref
  159.4 3.7 collective-permute-done.18
  165.1 14.6 %attend_forward.1 = (bf16[4,64,1024]{2,1,0:T(8,128)(2,1)}, bf16[4,64,1024]{2,1,0:T(8,128)(2,1)}, bf16[4,64,1024]{2,1,0:T(8,128)(2,1)}, bf16[4,64,1024]{2,1,0:T(8...) custom-call(s32[7]{0:T(128)} %pad_add_fusion.info_ref, f32[4,4,64,1024]{3,2,1,0:T(8,128)} %fusion.67.q_ref, ...), custom_call_target="tpu_custom_call" | custom-call | flops 1 | bytes 1 | tf_op jit(solution)/shard_map/attend_forward/pallas_call | solution.py:148
  179.8 3.7 convolution_convert_fusion
  188.7 16.2 %collective-permute-done.22.refs_5_.refs_6_ = bf16[256,2048]{1,0:T(8,128)(2,1)} collective-permute-done((bf16[256,2048]{1,0:T(8,128)(2,1)S(1)}, bf16[256,2048]{1,0:T(8,128)(2,1)}, u32[]{:S(2)}, u32[]{:S(2)}) %collective-permute-start.22) | collective-permute-done | bytes 1048608 | tf_op jit(solution)/shard_map/ppermute | solution.py:763
  205.2 10.1 %collective-permute-done.19 = bf16[128,2048]{1,0:T(8,128)(2,1)S(1)} collective-permute-done((bf16[128,2048]{1,0:T(8,128)(2,1)S(1)}, bf16[128,2048]{1,0:T(8,128)(2,1)S(1)}, u32[]{:S(2)}, u32[]{:S(2)}) %collective-permute-start.19) | collective-permute-done | bytes 524320 | tf_op jit(solution)/shard_map/ppermute | solution.py:763
  219.9 2.6 fusion.70
  222.5 19.1 %collective-permute-done.25 = bf16[256,2048]{1,0:T(8,128)(2,1)S(1)} collective-permute-done((bf16[256,2048]{1,0:T(8,128)(2,1)S(1)}, bf16[256,2048]{1,0:T(8,128)(2,1)S(1)}, u32[]{:S(2)}, u32[]{:S(2)}) %collective-permute-start.25) | collective-permute-done | bytes 1048608 | tf_op jit(solution)/shard_map/ppermute | solution.py:763
  243.6 2.8 multiply_reduce_fusion.2
  251.7 18.0 %feed_forward.3 = (bf16[256,1408]{1,0:T(8,128)(2,1)}, bf16[256,1408]{1,0:T(8,128)(2,1)}, bf16[256,1408]{1,0:T(8,128)(2,1)}, f32[256,2048]{1,0:T(8,128)}, f32[256,2048]{1,0:T(8,128)}, /*index=5*/bf16[256,2048]{1,0:T(8,128)(2,1)}) custom-call(bf16[128,2048]{1,0:T(8,128)(2,1)} %get-tuple-element.483.refs_0_, bf16[128,2048]{1,0:T(8,128)(2,1)} %get-tuple-element.482.refs_1_, ...), custom_call_target="tpu_custom_call" | custom-call | flops 1 | bytes 1 | tf_op jit(solution)/shard_map/feed_forward/pallas_call | solution.py:370
  275.5 29.1 %feed_forward.4 = (bf16[256,1408]{1,0:T(8,128)(2,1)}, bf16[256,1408]{1,0:T(8,128)(2,1)}, bf16[256,1408]{1,0:T(8,128)(2,1)}, bf16[256,1408]{1,0:T(8,128)(2,1)}, b...) custom-call(bf16[128,2048]{1,0:T(8,128)(2,1)} %collective-permute-do, ...), custom_call_target="tpu_custom_call" | custom-call | flops 1 | bytes 1 | tf_op jit(solution)/shard_map/feed_forward/pallas_call | solution.py:370
  304.7 10.0 %hidden_units.1 = (bf16[256,1408]{1,0:T(8,128)(2,1)}, bf16[256,2048]{1,0:T(8,128)(2,1)}) custom-call(bf16[128,2048]{1,0:T(8,128)(2,1)} %collective-permute-done.30.refs_0_, bf16[128,2048]{1,0:T(8,128)(2,1)} %collective-permute-done.31.refs_1_, bf16[8,4,64,2816]{3,2,1,0:T(8,128)(2,1)} %bitcast.181, bf16[8,4,64,2816]{3,2,1,0:T(8,128)(2,1)} %bitcast.182, ...), custom_call_target="tpu_custom_call" | custom-call | flops 1 | bytes 1 | tf_op jit(solution)/shard_map/hidden_units/pallas_call | solution.py:443
  314.8 13.4 %token_sum.4 = bf16[1408,2048]{1,0:T(8,128)(2,1)} custom-call(bf16[256,1408]{1,0:T(8,128)(2,1)} %get-tuple-element.277.refs_0_, bf16[256,1408]{1,0:T(8,128)(2,1)} %get-tuple-element.278.refs_1_, bf16[256,1408]{1,0:T(8,128)(2,1)} %get-tuple-element.279.refs_2_, bf16[256,1408]{1,0:T(8,128)(2,1)} %get-tuple-element.280.refs_3_, bf16[256,2048]{1,0:T(8,128)(2,1)} %copy-done.18, ...), custom_call_target="tpu_custom_call" | custom-call | flops 5905580032 | bytes 5767168 | tf_op jit(solution)/shard_map/token_sum/pallas_call | solution.py:610
  330.7 17.0 %feed_forward.5 = (bf16[256,1408]{1,0:T(8,128)(2,1)}, bf16[256,1408]{1,0:T(8,128)(2,1)}, bf16[256,1408]{1,0:T(8,128)(2,1)}, bf16[256,2048]{1,0:T(8,128)(2,1)}, b...) custom-call(bf16[256,2048]{1,0:T(8,128)(2,1)} %get-tuple-element.283.refs_0_, bf16[256,2048]{1,0:T(8,128)(2,1)} %copy-done.51, ...), custom_call_target="tpu_custom_call" | custom-call | flops 1 | bytes 1 | tf_op jit(solution)/shard_map/feed_forward/pallas_call | solution.py:370
  347.8 3.1 collective-permute-done.32
  350.9 11.8 %collective-permute-done.33 = bf16[256,2048]{1,0:T(8,128)(2,1)} collective-permute-done((bf16[256,2048]{1,0:T(8,128)(2,1)}, bf16[256,2048]{1,0:T(8,128)(2,1)}, u32[]{:S(2)}, u32[]{:S(2)}) %collective-permute-start.33) | collective-permute-done | bytes 1048608 | tf_op jit(solution)/shard_map/ppermute | solution.py:763
  362.7 19.1 %token_sum.5 = bf16[2048,2816]{1,0:T(8,128)(2,1)} custom-call(bf16[256,2048]{1,0:T(8,128)(2,1)} %get-tuple-element.302.refs_0_, bf16[256,2048]{1,0:T(8,128)(2,1)} %get-tuple-element.303.refs_1_, bf16[256,2048]{1,0:T(8,128)(2,1)} %get-tuple-element.304.refs_2_, bf16[256,2048]{1,0:T(8,128)(2,1)} %get-tuple-element.305.refs_3_, ...), custom_call_target="tpu_custom_call" | custom-call | flops 11811160064 | bytes 5767168 | tf_op jit(solution)/shard_map/token_sum/pallas_call | solution.py:610
  381.8 3.8 multiply_reduce_fusion
  387.7 3.0 collective-permute-start.35
  392.4 16.6 %collective-permute-done.35.refs_5_ = bf16[256,2048]{1,0:T(8,128)(2,1)S(1)} collective-permute-done((bf16[256,2048]{1,0:T(8,128)(2,1)S(1)}, bf16[256,2048]{1,0:T(8,128)(2,1)S(1)}, u32[]{:S(2)}, u32[]{:S(2)}) %collective-permute-start.35) | collective-permute-done | bytes 1048608 | tf_op jit(solution)/shard_map/ppermute | solution.py:763
  414.6 4.8 collective-permute-done.37
  424.4 11.1 %attend_backward.2 = (bf16[4,2,64,1024]{3,2,1,0:T(8,128)(2,1)}, bf16[4,4,2,64,512]{4,3,2,1,0:T(8,128)(2,1)}, bf16[4,4,2,64,512]{4,3,2,1,0:T(8,128)(2,1)}) custom-call(s32[7]{0:T(128)} %pad_add_fusion.info_ref, bf16[4,64,1024]{2,1,0:T(8,128)(2,1)} %get-tuple-element.253.refs_0_, bf16[4,64,1024]{2,1,0:T(8,128)(2,1)} %get-tuple-element.246.refs_1_, ...), custom_call_target="tpu_custom_call" | custom-call | flops 1 | bytes 1 | tf_op jit(solution)/shard_map/attend_backward/pallas_call | solution.py:245
  435.6 10.9 %attend_backward.3 = (bf16[4,2,64,1024]{3,2,1,0:T(8,128)(2,1)}, bf16[4,4,2,64,512]{4,3,2,1,0:T(8,128)(2,1)}, bf16[4,4,2,64,512]{4,3,2,1,0:T(8,128)(2,1)}) custom-call(s32[7]{0:T(128)} %pad_add_fusion.info_ref, bf16[4,64,1024]{2,1,0:T(8,128)(2,1)} %get-tuple-element.253.refs_0_, bf16[4,64,1024]{2,1,0:T(8,128)(2,1)} %get-tuple-element.246.refs_1_, ...), custom_call_target="tpu_custom_call" | custom-call | flops 1 | bytes 1 | tf_op jit(solution)/shard_map/attend_backward/pallas_call | solution.py:245
  451.4 2.6 fusion.47
  464.6 3.0 convert_add_fusion
  476.8 9.5 %token_grad.1 = (bf16[1024,512]{1,0:T(8,128)(2,1)}, bf16[1024,512]{1,0:T(8,128)(2,1)}) custom-call(s32[7]{0:T(128)} %pad_add_fusion.info_ref, bf16[256,1024]{1,0:T(8,128)(2,1)} %get-tuple-element.350.refs_0_, bf16[256,1024]{1,0:T(8,128)(2,1)} %copy-done.47, bf16[256,1024]{1,0:T(8,128)(2,1)} %collective-permute-done.11.refs_2_, ...), custom_call_target="tpu_custom_call" | custom-call | flops 2147483648 | bytes 2097152 | tf_op jit(solution)/shard_map/token_grad/pallas_call | solution.py:523
  491.0 4.0 collective-permute-done.47
  497.1 16.9 %reduce-scatter.6.cloned.1.call-done = bf16[256,2816]{1,0:T(8,128)(2,1)} async-done(((bf16[2048,2816]{1,0:T(8,128)(2,1)}), bf16[256,2816]{1,0:T(8,128)(2,1)}) %reduce-scatter.6.cloned.1.call-update) | async-done | bytes 1441808 | tf_op jit(solution)/shard_map/reduce_scatter | solution.py:961
  515.9 2.9 fusion.51
  526.5 16.1 %collective-permute-done.58 = bf16[256,2048]{1,0:T(8,128)(2,1)} collective-permute-done((bf16[256,2048]{1,0:T(8,128)(2,1)}, bf16[256,2048]{1,0:T(8,128)(2,1)}, u32[]{:S(2)}, u32[]{:S(2)}) %collective-permute-start.58) | collective-permute-done | bytes 1048608 | tf_op jit(solution)/shard_map/ppermute | solution.py:763
  549.6 17.3 %collective-permute-done.51 = bf16[128,512]{1,0:T(8,128)(2,1)S(1)} collective-permute-done((bf16[128,512]{1,0:T(8,128)(2,1)S(1)}, bf16[128,512]{1,0:T(8,128)(2,1)S(1)}, u32[]{:S(2)}, u32[]{:S(2)}) %collective-permute-start.51) | collective-permute-done | bytes 131104 | tf_op jit(solution)/shard_map/ppermute | solution.py:1020
  574.2 5.6 collective-permute-done.52
  587.0 4.3 all-to-all-start.2
  591.3 3.0 fusion.49
  602.5 5.8 all-to-all-done.2
  608.3 4.2 all-to-all-start.3
  614.8 12.0 %collective-permute-done.61 = bf16[128,512]{1,0:T(8,128)(2,1)} collective-permute-done((bf16[128,512]{1,0:T(8,128)(2,1)}, bf16[128,512]{1,0:T(8,128)(2,1)}, u32[]{:S(2)}, u32[]{:S(2)}) %collective-permute-start.61) | collective-permute-done | bytes 131104 | tf_op jit(solution)/shard_map/ppermute | solution.py:1020
  630.7 6.3 project_back.1
  646.6 3.7 collective-permute-done.68
  658.2 4.2 token_sum.6
  668.2 8.8 token_sum.7
  680.0 3.2 slice_dynamic-update-slice_fusion.1
  691.7 8.8 all-gather.8.cloned.1.call-done
  700.5 4.1 dynamic-slice_bitcast_fusion
  708.2 30.9 %collective-permute-done.65.refs_1_ = bf16[256,2816]{1,0:T(8,128)(2,1)S(1)} collective-permute-done((bf16[256,2816]{1,0:T(8,128)(2,1)S(1)}, bf16[256,2816]{1,0:T(8,128)(2,1)S(1)}, u32[]{:S(2)}, u32[]{:S(2)}) %collective-permute-start.65) | collective-permute-done | bytes 1441824 | tf_op jit(solution)/shard_map/ppermute | solution.py:763
  739.1 31.2 %collective-permute-done.66.refs_2_ = bf16[256,2816]{1,0:T(8,128)(2,1)S(1)} collective-permute-done((bf16[256,2816]{1,0:T(8,128)(2,1)S(1)}, bf16[256,2816]{1,0:T(8,128)(2,1)S(1)}, u32[]{:S(2)}, u32[]{:S(2)}) %collective-permute-start.66) | collective-permute-done | bytes 1441824 | tf_op jit(solution)/shard_map/ppermute | solution.py:763
  771.4 17.3 %reduce-scatter.8.cloned.1.call-done = bf16[496,1024]{1,0:T(8,128)(2,1)} async-done(((bf16[3968,1024]{1,0:T(8,128)(2,1)}), bf16[496,1024]{1,0:T(8,128)(2,1)}) %reduce-scatter.8.cloned.1.call-update) | async-done | bytes 1015824 | tf_op jit(solution)/shard_map/reduce_scatter | solution.py:1109
  789.9 4.4 add_convert_fusion.1
  795.9 9.5 %convert_element_type.344 = f32[1408,2048]{1,0:T(8,128)} convert(bf16[1408,2048]{1,0:T(8,128)(2,1)} %all-gather.10.cloned.1.call-done) | non-fusion elementwise | flops 2883584 | bytes 17301504 | tf_op jit(solution)/shard_map/convert_element_type | solution.py:1121
  805.4 17.8 %place_columns.1 = (f32[512,5632]{1,0:T(8,128)}, f32[512,5632]{1,0:T(8,128)}) custom-call(s32[7]{0:T(128)} %pad_add_fusion.info_ref, bf16[256,2816]{1,0:T(8,128)(2,1)} %get-tuple-element.416.refs_0_, bf16[256,2816]{1,0:T(8,128)(2,1)} %copy-done.43, bf16[256,2816]{1,0:T(8,128)(2,1)} %copy-done.44, bf16[256,2816]{1,0:T(8,128)(2,1)} %collective-permute-done.67.refs_3_, ...), custom_call_target="tpu_custom_call" | custom-call | flops 1 | bytes 1 | tf_op jit(solution)/shard_map/place_columns/pallas_call | solution.py:747
  823.2 45.5 %all-gather.12.cloned.1.call-done.o0_ref.o1_ref.refs_0_.refs_1_.refs_2_.refs_3_.refs_4_ = bf16[3968,1024]{1,0:T(8,128)(2,1)} async-done(((bf16[496,1024]{1,0:T(8,128)(2,1)}), bf16[3968,1024]{1,0:T(8,128)(2,1)}) %all-gather.12.cloned.1.call-update) | async-done | bytes 8126480 | tf_op jit(solution)/shard_map/all_gather | solution.py:1118
  870.9 8.6 unpack.1
  (525 shorter events, 233.1 us)
Async XLA Ops:
  14.7 120.7 %all-gather.14.cloned.1.call-start = ((), (), s32[]{:S(2)}) async-start(), calls=%async_computation.13 | async-start | bytes 2359296 | tf_op jit(solution)/shard_map/all_gather | solution.py:856
  16.1 25.2 %collective-permute-start = (bf16[272,1536]{1,0:T(8,128)(2,1)}, bf16[272,1536]{1,0:T(8,128)(2,1)S(1)}, u32[]{:S(2)}, u32[]{:S(2)}) collective-permute-start(bf16[272,1536]{1,0:T(8,128)(2,1)} %pad_maximum_fusion.5), channel_id=1, source_target_pairs={{0,1},{1,0},{2,3},{3,2},{4,5},{5,4},{6,7},{7,6},{8,9},{9,8},{10,11... | collective-permute-start | bytes 2506760 | tf_op jit(solution)/shard_map/ppermute | solution.py:763
  18.2 20.1 %collective-permute-start.1 = (bf16[272,1536]{1,0:T(8,128)(2,1)}, bf16[272,1536]{1,0:T(8,128)(2,1)}, u32[]{:S(2)}, u32[]{:S(2)}) collective-permute-start(bf16[272,1536]{1,0:T(8,128)(2,1)} %pad_maximum_fusion.5), channel_id=1, source_target_pairs={{0,2},{1,3},{2,0},{3,1},{4,6},{5,7},{6,4},{7,5},{8,10},{9,11},{10,... | collective-permute-start | bytes 2506760 | tf_op jit(solution)/shard_map/ppermute | solution.py:763
  66.2 33.7 %all-to-all-start = ((bf16[64,4,2816]{2,0,1:T(8,128)(2,1)}), bf16[64,4,2816]{2,0,1:T(8,128)(2,1)S(1)}, u32[]{:S(2)}, u32[]{:S(2)}) async-start(bf16[64,4,2816]{2,0,1:T(8,128)(2,1)} %bitcast.170), calls=%async_computation | async-start | bytes 2883584 | tf_op jit(solution)/shard_map/all_to_all | solution.py:848
  69.9 172.7 %all-gather.16.cloned.1.call-start = ((), (), s32[]{:S(2)}) async-start(), calls=%async_computation.14 | async-start | bytes 12976128 | tf_op jit(solution)/shard_map/all_gather | solution.py:888
  70.0 29.9 %collective-permute-start.10 = (bf16[256,1024]{1,0:T(8,128)(2,1)}, bf16[256,1024]{1,0:T(8,128)(2,1)S(1)}, u32[]{:S(2)}, u32[]{:S(2)}) collective-permute-start(bf16[256,1024]{1,0:T(8,128)(2,1)} %get-tuple-element.350.refs_0_), channel_id=1, source_target_pairs={{0,1},{1,0},{2,3},{3,2},{4,5},{5,4},{6,7},{7,6},{8,9},{9,8},{10,11... | collective-permute-start | bytes 1572872 | tf_op jit(solution)/shard_map/ppermute | solution.py:763
  71.9 28.0 %collective-permute-start.11 = (bf16[256,1024]{1,0:T(8,128)(2,1)}, bf16[256,1024]{1,0:T(8,128)(2,1)}, u32[]{:S(2)}, u32[]{:S(2)}) collective-permute-start(bf16[256,1024]{1,0:T(8,128)(2,1)} %get-tuple-element.350.refs_0_), channel_id=1, source_target_pairs={{0,2},{1,3},{2,0},{3,1},{4,6},{5,7},{6,4},{7,5},{8,10},{9,11},{10,... | collective-permute-start | bytes 1572872 | tf_op jit(solution)/shard_map/ppermute | solution.py:763
  101.2 345.3 %reduce-scatter.4.cloned.1.call-start = ((), (), s32[]{:S(2)}) async-start(), calls=%async_computation.7 | async-start | bytes 6488064 | tf_op jit(solution)/shard_map/reduce_scatter | solution.py:949
  103.7 31.7 %collective-permute-start.12 = (bf16[1024,512]{1,0:T(8,128)(2,1)}, bf16[1024,512]{1,0:T(8,128)(2,1)}, u32[]{:S(2)}, u32[]{:S(2)}) collective-permute-start(bf16[1024,512]{1,0:T(8,128)(2,1)} %stack_rows.1), channel_id=1, source_target_pairs={{0,1},{1,0},{2,3},{3,2},{4,5},{5,4},{6,7},{7,6},{8,9},{9,8},{10,11... | collective-permute-start | bytes 3145736 | tf_op jit(solution)/shard_map/ppermute | solution.py:763
  105.1 30.3 %collective-permute-start.13 = (bf16[1024,512]{1,0:T(8,128)(2,1)}, bf16[1024,512]{1,0:T(8,128)(2,1)}, u32[]{:S(2)}, u32[]{:S(2)}) collective-permute-start(bf16[1024,512]{1,0:T(8,128)(2,1)} %stack_rows.1), channel_id=1, source_target_pairs={{0,2},{1,3},{2,0},{3,1},{4,6},{5,7},{6,4},{7,5},{8,10},{9,11},{10,... | collective-permute-start | bytes 3145736 | tf_op jit(solution)/shard_map/ppermute | solution.py:763
  109.3 25.0 %collective-permute-start.14 = (bf16[128,1024]{1,0:T(8,128)(2,1)S(1)}, bf16[128,1024]{1,0:T(8,128)(2,1)S(1)}, u32[]{:S(2)}, u32[]{:S(2)}) collective-permute-start(bf16[128,1024]{1,0:T(8,128)(2,1)S(1)} %slice.366), channel_id=1, source_target_pairs={{0,1},{1,0},{2,3},{3,2},{4,5},{5,4},{6,7},{7,6},{8,9},{9,8},{10,11... | collective-permute-start | bytes 786440 | tf_op jit(solution)/shard_map/ppermute | solution.py:763
  110.8 24.6 %collective-permute-start.15 = (bf16[128,1024]{1,0:T(8,128)(2,1)S(1)}, bf16[128,1024]{1,0:T(8,128)(2,1)S(1)}, u32[]{:S(2)}, u32[]{:S(2)}) collective-permute-start(bf16[128,1024]{1,0:T(8,128)(2,1)S(1)} %slice.367), channel_id=1, source_target_pairs={{0,2},{1,3},{2,0},{3,1},{4,6},{5,7},{6,4},{7,5},{8,10},{9,11},{10,... | collective-permute-start | bytes 786440 | tf_op jit(solution)/shard_map/ppermute | solution.py:763
  155.9 32.7 %collective-permute-start.21 = (bf16[256,2048]{1,0:T(8,128)(2,1)S(1)}, bf16[256,2048]{1,0:T(8,128)(2,1)}, u32[]{:S(2)}, u32[]{:S(2)}) collective-permute-start(bf16[256,2048]{1,0:T(8,128)(2,1)S(1)} %bitcast_convert_fusion.refs_2_.refs_4_), channel_id=1, source_target_pairs={{0,1},{1,0},{2,3},{3,2},{4,5},{5,4},{6,7},{7,6},{8,9},{9,8},{10,11... | collective-permute-start | bytes 3145736 | tf_op jit(solution)/shard_map/ppermute | solution.py:763
  157.2 47.7 %collective-permute-start.22 = (bf16[256,2048]{1,0:T(8,128)(2,1)S(1)}, bf16[256,2048]{1,0:T(8,128)(2,1)}, u32[]{:S(2)}, u32[]{:S(2)}) collective-permute-start(bf16[256,2048]{1,0:T(8,128)(2,1)S(1)} %bitcast_convert_fusion.refs_2_.refs_4_), channel_id=1, source_target_pairs={{0,2},{1,3},{2,0},{3,1},{4,6},{5,7},{6,4},{7,5},{8,10},{9,11},{10,... | collective-permute-start | bytes 3145736 | tf_op jit(solution)/shard_map/ppermute | solution.py:763
  157.9 47.2 %collective-permute-start.23 = (bf16[256,2048]{1,0:T(8,128)(2,1)S(1)}, bf16[256,2048]{1,0:T(8,128)(2,1)S(1)}, u32[]{:S(2)}, u32[]{:S(2)}) collective-permute-start(bf16[256,2048]{1,0:T(8,128)(2,1)S(1)} %bitcast_convert_fusion.refs_2_.refs_4_), channel_id=1, source_target_pairs={{0,3},{1,2},{2,1},{3,0},{4,7},{5,6},{6,5},{7,4},{8,11},{9,10},{10,... | collective-permute-start | bytes 3145736 | tf_op jit(solution)/shard_map/ppermute | solution.py:763
  183.6 31.6 %collective-permute-start.19 = (bf16[128,2048]{1,0:T(8,128)(2,1)S(1)}, bf16[128,2048]{1,0:T(8,128)(2,1)S(1)}, u32[]{:S(2)}, u32[]{:S(2)}) collective-permute-start(bf16[128,2048]{1,0:T(8,128)(2,1)S(1)} %get-tuple-element.485), channel_id=1, source_target_pairs={{0,1},{1,0},{2,3},{3,2},{4,5},{5,4},{6,7},{7,6},{8,9},{9,8},{10,11... | collective-permute-start | bytes 1572872 | tf_op jit(solution)/shard_map/ppermute | solution.py:763
  185.0 31.2 %collective-permute-start.20 = (bf16[128,2048]{1,0:T(8,128)(2,1)S(1)}, bf16[128,2048]{1,0:T(8,128)(2,1)S(1)}, u32[]{:S(2)}, u32[]{:S(2)}) collective-permute-start(bf16[128,2048]{1,0:T(8,128)(2,1)S(1)} %get-tuple-element.484), channel_id=1, source_target_pairs={{0,2},{1,3},{2,0},{3,1},{4,6},{5,7},{6,4},{7,5},{8,10},{9,11},{10,... | collective-permute-start | bytes 1572872 | tf_op jit(solution)/shard_map/ppermute | solution.py:763
  216.4 25.2 %collective-permute-start.25 = (bf16[256,2048]{1,0:T(8,128)(2,1)S(1)}, bf16[256,2048]{1,0:T(8,128)(2,1)S(1)}, u32[]{:S(2)}, u32[]{:S(2)}) collective-permute-start(bf16[256,2048]{1,0:T(8,128)(2,1)S(1)} %pad_maximum_fusion.4), channel_id=1, source_target_pairs={{0,2},{1,3},{2,0},{3,1},{4,6},{5,7},{6,4},{7,5},{8,10},{9,11},{10,... | collective-permute-start | bytes 3145736 | tf_op jit(solution)/shard_map/ppermute | solution.py:763
  217.5 25.1 %collective-permute-start.24 = (bf16[256,2048]{1,0:T(8,128)(2,1)S(1)}, bf16[256,2048]{1,0:T(8,128)(2,1)S(1)}, u32[]{:S(2)}, u32[]{:S(2)}) collective-permute-start(bf16[256,2048]{1,0:T(8,128)(2,1)S(1)} %pad_maximum_fusion.3), channel_id=1, source_target_pairs={{0,1},{1,0},{2,3},{3,2},{4,5},{5,4},{6,7},{7,6},{8,9},{9,8},{10,11... | collective-permute-start | bytes 3145736 | tf_op jit(solution)/shard_map/ppermute | solution.py:763
  247.7 22.1 %collective-permute-start.26 = (bf16[128,2048]{1,0:T(8,128)(2,1)}, bf16[128,2048]{1,0:T(8,128)(2,1)}, u32[]{:S(2)}, u32[]{:S(2)}) collective-permute-start(bf16[128,2048]{1,0:T(8,128)(2,1)} %get-tuple-element.483.refs_0_), channel_id=1, source_target_pairs={{0,1},{1,0},{2,3},{3,2},{4,5},{5,4},{6,7},{7,6},{8,9},{9,8},{10,11... | collective-permute-start | bytes 1572872 | tf_op jit(solution)/shard_map/ppermute | solution.py:763
  248.7 23.6 %collective-permute-start.27 = (bf16[128,2048]{1,0:T(8,128)(2,1)}, bf16[128,2048]{1,0:T(8,128)(2,1)}, u32[]{:S(2)}, u32[]{:S(2)}) collective-permute-start(bf16[128,2048]{1,0:T(8,128)(2,1)} %get-tuple-element.482.refs_1_), channel_id=1, source_target_pairs={{0,1},{1,0},{2,3},{3,2},{4,5},{5,4},{6,7},{7,6},{8,9},{9,8},{10,11... | collective-permute-start | bytes 1572872 | tf_op jit(solution)/shard_map/ppermute | solution.py:763
  249.7 22.6 %collective-permute-start.28 = (bf16[128,2048]{1,0:T(8,128)(2,1)}, bf16[128,2048]{1,0:T(8,128)(2,1)}, u32[]{:S(2)}, u32[]{:S(2)}) collective-permute-start(bf16[128,2048]{1,0:T(8,128)(2,1)} %get-tuple-element.483.refs_0_), channel_id=1, source_target_pairs={{0,2},{1,3},{2,0},{3,1},{4,6},{5,7},{6,4},{7,5},{8,10},{9,11},{10,... | collective-permute-start | bytes 1572872 | tf_op jit(solution)/shard_map/ppermute | solution.py:763
  250.8 22.9 %collective-permute-start.29 = (bf16[128,2048]{1,0:T(8,128)(2,1)}, bf16[128,2048]{1,0:T(8,128)(2,1)}, u32[]{:S(2)}, u32[]{:S(2)}) collective-permute-start(bf16[128,2048]{1,0:T(8,128)(2,1)} %get-tuple-element.482.refs_1_), channel_id=1, source_target_pairs={{0,2},{1,3},{2,0},{3,1},{4,6},{5,7},{6,4},{7,5},{8,10},{9,11},{10,... | collective-permute-start | bytes 1572872 | tf_op jit(solution)/shard_map/ppermute | solution.py:763
  273.7 31.0 %collective-permute-start.30 = (bf16[128,2048]{1,0:T(8,128)(2,1)}, bf16[128,2048]{1,0:T(8,128)(2,1)}, u32[]{:S(2)}, u32[]{:S(2)}) collective-permute-start(bf16[128,2048]{1,0:T(8,128)(2,1)} %collective-permute-done.28.refs_2_), channel_id=1, source_target_pairs={{0,1},{1,0},{2,3},{3,2},{4,5},{5,4},{6,7},{7,6},{8,9},{9,8},{10,11... | collective-permute-start | bytes 1572872 | tf_op jit(solution)/shard_map/ppermute | solution.py:763
  274.3 30.4 %collective-permute-start.31 = (bf16[128,2048]{1,0:T(8,128)(2,1)}, bf16[128,2048]{1,0:T(8,128)(2,1)}, u32[]{:S(2)}, u32[]{:S(2)}) collective-permute-start(bf16[128,2048]{1,0:T(8,128)(2,1)} %collective-permute-done.27.refs_1_), channel_id=1, source_target_pairs={{0,2},{1,3},{2,0},{3,1},{4,6},{5,7},{6,4},{7,5},{8,10},{9,11},{10,... | collective-permute-start | bytes 1572872 | tf_op jit(solution)/shard_map/ppermute | solution.py:763
  328.2 185.8 %reduce-scatter.6.cloned.1.call-start = ((), (), s32[]{:S(2)}) async-start(), calls=%async_computation.8 | async-start | bytes 12976128 | tf_op jit(solution)/shard_map/reduce_scatter | solution.py:961
  328.4 22.5 %collective-permute-start.32 = (bf16[256,2048]{1,0:T(8,128)(2,1)}, bf16[256,2048]{1,0:T(8,128)(2,1)}, u32[]{:S(2)}, u32[]{:S(2)}) collective-permute-start(bf16[256,2048]{1,0:T(8,128)(2,1)} %get-tuple-element.297), channel_id=1, source_target_pairs={{0,1},{1,0},{2,3},{3,2},{4,5},{5,4},{6,7},{7,6},{8,9},{9,8},{10,11... | collective-permute-start | bytes 3145736 | tf_op jit(solution)/shard_map/ppermute | solution.py:763
  329.5 33.2 %collective-permute-start.33 = (bf16[256,2048]{1,0:T(8,128)(2,1)}, bf16[256,2048]{1,0:T(8,128)(2,1)}, u32[]{:S(2)}, u32[]{:S(2)}) collective-permute-start(bf16[256,2048]{1,0:T(8,128)(2,1)} %get-tuple-element.298), channel_id=1, source_target_pairs={{0,2},{1,3},{2,0},{3,1},{4,6},{5,7},{6,4},{7,5},{8,10},{9,11},{10,... | collective-permute-start | bytes 3145736 | tf_op jit(solution)/shard_map/ppermute | solution.py:763
  362.7 19.1 %collective-permute-start.34 = (bf16[256,2048]{1,0:T(8,128)(2,1)}, bf16[256,2048]{1,0:T(8,128)(2,1)}, u32[]{:S(2)}, u32[]{:S(2)}) collective-permute-start(bf16[256,2048]{1,0:T(8,128)(2,1)} %get-tuple-element.301), channel_id=1, source_target_pairs={{0,3},{1,2},{2,1},{3,0},{4,7},{5,6},{6,5},{7,4},{8,11},{9,10},{10,... | collective-permute-start | bytes 3145736 | tf_op jit(solution)/shard_map/ppermute | solution.py:763
  381.8 309.7 %all-gather.10.cloned.1.call-start = ((), (), s32[]{:S(2)}) async-start(), calls=%async_computation.10 | async-start | bytes 6488064 | tf_op jit(solution)/shard_map/all_gather | solution.py:988
  387.7 21.4 %collective-permute-start.35 = (bf16[256,2048]{1,0:T(8,128)(2,1)S(1)}, bf16[256,2048]{1,0:T(8,128)(2,1)S(1)}, u32[]{:S(2)}, u32[]{:S(2)}) collective-permute-start(bf16[256,2048]{1,0:T(8,128)(2,1)S(1)} %get-tuple-element.441.refs_4_), channel_id=1, source_target_pairs={{0,1},{1,0},{2,3},{3,2},{4,5},{5,4},{6,7},{7,6},{8,9},{9,8},{10,11... | collective-permute-start | bytes 3145736 | tf_op jit(solution)/shard_map/ppermute | solution.py:763
  390.6 19.4 %collective-permute-start.36 = (bf16[256,2048]{1,0:T(8,128)(2,1)S(1)}, bf16[256,2048]{1,0:T(8,128)(2,1)S(1)}, u32[]{:S(2)}, u32[]{:S(2)}) collective-permute-start(bf16[256,2048]{1,0:T(8,128)(2,1)S(1)} %get-tuple-element.441.refs_4_), channel_id=1, source_target_pairs={{0,2},{1,3},{2,0},{3,1},{4,6},{5,7},{6,4},{7,5},{8,10},{9,11},{10,... | collective-permute-start | bytes 3145736 | tf_op jit(solution)/shard_map/ppermute | solution.py:763
  446.5 254.1 %all-gather.8.cloned.1.call-start = ((), (), s32[]{:S(2)}) async-start(), calls=%async_computation.9 | async-start | bytes 7208960 | tf_op jit(solution)/shard_map/all_gather | solution.py:1013
  468.6 17.8 %collective-permute-start.45 = (bf16[256,512]{1,0:T(8,128)(2,1)}, bf16[256,512]{1,0:T(8,128)(2,1)}, u32[]{:S(2)}, u32[]{:S(2)}) collective-permute-start(bf16[256,512]{1,0:T(8,128)(2,1)} %bitcast.42), channel_id=1, source_target_pairs={{0,1},{1,0},{2,3},{3,2},{4,5},{5,4},{6,7},{7,6},{8,9},{9,8},{10,11... | collective-permute-start | bytes 786440 | tf_op jit(solution)/shard_map/ppermute | solution.py:763
  469.3 20.3 %collective-permute-start.46 = (bf16[256,512]{1,0:T(8,128)(2,1)}, bf16[256,512]{1,0:T(8,128)(2,1)}, u32[]{:S(2)}, u32[]{:S(2)}) collective-permute-start(bf16[256,512]{1,0:T(8,128)(2,1)} %bitcast.43), channel_id=1, source_target_pairs={{0,2},{1,3},{2,0},{3,1},{4,6},{5,7},{6,4},{7,5},{8,10},{9,11},{10,... | collective-permute-start | bytes 786440 | tf_op jit(solution)/shard_map/ppermute | solution.py:763
  471.2 25.8 %collective-permute-start.44 = (bf16[512,512]{1,0:T(8,128)(2,1)}, bf16[512,512]{1,0:T(8,128)(2,1)}, u32[]{:S(2)}, u32[]{:S(2)}) collective-permute-start(bf16[512,512]{1,0:T(8,128)(2,1)} %pad_maximum_fusion.13), channel_id=1, source_target_pairs={{0,2},{1,3},{2,0},{3,1},{4,6},{5,7},{6,4},{7,5},{8,10},{9,11},{10,... | collective-permute-start | bytes 1572872 | tf_op jit(solution)/shard_map/ppermute | solution.py:763
  473.2 23.9 %collective-permute-start.43 = (bf16[512,512]{1,0:T(8,128)(2,1)}, bf16[512,512]{1,0:T(8,128)(2,1)}, u32[]{:S(2)}, u32[]{:S(2)}) collective-permute-start(bf16[512,512]{1,0:T(8,128)(2,1)} %pad_maximum_fusion.12), channel_id=1, source_target_pairs={{0,1},{1,0},{2,3},{3,2},{4,5},{5,4},{6,7},{7,6},{8,9},{9,8},{10,11... | collective-permute-start | bytes 1572872 | tf_op jit(solution)/shard_map/ppermute | solution.py:763
  475.3 19.6 %collective-permute-start.47 = (bf16[128,1024]{1,0:T(8,128)(2,1)}, bf16[128,1024]{1,0:T(8,128)(2,1)}, u32[]{:S(2)}, u32[]{:S(2)}) collective-permute-start(bf16[128,1024]{1,0:T(8,128)(2,1)} %get-tuple-element.497), channel_id=1, source_target_pairs={{0,1},{1,0},{2,3},{3,2},{4,5},{5,4},{6,7},{7,6},{8,9},{9,8},{10,11... | collective-permute-start | bytes 786440 | tf_op jit(solution)/shard_map/ppermute | solution.py:763
  489.7 35.5 %collective-permute-start.57 = (bf16[256,2048]{1,0:T(8,128)(2,1)}, bf16[256,2048]{1,0:T(8,128)(2,1)}, u32[]{:S(2)}, u32[]{:S(2)}) collective-permute-start(bf16[256,2048]{1,0:T(8,128)(2,1)} %get-tuple-element.367), channel_id=1, source_target_pairs={{0,1},{1,0},{2,3},{3,2},{4,5},{5,4},{6,7},{7,6},{8,9},{9,8},{10,11... | collective-permute-start | bytes 3145736 | tf_op jit(solution)/shard_map/ppermute | solution.py:763
  494.9 47.6 %collective-permute-start.58 = (bf16[256,2048]{1,0:T(8,128)(2,1)}, bf16[256,2048]{1,0:T(8,128)(2,1)}, u32[]{:S(2)}, u32[]{:S(2)}) collective-permute-start(bf16[256,2048]{1,0:T(8,128)(2,1)} %get-tuple-element.368), channel_id=1, source_target_pairs={{0,2},{1,3},{2,0},{3,1},{4,6},{5,7},{6,4},{7,5},{8,10},{9,11},{10,... | collective-permute-start | bytes 3145736 | tf_op jit(solution)/shard_map/ppermute | solution.py:763
  495.9 49.6 %collective-permute-start.59 = (bf16[256,2048]{1,0:T(8,128)(2,1)}, bf16[256,2048]{1,0:T(8,128)(2,1)}, u32[]{:S(2)}, u32[]{:S(2)}) collective-permute-start(bf16[256,2048]{1,0:T(8,128)(2,1)} %get-tuple-element.369), channel_id=1, source_target_pairs={{0,3},{1,2},{2,1},{3,0},{4,7},{5,6},{6,5},{7,4},{8,11},{9,10},{10,... | collective-permute-start | bytes 3145736 | tf_op jit(solution)/shard_map/ppermute | solution.py:763
  519.9 26.3 %collective-permute-start.49 = (bf16[128,512]{1,0:T(8,128)(2,1)S(1)}, bf16[128,512]{1,0:T(8,128)(2,1)S(1)}, u32[]{:S(2)}, u32[]{:S(2)}) collective-permute-start(bf16[128,512]{1,0:T(8,128)(2,1)S(1)} %get-tuple-element.495), channel_id=1, source_target_pairs={{8,0},{12,4},{16,8},{20,12},{24,16},{28,20},{9,1},{13,5},{17,9},{2... | collective-permute-start | bytes 393224 | tf_op jit(solution)/shard_map/ppermute | solution.py:1020
  521.4 58.4 %collective-permute-start.56 = (bf16[1024,512]{1,0:T(8,128)(2,1)}, bf16[1024,512]{1,0:T(8,128)(2,1)}, u32[]{:S(2)}, u32[]{:S(2)}) collective-permute-start(bf16[1024,512]{1,0:T(8,128)(2,1)} %get-tuple-element.365), channel_id=1, source_target_pairs={{0,4},{4,0},{8,12},{12,8},{16,20},{20,16},{24,28},{28,24},{1,5},{5... | collective-permute-start | bytes 3145736 | tf_op jit(solution)/shard_map/core_swap/ppermute | solution.py:767
  525.2 23.1 %collective-permute-start.50 = (bf16[128,512]{1,0:T(8,128)(2,1)S(1)}, bf16[128,512]{1,0:T(8,128)(2,1)S(1)}, u32[]{:S(2)}, u32[]{:S(2)}) collective-permute-start(bf16[128,512]{1,0:T(8,128)(2,1)S(1)} %get-tuple-element.494), channel_id=1, source_target_pairs={{16,0},{20,4},{24,8},{28,12},{17,1},{21,5},{25,9},{29,13},{18,2},{... | collective-permute-start | bytes 393224 | tf_op jit(solution)/shard_map/ppermute | solution.py:1020
  542.6 24.4 %collective-permute-start.51 = (bf16[128,512]{1,0:T(8,128)(2,1)S(1)}, bf16[128,512]{1,0:T(8,128)(2,1)S(1)}, u32[]{:S(2)}, u32[]{:S(2)}) collective-permute-start(bf16[128,512]{1,0:T(8,128)(2,1)S(1)} %get-tuple-element.493), channel_id=1, source_target_pairs={{24,0},{28,4},{25,1},{29,5},{26,2},{30,6},{27,3},{31,7}} | collective-permute-start | bytes 393224 | tf_op jit(solution)/shard_map/ppermute | solution.py:1020
  545.5 28.7 %collective-permute-start.55 = (bf16[256,1024]{1,0:T(8,128)(2,1)}, bf16[256,1024]{1,0:T(8,128)(2,1)}, u32[]{:S(2)}, u32[]{:S(2)}) collective-permute-start(bf16[256,1024]{1,0:T(8,128)(2,1)} %pad_maximum_fusion.17), channel_id=1, source_target_pairs={{0,2},{1,3},{2,0},{3,1},{4,6},{5,7},{6,4},{7,5},{8,10},{9,11},{10,... | collective-permute-start | bytes 1572872 | tf_op jit(solution)/shard_map/ppermute | solution.py:763
  546.3 28.0 %collective-permute-start.54 = (bf16[256,1024]{1,0:T(8,128)(2,1)}, bf16[256,1024]{1,0:T(8,128)(2,1)}, u32[]{:S(2)}, u32[]{:S(2)}) collective-permute-start(bf16[256,1024]{1,0:T(8,128)(2,1)} %pad_maximum_fusion.16), channel_id=1, source_target_pairs={{0,1},{1,0},{2,3},{3,2},{4,5},{5,4},{6,7},{7,6},{8,9},{9,8},{10,11... | collective-permute-start | bytes 1572872 | tf_op jit(solution)/shard_map/ppermute | solution.py:763
  548.3 25.9 %collective-permute-start.53 = (bf16[512,512]{1,0:T(8,128)(2,1)}, bf16[512,512]{1,0:T(8,128)(2,1)}, u32[]{:S(2)}, u32[]{:S(2)}) collective-permute-start(bf16[512,512]{1,0:T(8,128)(2,1)} %pad_maximum_fusion.15), channel_id=1, source_target_pairs={{0,2},{1,3},{2,0},{3,1},{4,6},{5,7},{6,4},{7,5},{8,10},{9,11},{10,... | collective-permute-start | bytes 1572872 | tf_op jit(solution)/shard_map/ppermute | solution.py:763
  584.0 42.8 %collective-permute-start.63 = (bf16[256,1024]{1,0:T(8,128)(2,1)}, bf16[256,1024]{1,0:T(8,128)(2,1)}, u32[]{:S(2)}, u32[]{:S(2)}) collective-permute-start(bf16[256,1024]{1,0:T(8,128)(2,1)} %subtract_convert_fusion.refs_4_), channel_id=1, source_target_pairs={{0,1},{1,0},{2,3},{3,2},{4,5},{5,4},{6,7},{7,6},{8,9},{9,8},{10,11... | collective-permute-start | bytes 1572872 | tf_op jit(solution)/shard_map/ppermute | solution.py:763
  585.7 41.0 %collective-permute-start.64 = (bf16[256,1024]{1,0:T(8,128)(2,1)}, bf16[256,1024]{1,0:T(8,128)(2,1)}, u32[]{:S(2)}, u32[]{:S(2)}) collective-permute-start(bf16[256,1024]{1,0:T(8,128)(2,1)} %subtract_convert_fusion.refs_4_), channel_id=1, source_target_pairs={{0,2},{1,3},{2,0},{3,1},{4,6},{5,7},{6,4},{7,5},{8,10},{9,11},{10,... | collective-permute-start | bytes 1572872 | tf_op jit(solution)/shard_map/ppermute | solution.py:763
  587.0 21.3 %all-to-all-start.2 = ((bf16[256,4,512]{2,0,1:T(8,128)(2,1)}), bf16[256,4,512]{2,0,1:T(8,128)(2,1)}, u32[]{:S(2)}, u32[]{:S(2)}) async-start(bf16[256,4,512]{2,0,1:T(8,128)(2,1)} %bitcast.208), calls=%async_computation.4 | async-start | bytes 2097152 | tf_op jit(solution)/shard_map/all_to_all | solution.py:1040
  595.0 19.8 %collective-permute-start.60 = (bf16[128,512]{1,0:T(8,128)(2,1)}, bf16[128,512]{1,0:T(8,128)(2,1)}, u32[]{:S(2)}, u32[]{:S(2)}) collective-permute-start(bf16[128,512]{1,0:T(8,128)(2,1)} %get-tuple-element.492), channel_id=1, source_target_pairs={{8,0},{12,4},{16,8},{20,12},{24,16},{28,20},{9,1},{13,5},{17,9},{2... | collective-permute-start | bytes 393224 | tf_op jit(solution)/shard_map/ppermute | solution.py:1020
  596.3 30.5 %collective-permute-start.61 = (bf16[128,512]{1,0:T(8,128)(2,1)}, bf16[128,512]{1,0:T(8,128)(2,1)}, u32[]{:S(2)}, u32[]{:S(2)}) collective-permute-start(bf16[128,512]{1,0:T(8,128)(2,1)} %get-tuple-element.491), channel_id=1, source_target_pairs={{16,0},{20,4},{24,8},{28,12},{17,1},{21,5},{25,9},{29,13},{18,2},{... | collective-permute-start | bytes 393224 | tf_op jit(solution)/shard_map/ppermute | solution.py:1020
  597.6 29.2 %collective-permute-start.62 = (bf16[128,512]{1,0:T(8,128)(2,1)}, bf16[128,512]{1,0:T(8,128)(2,1)}, u32[]{:S(2)}, u32[]{:S(2)}) collective-permute-start(bf16[128,512]{1,0:T(8,128)(2,1)} %get-tuple-element.490), channel_id=1, source_target_pairs={{24,0},{28,4},{25,1},{29,5},{26,2},{30,6},{27,3},{31,7}} | collective-permute-start | bytes 393224 | tf_op jit(solution)/shard_map/ppermute | solution.py:1020
  608.3 54.0 %all-to-all-start.3 = ((bf16[4,256,512]{2,1,0:T(8,128)(2,1)}), bf16[4,256,512]{2,1,0:T(8,128)(2,1)}, u32[]{:S(2)}, u32[]{:S(2)}) async-start(bf16[4,256,512]{2,1,0:T(8,128)(2,1)} %bitcast.207), calls=%async_computation.5 | async-start | bytes 2097152 | tf_op jit(solution)/shard_map/all_to_all | solution.py:1047
  612.5 176.2 %reduce-scatter.8.cloned.1.call-start = ((), (), s32[]{:S(2)}) async-start(), calls=%async_computation.11 | async-start | bytes 9142272 | tf_op jit(solution)/shard_map/reduce_scatter | solution.py:1109
  691.5 177.2 %all-gather.12.cloned.1.call-start = ((), (), s32[]{:S(2)}) async-start(), calls=%async_computation.12 | async-start | bytes 9142272 | tf_op jit(solution)/shard_map/all_gather | solution.py:1118
  704.7 34.4 %collective-permute-start.65 = (bf16[256,2816]{1,0:T(8,128)(2,1)S(1)}, bf16[256,2816]{1,0:T(8,128)(2,1)S(1)}, u32[]{:S(2)}, u32[]{:S(2)}) collective-permute-start(bf16[256,2816]{1,0:T(8,128)(2,1)S(1)} %get-tuple-element.450), channel_id=1, source_target_pairs={{0,1},{1,0},{2,3},{3,2},{4,5},{5,4},{6,7},{7,6},{8,9},{9,8},{10,11... | collective-permute-start | bytes 4325384 | tf_op jit(solution)/shard_map/ppermute | solution.py:763
  706.2 64.2 %collective-permute-start.66 = (bf16[256,2816]{1,0:T(8,128)(2,1)S(1)}, bf16[256,2816]{1,0:T(8,128)(2,1)S(1)}, u32[]{:S(2)}, u32[]{:S(2)}) collective-permute-start(bf16[256,2816]{1,0:T(8,128)(2,1)S(1)} %get-tuple-element.449), channel_id=1, source_target_pairs={{0,2},{1,3},{2,0},{3,1},{4,6},{5,7},{6,4},{7,5},{8,10},{9,11},{10,... | collective-permute-start | bytes 4325384 | tf_op jit(solution)/shard_map/ppermute | solution.py:763
  707.6 63.8 %collective-permute-start.67 = (bf16[256,2816]{1,0:T(8,128)(2,1)S(1)}, bf16[256,2816]{1,0:T(8,128)(2,1)}, u32[]{:S(2)}, u32[]{:S(2)}) collective-permute-start(bf16[256,2816]{1,0:T(8,128)(2,1)S(1)} %get-tuple-element.448), channel_id=1, source_target_pairs={{0,3},{1,2},{2,1},{3,0},{4,7},{5,6},{6,5},{7,4},{8,11},{9,10},{10,... | collective-permute-start | bytes 4325384 | tf_op jit(solution)/shard_map/ppermute | solution.py:763
  788.8 16.6 %collective-permute-start.74 = (bf16[256,2816]{1,0:T(8,128)(2,1)}, bf16[256,2816]{1,0:T(8,128)(2,1)}, u32[]{:S(2)}, u32[]{:S(2)}) collective-permute-start(bf16[256,2816]{1,0:T(8,128)(2,1)} %get-tuple-element.416.refs_0_), channel_id=1, source_target_pairs={{0,4},{4,0},{8,12},{12,8},{16,20},{20,16},{24,28},{28,24},{1,5},{5... | collective-permute-start | bytes 4325384 | tf_op jit(solution)/shard_map/core_swap/ppermute | solution.py:767
  788.9 16.5 %collective-permute-start.75 = (bf16[256,2816]{1,0:T(8,128)(2,1)}, bf16[256,2816]{1,0:T(8,128)(2,1)}, u32[]{:S(2)}, u32[]{:S(2)}) collective-permute-start(bf16[256,2816]{1,0:T(8,128)(2,1)} %copy-done.43), channel_id=1, source_target_pairs={{0,4},{4,0},{8,12},{12,8},{16,20},{20,16},{24,28},{28,24},{1,5},{5... | collective-permute-start | bytes 4325384 | tf_op jit(solution)/shard_map/core_swap/ppermute | solution.py:767
  789.4 16.0 %collective-permute-start.76 = (bf16[256,2816]{1,0:T(8,128)(2,1)}, bf16[256,2816]{1,0:T(8,128)(2,1)}, u32[]{:S(2)}, u32[]{:S(2)}) collective-permute-start(bf16[256,2816]{1,0:T(8,128)(2,1)} %copy-done.44), channel_id=1, source_target_pairs={{0,4},{4,0},{8,12},{12,8},{16,20},{20,16},{24,28},{28,24},{1,5},{5... | collective-permute-start | bytes 4325384 | tf_op jit(solution)/shard_map/core_swap/ppermute | solution.py:767
  789.5 15.9 %collective-permute-start.77 = (bf16[256,2816]{1,0:T(8,128)(2,1)}, bf16[256,2816]{1,0:T(8,128)(2,1)}, u32[]{:S(2)}, u32[]{:S(2)}) collective-permute-start(bf16[256,2816]{1,0:T(8,128)(2,1)} %collective-permute-done.67.refs_3_), channel_id=1, source_target_pairs={{0,4},{4,0},{8,12},{12,8},{16,20},{20,16},{24,28},{28,24},{1,5},{5... | collective-permute-start | bytes 4325384 | tf_op jit(solution)/shard_map/core_swap/ppermute | solution.py:767
  (127 other events, 1060.4 us)
Sparse Core Ops, SparseCore 0:
  22.1 29.0 all-gather.13
  101.3 108.3 all-gather.15
  328.3 65.2 reduce-scatter.3
  396.3 117.6 reduce-scatter.5
  515.5 67.5 all-gather.9
  584.5 116.0 all-gather.7
  703.4 85.2 reduce-scatter.7
  790.4 78.2 all-gather.11

commit v6 on v5

--- a/solution.py
+++ b/solution.py
@@ -886,16 +886,21 @@
         gu = turn(gu_share, gu_cols)
         kv_line, norm_got, gu = fence(kv_line, norm_got, gu)
         gu = lax.all_gather(gu, "ctx")
-        kv_mine = stack_rows([kv_own] + kv_line)
-        kv_got = gather_first(kv_mine)
+        kv_parts_own = [kv_own] + kv_line
+        if square:
+            kv_halves = [stack_rows(kv_parts_own[: nz // 2]), stack_rows(kv_parts_own[nz // 2 :])]
+            kv_got = [[swap(x, j) for x in kv_halves] for j in (1, 2)]
+        else:
+            kv_halves = [stack_rows(kv_parts_own)]
+            kv_got = [[swap(kv_halves[0], j)] for j in range(1, nf)]
         norm_more = gather_second(norm_got)
         kv_got, norm_more, qb = fence(kv_got, norm_more, qb)
         qb = column_slice(qb)
-        kv_more = gather_second(kv_got)
+        kv_more = [swap(kv_got[1][0], 1), swap(kv_got[0][1], 2)] if square else []
         norm_blocks = gather_done(query_norm, norm_got, norm_more)
         queries = dot(jnp.concatenate(norm_blocks, axis=0), qb).reshape(nf, seqs, span, head_cols)
         kv_more, queries, signal_low = fence(kv_more, queries, signal_low)
-        kv_near = jnp.concatenate(gather_done(kv_mine, kv_got, kv_more), axis=0)
+        kv_near = stack_rows(kv_halves + [x for got in kv_got for x in got] + kv_more)
         kv_far = core_swap(kv_near)
         signal_got = [swap(signal_low, j) for j in range(1, nf)]
         kv_near = kv_near.reshape(nf, nz, seqs, span, 2 * HD)

time: 899 us -> 902 us (level)
  local copies, waits for them, and re-layouts: 90.7 us -> 73.7 us
  starting transfers between devices: 105 us -> 118 us
    unnamed x217 -> x215, local copies, waits for them, and re-layouts: 36.4 us -> 23.8 us
    ppermute x58 -> x60, starting transfers between devices: 65.7 us -> 78 us  [swap(): return lax.ppermute(x, 'fsdp', [(i, i ^ j) for i in range(nf)])]
    ppermute x58 -> x60, waiting for transfers between devices: 228 us -> 230 us  [swap(): return lax.ppermute(x, 'fsdp', [(i, i ^ j) for i in range(nf)])]
  transfers between devices with their start and end apart: 90 -> 92, of which waited for: 41 -> 42; matrix products, arithmetic and copies ran while one was open for 18% -> 17% of each run, Pallas kernels for 20% -> 20%
where the time goes in v6:
time: 902 us; the launch traced here: 895 us
  waiting for transfers between devices  372 us (41%)
  Pallas kernels  214 us (24%)
  starting transfers between devices  118 us (13%)
  other arithmetic  77.1 us (9%)
  local copies, waits for them, and re-layouts  73.7 us (8%)
  matrix products  24.2 us (3%)
  between operations  16.2 us (2%)
    ppermute x60, waiting for transfers between devices, swap(): return lax.ppermute(x, 'fsdp', [(i, i ^ j) for i in range(nf)])  230 us
    ppermute x60, starting transfers between devices, swap(): return lax.ppermute(x, 'fsdp', [(i, i ^ j) for i in range(nf)])  78 us
    pallas_call x3, Pallas kernels, feed_forward(): pl.pallas_call(kernel, grid=(steps,), in_specs=[piece] * pieces + [whole]...  64.1 us
    all_gather x1, waiting for transfers between devices, on_device(): buffer = lax.all_gather(buffer_share, 'ctx', tiled=True)  45.5 us
    pallas_call x4, Pallas kernels, token_sum(): pl.pallas_call(kernel, grid=(height // tile,), in_specs=[pl.BlockSpec((to...  45.5 us
    ppermute x6, waiting for transfers between devices, line_start(): lax.ppermute(low[s], 'ctx', [(i, i - 2 * s) for i in range(2 * s, nc)])  27.6 us
    unnamed x215, local copies, waits for them, and re-layouts  23.8 us
    pallas_call x2, Pallas kernels, attend_backward(): pl.pallas_call(kernel, grid_spec=pltpu.PrefetchScalarGridSpec(num_scalar_...  21.9 us
  transfers between devices with their start and end apart: 92, of which 42 were waited for; matrix products, arithmetic and copies ran while one was open for 17% of the time, Pallas kernels for 20%

profile of v6, /device:TPU:0, one launch (start us, length us, event | category | flops | bytes accessed | tf_op | source)
XLA Modules:
  0.0 895.1 jit_solution(14875148948563785301)
XLA Ops:
  9.5 5.2 all-to-all-start.1
  24.6 13.6 %collective-permute-done.1.refs_1_ = bf16[272,1536]{1,0:T(8,128)(2,1)} collective-permute-done((bf16[272,1536]{1,0:T(8,128)(2,1)}, bf16[272,1536]{1,0:T(8,128)(2,1)}, u32[]{:S(2)}, u32[]{:S(2)}) %collective-permute-start.1) | collective-permute-done | bytes 835616 | tf_op jit(solution)/shard_map/ppermute | solution.py:763
  47.2 3.6 collective-permute-done.2
  58.6 6.6 project.1
  66.4 3.7 all-to-all-start
  73.6 3.5 collective-permute-start.7
  77.0 4.5 collective-permute-start.8
  83.7 5.7 collective-permute-done.8.refs_0_
  89.3 4.3 collective-permute-done.9.refs_1_
  93.6 6.4 collective-permute-done.10.refs_1_
  112.8 23.1 %collective-permute-done.16 = bf16[128,1024]{1,0:T(8,128)(2,1)S(1)} collective-permute-done((bf16[128,1024]{1,0:T(8,128)(2,1)S(1)}, bf16[128,1024]{1,0:T(8,128)(2,1)S(1)}, u32[]{:S(2)}, u32[]{:S(2)}) %collective-permute-start.16) | collective-permute-done | bytes 262176 | tf_op jit(solution)/shard_map/ppermute | solution.py:763
  137.5 5.5 collective-permute-done.17
  147.9 4.4 fusion.67.q_ref
  152.3 5.7 collective-permute-done.18.refs_6_
  159.1 4.4 stack_rows.5
  167.0 4.0 collective-permute-done.20
  171.0 14.7 %attend_forward.1 = (bf16[4,64,1024]{2,1,0:T(8,128)(2,1)}, bf16[4,64,1024]{2,1,0:T(8,128)(2,1)}, bf16[4,64,1024]{2,1,0:T(8,128)(2,1)}, bf16[4,64,1024]{2,1,0:T(8...) custom-call(s32[7]{0:T(128)} %pad_add_fusion.info_ref, f32[4,4,64,1024]{3,2,1,0:T(8,128)} %fusion.67.q_ref, ...), custom_call_target="tpu_custom_call" | custom-call | flops 1 | bytes 1 | tf_op jit(solution)/shard_map/attend_forward/pallas_call | solution.py:148
  185.8 3.8 convolution_convert_fusion
  194.8 17.3 %collective-permute-done.24.refs_5_.refs_6_ = bf16[256,2048]{1,0:T(8,128)(2,1)} collective-permute-done((bf16[256,2048]{1,0:T(8,128)(2,1)S(1)}, bf16[256,2048]{1,0:T(8,128)(2,1)}, u32[]{:S(2)}, u32[]{:S(2)}) %collective-permute-start.24) | collective-permute-done | bytes 1048608 | tf_op jit(solution)/shard_map/ppermute | solution.py:763
  212.6 10.3 %collective-permute-done.21 = bf16[128,2048]{1,0:T(8,128)(2,1)S(1)} collective-permute-done((bf16[128,2048]{1,0:T(8,128)(2,1)S(1)}, bf16[128,2048]{1,0:T(8,128)(2,1)S(1)}, u32[]{:S(2)}, u32[]{:S(2)}) %collective-permute-start.21) | collective-permute-done | bytes 524320 | tf_op jit(solution)/shard_map/ppermute | solution.py:763
  227.3 2.6 fusion.70
  229.9 19.1 %collective-permute-done.27 = bf16[256,2048]{1,0:T(8,128)(2,1)S(1)} collective-permute-done((bf16[256,2048]{1,0:T(8,128)(2,1)S(1)}, bf16[256,2048]{1,0:T(8,128)(2,1)S(1)}, u32[]{:S(2)}, u32[]{:S(2)}) %collective-permute-start.27) | collective-permute-done | bytes 1048608 | tf_op jit(solution)/shard_map/ppermute | solution.py:763
  251.0 2.8 multiply_reduce_fusion.2
  259.1 18.0 %feed_forward.3 = (bf16[256,1408]{1,0:T(8,128)(2,1)}, bf16[256,1408]{1,0:T(8,128)(2,1)}, bf16[256,1408]{1,0:T(8,128)(2,1)}, f32[256,2048]{1,0:T(8,128)}, f32[256,2048]{1,0:T(8,128)}, /*index=5*/bf16[256,2048]{1,0:T(8,128)(2,1)}) custom-call(bf16[128,2048]{1,0:T(8,128)(2,1)} %get-tuple-element.487.refs_0_, bf16[128,2048]{1,0:T(8,128)(2,1)} %get-tuple-element.486.refs_1_, ...), custom_call_target="tpu_custom_call" | custom-call | flops 1 | bytes 1 | tf_op jit(solution)/shard_map/feed_forward/pallas_call | solution.py:370
  283.0 29.1 %feed_forward.4 = (bf16[256,1408]{1,0:T(8,128)(2,1)}, bf16[256,1408]{1,0:T(8,128)(2,1)}, bf16[256,1408]{1,0:T(8,128)(2,1)}, bf16[256,1408]{1,0:T(8,128)(2,1)}, b...) custom-call(bf16[128,2048]{1,0:T(8,128)(2,1)} %collective-permute-do, ...), custom_call_target="tpu_custom_call" | custom-call | flops 1 | bytes 1 | tf_op jit(solution)/shard_map/feed_forward/pallas_call | solution.py:370
  312.1 10.0 %hidden_units.1 = (bf16[256,1408]{1,0:T(8,128)(2,1)}, bf16[256,2048]{1,0:T(8,128)(2,1)}) custom-call(bf16[128,2048]{1,0:T(8,128)(2,1)} %collective-permute-done.32.refs_0_, bf16[128,2048]{1,0:T(8,128)(2,1)} %collective-permute-done.33.refs_1_, bf16[8,4,64,2816]{3,2,1,0:T(8,128)(2,1)} %bitcast.181, bf16[8,4,64,2816]{3,2,1,0:T(8,128)(2,1)} %bitcast.182, ...), custom_call_target="tpu_custom_call" | custom-call | flops 1 | bytes 1 | tf_op jit(solution)/shard_map/hidden_units/pallas_call | solution.py:443
  322.2 13.4 %token_sum.4 = bf16[1408,2048]{1,0:T(8,128)(2,1)} custom-call(bf16[256,1408]{1,0:T(8,128)(2,1)} %get-tuple-element.281.refs_0_, bf16[256,1408]{1,0:T(8,128)(2,1)} %get-tuple-element.282.refs_1_, bf16[256,1408]{1,0:T(8,128)(2,1)} %get-tuple-element.283.refs_2_, bf16[256,1408]{1,0:T(8,128)(2,1)} %get-tuple-element.284.refs_3_, bf16[256,2048]{1,0:T(8,128)(2,1)} %copy-done.15, ...), custom_call_target="tpu_custom_call" | custom-call | flops 5905580032 | bytes 5767168 | tf_op jit(solution)/shard_map/token_sum/pallas_call | solution.py:610
  338.1 17.0 %feed_forward.5 = (bf16[256,1408]{1,0:T(8,128)(2,1)}, bf16[256,1408]{1,0:T(8,128)(2,1)}, bf16[256,1408]{1,0:T(8,128)(2,1)}, bf16[256,2048]{1,0:T(8,128)(2,1)}, b...) custom-call(bf16[256,2048]{1,0:T(8,128)(2,1)} %get-tuple-element.287.refs_0_, bf16[256,2048]{1,0:T(8,128)(2,1)} %copy-done.49, ...), custom_call_target="tpu_custom_call" | custom-call | flops 1 | bytes 1 | tf_op jit(solution)/shard_map/feed_forward/pallas_call | solution.py:370
  355.1 3.1 collective-permute-done.34
  359.3 12.9 %collective-permute-start.36 = (bf16[256,2048]{1,0:T(8,128)(2,1)}, bf16[256,2048]{1,0:T(8,128)(2,1)}, u32[]{:S(2)}, u32[]{:S(2)}) collective-permute-start(bf16[256,2048]{1,0:T(8,128)(2,1)} %get-tuple-element.305), channel_id=1, source_target_pairs={{0,3},{1,2},{2,1},{3,0},{4,7},{5,6},{6,5},{7,4},{8,11},{9,10},{10,... | collective-permute-start | bytes 3145736 | tf_op jit(solution)/shard_map/ppermute | solution.py:763
  372.1 19.1 %token_sum.5 = bf16[2048,2816]{1,0:T(8,128)(2,1)} custom-call(bf16[256,2048]{1,0:T(8,128)(2,1)} %get-tuple-element.306.refs_0_, bf16[256,2048]{1,0:T(8,128)(2,1)} %get-tuple-element.307.refs_1_, bf16[256,2048]{1,0:T(8,128)(2,1)} %get-tuple-element.308.refs_2_, bf16[256,2048]{1,0:T(8,128)(2,1)} %get-tuple-element.309.refs_3_, ...), custom_call_target="tpu_custom_call" | custom-call | flops 11811160064 | bytes 5767168 | tf_op jit(solution)/shard_map/token_sum/pallas_call | solution.py:610
  391.3 3.7 multiply_reduce_fusion
  399.4 17.7 %collective-permute-done.37.refs_5_ = bf16[256,2048]{1,0:T(8,128)(2,1)S(1)} collective-permute-done((bf16[256,2048]{1,0:T(8,128)(2,1)S(1)}, bf16[256,2048]{1,0:T(8,128)(2,1)S(1)}, u32[]{:S(2)}, u32[]{:S(2)}) %collective-permute-start.37) | collective-permute-done | bytes 1048608 | tf_op jit(solution)/shard_map/ppermute | solution.py:763
  422.4 4.9 collective-permute-done.39
  432.2 11.2 %attend_backward.2 = (bf16[4,2,64,1024]{3,2,1,0:T(8,128)(2,1)}, bf16[4,4,2,64,512]{4,3,2,1,0:T(8,128)(2,1)}, bf16[4,4,2,64,512]{4,3,2,1,0:T(8,128)(2,1)}) custom-call(s32[7]{0:T(128)} %pad_add_fusion.info_ref, bf16[4,64,1024]{2,1,0:T(8,128)(2,1)} %get-tuple-element.257.refs_0_, bf16[4,64,1024]{2,1,0:T(8,128)(2,1)} %get-tuple-element.250.refs_1_, ...), custom_call_target="tpu_custom_call" | custom-call | flops 1 | bytes 1 | tf_op jit(solution)/shard_map/attend_backward/pallas_call | solution.py:245
  443.5 10.7 %attend_backward.3 = (bf16[4,2,64,1024]{3,2,1,0:T(8,128)(2,1)}, bf16[4,4,2,64,512]{4,3,2,1,0:T(8,128)(2,1)}, bf16[4,4,2,64,512]{4,3,2,1,0:T(8,128)(2,1)}) custom-call(s32[7]{0:T(128)} %pad_add_fusion.info_ref, bf16[4,64,1024]{2,1,0:T(8,128)(2,1)} %get-tuple-element.257.refs_0_, bf16[4,64,1024]{2,1,0:T(8,128)(2,1)} %get-tuple-element.250.refs_1_, ...), custom_call_target="tpu_custom_call" | custom-call | flops 1 | bytes 1 | tf_op jit(solution)/shard_map/attend_backward/pallas_call | solution.py:245
  459.3 2.6 fusion.47
  472.2 3.0 convert_add_fusion
  484.7 9.6 %token_grad.1 = (bf16[1024,512]{1,0:T(8,128)(2,1)}, bf16[1024,512]{1,0:T(8,128)(2,1)}) custom-call(s32[7]{0:T(128)} %pad_add_fusion.info_ref, bf16[256,1024]{1,0:T(8,128)(2,1)} %get-tuple-element.354.refs_0_, bf16[256,1024]{1,0:T(8,128)(2,1)} %copy-done.43, bf16[256,1024]{1,0:T(8,128)(2,1)} %copy-done.45, bf16[256,1024]{1,0:T(8,128)(2,1)} %pad_maximum_fusion.11.refs_3_, ...), custom_call_target="tpu_custom_call" | custom-call | flops 2147483648 | bytes 2097152 | tf_op jit(solution)/shard_map/token_grad/pallas_call | solution.py:523
  498.7 3.9 collective-permute-done.49
  505.0 16.5 %reduce-scatter.6.cloned.1.call-done = bf16[256,2816]{1,0:T(8,128)(2,1)} async-done(((bf16[2048,2816]{1,0:T(8,128)(2,1)}), bf16[256,2816]{1,0:T(8,128)(2,1)}) %reduce-scatter.6.cloned.1.call-update) | async-done | bytes 1441808 | tf_op jit(solution)/shard_map/reduce_scatter | solution.py:966
  523.4 2.9 fusion.51
  534.0 15.6 %collective-permute-done.60 = bf16[256,2048]{1,0:T(8,128)(2,1)} collective-permute-done((bf16[256,2048]{1,0:T(8,128)(2,1)}, bf16[256,2048]{1,0:T(8,128)(2,1)}, u32[]{:S(2)}, u32[]{:S(2)}) %collective-permute-start.60) | collective-permute-done | bytes 1048608 | tf_op jit(solution)/shard_map/ppermute | solution.py:763
  555.6 13.8 %collective-permute-done.53 = bf16[128,512]{1,0:T(8,128)(2,1)S(1)} collective-permute-done((bf16[128,512]{1,0:T(8,128)(2,1)S(1)}, bf16[128,512]{1,0:T(8,128)(2,1)S(1)}, u32[]{:S(2)}, u32[]{:S(2)}) %collective-permute-start.53) | collective-permute-done | bytes 131104 | tf_op jit(solution)/shard_map/ppermute | solution.py:1025
  586.3 4.2 all-to-all-start.2
  590.6 2.9 fusion.49
  601.7 3.6 all-to-all-done.2
  605.3 4.3 all-to-all-start.3
  611.8 13.8 %collective-permute-done.63 = bf16[128,512]{1,0:T(8,128)(2,1)} collective-permute-done((bf16[128,512]{1,0:T(8,128)(2,1)}, bf16[128,512]{1,0:T(8,128)(2,1)}, u32[]{:S(2)}, u32[]{:S(2)}) %collective-permute-start.63) | collective-permute-done | bytes 131104 | tf_op jit(solution)/shard_map/ppermute | solution.py:1025
  629.5 6.3 project_back.1
  646.3 3.3 collective-permute-done.71
  656.0 4.2 token_sum.6
  666.9 8.8 token_sum.7
  678.6 3.3 slice_dynamic-update-slice_fusion.1
  690.3 15.2 %all-gather.8.cloned.1.call-done = bf16[1024,2816]{1,0:T(8,128)(2,1)} async-done(((bf16[256,2816]{1,0:T(8,128)(2,1)}), bf16[1024,2816]{1,0:T(8,128)(2,1)}) %all-gather.8.cloned.1.call-update) | async-done | bytes 5767184 | tf_op jit(solution)/shard_map/all_gather | solution.py:1018
  705.5 4.1 dynamic-slice_bitcast_fusion
  713.1 30.9 %collective-permute-done.67.refs_1_ = bf16[256,2816]{1,0:T(8,128)(2,1)S(1)} collective-permute-done((bf16[256,2816]{1,0:T(8,128)(2,1)S(1)}, bf16[256,2816]{1,0:T(8,128)(2,1)S(1)}, u32[]{:S(2)}, u32[]{:S(2)}) %collective-permute-start.67) | collective-permute-done | bytes 1441824 | tf_op jit(solution)/shard_map/ppermute | solution.py:763
  744.1 31.3 %collective-permute-done.68.refs_2_ = bf16[256,2816]{1,0:T(8,128)(2,1)S(1)} collective-permute-done((bf16[256,2816]{1,0:T(8,128)(2,1)S(1)}, bf16[256,2816]{1,0:T(8,128)(2,1)S(1)}, u32[]{:S(2)}, u32[]{:S(2)}) %collective-permute-start.68) | collective-permute-done | bytes 1441824 | tf_op jit(solution)/shard_map/ppermute | solution.py:763
  776.5 17.3 %reduce-scatter.8.cloned.1.call-done = bf16[496,1024]{1,0:T(8,128)(2,1)} async-done(((bf16[3968,1024]{1,0:T(8,128)(2,1)}), bf16[496,1024]{1,0:T(8,128)(2,1)}) %reduce-scatter.8.cloned.1.call-update) | async-done | bytes 1015824 | tf_op jit(solution)/shard_map/reduce_scatter | solution.py:1114
  795.0 4.4 add_convert_fusion.1
  801.0 9.5 %convert_element_type.344 = f32[1408,2048]{1,0:T(8,128)} convert(bf16[1408,2048]{1,0:T(8,128)(2,1)} %all-gather.10.cloned.1.call-done) | non-fusion elementwise | flops 2883584 | bytes 17301504 | tf_op jit(solution)/shard_map/convert_element_type | solution.py:1126
  810.5 17.8 %place_columns.1 = (f32[512,5632]{1,0:T(8,128)}, f32[512,5632]{1,0:T(8,128)}) custom-call(s32[7]{0:T(128)} %pad_add_fusion.info_ref, bf16[256,2816]{1,0:T(8,128)(2,1)} %get-tuple-element.420.refs_0_, bf16[256,2816]{1,0:T(8,128)(2,1)} %copy-done.39, bf16[256,2816]{1,0:T(8,128)(2,1)} %copy-done.40, bf16[256,2816]{1,0:T(8,128)(2,1)} %collective-permute-done.69.refs_3_, ...), custom_call_target="tpu_custom_call" | custom-call | flops 1 | bytes 1 | tf_op jit(solution)/shard_map/place_columns/pallas_call | solution.py:747
  828.3 45.5 %all-gather.12.cloned.1.call-done.o0_ref.o1_ref.refs_0_.refs_1_.refs_2_.refs_3_.refs_4_ = bf16[3968,1024]{1,0:T(8,128)(2,1)} async-done(((bf16[496,1024]{1,0:T(8,128)(2,1)}), bf16[3968,1024]{1,0:T(8,128)(2,1)}) %all-gather.12.cloned.1.call-update) | async-done | bytes 8126480 | tf_op jit(solution)/shard_map/all_gather | solution.py:1123
  876.0 8.6 unpack.1
  (526 shorter events, 226.4 us)
Async XLA Ops:
  14.7 128.4 %all-gather.14.cloned.1.call-start = ((), (), s32[]{:S(2)}) async-start(), calls=%async_computation.13 | async-start | bytes 2359296 | tf_op jit(solution)/shard_map/all_gather | solution.py:856
  16.1 25.2 %collective-permute-start = (bf16[272,1536]{1,0:T(8,128)(2,1)}, bf16[272,1536]{1,0:T(8,128)(2,1)S(1)}, u32[]{:S(2)}, u32[]{:S(2)}) collective-permute-start(bf16[272,1536]{1,0:T(8,128)(2,1)} %pad_maximum_fusion.5), channel_id=1, source_target_pairs={{0,1},{1,0},{2,3},{3,2},{4,5},{5,4},{6,7},{7,6},{8,9},{9,8},{10,11... | collective-permute-start | bytes 2506760 | tf_op jit(solution)/shard_map/ppermute | solution.py:763
  18.1 20.1 %collective-permute-start.1 = (bf16[272,1536]{1,0:T(8,128)(2,1)}, bf16[272,1536]{1,0:T(8,128)(2,1)}, u32[]{:S(2)}, u32[]{:S(2)}) collective-permute-start(bf16[272,1536]{1,0:T(8,128)(2,1)} %pad_maximum_fusion.5), channel_id=1, source_target_pairs={{0,2},{1,3},{2,0},{3,1},{4,6},{5,7},{6,4},{7,5},{8,10},{9,11},{10,... | collective-permute-start | bytes 2506760 | tf_op jit(solution)/shard_map/ppermute | solution.py:763
  66.4 33.7 %all-to-all-start = ((bf16[64,4,2816]{2,0,1:T(8,128)(2,1)}), bf16[64,4,2816]{2,0,1:T(8,128)(2,1)S(1)}, u32[]{:S(2)}, u32[]{:S(2)}) async-start(bf16[64,4,2816]{2,0,1:T(8,128)(2,1)} %bitcast.170), calls=%async_computation | async-start | bytes 2883584 | tf_op jit(solution)/shard_map/all_to_all | solution.py:848
  70.1 179.9 %all-gather.16.cloned.1.call-start = ((), (), s32[]{:S(2)}) async-start(), calls=%async_computation.14 | async-start | bytes 12976128 | tf_op jit(solution)/shard_map/all_gather | solution.py:888
  70.2 29.9 %collective-permute-start.10 = (bf16[256,1024]{1,0:T(8,128)(2,1)S(1)}, bf16[256,1024]{1,0:T(8,128)(2,1)S(1)}, u32[]{:S(2)}, u32[]{:S(2)}) collective-permute-start(bf16[256,1024]{1,0:T(8,128)(2,1)S(1)} %copy-done.69), channel_id=1, source_target_pairs={{0,1},{1,0},{2,3},{3,2},{4,5},{5,4},{6,7},{7,6},{8,9},{9,8},{10,11... | collective-permute-start | bytes 1572872 | tf_op jit(solution)/shard_map/ppermute | solution.py:763
  72.1 28.0 %collective-permute-start.11 = (bf16[256,1024]{1,0:T(8,128)(2,1)S(1)}, bf16[256,1024]{1,0:T(8,128)(2,1)S(1)}, u32[]{:S(2)}, u32[]{:S(2)}) collective-permute-start(bf16[256,1024]{1,0:T(8,128)(2,1)S(1)} %copy-done.69), channel_id=1, source_target_pairs={{0,2},{1,3},{2,0},{3,1},{4,6},{5,7},{6,4},{7,5},{8,10},{9,11},{10,... | collective-permute-start | bytes 1572872 | tf_op jit(solution)/shard_map/ppermute | solution.py:763
  101.3 352.9 %reduce-scatter.4.cloned.1.call-start = ((), (), s32[]{:S(2)}) async-start(), calls=%async_computation.7 | async-start | bytes 6488064 | tf_op jit(solution)/shard_map/reduce_scatter | solution.py:954
  105.3 37.7 %collective-permute-start.13 = (bf16[512,512]{1,0:T(8,128)(2,1)}, bf16[512,512]{1,0:T(8,128)(2,1)}, u32[]{:S(2)}, u32[]{:S(2)}) collective-permute-start(bf16[512,512]{1,0:T(8,128)(2,1)} %stack_rows.4.refs_1_), channel_id=1, source_target_pairs={{0,1},{1,0},{2,3},{3,2},{4,5},{5,4},{6,7},{7,6},{8,9},{9,8},{10,11... | collective-permute-start | bytes 1572872 | tf_op jit(solution)/shard_map/ppermute | solution.py:763
  106.6 36.4 %collective-permute-start.15 = (bf16[512,512]{1,0:T(8,128)(2,1)}, bf16[512,512]{1,0:T(8,128)(2,1)}, u32[]{:S(2)}, u32[]{:S(2)}) collective-permute-start(bf16[512,512]{1,0:T(8,128)(2,1)} %stack_rows.4.refs_1_), channel_id=1, source_target_pairs={{0,2},{1,3},{2,0},{3,1},{4,6},{5,7},{6,4},{7,5},{8,10},{9,11},{10,... | collective-permute-start | bytes 1572872 | tf_op jit(solution)/shard_map/ppermute | solution.py:763
  109.3 33.8 %collective-permute-start.12 = (bf16[512,512]{1,0:T(8,128)(2,1)}, bf16[512,512]{1,0:T(8,128)(2,1)}, u32[]{:S(2)}, u32[]{:S(2)}) collective-permute-start(bf16[512,512]{1,0:T(8,128)(2,1)} %stack_rows.3.refs_0_), channel_id=1, source_target_pairs={{0,1},{1,0},{2,3},{3,2},{4,5},{5,4},{6,7},{7,6},{8,9},{9,8},{10,11... | collective-permute-start | bytes 1572872 | tf_op jit(solution)/shard_map/ppermute | solution.py:763
  110.7 32.4 %collective-permute-start.14 = (bf16[512,512]{1,0:T(8,128)(2,1)}, bf16[512,512]{1,0:T(8,128)(2,1)}, u32[]{:S(2)}, u32[]{:S(2)}) collective-permute-start(bf16[512,512]{1,0:T(8,128)(2,1)} %stack_rows.3.refs_0_), channel_id=1, source_target_pairs={{0,2},{1,3},{2,0},{3,1},{4,6},{5,7},{6,4},{7,5},{8,10},{9,11},{10,... | collective-permute-start | bytes 1572872 | tf_op jit(solution)/shard_map/ppermute | solution.py:763
  111.3 24.6 %collective-permute-start.16 = (bf16[128,1024]{1,0:T(8,128)(2,1)S(1)}, bf16[128,1024]{1,0:T(8,128)(2,1)S(1)}, u32[]{:S(2)}, u32[]{:S(2)}) collective-permute-start(bf16[128,1024]{1,0:T(8,128)(2,1)S(1)} %slice.360), channel_id=1, source_target_pairs={{0,1},{1,0},{2,3},{3,2},{4,5},{5,4},{6,7},{7,6},{8,9},{9,8},{10,11... | collective-permute-start | bytes 786440 | tf_op jit(solution)/shard_map/ppermute | solution.py:763
  163.5 31.2 %collective-permute-start.23 = (bf16[256,2048]{1,0:T(8,128)(2,1)S(1)}, bf16[256,2048]{1,0:T(8,128)(2,1)}, u32[]{:S(2)}, u32[]{:S(2)}) collective-permute-start(bf16[256,2048]{1,0:T(8,128)(2,1)S(1)} %bitcast_convert_fusion.refs_2_.refs_4_), channel_id=1, source_target_pairs={{0,1},{1,0},{2,3},{3,2},{4,5},{5,4},{6,7},{7,6},{8,9},{9,8},{10,11... | collective-permute-start | bytes 3145736 | tf_op jit(solution)/shard_map/ppermute | solution.py:763
  164.5 47.6 %collective-permute-start.24 = (bf16[256,2048]{1,0:T(8,128)(2,1)S(1)}, bf16[256,2048]{1,0:T(8,128)(2,1)}, u32[]{:S(2)}, u32[]{:S(2)}) collective-permute-start(bf16[256,2048]{1,0:T(8,128)(2,1)S(1)} %bitcast_convert_fusion.refs_2_.refs_4_), channel_id=1, source_target_pairs={{0,2},{1,3},{2,0},{3,1},{4,6},{5,7},{6,4},{7,5},{8,10},{9,11},{10,... | collective-permute-start | bytes 3145736 | tf_op jit(solution)/shard_map/ppermute | solution.py:763
  165.7 46.9 %collective-permute-start.25 = (bf16[256,2048]{1,0:T(8,128)(2,1)S(1)}, bf16[256,2048]{1,0:T(8,128)(2,1)S(1)}, u32[]{:S(2)}, u32[]{:S(2)}) collective-permute-start(bf16[256,2048]{1,0:T(8,128)(2,1)S(1)} %bitcast_convert_fusion.refs_2_.refs_4_), channel_id=1, source_target_pairs={{0,3},{1,2},{2,1},{3,0},{4,7},{5,6},{6,5},{7,4},{8,11},{9,10},{10,... | collective-permute-start | bytes 3145736 | tf_op jit(solution)/shard_map/ppermute | solution.py:763
  189.6 33.2 %collective-permute-start.21 = (bf16[128,2048]{1,0:T(8,128)(2,1)S(1)}, bf16[128,2048]{1,0:T(8,128)(2,1)S(1)}, u32[]{:S(2)}, u32[]{:S(2)}) collective-permute-start(bf16[128,2048]{1,0:T(8,128)(2,1)S(1)} %get-tuple-element.489), channel_id=1, source_target_pairs={{0,1},{1,0},{2,3},{3,2},{4,5},{5,4},{6,7},{7,6},{8,9},{9,8},{10,11... | collective-permute-start | bytes 1572872 | tf_op jit(solution)/shard_map/ppermute | solution.py:763
  191.0 32.5 %collective-permute-start.22 = (bf16[128,2048]{1,0:T(8,128)(2,1)S(1)}, bf16[128,2048]{1,0:T(8,128)(2,1)S(1)}, u32[]{:S(2)}, u32[]{:S(2)}) collective-permute-start(bf16[128,2048]{1,0:T(8,128)(2,1)S(1)} %get-tuple-element.488), channel_id=1, source_target_pairs={{0,2},{1,3},{2,0},{3,1},{4,6},{5,7},{6,4},{7,5},{8,10},{9,11},{10,... | collective-permute-start | bytes 1572872 | tf_op jit(solution)/shard_map/ppermute | solution.py:763
  223.7 25.2 %collective-permute-start.27 = (bf16[256,2048]{1,0:T(8,128)(2,1)S(1)}, bf16[256,2048]{1,0:T(8,128)(2,1)S(1)}, u32[]{:S(2)}, u32[]{:S(2)}) collective-permute-start(bf16[256,2048]{1,0:T(8,128)(2,1)S(1)} %pad_maximum_fusion.4), channel_id=1, source_target_pairs={{0,2},{1,3},{2,0},{3,1},{4,6},{5,7},{6,4},{7,5},{8,10},{9,11},{10,... | collective-permute-start | bytes 3145736 | tf_op jit(solution)/shard_map/ppermute | solution.py:763
  225.3 24.7 %collective-permute-start.26 = (bf16[256,2048]{1,0:T(8,128)(2,1)S(1)}, bf16[256,2048]{1,0:T(8,128)(2,1)S(1)}, u32[]{:S(2)}, u32[]{:S(2)}) collective-permute-start(bf16[256,2048]{1,0:T(8,128)(2,1)S(1)} %pad_maximum_fusion.3), channel_id=1, source_target_pairs={{0,1},{1,0},{2,3},{3,2},{4,5},{5,4},{6,7},{7,6},{8,9},{9,8},{10,11... | collective-permute-start | bytes 3145736 | tf_op jit(solution)/shard_map/ppermute | solution.py:763
  255.1 22.1 %collective-permute-start.28 = (bf16[128,2048]{1,0:T(8,128)(2,1)}, bf16[128,2048]{1,0:T(8,128)(2,1)}, u32[]{:S(2)}, u32[]{:S(2)}) collective-permute-start(bf16[128,2048]{1,0:T(8,128)(2,1)} %get-tuple-element.487.refs_0_), channel_id=1, source_target_pairs={{0,1},{1,0},{2,3},{3,2},{4,5},{5,4},{6,7},{7,6},{8,9},{9,8},{10,11... | collective-permute-start | bytes 1572872 | tf_op jit(solution)/shard_map/ppermute | solution.py:763
  256.1 23.6 %collective-permute-start.29 = (bf16[128,2048]{1,0:T(8,128)(2,1)}, bf16[128,2048]{1,0:T(8,128)(2,1)}, u32[]{:S(2)}, u32[]{:S(2)}) collective-permute-start(bf16[128,2048]{1,0:T(8,128)(2,1)} %get-tuple-element.486.refs_1_), channel_id=1, source_target_pairs={{0,1},{1,0},{2,3},{3,2},{4,5},{5,4},{6,7},{7,6},{8,9},{9,8},{10,11... | collective-permute-start | bytes 1572872 | tf_op jit(solution)/shard_map/ppermute | solution.py:763
  257.1 22.6 %collective-permute-start.30 = (bf16[128,2048]{1,0:T(8,128)(2,1)}, bf16[128,2048]{1,0:T(8,128)(2,1)}, u32[]{:S(2)}, u32[]{:S(2)}) collective-permute-start(bf16[128,2048]{1,0:T(8,128)(2,1)} %get-tuple-element.487.refs_0_), channel_id=1, source_target_pairs={{0,2},{1,3},{2,0},{3,1},{4,6},{5,7},{6,4},{7,5},{8,10},{9,11},{10,... | collective-permute-start | bytes 1572872 | tf_op jit(solution)/shard_map/ppermute | solution.py:763
  258.1 23.0 %collective-permute-start.31 = (bf16[128,2048]{1,0:T(8,128)(2,1)}, bf16[128,2048]{1,0:T(8,128)(2,1)}, u32[]{:S(2)}, u32[]{:S(2)}) collective-permute-start(bf16[128,2048]{1,0:T(8,128)(2,1)} %get-tuple-element.486.refs_1_), channel_id=1, source_target_pairs={{0,2},{1,3},{2,0},{3,1},{4,6},{5,7},{6,4},{7,5},{8,10},{9,11},{10,... | collective-permute-start | bytes 1572872 | tf_op jit(solution)/shard_map/ppermute | solution.py:763
  281.1 31.0 %collective-permute-start.32 = (bf16[128,2048]{1,0:T(8,128)(2,1)}, bf16[128,2048]{1,0:T(8,128)(2,1)}, u32[]{:S(2)}, u32[]{:S(2)}) collective-permute-start(bf16[128,2048]{1,0:T(8,128)(2,1)} %collective-permute-done.30.refs_2_), channel_id=1, source_target_pairs={{0,1},{1,0},{2,3},{3,2},{4,5},{5,4},{6,7},{7,6},{8,9},{9,8},{10,11... | collective-permute-start | bytes 1572872 | tf_op jit(solution)/shard_map/ppermute | solution.py:763
  282.2 29.9 %collective-permute-start.33 = (bf16[128,2048]{1,0:T(8,128)(2,1)}, bf16[128,2048]{1,0:T(8,128)(2,1)}, u32[]{:S(2)}, u32[]{:S(2)}) collective-permute-start(bf16[128,2048]{1,0:T(8,128)(2,1)} %collective-permute-done.29.refs_1_), channel_id=1, source_target_pairs={{0,2},{1,3},{2,0},{3,1},{4,6},{5,7},{6,4},{7,5},{8,10},{9,11},{10,... | collective-permute-start | bytes 1572872 | tf_op jit(solution)/shard_map/ppermute | solution.py:763
  335.6 185.9 %reduce-scatter.6.cloned.1.call-start = ((), (), s32[]{:S(2)}) async-start(), calls=%async_computation.8 | async-start | bytes 12976128 | tf_op jit(solution)/shard_map/reduce_scatter | solution.py:966
  335.8 22.4 %collective-permute-start.34 = (bf16[256,2048]{1,0:T(8,128)(2,1)}, bf16[256,2048]{1,0:T(8,128)(2,1)}, u32[]{:S(2)}, u32[]{:S(2)}) collective-permute-start(bf16[256,2048]{1,0:T(8,128)(2,1)} %get-tuple-element.301), channel_id=1, source_target_pairs={{0,1},{1,0},{2,3},{3,2},{4,5},{5,4},{6,7},{7,6},{8,9},{9,8},{10,11... | collective-permute-start | bytes 3145736 | tf_op jit(solution)/shard_map/ppermute | solution.py:763
  336.8 22.4 %collective-permute-start.35 = (bf16[256,2048]{1,0:T(8,128)(2,1)}, bf16[256,2048]{1,0:T(8,128)(2,1)}, u32[]{:S(2)}, u32[]{:S(2)}) collective-permute-start(bf16[256,2048]{1,0:T(8,128)(2,1)} %get-tuple-element.302), channel_id=1, source_target_pairs={{0,2},{1,3},{2,0},{3,1},{4,6},{5,7},{6,4},{7,5},{8,10},{9,11},{10,... | collective-permute-start | bytes 3145736 | tf_op jit(solution)/shard_map/ppermute | solution.py:763
  359.3 31.9 %collective-permute-start.36 = (bf16[256,2048]{1,0:T(8,128)(2,1)}, bf16[256,2048]{1,0:T(8,128)(2,1)}, u32[]{:S(2)}, u32[]{:S(2)}) collective-permute-start(bf16[256,2048]{1,0:T(8,128)(2,1)} %get-tuple-element.305), channel_id=1, source_target_pairs={{0,3},{1,2},{2,1},{3,0},{4,7},{5,6},{6,5},{7,4},{8,11},{9,10},{10,... | collective-permute-start | bytes 3145736 | tf_op jit(solution)/shard_map/ppermute | solution.py:763
  391.2 298.8 %all-gather.10.cloned.1.call-start = ((), (), s32[]{:S(2)}) async-start(), calls=%async_computation.10 | async-start | bytes 6488064 | tf_op jit(solution)/shard_map/all_gather | solution.py:993
  397.0 20.0 %collective-permute-start.37 = (bf16[256,2048]{1,0:T(8,128)(2,1)S(1)}, bf16[256,2048]{1,0:T(8,128)(2,1)S(1)}, u32[]{:S(2)}, u32[]{:S(2)}) collective-permute-start(bf16[256,2048]{1,0:T(8,128)(2,1)S(1)} %get-tuple-element.445.refs_4_), channel_id=1, source_target_pairs={{0,1},{1,0},{2,3},{3,2},{4,5},{5,4},{6,7},{7,6},{8,9},{9,8},{10,11... | collective-permute-start | bytes 3145736 | tf_op jit(solution)/shard_map/ppermute | solution.py:763
  398.0 20.0 %collective-permute-start.38 = (bf16[256,2048]{1,0:T(8,128)(2,1)S(1)}, bf16[256,2048]{1,0:T(8,128)(2,1)S(1)}, u32[]{:S(2)}, u32[]{:S(2)}) collective-permute-start(bf16[256,2048]{1,0:T(8,128)(2,1)S(1)} %get-tuple-element.445.refs_4_), channel_id=1, source_target_pairs={{0,2},{1,3},{2,0},{3,1},{4,6},{5,7},{6,4},{7,5},{8,10},{9,11},{10,... | collective-permute-start | bytes 3145736 | tf_op jit(solution)/shard_map/ppermute | solution.py:763
  454.3 251.2 %all-gather.8.cloned.1.call-start = ((), (), s32[]{:S(2)}) async-start(), calls=%async_computation.9 | async-start | bytes 7208960 | tf_op jit(solution)/shard_map/all_gather | solution.py:1018
  476.3 18.1 %collective-permute-start.47 = (bf16[256,512]{1,0:T(8,128)(2,1)}, bf16[256,512]{1,0:T(8,128)(2,1)}, u32[]{:S(2)}, u32[]{:S(2)}) collective-permute-start(bf16[256,512]{1,0:T(8,128)(2,1)} %bitcast.42), channel_id=1, source_target_pairs={{0,1},{1,0},{2,3},{3,2},{4,5},{5,4},{6,7},{7,6},{8,9},{9,8},{10,11... | collective-permute-start | bytes 786440 | tf_op jit(solution)/shard_map/ppermute | solution.py:763
  477.3 20.3 %collective-permute-start.48 = (bf16[256,512]{1,0:T(8,128)(2,1)}, bf16[256,512]{1,0:T(8,128)(2,1)}, u32[]{:S(2)}, u32[]{:S(2)}) collective-permute-start(bf16[256,512]{1,0:T(8,128)(2,1)} %bitcast.43), channel_id=1, source_target_pairs={{0,2},{1,3},{2,0},{3,1},{4,6},{5,7},{6,4},{7,5},{8,10},{9,11},{10,... | collective-permute-start | bytes 786440 | tf_op jit(solution)/shard_map/ppermute | solution.py:763
  479.1 25.9 %collective-permute-start.46 = (bf16[512,512]{1,0:T(8,128)(2,1)}, bf16[512,512]{1,0:T(8,128)(2,1)}, u32[]{:S(2)}, u32[]{:S(2)}) collective-permute-start(bf16[512,512]{1,0:T(8,128)(2,1)} %pad_maximum_fusion.13), channel_id=1, source_target_pairs={{0,2},{1,3},{2,0},{3,1},{4,6},{5,7},{6,4},{7,5},{8,10},{9,11},{10,... | collective-permute-start | bytes 1572872 | tf_op jit(solution)/shard_map/ppermute | solution.py:763
  481.1 23.9 %collective-permute-start.45 = (bf16[512,512]{1,0:T(8,128)(2,1)}, bf16[512,512]{1,0:T(8,128)(2,1)}, u32[]{:S(2)}, u32[]{:S(2)}) collective-permute-start(bf16[512,512]{1,0:T(8,128)(2,1)} %pad_maximum_fusion.12), channel_id=1, source_target_pairs={{0,1},{1,0},{2,3},{3,2},{4,5},{5,4},{6,7},{7,6},{8,9},{9,8},{10,11... | collective-permute-start | bytes 1572872 | tf_op jit(solution)/shard_map/ppermute | solution.py:763
  483.0 19.6 %collective-permute-start.49 = (bf16[128,1024]{1,0:T(8,128)(2,1)}, bf16[128,1024]{1,0:T(8,128)(2,1)}, u32[]{:S(2)}, u32[]{:S(2)}) collective-permute-start(bf16[128,1024]{1,0:T(8,128)(2,1)} %get-tuple-element.501), channel_id=1, source_target_pairs={{0,1},{1,0},{2,3},{3,2},{4,5},{5,4},{6,7},{7,6},{8,9},{9,8},{10,11... | collective-permute-start | bytes 786440 | tf_op jit(solution)/shard_map/ppermute | solution.py:763
  497.5 35.2 %collective-permute-start.59 = (bf16[256,2048]{1,0:T(8,128)(2,1)}, bf16[256,2048]{1,0:T(8,128)(2,1)}, u32[]{:S(2)}, u32[]{:S(2)}) collective-permute-start(bf16[256,2048]{1,0:T(8,128)(2,1)} %get-tuple-element.371), channel_id=1, source_target_pairs={{0,1},{1,0},{2,3},{3,2},{4,5},{5,4},{6,7},{7,6},{8,9},{9,8},{10,11... | collective-permute-start | bytes 3145736 | tf_op jit(solution)/shard_map/ppermute | solution.py:763
  502.6 47.0 %collective-permute-start.60 = (bf16[256,2048]{1,0:T(8,128)(2,1)}, bf16[256,2048]{1,0:T(8,128)(2,1)}, u32[]{:S(2)}, u32[]{:S(2)}) collective-permute-start(bf16[256,2048]{1,0:T(8,128)(2,1)} %get-tuple-element.372), channel_id=1, source_target_pairs={{0,2},{1,3},{2,0},{3,1},{4,6},{5,7},{6,4},{7,5},{8,10},{9,11},{10,... | collective-permute-start | bytes 3145736 | tf_op jit(solution)/shard_map/ppermute | solution.py:763
  503.6 48.9 %collective-permute-start.61 = (bf16[256,2048]{1,0:T(8,128)(2,1)}, bf16[256,2048]{1,0:T(8,128)(2,1)}, u32[]{:S(2)}, u32[]{:S(2)}) collective-permute-start(bf16[256,2048]{1,0:T(8,128)(2,1)} %get-tuple-element.373), channel_id=1, source_target_pairs={{0,3},{1,2},{2,1},{3,0},{4,7},{5,6},{6,5},{7,4},{8,11},{9,10},{10,... | collective-permute-start | bytes 3145736 | tf_op jit(solution)/shard_map/ppermute | solution.py:763
  527.4 26.9 %collective-permute-start.51 = (bf16[128,512]{1,0:T(8,128)(2,1)S(1)}, bf16[128,512]{1,0:T(8,128)(2,1)S(1)}, u32[]{:S(2)}, u32[]{:S(2)}) collective-permute-start(bf16[128,512]{1,0:T(8,128)(2,1)S(1)} %get-tuple-element.499), channel_id=1, source_target_pairs={{8,0},{12,4},{16,8},{20,12},{24,16},{28,20},{9,1},{13,5},{17,9},{2... | collective-permute-start | bytes 393224 | tf_op jit(solution)/shard_map/ppermute | solution.py:1025
  528.9 50.0 %collective-permute-start.58 = (bf16[1024,512]{1,0:T(8,128)(2,1)}, bf16[1024,512]{1,0:T(8,128)(2,1)}, u32[]{:S(2)}, u32[]{:S(2)}) collective-permute-start(bf16[1024,512]{1,0:T(8,128)(2,1)} %get-tuple-element.369), channel_id=1, source_target_pairs={{0,4},{4,0},{8,12},{12,8},{16,20},{20,16},{24,28},{28,24},{1,5},{5... | collective-permute-start | bytes 3145736 | tf_op jit(solution)/shard_map/core_swap/ppermute | solution.py:767
  532.7 22.5 %collective-permute-start.52 = (bf16[128,512]{1,0:T(8,128)(2,1)S(1)}, bf16[128,512]{1,0:T(8,128)(2,1)S(1)}, u32[]{:S(2)}, u32[]{:S(2)}) collective-permute-start(bf16[128,512]{1,0:T(8,128)(2,1)S(1)} %get-tuple-element.498), channel_id=1, source_target_pairs={{16,0},{20,4},{24,8},{28,12},{17,1},{21,5},{25,9},{29,13},{18,2},{... | collective-permute-start | bytes 393224 | tf_op jit(solution)/shard_map/ppermute | solution.py:1025
  549.6 19.7 %collective-permute-start.53 = (bf16[128,512]{1,0:T(8,128)(2,1)S(1)}, bf16[128,512]{1,0:T(8,128)(2,1)S(1)}, u32[]{:S(2)}, u32[]{:S(2)}) collective-permute-start(bf16[128,512]{1,0:T(8,128)(2,1)S(1)} %get-tuple-element.497), channel_id=1, source_target_pairs={{24,0},{28,4},{25,1},{29,5},{26,2},{30,6},{27,3},{31,7}} | collective-permute-start | bytes 393224 | tf_op jit(solution)/shard_map/ppermute | solution.py:1025
  552.6 23.5 %collective-permute-start.57 = (bf16[256,1024]{1,0:T(8,128)(2,1)}, bf16[256,1024]{1,0:T(8,128)(2,1)}, u32[]{:S(2)}, u32[]{:S(2)}) collective-permute-start(bf16[256,1024]{1,0:T(8,128)(2,1)} %pad_maximum_fusion.17), channel_id=1, source_target_pairs={{0,2},{1,3},{2,0},{3,1},{4,6},{5,7},{6,4},{7,5},{8,10},{9,11},{10,... | collective-permute-start | bytes 1572872 | tf_op jit(solution)/shard_map/ppermute | solution.py:763
  554.3 21.7 %collective-permute-start.56 = (bf16[256,1024]{1,0:T(8,128)(2,1)}, bf16[256,1024]{1,0:T(8,128)(2,1)}, u32[]{:S(2)}, u32[]{:S(2)}) collective-permute-start(bf16[256,1024]{1,0:T(8,128)(2,1)} %pad_maximum_fusion.16), channel_id=1, source_target_pairs={{0,1},{1,0},{2,3},{3,2},{4,5},{5,4},{6,7},{7,6},{8,9},{9,8},{10,11... | collective-permute-start | bytes 1572872 | tf_op jit(solution)/shard_map/ppermute | solution.py:763
  555.3 21.7 %collective-permute-start.55 = (bf16[512,512]{1,0:T(8,128)(2,1)}, bf16[512,512]{1,0:T(8,128)(2,1)}, u32[]{:S(2)}, u32[]{:S(2)}) collective-permute-start(bf16[512,512]{1,0:T(8,128)(2,1)} %pad_maximum_fusion.15), channel_id=1, source_target_pairs={{0,2},{1,3},{2,0},{3,1},{4,6},{5,7},{6,4},{7,5},{8,10},{9,11},{10,... | collective-permute-start | bytes 1572872 | tf_op jit(solution)/shard_map/ppermute | solution.py:763
  582.9 42.6 %collective-permute-start.65 = (bf16[256,1024]{1,0:T(8,128)(2,1)}, bf16[256,1024]{1,0:T(8,128)(2,1)}, u32[]{:S(2)}, u32[]{:S(2)}) collective-permute-start(bf16[256,1024]{1,0:T(8,128)(2,1)} %subtract_convert_fusion.refs_4_), channel_id=1, source_target_pairs={{0,1},{1,0},{2,3},{3,2},{4,5},{5,4},{6,7},{7,6},{8,9},{9,8},{10,11... | collective-permute-start | bytes 1572872 | tf_op jit(solution)/shard_map/ppermute | solution.py:763
  584.4 41.2 %collective-permute-start.66 = (bf16[256,1024]{1,0:T(8,128)(2,1)}, bf16[256,1024]{1,0:T(8,128)(2,1)}, u32[]{:S(2)}, u32[]{:S(2)}) collective-permute-start(bf16[256,1024]{1,0:T(8,128)(2,1)} %subtract_convert_fusion.refs_4_), channel_id=1, source_target_pairs={{0,2},{1,3},{2,0},{3,1},{4,6},{5,7},{6,4},{7,5},{8,10},{9,11},{10,... | collective-permute-start | bytes 1572872 | tf_op jit(solution)/shard_map/ppermute | solution.py:763
  586.3 19.0 %all-to-all-start.2 = ((bf16[256,4,512]{2,0,1:T(8,128)(2,1)}), bf16[256,4,512]{2,0,1:T(8,128)(2,1)}, u32[]{:S(2)}, u32[]{:S(2)}) async-start(bf16[256,4,512]{2,0,1:T(8,128)(2,1)} %bitcast.205), calls=%async_computation.4 | async-start | bytes 2097152 | tf_op jit(solution)/shard_map/all_to_all | solution.py:1045
  594.2 17.6 %collective-permute-start.62 = (bf16[128,512]{1,0:T(8,128)(2,1)}, bf16[128,512]{1,0:T(8,128)(2,1)}, u32[]{:S(2)}, u32[]{:S(2)}) collective-permute-start(bf16[128,512]{1,0:T(8,128)(2,1)} %get-tuple-element.496), channel_id=1, source_target_pairs={{8,0},{12,4},{16,8},{20,12},{24,16},{28,20},{9,1},{13,5},{17,9},{2... | collective-permute-start | bytes 393224 | tf_op jit(solution)/shard_map/ppermute | solution.py:1025
  595.5 30.1 %collective-permute-start.63 = (bf16[128,512]{1,0:T(8,128)(2,1)}, bf16[128,512]{1,0:T(8,128)(2,1)}, u32[]{:S(2)}, u32[]{:S(2)}) collective-permute-start(bf16[128,512]{1,0:T(8,128)(2,1)} %get-tuple-element.495), channel_id=1, source_target_pairs={{16,0},{20,4},{24,8},{28,12},{17,1},{21,5},{25,9},{29,13},{18,2},{... | collective-permute-start | bytes 393224 | tf_op jit(solution)/shard_map/ppermute | solution.py:1025
  596.8 28.8 %collective-permute-start.64 = (bf16[128,512]{1,0:T(8,128)(2,1)}, bf16[128,512]{1,0:T(8,128)(2,1)}, u32[]{:S(2)}, u32[]{:S(2)}) collective-permute-start(bf16[128,512]{1,0:T(8,128)(2,1)} %get-tuple-element.494), channel_id=1, source_target_pairs={{24,0},{28,4},{25,1},{29,5},{26,2},{30,6},{27,3},{31,7}} | collective-permute-start | bytes 393224 | tf_op jit(solution)/shard_map/ppermute | solution.py:1025
  605.3 54.9 %all-to-all-start.3 = ((bf16[4,256,512]{2,1,0:T(8,128)(2,1)}), bf16[4,256,512]{2,1,0:T(8,128)(2,1)}, u32[]{:S(2)}, u32[]{:S(2)}) async-start(bf16[4,256,512]{2,1,0:T(8,128)(2,1)} %bitcast.204), calls=%async_computation.5 | async-start | bytes 2097152 | tf_op jit(solution)/shard_map/all_to_all | solution.py:1052
  609.5 184.3 %reduce-scatter.8.cloned.1.call-start = ((), (), s32[]{:S(2)}) async-start(), calls=%async_computation.11 | async-start | bytes 9142272 | tf_op jit(solution)/shard_map/reduce_scatter | solution.py:1114
  690.1 183.7 %all-gather.12.cloned.1.call-start = ((), (), s32[]{:S(2)}) async-start(), calls=%async_computation.12 | async-start | bytes 9142272 | tf_op jit(solution)/shard_map/all_gather | solution.py:1123
  709.6 34.4 %collective-permute-start.67 = (bf16[256,2816]{1,0:T(8,128)(2,1)S(1)}, bf16[256,2816]{1,0:T(8,128)(2,1)S(1)}, u32[]{:S(2)}, u32[]{:S(2)}) collective-permute-start(bf16[256,2816]{1,0:T(8,128)(2,1)S(1)} %get-tuple-element.454), channel_id=1, source_target_pairs={{0,1},{1,0},{2,3},{3,2},{4,5},{5,4},{6,7},{7,6},{8,9},{9,8},{10,11... | collective-permute-start | bytes 4325384 | tf_op jit(solution)/shard_map/ppermute | solution.py:763
  711.3 64.2 %collective-permute-start.68 = (bf16[256,2816]{1,0:T(8,128)(2,1)S(1)}, bf16[256,2816]{1,0:T(8,128)(2,1)S(1)}, u32[]{:S(2)}, u32[]{:S(2)}) collective-permute-start(bf16[256,2816]{1,0:T(8,128)(2,1)S(1)} %get-tuple-element.453), channel_id=1, source_target_pairs={{0,2},{1,3},{2,0},{3,1},{4,6},{5,7},{6,4},{7,5},{8,10},{9,11},{10,... | collective-permute-start | bytes 4325384 | tf_op jit(solution)/shard_map/ppermute | solution.py:763
  712.7 63.8 %collective-permute-start.69 = (bf16[256,2816]{1,0:T(8,128)(2,1)S(1)}, bf16[256,2816]{1,0:T(8,128)(2,1)}, u32[]{:S(2)}, u32[]{:S(2)}) collective-permute-start(bf16[256,2816]{1,0:T(8,128)(2,1)S(1)} %get-tuple-element.452), channel_id=1, source_target_pairs={{0,3},{1,2},{2,1},{3,0},{4,7},{5,6},{6,5},{7,4},{8,11},{9,10},{10,... | collective-permute-start | bytes 4325384 | tf_op jit(solution)/shard_map/ppermute | solution.py:763
  793.9 16.6 %collective-permute-start.76 = (bf16[256,2816]{1,0:T(8,128)(2,1)}, bf16[256,2816]{1,0:T(8,128)(2,1)}, u32[]{:S(2)}, u32[]{:S(2)}) collective-permute-start(bf16[256,2816]{1,0:T(8,128)(2,1)} %get-tuple-element.420.refs_0_), channel_id=1, source_target_pairs={{0,4},{4,0},{8,12},{12,8},{16,20},{20,16},{24,28},{28,24},{1,5},{5... | collective-permute-start | bytes 4325384 | tf_op jit(solution)/shard_map/core_swap/ppermute | solution.py:767
  794.0 16.5 %collective-permute-start.77 = (bf16[256,2816]{1,0:T(8,128)(2,1)}, bf16[256,2816]{1,0:T(8,128)(2,1)}, u32[]{:S(2)}, u32[]{:S(2)}) collective-permute-start(bf16[256,2816]{1,0:T(8,128)(2,1)} %copy-done.39), channel_id=1, source_target_pairs={{0,4},{4,0},{8,12},{12,8},{16,20},{20,16},{24,28},{28,24},{1,5},{5... | collective-permute-start | bytes 4325384 | tf_op jit(solution)/shard_map/core_swap/ppermute | solution.py:767
  794.5 16.0 %collective-permute-start.78 = (bf16[256,2816]{1,0:T(8,128)(2,1)}, bf16[256,2816]{1,0:T(8,128)(2,1)}, u32[]{:S(2)}, u32[]{:S(2)}) collective-permute-start(bf16[256,2816]{1,0:T(8,128)(2,1)} %copy-done.40), channel_id=1, source_target_pairs={{0,4},{4,0},{8,12},{12,8},{16,20},{20,16},{24,28},{28,24},{1,5},{5... | collective-permute-start | bytes 4325384 | tf_op jit(solution)/shard_map/core_swap/ppermute | solution.py:767
  (130 other events, 1067.4 us)
Sparse Core Ops, SparseCore 0:
  22.2 29.0 all-gather.13
  101.4 108.3 all-gather.15
  335.7 65.3 reduce-scatter.3
  403.8 117.6 reduce-scatter.5
  523.0 67.5 all-gather.9
  592.0 113.4 all-gather.7
  708.4 85.4 reduce-scatter.7
  795.5 78.2 all-gather.11
